TPU v7x, 32 devices: a whole 2x2x4 slice. The times are simulated.
32 devices in a mesh: segment: 2 (over x), blk: 4 (over z), mp: 4 (over y, core).
Axes of the slice: x: 2, y: 2, z: 4, core: 2. Of those that a mesh axis runs over, the one named last changes fastest.
Arguments:
- segment_in: bfloat16 [2, 1024, 4096], P('segment', 'blk'), may hold values from -7.5 to 7.5
- norm_gains: float32 [2, 4096], P('segment'), may hold values from 0.25 to 1.75
- projections: bfloat16 [2, 4096, 2, 2048], P('segment', None, None, 'mp'), may hold values from -2 to 2
- live_counts: int32 [2, 4], P(None, 'blk'), may hold values from 1 to 256, 768 in all within a row
- cotangent: bfloat16 [1024, 4096], P('blk', 'mp'), may hold values from -6 to 6
Outputs:
- segment_out: bfloat16 [2, 1024, 4096], P('segment', 'blk', 'mp')
- state_grads: bfloat16 [2, 1024, 4096], P('segment', 'blk', 'mp')
Inputs may be any that keep to these rules, and one draw needn't show every extreme that they name: `live_counts`: each row sums to 768; every entry is at least 1; each row has an entry equal to 256.
All inputs are finite; a program needn't handle non-finite values. No bound on the sum of `live_counts` on one device may be relied on, other than what follows from the above.
Results may differ from a plain program's by a relative error of at most 0.015.
Values may be sent and summed in bfloat16 or wider, within the bound.
No kernel may reach another device: no remote copies, remote signals or barrier semaphores. Data moves between devices by JAX's collectives and lax.ppermute only.
A program may use at most 128 MiB of HBM per device.

v0:
```python
import functools

import jax
import jax.numpy as jnp
from jax import lax
from jax.experimental import pallas as pl
from jax.experimental.pallas import tpu as pltpu
from jax.sharding import PartitionSpec as P


DH = 64
WIN = 4


EPSILON = 1e-06
SCALE = 0.125
NEGATIVE = -1e30
LANES = 128
TAIL = 16
AXES = ("segment", "blk", "mp")

F32 = jnp.float32
BF16 = jnp.bfloat16


def from_behind(x, axis, by):
    size = lax.axis_size(axis)
    pairs = [(i, i + by) for i in range(size) if 0 <= i + by < size]
    return lax.ppermute(x, axis, pairs)


def normalize(states, gain_row):
    widened = states.astype(jnp.float32)
    spread = jnp.sqrt(jnp.mean(widened * widened, axis=-1, keepdims=True) + EPSILON)
    return ((widened / spread * gain_row).astype(jnp.bfloat16), spread)


def right_product(left, right):
    return lax.dot_general(
        left, right, (((1,), (1,)), ((), ())), preferred_element_type=jnp.float32
    )


def per_device_windows(segment_in, norm_gains, projections, live_counts, cotangent):
    segment_pos = lax.axis_index("segment")
    model_index = lax.axis_index("mp")
    states = segment_in[0]
    gain_row = norm_gains[0]
    row_count, full_width = states.shape
    feature_width = cotangent.shape[1]
    w_primary = projections[0, :, 0, :]
    w_secondary = projections[0, :, 1, :]
    group_width = w_primary.shape[1]
    group_heads = group_width // DH
    normed, spread = normalize(states, gain_row)
    primary = jnp.dot(normed, w_primary, preferred_element_type=jnp.float32).astype(jnp.bfloat16)
    secondary = lax.cond(
        segment_pos == 0,
        lambda: jnp.dot(normed, w_secondary, preferred_element_type=jnp.float32).astype(
            jnp.bfloat16
        ),
        lambda: jnp.zeros_like(primary),
    )
    doc_keys, doc_values = from_behind((primary, secondary), "segment", 1)
    own_block = (doc_keys, doc_values, live_counts[0])
    window = [own_block]
    moving = own_block
    for _ in range(1, WIN):
        moving = from_behind((moving[0], moving[1], moving[2]), "blk", 1)
        window.append(moving)
    position = jnp.arange(row_count, dtype=jnp.int32)
    all_keys = jnp.concatenate([piece[0] for piece in window], 0).reshape(
        WIN * row_count, group_heads, DH
    )
    all_values = jnp.concatenate([piece[1] for piece in window], 0).reshape(
        WIN * row_count, group_heads, DH
    )
    key_live = jnp.concatenate([position < piece[2][0] for piece in window], 0)
    query_live = position < live_counts[1][0]
    query_heads = primary.reshape(row_count, group_heads, DH)
    scores = (
        jnp.einsum("qhd,khd->hqk", query_heads, all_keys, preferred_element_type=jnp.float32)
        * SCALE
    )
    scores = jnp.where(key_live[None, None, :], scores, NEGATIVE)
    row_max = jnp.max(scores, axis=-1, keepdims=True)
    expo = jnp.exp(scores - row_max)
    row_total = jnp.sum(expo, axis=-1, keepdims=True)
    softmax_out = expo / row_total
    weights_low = softmax_out.astype(jnp.bfloat16)
    attended = jnp.einsum(
        "hqk,khd->qhd", weights_low, all_values, preferred_element_type=jnp.float32
    ).astype(jnp.bfloat16)
    attended = jnp.where(query_live[:, None, None], attended, jnp.zeros_like(attended)).reshape(
        row_count, group_width
    )
    projected = lax.cond(
        segment_pos == 1,
        lambda: right_product(attended, w_secondary),
        lambda: jnp.zeros((row_count, full_width), jnp.float32),
    )
    layer_out = lax.psum_scatter(
        projected.astype(jnp.bfloat16), "mp", scatter_dimension=1, tiled=True
    )
    own_normed = lax.dynamic_slice_in_dim(normed, model_index * feature_width, feature_width, 1)
    segment_out = jnp.where(segment_pos == 0, own_normed, layer_out)[None]
    grad_out = jnp.dot(
        lax.all_gather(cotangent, "mp", axis=1, tiled=True),
        w_secondary,
        preferred_element_type=jnp.float32,
    )
    grad_out = grad_out.astype(jnp.bfloat16)
    grad_out = jnp.where(query_live[:, None], grad_out, jnp.zeros_like(grad_out))
    grad_heads = grad_out.reshape(row_count, group_heads, DH)
    grad_probs = jnp.einsum(
        "qhd,khd->hqk", grad_heads, all_values, preferred_element_type=jnp.float32
    )
    row_delta = jnp.sum(softmax_out * grad_probs, axis=-1, keepdims=True)
    grad_scores = (softmax_out * (grad_probs - row_delta)).astype(jnp.bfloat16)
    grad_queries = (
        (
            SCALE
            * jnp.einsum("hqk,khd->qhd", grad_scores, all_keys, preferred_element_type=jnp.float32)
        )
        .astype(jnp.bfloat16)
        .reshape(row_count, group_width)
    )
    key_parts = (
        SCALE
        * jnp.einsum("hqk,qhd->khd", grad_scores, query_heads, preferred_element_type=jnp.float32)
    ).reshape(WIN, row_count, group_width)
    value_parts = jnp.einsum(
        "hqk,qhd->khd", weights_low, grad_heads, preferred_element_type=jnp.float32
    ).reshape(WIN, row_count, group_width)
    key_total = key_parts[WIN - 1]
    value_total = value_parts[WIN - 1]
    for offset in range(WIN - 2, -1, -1):
        arrived = (
            from_behind(key_total.astype(jnp.bfloat16), "blk", -1).astype(key_total.dtype),
            from_behind(value_total.astype(jnp.bfloat16), "blk", -1).astype(value_total.dtype),
        )
        key_total = arrived[0] + key_parts[offset]
        value_total = arrived[1] + value_parts[offset]
    grad_keys = key_total.astype(jnp.bfloat16)
    grad_values = value_total.astype(jnp.bfloat16)
    back_keys, back_values = from_behind((grad_keys, grad_values), "segment", -1)
    partial_grad = lax.cond(
        segment_pos == 0,
        lambda: right_product(back_keys, w_primary) + right_product(back_values, w_secondary),
        lambda: right_product(grad_queries, w_primary),
    )
    widened = states.astype(jnp.float32)
    summed = lax.psum_scatter(
        partial_grad.astype(jnp.bfloat16), "mp", scatter_dimension=1, tiled=True
    ).astype(jnp.float32)
    own_states = lax.dynamic_slice_in_dim(widened, model_index * feature_width, feature_width, 1)
    own_gain = lax.dynamic_slice_in_dim(gain_row, model_index * feature_width, feature_width, 0)
    row_term = lax.psum(jnp.sum(summed * own_gain * own_states, axis=-1, keepdims=True), "mp")
    input_grad = (
        own_gain * summed / spread - own_states * row_term / (full_width * spread**3)
    ).astype(jnp.bfloat16)
    return (segment_out, input_grad[None])


def place(sizes):
    seg = lax.axis_index("segment")
    return seg, seg * sizes[1] + lax.axis_index("blk"), lax.axis_index("mp")


def enter_kernel(sizes, states, gain, w, *rest):
    n_mp = sizes[2]
    wp, ws = rest[0], rest[1 : 1 + n_mp]
    own, own_states, own_gain, spread, prim, sec = rest[1 + n_mp : 7 + n_mp]
    xbuf, gbuf, wbuf, normed, pacc, sacc, sems, ready = rest[7 + n_mp :]
    seg, _, model = place(sizes)
    rows, width = xbuf.shape
    depth = width // n_mp
    tiles = wp.shape[2] // LANES
    pack = 2 * tiles
    group = 2 * LANES // pack
    lines = depth * pack
    first_copies = [
        pltpu.make_async_copy(states, xbuf, ready.at[0]),
        pltpu.make_async_copy(gain, gbuf, ready.at[1]),
    ]
    copies = []
    for c in range(n_mp):
        start = pl.multiple_of(jnp.bitwise_xor(model, c) * lines, lines)
        copies.append(
            pltpu.make_async_copy(
                w.at[pl.ds(start, lines), :], wbuf.at[pl.ds(c * lines, lines), :], sems.at[c]
            )
        )
    for copy in first_copies + copies:
        copy.start()
    here = lax.broadcasted_iota(jnp.int32, (2 * LANES, 2 * LANES), 0)
    there = lax.broadcasted_iota(jnp.int32, (2 * LANES, 2 * LANES), 1)
    source = pack * lax.rem(here, group) + lax.div(here, group)
    mix = jnp.where(there == source, 1.0, 0.0).astype(BF16)
    for copy in first_copies:
        copy.wait()
    part_rows = 32

    def norm_rows(at, _):
        line = pl.ds(pl.multiple_of(at * part_rows, part_rows), part_rows)
        wide = xbuf[line, :].astype(F32)
        mean = jnp.sum(wide * wide, axis=1, keepdims=True) * (1.0 / width)
        root = jnp.sqrt(mean + EPSILON)
        normed[line, :] = (wide * (1.0 / root) * gbuf[...]).astype(BF16)
        spread[line, :] = jnp.broadcast_to(root, (part_rows, LANES))
        return 0

    lax.fori_loop(0, rows // part_rows, norm_rows, 0)
    for c in range(n_mp):
        copies[c].wait()
        for pair in range(depth // (2 * group)):
            base = c * lines + pair * 4 * LANES
            left = wbuf[base : base + 2 * LANES, :]
            right = wbuf[base + 2 * LANES : base + 4 * LANES, :]
            both = jnp.concatenate([left, right], axis=1)
            ordered = jnp.dot(mix, both, preferred_element_type=F32).astype(BF16)
            first = 2 * pair * group
            for slot in range(pack):
                target = (wp.at[c], ws[c])[slot % 2]
                tile = slice(slot // 2 * LANES, (slot // 2 + 1) * LANES)
                part = ordered[slot * group : (slot + 1) * group, :]
                target[first : first + group, tile] = part[:, :LANES]
                target[first + group : first + 2 * group, tile] = part[:, LANES:]
        span = pl.ds(pl.multiple_of(jnp.bitwise_xor(model, c) * depth, depth), depth)
        term = jnp.dot(normed[:, span], wp[c], preferred_element_type=F32)
        if c == 0:
            pacc[...] = term
        else:
            pacc[...] += term

        @pl.when(seg == 0)
        def _():
            other = jnp.dot(normed[:, span], ws[c][...], preferred_element_type=F32)
            if c == 0:
                sacc[...] = other
            else:
                sacc[...] += other

    prim[...] = pacc[...].astype(BF16)

    @pl.when(seg == 0)
    def _():
        sec[...] = sacc[...].astype(BF16)

    mine = pl.ds(pl.multiple_of(model * depth, depth), depth)
    own[...] = normed[:, mine]
    own_states[...] = xbuf[:, mine]
    own_gain[...] = gbuf[:, mine]


def part_kernel(c0, c1, c2, w0, w1, w2, acc):
    @pl.when(lax.axis_index("segment") == 1)
    def _():
        acc[...] = jnp.dot(c0[...], w0[...], preferred_element_type=F32)
        acc[...] += jnp.dot(c1[...], w1[...], preferred_element_type=F32)
        acc[...] += jnp.dot(c2[...], w2[...], preferred_element_type=F32)


def pack_kernel(sizes, counts, prim, sec, acc, c3, w3, *rest):
    heads = sizes[0] * sizes[1]
    second, outs = rest[0], rest[1:]
    seg, entry, _ = place(sizes)
    rows = prim.shape[0]

    @pl.when(seg == 0)
    def _():
        second[...] = sec[...]

    @pl.when(seg == 1)
    def _():
        total = acc[...] + jnp.dot(c3[...], w3[...], preferred_element_type=F32)
        line = lax.broadcasted_iota(jnp.int32, acc.shape, 0)
        second[...] = jnp.where(line < counts[0, 1], total, 0.0).astype(BF16)

    tail = jnp.full((TAIL, LANES), 1.0, F32) * counts[0, 0].astype(F32)
    for head in range(heads):
        cols = slice(head * DH, (head + 1) * DH)
        pair = jnp.concatenate([prim[:, cols], second[:, cols]], axis=1)
        for k, out in enumerate(outs):

            @pl.when(jnp.bitwise_xor(entry, k) == head)
            def _():
                out[:rows, :] = pair
                out[rows:, :] = tail.astype(BF16)


def live_keys(piece, rows):
    position = lax.broadcasted_iota(jnp.int32, (1, rows), 1).astype(F32)
    count = piece[rows : rows + 1, :].astype(F32)
    return position < jnp.concatenate([count] * (rows // LANES), axis=1)


def attend_kernel(sizes, *rest):
    heads = sizes[0] * sizes[1]
    blocks = sizes[1]
    ins, outs = rest[:heads], rest[heads : 2 * heads]
    parts, back, totals = rest[2 * heads :]
    _, entry, _ = place(sizes)
    rows = outs[0].shape[0]
    for k, piece in enumerate(ins):
        parts[jnp.bitwise_xor(entry, k)] = piece[...]
    low = lax.broadcasted_iota(jnp.int32, (rows, LANES), 1) < DH
    zero = jnp.zeros((rows, LANES), BF16)
    live = [live_keys(parts[j], rows) for j in range(blocks)]
    for i in range(blocks):
        both = parts[blocks + i, :rows, :]
        query = jnp.where(low, both * BF16(SCALE), zero)
        grad = jnp.where(low, zero, both)
        flip_query = query.astype(F32).T.astype(BF16)
        flip_grad = grad.astype(F32).T.astype(BF16)
        scores = []
        for j in range(i + 1):
            product = right_product(query, parts[j, :rows, :])
            scores.append(jnp.where(live[j], product, NEGATIVE))
        top = jnp.max(functools.reduce(jnp.maximum, scores), axis=1, keepdims=True)
        expo = [jnp.exp(s - top) for s in scores]
        total = jnp.sum(functools.reduce(jnp.add, expo), axis=1, keepdims=True)
        share = 1.0 / total
        probs = [e * share for e in expo]
        slopes = [right_product(grad, parts[j, :rows, :]) for j in range(i + 1)]
        delta = functools.reduce(jnp.add, [p * g for p, g in zip(probs, slopes)])
        delta = jnp.sum(delta, axis=1, keepdims=True)
        out = jnp.zeros((rows, LANES), F32)
        other = jnp.zeros((rows, LANES), F32)
        for j in range(i + 1):
            prob = probs[j].astype(BF16)
            slope = (probs[j] * (slopes[j] - delta)).astype(BF16)
            other += jnp.dot(slope, parts[j, :rows, :], preferred_element_type=F32)
            out += jnp.dot(prob, parts[j, :rows, :], preferred_element_type=F32)
            tall = jnp.dot(flip_query, slope, preferred_element_type=F32)
            tall += jnp.dot(flip_grad, prob, preferred_element_type=F32)
            if i == j:
                totals[j] = tall
            else:
                totals[j] += tall
        back[blocks + i] = jnp.where(low, other * SCALE, out).astype(BF16)
    for j in range(blocks):
        back[j] = totals[j].T.astype(BF16)
    for k, out in enumerate(outs):
        out[...] = back[jnp.bitwise_xor(entry, k)]


def split_rows(column):
    row = jnp.broadcast_to(column, (column.shape[0], LANES)).T[:TAIL, :]
    high = row.astype(BF16).astype(F32)
    line = lax.broadcasted_iota(jnp.int32, row.shape, 0)
    return jnp.where(line == 0, high, row - high).astype(BF16)


def regroup_kernel(sizes, counts, *rest):
    heads = sizes[0] * sizes[1]
    ins, (lp, ls, parts) = rest[:heads], rest[heads:]
    seg, entry, _ = place(sizes)
    rows = lp.shape[0]
    for k, piece in enumerate(ins):
        parts[jnp.bitwise_xor(entry, k)] = piece[...]
    line = lax.broadcasted_iota(jnp.int32, (rows, DH), 0)
    alive = line < jnp.where(seg == 0, rows, counts[0, 1])
    for head in range(heads):
        cols = slice(head * DH, (head + 1) * DH)
        lp[:, cols] = parts[head, :, :DH]
        ls[:, cols] = jnp.where(alive, parts[head, :, DH:].astype(F32), 0.0).astype(BF16)


def project_block(seg, wp, ws, lp, ls, out, slot):
    rows = lp.shape[0]

    @pl.when(seg == 0)
    def _():
        total = right_product(lp[...], wp) + right_product(ls[...], ws)
        out[slot, :rows, :] = total.astype(BF16)

    @pl.when(seg == 1)
    def _():
        out[slot, :rows, :] = right_product(lp[...], wp).astype(BF16)


def send_kernel(sizes, lp, ls, prim, second, spread, wp, w3, w1, sent):
    seg, _, _ = place(sizes)
    rows, feats = prim.shape[0], sent.shape[2]
    project_block(seg, wp[3], w3[...], lp, ls, sent, 0)
    project_block(seg, wp[1], w1[...], lp, ls, sent, 1)
    term = lp[...].astype(F32) * prim[...].astype(F32)
    also = ls[...].astype(F32) * second[...].astype(F32)
    term = term + jnp.where(seg == 0, also, 0.0)
    column = jnp.sum(term, axis=1, keepdims=True) * spread[:, :1]
    sent[0, rows:, :] = jnp.zeros((TAIL, feats), BF16)
    sent[1, rows:, :] = jnp.zeros((TAIL, feats), BF16)
    sent[0, rows:, :rows] = split_rows(column)


def keep_kernel(sizes, lp, ls, wp, w2, w0, kept):
    seg, _, _ = place(sizes)
    project_block(seg, wp[2], w2[...], lp, ls, kept, 0)
    project_block(seg, wp[0], w0[...], lp, ls, kept, 1)


def layer_kernel(a0, a1, a2, a3, w0, w1, w2, w3, own, out, obuf, sem):
    seg = lax.axis_index("segment")

    @pl.when(seg == 0)
    def _():
        obuf[...] = own[...]

    @pl.when(seg == 1)
    def _():
        total = right_product(a0[...], w0[...])
        for a, w in ((a1, w1), (a2, w2), (a3, w3)):
            total += right_product(a[...], w[...])
        obuf[...] = total.astype(BF16)

    leaving = pltpu.make_async_copy(obuf, out, sem)
    leaving.start()
    leaving.wait()


def fold_kernel(kept, got, sent, out):
    rows = kept.shape[1]
    out[:rows, :] = (kept[0].astype(F32) + got[0, :rows, :].astype(F32)).astype(BF16)
    mine = sent[0, rows:, :].astype(F32)
    theirs = got[0, rows:, :].astype(F32)
    total = mine[0:1] + mine[1:2] + theirs[0:1] + theirs[1:2]
    total = jnp.broadcast_to(total, mine.shape)
    high = total.astype(BF16).astype(F32)
    line = lax.broadcasted_iota(jnp.int32, mine.shape, 0)
    out[rows:, :] = jnp.where(line == 0, high, total - high).astype(BF16)


ANYWHERE = pl.BlockSpec(memory_space=pltpu.HBM)
INSIDE = pl.BlockSpec(memory_space=pltpu.VMEM)
SCALARS = pl.BlockSpec(memory_space=pltpu.SMEM)


def call(body, ins, specs, outs, scratch=(), limit=16, flops=0, out_specs=None):
    inside = out_specs is None
    ins = [
        pltpu.with_memory_space_constraint(x, pltpu.HBM) if spec is ANYWHERE else x
        for x, spec in zip(ins, specs)
    ]
    return pl.pallas_call(
        body,
        in_specs=list(specs),
        out_specs=[INSIDE] * len(outs) if inside else out_specs,
        out_shape=[(pltpu.VMEM if inside else jax.ShapeDtypeStruct)(s, d) for s, d in outs],
        scratch_shapes=list(scratch),
        compiler_params=pltpu.CompilerParams(vmem_limit_bytes=limit << 20),
        cost_estimate=pl.CostEstimate(flops=flops, transcendentals=0, bytes_accessed=1 << 20),
    )(*ins)


def leave_kernel(width, kept, got, half, far, states, gain, spread, grad):
    rows = states.shape[0]
    ends = half[rows:, :].astype(F32) + far[rows:, :].astype(F32)
    row = jnp.broadcast_to(ends[0:1, :rows] + ends[1:2, :rows], (LANES, rows))
    term = row.T[:, :1]
    root = spread[:, :1]
    scaled = term / (width * root * root * root)
    total = kept[1].astype(F32) + got[1, :rows, :].astype(F32) + far[:rows, :].astype(F32)
    grad[...] = (gain[...] * total * (1.0 / root) - states[...].astype(F32) * scaled).astype(BF16)


def per_device_heads(sizes, segment_in, norm_gains, projections, live_counts, cotangent):
    n_seg, n_blk, n_mp = sizes
    heads = n_seg * n_blk
    states = segment_in[0]
    rows, width = states.shape
    feats = cotangent.shape[1]
    group = projections.shape[3]
    counts = live_counts.T

    def swap(x, over_heads, over_mp, least=0):
        pairs = [
            (e * n_mp + m, (e ^ over_heads) * n_mp + (m ^ over_mp))
            for e in range(least * n_blk, heads)
            for m in range(n_mp)
        ]
        return lax.ppermute(x, AXES, pairs)

    def exchange(pieces):
        far_first = sorted(range(1, heads), key=lambda k: -((k % n_blk) * 2 + 1 - k // n_blk))
        moved = {k: swap(pieces[k], k, 0) for k in far_first}
        return [pieces[0]] + [moved[k] for k in range(1, heads)]

    far_cot = swap(cotangent, 0, 2, 1)
    tiles = group // LANES
    mixed = projections.reshape(width, 2, tiles, LANES).transpose(0, 2, 1, 3)
    mixed = mixed.reshape(width * 2 * tiles, LANES)
    made = call(
        functools.partial(enter_kernel, sizes),
        (states, norm_gains, mixed),
        [ANYWHERE] * 3,
        [((n_mp, feats, group), BF16)]
        + [((feats, group), BF16)] * n_mp
        + [
            ((rows, feats), BF16),
            ((rows, feats), BF16),
            ((1, feats), F32),
            ((rows, LANES), F32),
            ((rows, group), BF16),
            ((rows, group), BF16),
        ],
        [
            pltpu.VMEM((rows, width), BF16),
            pltpu.VMEM((1, width), F32),
            pltpu.VMEM((width * 2 * tiles, LANES), BF16),
            pltpu.VMEM((rows, width), BF16),
            pltpu.VMEM((rows, group), F32),
            pltpu.VMEM((rows, group), F32),
            pltpu.SemaphoreType.DMA((n_mp,)),
            pltpu.SemaphoreType.DMA((2,)),
        ],
        24,
        8 << 30,
    )
    wp, ws = made[0], made[1 : 1 + n_mp]
    own, own_states, own_gain, spread, prim, sec = made[1 + n_mp :]
    near_from, spread = lax.optimization_barrier((cotangent, spread))
    near_cot = swap(near_from, 0, 1, 1)
    lent_1 = swap(ws[1], 0, 1, 1)
    far_cot, spread = lax.optimization_barrier((far_cot, spread))
    cross_cot = swap(far_cot, 0, 1, 1)
    acc = call(
        part_kernel,
        (cotangent, near_cot, far_cot, *ws[:3]),
        [INSIDE] * 6,
        [((rows, group), F32)],
        (),
        16,
        1 << 30,
    )[0]
    lent_2, lent_3, far_cot = lax.optimization_barrier((ws[2], ws[3], far_cot))
    lent_2 = swap(lent_2, 0, 2, 1)
    lent_3 = swap(lent_3, 0, 3, 1)
    made = call(
        functools.partial(pack_kernel, sizes),
        (counts, prim, sec, acc, cross_cot, ws[3]),
        [SCALARS] + [INSIDE] * 5,
        [((rows, group), BF16)] + [((rows + TAIL, LANES), BF16)] * heads,
        (),
        16,
        1 << 30,
    )
    second, pieces = made[0], made[1:]
    pieces = exchange(pieces)
    pieces = call(
        functools.partial(attend_kernel, sizes),
        pieces,
        [INSIDE] * heads,
        [((rows, LANES), BF16)] * heads,
        [
            pltpu.VMEM((heads, rows + TAIL, LANES), BF16),
            pltpu.VMEM((heads, rows, LANES), BF16),
            pltpu.VMEM((n_blk, LANES, rows), F32),
        ],
        24,
        4 << 30,
    )
    pieces = exchange(pieces)
    lp, ls = call(
        functools.partial(regroup_kernel, sizes),
        (counts, *pieces),
        [SCALARS] + [INSIDE] * heads,
        [((rows, group), BF16)] * 2,
        [pltpu.VMEM((heads, rows, LANES), BF16)],
    )
    far_att = swap(ls, 0, 2, 1)
    (sent,) = call(
        functools.partial(send_kernel, sizes),
        (lp, ls, prim, second, spread, wp, ws[3], ws[1]),
        [INSIDE] * 8,
        [((2, rows + TAIL, feats), BF16)],
        (),
        16,
        2 << 30,
    )
    got = swap(sent, 0, 1)
    (kept,) = call(
        functools.partial(keep_kernel, sizes),
        (lp, ls, wp, ws[2], ws[0]),
        [INSIDE] * 5,
        [((2, rows, feats), BF16)],
        (),
        16,
        2 << 30,
    )
    (half,) = call(fold_kernel, (kept, got, sent), [INSIDE] * 3, [((rows + TAIL, feats), BF16)])
    far = swap(half, 0, 2)
    far_att, own_att, half_seen = lax.optimization_barrier((far_att, ls, half))
    near_att = swap(own_att, 0, 1, 1)
    cross_att = swap(far_att, 0, 1, 1)
    (out,) = call(
        layer_kernel,
        (ls, near_att, far_att, cross_att, ws[0], lent_1, lent_2, lent_3, own),
        [INSIDE] * 9,
        [((rows, feats), BF16)],
        [pltpu.VMEM((rows, feats), BF16), pltpu.SemaphoreType.DMA],
        16,
        2 << 30,
        [ANYWHERE],
    )
    (grad,) = call(
        functools.partial(leave_kernel, width),
        (kept, got, half_seen, far, own_states, own_gain, spread),
        [INSIDE] * 7,
        [((rows, feats), BF16)],
        out_specs=[INSIDE],
    )
    return (out[None], grad[None])


def solution(mesh):
    sizes = tuple(mesh.shape[axis] for axis in AXES)
    n_seg, n_blk, n_mp = sizes
    by_heads = n_seg == 2 and n_blk <= WIN and n_blk & (n_blk - 1) == 0 and n_mp == 4

    def body(segment_in, norm_gains, projections, live_counts, cotangent):
        rows, group = segment_in.shape[1], projections.shape[3]
        if by_heads:
            assert n_seg * n_blk * DH == group and group == 4 * LANES and rows % LANES == 0
            return per_device_heads(
                sizes, segment_in, norm_gains, projections, live_counts, cotangent
            )
        return per_device_windows(segment_in, norm_gains, projections, live_counts, cotangent)

    in_specs = (
        P("segment", "blk", None),
        P("segment", None),
        P("segment", None, None, "mp"),
        P(None, "blk"),
        P("blk", "mp"),
    )
    out_specs = (P("segment", "blk", "mp"), P("segment", "blk", "mp"))
    return jax.shard_map(body, mesh=mesh, in_specs=in_specs, out_specs=out_specs, check_vma=False)
```

profile of v0, /device:TPU:2, one launch (start us, length us, event | category | flops | bytes accessed | tf_op | source)
XLA Modules:
  0.0 131.9 jit_solution(10564774707788103553)
XLA Ops:
  0.6 3.4 %collective-permute-start.1 = (bf16[256,1024]{1,0:T(8,128)(2,1)}, bf16[256,1024]{1,0:T(8,128)(2,1)S(1)}, u32[]{:S(2)}, u32[]{:S(2)}) collective-permute-start(bf16[256,1024]{1,0:T(8,128)(2,1)} %c0.1), channel_id=1, source_target_pairs={{16,18},{17,19},{18,16},{19,17},{20,22},{21,23},{22,20},{23,21},{2... | collective-permute-start | bytes 1572872 | tf_op jit(solution)/shard_map/ppermute | solution.py:482
  4.1 8.9 %shard_map.68 = (bf16[4,1024,512]{2,1,0:T(8,128)(2,1)S(1)}, bf16[1024,512]{1,0:T(8,128)(2,1)S(1)}, bf16[1024,512]{1,0:T(8,128)(2,1)S(1)}, bf16[1024,512]{1,0:T(8...) custom-call(bf16[256,4096]{1,0:T(8,128)(2,1)} %bitcast.13, ...), custom_call_target="tpu_custom_call" | custom-call | flops 8589934592 | bytes 1048576 | tf_op jit(solution)/shard_map/pallas_call | solution.py:445
  13.0 1.9 %collective-permute-start = (bf16[256,1024]{1,0:T(8,128)(2,1)S(1)}, bf16[256,1024]{1,0:T(8,128)(2,1)S(1)}, u32[]{:S(2)}, u32[]{:S(2)}) collective-permute-start(bf16[256,1024]{1,0:T(8,128)(2,1)S(1)} %copy-done), channel_id=1, source_target_pairs={{16,17},{17,16},{18,19},{19,18},{20,21},{21,20},{22,23},{23,22},{2... | collective-permute-start | bytes 1572872 | tf_op jit(solution)/shard_map/ppermute | solution.py:482
  14.9 1.5 %collective-permute-done.1.c2 = bf16[256,1024]{1,0:T(8,128)(2,1)S(1)} collective-permute-done((bf16[256,1024]{1,0:T(8,128)(2,1)}, bf16[256,1024]{1,0:T(8,128)(2,1)S(1)}, u32[]{:S(2)}, u32[]{:S(2)}) %collective-permute-start.1) | collective-permute-done | bytes 524320 | tf_op jit(solution)/shard_map/ppermute | solution.py:482
  16.4 1.9 %collective-permute-start.2 = (bf16[256,1024]{1,0:T(8,128)(2,1)S(1)}, bf16[256,1024]{1,0:T(8,128)(2,1)S(1)}, u32[]{:S(2)}, u32[]{:S(2)}) collective-permute-start(bf16[256,1024]{1,0:T(8,128)(2,1)S(1)} %collective-permute-done.1.c2), channel_id=1, source_target_pairs={{16,17},{17,16},{18,19},{19,18},{20,21},{21,20},{22,23},{23,22},{2... | collective-permute-start | bytes 1572872 | tf_op jit(solution)/shard_map/ppermute | solution.py:482
  20.2 1.9 %shard_map.70 = (bf16[256,512]{1,0:T(8,128)(2,1)S(1)}, bf16[272,128]{1,0:T(8,128)(2,1)S(1)}, bf16[272,128]{1,0:T(8,128)(2,1)S(1)}, bf16[272,128]{1,0:T(8,128)(2,...) custom-call(s32[1,2]{1,0:T(1,128)S(1)} %bitcast.9, ...), custom_call_target="tpu_custom_call" | custom-call | flops 1073741824 | bytes 1048576 | tf_op jit(solution)/shard_map/pallas_call | solution.py:445
  22.1 1.6 %collective-permute-start.3 = (bf16[272,128]{1,0:T(8,128)(2,1)S(1)}, bf16[272,128]{1,0:T(8,128)(2,1)S(1)}, u32[]{:S(2)}, u32[]{:S(2)}) collective-permute-start(bf16[272,128]{1,0:T(8,128)(2,1)S(1)} %get-tuple-element.52), channel_id=1, source_target_pairs={{0,4},{1,5},{2,6},{3,7},{4,0},{5,1},{6,2},{7,3},{8,12},{9,13},{10,... | collective-permute-start | bytes 208904 | tf_op jit(solution)/shard_map/ppermute | solution.py:482
  23.8 2.6 %collective-permute-start.4 = (bf16[272,128]{1,0:T(8,128)(2,1)S(1)}, bf16[272,128]{1,0:T(8,128)(2,1)S(1)}, u32[]{:S(2)}, u32[]{:S(2)}) collective-permute-start(bf16[272,128]{1,0:T(8,128)(2,1)S(1)} %get-tuple-element.53), channel_id=1, source_target_pairs={{0,8},{1,9},{2,10},{3,11},{4,12},{5,13},{6,14},{7,15},{8,0},{9,1},... | collective-permute-start | bytes 208904 | tf_op jit(solution)/shard_map/ppermute | solution.py:482
  26.6 2.1 %collective-permute-start.7 = (bf16[272,128]{1,0:T(8,128)(2,1)S(1)}, bf16[272,128]{1,0:T(8,128)(2,1)S(1)}, u32[]{:S(2)}, u32[]{:S(2)}) collective-permute-start(bf16[272,128]{1,0:T(8,128)(2,1)S(1)} %get-tuple-element.56), channel_id=1, source_target_pairs={{0,20},{1,21},{2,22},{3,23},{4,16},{5,17},{6,18},{7,19},{8,28},{9,... | collective-permute-start | bytes 208904 | tf_op jit(solution)/shard_map/ppermute | solution.py:482
  28.7 2.9 %collective-permute-start.8 = (bf16[272,128]{1,0:T(8,128)(2,1)S(1)}, bf16[272,128]{1,0:T(8,128)(2,1)S(1)}, u32[]{:S(2)}, u32[]{:S(2)}) collective-permute-start(bf16[272,128]{1,0:T(8,128)(2,1)S(1)} %get-tuple-element.57), channel_id=1, source_target_pairs={{0,24},{1,25},{2,26},{3,27},{4,28},{5,29},{6,30},{7,31},{8,16},{9,... | collective-permute-start | bytes 208904 | tf_op jit(solution)/shard_map/ppermute | solution.py:482
  31.7 1.7 %collective-permute-start.9 = (bf16[272,128]{1,0:T(8,128)(2,1)S(1)}, bf16[272,128]{1,0:T(8,128)(2,1)S(1)}, u32[]{:S(2)}, u32[]{:S(2)}) collective-permute-start(bf16[272,128]{1,0:T(8,128)(2,1)S(1)} %get-tuple-element.58), channel_id=1, source_target_pairs={{0,28},{1,29},{2,30},{3,31},{4,24},{5,25},{6,26},{7,27},{8,20},{9,... | collective-permute-start | bytes 208904 | tf_op jit(solution)/shard_map/ppermute | solution.py:482
  33.4 3.5 %collective-permute-done.8.rest_6_ = bf16[272,128]{1,0:T(8,128)(2,1)S(1)} collective-permute-done((bf16[272,128]{1,0:T(8,128)(2,1)S(1)}, bf16[272,128]{1,0:T(8,128)(2,1)S(1)}, u32[]{:S(2)}, u32[]{:S(2)}) %collective-permute-start.8) | collective-permute-done | bytes 69664 | tf_op jit(solution)/shard_map/ppermute | solution.py:482
  36.9 1.8 %collective-permute-done.9.rest_7_ = bf16[272,128]{1,0:T(8,128)(2,1)S(1)} collective-permute-done((bf16[272,128]{1,0:T(8,128)(2,1)S(1)}, bf16[272,128]{1,0:T(8,128)(2,1)S(1)}, u32[]{:S(2)}, u32[]{:S(2)}) %collective-permute-start.9) | collective-permute-done | bytes 69664 | tf_op jit(solution)/shard_map/ppermute | solution.py:482
  38.7 3.4 %shard_map.71 = (bf16[256,128]{1,0:T(8,128)(2,1)S(1)}, bf16[256,128]{1,0:T(8,128)(2,1)S(1)}, bf16[256,128]{1,0:T(8,128)(2,1)S(1)}, bf16[256,128]{1,0:T(8,128)(2,...) custom-call(bf16[272,128]{1,0:T(8,128)(2,1)S(1)} %get-tuple-element., ...), custom_call_target="tpu_custom_call" | custom-call | flops 4294967296 | bytes 1048576 | tf_op jit(solution)/shard_map/pallas_call | solution.py:445
  42.2 4.1 %collective-permute-start.11 = (bf16[256,128]{1,0:T(8,128)(2,1)S(1)}, bf16[256,128]{1,0:T(8,128)(2,1)S(1)}, u32[]{:S(2)}, u32[]{:S(2)}) collective-permute-start(bf16[256,128]{1,0:T(8,128)(2,1)S(1)} %get-tuple-element.61), channel_id=1, source_target_pairs={{0,8},{1,9},{2,10},{3,11},{4,12},{5,13},{6,14},{7,15},{8,0},{9,1},... | collective-permute-start | bytes 196616 | tf_op jit(solution)/shard_map/ppermute | solution.py:482
  46.5 2.0 %collective-permute-start.13 = (bf16[256,128]{1,0:T(8,128)(2,1)S(1)}, bf16[256,128]{1,0:T(8,128)(2,1)S(1)}, u32[]{:S(2)}, u32[]{:S(2)}) collective-permute-start(bf16[256,128]{1,0:T(8,128)(2,1)S(1)} %get-tuple-element.63), channel_id=1, source_target_pairs={{0,16},{1,17},{2,18},{3,19},{4,20},{5,21},{6,22},{7,23},{8,24},{9,... | collective-permute-start | bytes 196616 | tf_op jit(solution)/shard_map/ppermute | solution.py:482
  48.5 3.0 %collective-permute-start.15 = (bf16[256,128]{1,0:T(8,128)(2,1)S(1)}, bf16[256,128]{1,0:T(8,128)(2,1)S(1)}, u32[]{:S(2)}, u32[]{:S(2)}) collective-permute-start(bf16[256,128]{1,0:T(8,128)(2,1)S(1)} %get-tuple-element.65), channel_id=1, source_target_pairs={{0,24},{1,25},{2,26},{3,27},{4,28},{5,29},{6,30},{7,31},{8,16},{9,... | collective-permute-start | bytes 196616 | tf_op jit(solution)/shard_map/ppermute | solution.py:482
  51.6 1.7 %collective-permute-start.16 = (bf16[256,128]{1,0:T(8,128)(2,1)S(1)}, bf16[256,128]{1,0:T(8,128)(2,1)S(1)}, u32[]{:S(2)}, u32[]{:S(2)}) collective-permute-start(bf16[256,128]{1,0:T(8,128)(2,1)S(1)} %get-tuple-element.66), channel_id=1, source_target_pairs={{0,28},{1,29},{2,30},{3,31},{4,24},{5,25},{6,26},{7,27},{8,20},{9,... | collective-permute-start | bytes 196616 | tf_op jit(solution)/shard_map/ppermute | solution.py:482
  53.9 2.0 %collective-permute-done.15.rest_6_ = bf16[256,128]{1,0:T(8,128)(2,1)S(1)} collective-permute-done((bf16[256,128]{1,0:T(8,128)(2,1)S(1)}, bf16[256,128]{1,0:T(8,128)(2,1)S(1)}, u32[]{:S(2)}, u32[]{:S(2)}) %collective-permute-start.15) | collective-permute-done | bytes 65568 | tf_op jit(solution)/shard_map/ppermute | solution.py:482
  55.8 2.7 %collective-permute-done.16.rest_7_ = bf16[256,128]{1,0:T(8,128)(2,1)S(1)} collective-permute-done((bf16[256,128]{1,0:T(8,128)(2,1)S(1)}, bf16[256,128]{1,0:T(8,128)(2,1)S(1)}, u32[]{:S(2)}, u32[]{:S(2)}) %collective-permute-start.16) | collective-permute-done | bytes 65568 | tf_op jit(solution)/shard_map/ppermute | solution.py:482
  59.5 1.7 %shard_map.74.sent = bf16[2,272,1024]{2,1,0:T(8,128)(2,1)S(1)} custom-call(bf16[256,512]{1,0:T(8,128)(2,1)S(1)} %get-tuple-element.68.lp, bf16[256,512]{1,0:T(8,128)(2,1)S(1)} %get-tuple-element.72.ls.a0, bf16[256,512]{1,0:T(8,128)(2,1)S(1)} %get-tuple-element.41.prim, bf16[256,512]{1,0:T(8,128)(2,1)S(1)} %get-tuple-element.70.second, ...), custom_call_target="tpu_custom_call" | custom-call | flops 2147483648 | bytes 1048576 | tf_op jit(solution)/shard_map/pallas_call | solution.py:445
  61.3 2.4 %collective-permute-start.21 = (bf16[1024,512]{1,0:T(8,128)(2,1)S(1)}, bf16[1024,512]{1,0:T(8,128)(2,1)S(1)}, u32[]{:S(2)}, u32[]{:S(2)}) collective-permute-start(bf16[1024,512]{1,0:T(8,128)(2,1)S(1)} %get-tuple-element.48.w1), channel_id=1, source_target_pairs={{16,17},{17,16},{18,19},{19,18},{20,21},{21,20},{22,23},{23,22},{2... | collective-permute-start | bytes 3145736 | tf_op jit(solution)/shard_map/ppermute | solution.py:482
  63.7 3.4 %collective-permute-start.22 = (bf16[1024,512]{1,0:T(8,128)(2,1)S(1)}, bf16[1024,512]{1,0:T(8,128)(2,1)S(1)}, u32[]{:S(2)}, u32[]{:S(2)}) collective-permute-start(bf16[1024,512]{1,0:T(8,128)(2,1)S(1)} %get-tuple-element.74.w2), channel_id=1, source_target_pairs={{16,18},{17,19},{18,16},{19,17},{20,22},{21,23},{22,20},{23,21},{2... | collective-permute-start | bytes 3145736 | tf_op jit(solution)/shard_map/ppermute | solution.py:482
  67.1 1.9 %collective-permute-start.23 = (bf16[1024,512]{1,0:T(8,128)(2,1)S(1)}, bf16[1024,512]{1,0:T(8,128)(2,1)S(1)}, u32[]{:S(2)}, u32[]{:S(2)}) collective-permute-start(bf16[1024,512]{1,0:T(8,128)(2,1)S(1)} %get-tuple-element.75.w3), channel_id=1, source_target_pairs={{16,19},{17,18},{18,17},{19,16},{20,23},{21,22},{22,21},{23,20},{2... | collective-permute-start | bytes 3145736 | tf_op jit(solution)/shard_map/ppermute | solution.py:482
  69.0 3.3 %collective-permute-start.17 = (bf16[256,512]{1,0:T(8,128)(2,1)S(1)}, bf16[256,512]{1,0:T(8,128)(2,1)S(1)}, u32[]{:S(2)}, u32[]{:S(2)}) collective-permute-start(bf16[256,512]{1,0:T(8,128)(2,1)S(1)} %get-tuple-element.72.ls.a0), channel_id=1, source_target_pairs={{16,18},{17,19},{18,16},{19,17},{20,22},{21,23},{22,20},{23,21},{2... | collective-permute-start | bytes 786440 | tf_op jit(solution)/shard_map/ppermute | solution.py:482
  72.3 1.2 shard_map.73.kept
  74.4 45.3 %collective-permute-done.17.a2 = bf16[256,512]{1,0:T(8,128)(2,1)S(1)} collective-permute-done((bf16[256,512]{1,0:T(8,128)(2,1)S(1)}, bf16[256,512]{1,0:T(8,128)(2,1)S(1)}, u32[]{:S(2)}, u32[]{:S(2)}) %collective-permute-start.17) | collective-permute-done | bytes 262176 | tf_op jit(solution)/shard_map/ppermute | solution.py:482
  119.7 1.9 %collective-permute-start.19 = (bf16[256,512]{1,0:T(8,128)(2,1)S(1)}, bf16[256,512]{1,0:T(8,128)(2,1)S(1)}, u32[]{:S(2)}, u32[]{:S(2)}) collective-permute-start(bf16[256,512]{1,0:T(8,128)(2,1)S(1)} %get-tuple-element.72.ls.a0), channel_id=1, source_target_pairs={{16,17},{17,16},{18,19},{19,18},{20,21},{21,20},{22,23},{23,22},{2... | collective-permute-start | bytes 786440 | tf_op jit(solution)/shard_map/ppermute | solution.py:482
  121.6 2.4 %collective-permute-start.20 = (bf16[256,512]{1,0:T(8,128)(2,1)S(1)}, bf16[256,512]{1,0:T(8,128)(2,1)S(1)}, u32[]{:S(2)}, u32[]{:S(2)}) collective-permute-start(bf16[256,512]{1,0:T(8,128)(2,1)S(1)} %collective-permute-done.17.a2), channel_id=1, source_target_pairs={{16,17},{17,16},{18,19},{19,18},{20,21},{21,20},{22,23},{23,22},{2... | collective-permute-start | bytes 786440 | tf_op jit(solution)/shard_map/ppermute | solution.py:482
  125.2 2.1 %shard_map.76 = bf16[256,1024]{1,0:T(8,128)(2,1)} custom-call(bf16[256,512]{1,0:T(8,128)(2,1)S(1)} %get-tuple-element.72.ls.a0, bf16[256,512]{1,0:T(8,128)(2,1)S(1)} %collective-permute-done.19.a1, bf16[256,512]{1,0:T(8,128)(2,1)S(1)} %collective-permute-done.17.a2, bf16[256,512]{1,0:T(8,128)(2,1)S(1)} %collective-permute-done.20.a3, ...), custom_call_target="tpu_custom_call" | custom-call | flops 2147483648 | bytes 1048576 | tf_op jit(solution)/shard_map/pallas_call | solution.py:445
  127.3 3.4 %collective-permute-done.24.far = bf16[272,1024]{1,0:T(8,128)(2,1)S(1)} collective-permute-done((bf16[272,1024]{1,0:T(8,128)(2,1)S(1)}, bf16[272,1024]{1,0:T(8,128)(2,1)S(1)}, u32[]{:S(2)}, u32[]{:S(2)}) %collective-permute-start.24) | collective-permute-done | bytes 557088 | tf_op jit(solution)/shard_map/ppermute | solution.py:482
  130.7 1.2 shard_map.77
  (32 shorter events, 6.0 us)
Async XLA Ops:
  0.6 15.8 %collective-permute-start.1 = (bf16[256,1024]{1,0:T(8,128)(2,1)}, bf16[256,1024]{1,0:T(8,128)(2,1)S(1)}, u32[]{:S(2)}, u32[]{:S(2)}) collective-permute-start(bf16[256,1024]{1,0:T(8,128)(2,1)} %c0.1), channel_id=1, source_target_pairs={{16,18},{17,19},{18,16},{19,17},{20,22},{21,23},{22,20},{23,21},{2... | collective-permute-start | bytes 1572872 | tf_op jit(solution)/shard_map/ppermute | solution.py:482
  4.1 8.9 %copy-start = (bf16[256,1024]{1,0:T(8,128)(2,1)S(1)}, bf16[256,1024]{1,0:T(8,128)(2,1)}, u32[]{:S(2)}) copy-start(bf16[256,1024]{1,0:T(8,128)(2,1)} %c0.1) | copy-start | bytes 1572868
  13.0 5.4 %collective-permute-start = (bf16[256,1024]{1,0:T(8,128)(2,1)S(1)}, bf16[256,1024]{1,0:T(8,128)(2,1)S(1)}, u32[]{:S(2)}, u32[]{:S(2)}) collective-permute-start(bf16[256,1024]{1,0:T(8,128)(2,1)S(1)} %copy-done), channel_id=1, source_target_pairs={{16,17},{17,16},{18,19},{19,18},{20,21},{21,20},{22,23},{23,22},{2... | collective-permute-start | bytes 1572872 | tf_op jit(solution)/shard_map/ppermute | solution.py:482
  16.4 3.8 %collective-permute-start.2 = (bf16[256,1024]{1,0:T(8,128)(2,1)S(1)}, bf16[256,1024]{1,0:T(8,128)(2,1)S(1)}, u32[]{:S(2)}, u32[]{:S(2)}) collective-permute-start(bf16[256,1024]{1,0:T(8,128)(2,1)S(1)} %collective-permute-done.1.c2), channel_id=1, source_target_pairs={{16,17},{17,16},{18,19},{19,18},{20,21},{21,20},{22,23},{23,22},{2... | collective-permute-start | bytes 1572872 | tf_op jit(solution)/shard_map/ppermute | solution.py:482
  18.3 1.9 %copy-start.1 = (s32[2,1]{0,1:T(1,128)S(1)}, s32[2,1]{0,1:T(1,128)}, u32[]{:S(2)}) copy-start(s32[2,1]{0,1:T(1,128)} %param.8) | copy-start | bytes 28
  22.1 6.6 %collective-permute-start.3 = (bf16[272,128]{1,0:T(8,128)(2,1)S(1)}, bf16[272,128]{1,0:T(8,128)(2,1)S(1)}, u32[]{:S(2)}, u32[]{:S(2)}) collective-permute-start(bf16[272,128]{1,0:T(8,128)(2,1)S(1)} %get-tuple-element.52), channel_id=1, source_target_pairs={{0,4},{1,5},{2,6},{3,7},{4,0},{5,1},{6,2},{7,3},{8,12},{9,13},{10,... | collective-permute-start | bytes 208904 | tf_op jit(solution)/shard_map/ppermute | solution.py:482
  23.8 7.9 %collective-permute-start.4 = (bf16[272,128]{1,0:T(8,128)(2,1)S(1)}, bf16[272,128]{1,0:T(8,128)(2,1)S(1)}, u32[]{:S(2)}, u32[]{:S(2)}) collective-permute-start(bf16[272,128]{1,0:T(8,128)(2,1)S(1)} %get-tuple-element.53), channel_id=1, source_target_pairs={{0,8},{1,9},{2,10},{3,11},{4,12},{5,13},{6,14},{7,15},{8,0},{9,1},... | collective-permute-start | bytes 208904 | tf_op jit(solution)/shard_map/ppermute | solution.py:482
  26.4 7.0 %collective-permute-start.5 = (bf16[272,128]{1,0:T(8,128)(2,1)S(1)}, bf16[272,128]{1,0:T(8,128)(2,1)S(1)}, u32[]{:S(2)}, u32[]{:S(2)}) collective-permute-start(bf16[272,128]{1,0:T(8,128)(2,1)S(1)} %get-tuple-element.54), channel_id=1, source_target_pairs={{0,12},{1,13},{2,14},{3,15},{4,8},{5,9},{6,10},{7,11},{8,4},{9,5},... | collective-permute-start | bytes 208904 | tf_op jit(solution)/shard_map/ppermute | solution.py:482
  26.6 6.8 %collective-permute-start.6 = (bf16[272,128]{1,0:T(8,128)(2,1)S(1)}, bf16[272,128]{1,0:T(8,128)(2,1)S(1)}, u32[]{:S(2)}, u32[]{:S(2)}) collective-permute-start(bf16[272,128]{1,0:T(8,128)(2,1)S(1)} %get-tuple-element.55), channel_id=1, source_target_pairs={{0,16},{1,17},{2,18},{3,19},{4,20},{5,21},{6,22},{7,23},{8,24},{9,... | collective-permute-start | bytes 208904 | tf_op jit(solution)/shard_map/ppermute | solution.py:482
  26.6 6.8 %collective-permute-start.7 = (bf16[272,128]{1,0:T(8,128)(2,1)S(1)}, bf16[272,128]{1,0:T(8,128)(2,1)S(1)}, u32[]{:S(2)}, u32[]{:S(2)}) collective-permute-start(bf16[272,128]{1,0:T(8,128)(2,1)S(1)} %get-tuple-element.56), channel_id=1, source_target_pairs={{0,20},{1,21},{2,22},{3,23},{4,16},{5,17},{6,18},{7,19},{8,28},{9,... | collective-permute-start | bytes 208904 | tf_op jit(solution)/shard_map/ppermute | solution.py:482
  28.7 8.1 %collective-permute-start.8 = (bf16[272,128]{1,0:T(8,128)(2,1)S(1)}, bf16[272,128]{1,0:T(8,128)(2,1)S(1)}, u32[]{:S(2)}, u32[]{:S(2)}) collective-permute-start(bf16[272,128]{1,0:T(8,128)(2,1)S(1)} %get-tuple-element.57), channel_id=1, source_target_pairs={{0,24},{1,25},{2,26},{3,27},{4,28},{5,29},{6,30},{7,31},{8,16},{9,... | collective-permute-start | bytes 208904 | tf_op jit(solution)/shard_map/ppermute | solution.py:482
  31.7 7.0 %collective-permute-start.9 = (bf16[272,128]{1,0:T(8,128)(2,1)S(1)}, bf16[272,128]{1,0:T(8,128)(2,1)S(1)}, u32[]{:S(2)}, u32[]{:S(2)}) collective-permute-start(bf16[272,128]{1,0:T(8,128)(2,1)S(1)} %get-tuple-element.58), channel_id=1, source_target_pairs={{0,28},{1,29},{2,30},{3,31},{4,24},{5,25},{6,26},{7,27},{8,20},{9,... | collective-permute-start | bytes 208904 | tf_op jit(solution)/shard_map/ppermute | solution.py:482
  42.1 6.5 %collective-permute-start.10 = (bf16[256,128]{1,0:T(8,128)(2,1)S(1)}, bf16[256,128]{1,0:T(8,128)(2,1)S(1)}, u32[]{:S(2)}, u32[]{:S(2)}) collective-permute-start(bf16[256,128]{1,0:T(8,128)(2,1)S(1)} %get-tuple-element.60), channel_id=1, source_target_pairs={{0,4},{1,5},{2,6},{3,7},{4,0},{5,1},{6,2},{7,3},{8,12},{9,13},{10,... | collective-permute-start | bytes 196616 | tf_op jit(solution)/shard_map/ppermute | solution.py:482
  42.2 9.4 %collective-permute-start.11 = (bf16[256,128]{1,0:T(8,128)(2,1)S(1)}, bf16[256,128]{1,0:T(8,128)(2,1)S(1)}, u32[]{:S(2)}, u32[]{:S(2)}) collective-permute-start(bf16[256,128]{1,0:T(8,128)(2,1)S(1)} %get-tuple-element.61), channel_id=1, source_target_pairs={{0,8},{1,9},{2,10},{3,11},{4,12},{5,13},{6,14},{7,15},{8,0},{9,1},... | collective-permute-start | bytes 196616 | tf_op jit(solution)/shard_map/ppermute | solution.py:482
  46.3 7.0 %collective-permute-start.12 = (bf16[256,128]{1,0:T(8,128)(2,1)S(1)}, bf16[256,128]{1,0:T(8,128)(2,1)S(1)}, u32[]{:S(2)}, u32[]{:S(2)}) collective-permute-start(bf16[256,128]{1,0:T(8,128)(2,1)S(1)} %get-tuple-element.62), channel_id=1, source_target_pairs={{0,12},{1,13},{2,14},{3,15},{4,8},{5,9},{6,10},{7,11},{8,4},{9,5},... | collective-permute-start | bytes 196616 | tf_op jit(solution)/shard_map/ppermute | solution.py:482
  46.5 6.8 %collective-permute-start.13 = (bf16[256,128]{1,0:T(8,128)(2,1)S(1)}, bf16[256,128]{1,0:T(8,128)(2,1)S(1)}, u32[]{:S(2)}, u32[]{:S(2)}) collective-permute-start(bf16[256,128]{1,0:T(8,128)(2,1)S(1)} %get-tuple-element.63), channel_id=1, source_target_pairs={{0,16},{1,17},{2,18},{3,19},{4,20},{5,21},{6,22},{7,23},{8,24},{9,... | collective-permute-start | bytes 196616 | tf_op jit(solution)/shard_map/ppermute | solution.py:482
  48.5 5.3 %collective-permute-start.14 = (bf16[256,128]{1,0:T(8,128)(2,1)S(1)}, bf16[256,128]{1,0:T(8,128)(2,1)S(1)}, u32[]{:S(2)}, u32[]{:S(2)}) collective-permute-start(bf16[256,128]{1,0:T(8,128)(2,1)S(1)} %get-tuple-element.64), channel_id=1, source_target_pairs={{0,20},{1,21},{2,22},{3,23},{4,16},{5,17},{6,18},{7,19},{8,28},{9,... | collective-permute-start | bytes 196616 | tf_op jit(solution)/shard_map/ppermute | solution.py:482
  48.5 7.3 %collective-permute-start.15 = (bf16[256,128]{1,0:T(8,128)(2,1)S(1)}, bf16[256,128]{1,0:T(8,128)(2,1)S(1)}, u32[]{:S(2)}, u32[]{:S(2)}) collective-permute-start(bf16[256,128]{1,0:T(8,128)(2,1)S(1)} %get-tuple-element.65), channel_id=1, source_target_pairs={{0,24},{1,25},{2,26},{3,27},{4,28},{5,29},{6,30},{7,31},{8,16},{9,... | collective-permute-start | bytes 196616 | tf_op jit(solution)/shard_map/ppermute | solution.py:482
  51.6 7.0 %collective-permute-start.16 = (bf16[256,128]{1,0:T(8,128)(2,1)S(1)}, bf16[256,128]{1,0:T(8,128)(2,1)S(1)}, u32[]{:S(2)}, u32[]{:S(2)}) collective-permute-start(bf16[256,128]{1,0:T(8,128)(2,1)S(1)} %get-tuple-element.66), channel_id=1, source_target_pairs={{0,28},{1,29},{2,30},{3,31},{4,24},{5,25},{6,26},{7,27},{8,20},{9,... | collective-permute-start | bytes 196616 | tf_op jit(solution)/shard_map/ppermute | solution.py:482
  61.2 12.3 %collective-permute-start.18 = (bf16[2,272,1024]{2,1,0:T(8,128)(2,1)S(1)}, bf16[2,272,1024]{2,1,0:T(8,128)(2,1)S(1)}, u32[]{:S(2)}, u32[]{:S(2)}) collective-permute-start(bf16[2,272,1024]{2,1,0:T(8,128)(2,1)S(1)} %shard_map.74.sent), channel_id=1, source_target_pairs={{0,1},{1,0},{2,3},{3,2},{4,5},{5,4},{6,7},{7,6},{8,9},{9,8},{10,11... | collective-permute-start | bytes 3342344 | tf_op jit(solution)/shard_map/ppermute | solution.py:482
  61.3 60.3 %collective-permute-start.21 = (bf16[1024,512]{1,0:T(8,128)(2,1)S(1)}, bf16[1024,512]{1,0:T(8,128)(2,1)S(1)}, u32[]{:S(2)}, u32[]{:S(2)}) collective-permute-start(bf16[1024,512]{1,0:T(8,128)(2,1)S(1)} %get-tuple-element.48.w1), channel_id=1, source_target_pairs={{16,17},{17,16},{18,19},{19,18},{20,21},{21,20},{22,23},{23,22},{2... | collective-permute-start | bytes 3145736 | tf_op jit(solution)/shard_map/ppermute | solution.py:482
  63.7 60.4 %collective-permute-start.22 = (bf16[1024,512]{1,0:T(8,128)(2,1)S(1)}, bf16[1024,512]{1,0:T(8,128)(2,1)S(1)}, u32[]{:S(2)}, u32[]{:S(2)}) collective-permute-start(bf16[1024,512]{1,0:T(8,128)(2,1)S(1)} %get-tuple-element.74.w2), channel_id=1, source_target_pairs={{16,18},{17,19},{18,16},{19,17},{20,22},{21,23},{22,20},{23,21},{2... | collective-permute-start | bytes 3145736 | tf_op jit(solution)/shard_map/ppermute | solution.py:482
  67.1 56.9 %collective-permute-start.23 = (bf16[1024,512]{1,0:T(8,128)(2,1)S(1)}, bf16[1024,512]{1,0:T(8,128)(2,1)S(1)}, u32[]{:S(2)}, u32[]{:S(2)}) collective-permute-start(bf16[1024,512]{1,0:T(8,128)(2,1)S(1)} %get-tuple-element.75.w3), channel_id=1, source_target_pairs={{16,19},{17,18},{18,17},{19,16},{20,23},{21,22},{22,21},{23,20},{2... | collective-permute-start | bytes 3145736 | tf_op jit(solution)/shard_map/ppermute | solution.py:482
  69.0 50.7 %collective-permute-start.17 = (bf16[256,512]{1,0:T(8,128)(2,1)S(1)}, bf16[256,512]{1,0:T(8,128)(2,1)S(1)}, u32[]{:S(2)}, u32[]{:S(2)}) collective-permute-start(bf16[256,512]{1,0:T(8,128)(2,1)S(1)} %get-tuple-element.72.ls.a0), channel_id=1, source_target_pairs={{16,18},{17,19},{18,16},{19,17},{20,22},{21,23},{22,20},{23,21},{2... | collective-permute-start | bytes 786440 | tf_op jit(solution)/shard_map/ppermute | solution.py:482
  73.7 57.0 %collective-permute-start.24 = (bf16[272,1024]{1,0:T(8,128)(2,1)S(1)}, bf16[272,1024]{1,0:T(8,128)(2,1)S(1)}, u32[]{:S(2)}, u32[]{:S(2)}) collective-permute-start(bf16[272,1024]{1,0:T(8,128)(2,1)S(1)} %shard_map.75.half), channel_id=1, source_target_pairs={{0,2},{1,3},{2,0},{3,1},{4,6},{5,7},{6,4},{7,5},{8,10},{9,11},{10,... | collective-permute-start | bytes 1671176 | tf_op jit(solution)/shard_map/ppermute | solution.py:482
  119.7 4.4 %collective-permute-start.19 = (bf16[256,512]{1,0:T(8,128)(2,1)S(1)}, bf16[256,512]{1,0:T(8,128)(2,1)S(1)}, u32[]{:S(2)}, u32[]{:S(2)}) collective-permute-start(bf16[256,512]{1,0:T(8,128)(2,1)S(1)} %get-tuple-element.72.ls.a0), channel_id=1, source_target_pairs={{16,17},{17,16},{18,19},{19,18},{20,21},{21,20},{22,23},{23,22},{2... | collective-permute-start | bytes 786440 | tf_op jit(solution)/shard_map/ppermute | solution.py:482
  121.6 3.6 %collective-permute-start.20 = (bf16[256,512]{1,0:T(8,128)(2,1)S(1)}, bf16[256,512]{1,0:T(8,128)(2,1)S(1)}, u32[]{:S(2)}, u32[]{:S(2)}) collective-permute-start(bf16[256,512]{1,0:T(8,128)(2,1)S(1)} %collective-permute-done.17.a2), channel_id=1, source_target_pairs={{16,17},{17,16},{18,19},{19,18},{20,21},{21,20},{22,23},{23,22},{2... | collective-permute-start | bytes 786440 | tf_op jit(solution)/shard_map/ppermute | solution.py:482
where the time goes:
time: 132 us
  waiting for transfers between devices  62.8 us (48%)
  starting transfers between devices  45.8 us (35%)
  Pallas kernels  22.4 us (17%)
    ppermute x25, waiting for transfers between devices, swap(): return lax.ppermute(x, AXES, pairs)  62.8 us
    ppermute x25, starting transfers between devices, swap(): return lax.ppermute(x, AXES, pairs)  45.8 us
    pallas_call x10, Pallas kernels, call(): pl.pallas_call(body, in_specs=list(specs), out_specs=[INSIDE] * len(outs)...  22.4 us
  transfers between devices with their start and end apart: 25, of which 10 were waited for; matrix products, arithmetic and copies ran while one was open for 0% of the time, Pallas kernels for 10%

commit v1 on v0

--- a/solution.py
+++ b/solution.py
@@ -453,15 +453,20 @@
     )(*ins)
 
 
-def leave_kernel(width, kept, got, half, far, states, gain, spread, grad):
+def scales_kernel(width, spread, inverse, shrink):
+    root = spread[...]
+    inverse[...] = 1.0 / root
+    shrink[...] = 1.0 / (width * root * root * root)
+
+
+def leave_kernel(kept, got, half, far, states, gain, inverse, shrink, grad):
     rows = states.shape[0]
     ends = half[rows:, :].astype(F32) + far[rows:, :].astype(F32)
     row = jnp.broadcast_to(ends[0:1, :rows] + ends[1:2, :rows], (LANES, rows))
     term = row.T[:, :1]
-    root = spread[:, :1]
-    scaled = term / (width * root * root * root)
+    scaled = term * shrink[:, :1]
     total = kept[1].astype(F32) + got[1, :rows, :].astype(F32) + far[:rows, :].astype(F32)
-    grad[...] = (gain[...] * total * (1.0 / root) - states[...].astype(F32) * scaled).astype(BF16)
+    grad[...] = (gain[...] * total * inverse[:, :1] - states[...].astype(F32) * scaled).astype(BF16)
 
 
 def per_device_heads(sizes, segment_in, norm_gains, projections, live_counts, cotangent):
@@ -481,12 +486,16 @@
         ]
         return lax.ppermute(x, AXES, pairs)
 
+    far_first = sorted(range(1, heads), key=lambda k: -((k % n_blk) * 2 + 1 - k // n_blk))
+
     def exchange(pieces):
-        far_first = sorted(range(1, heads), key=lambda k: -((k % n_blk) * 2 + 1 - k // n_blk))
-        moved = {k: swap(pieces[k], k, 0) for k in far_first}
+        moved = {}
+        for k in far_first:
+            moved[k] = swap(pieces[k], k, 0)
         return [pieces[0]] + [moved[k] for k in range(1, heads)]
 
     far_cot = swap(cotangent, 0, 2, 1)
+    near_cot = swap(cotangent, 0, 1, 1)
     tiles = group // LANES
     mixed = projections.reshape(width, 2, tiles, LANES).transpose(0, 2, 1, 3)
     mixed = mixed.reshape(width * 2 * tiles, LANES)
@@ -519,8 +528,6 @@
     )
     wp, ws = made[0], made[1 : 1 + n_mp]
     own, own_states, own_gain, spread, prim, sec = made[1 + n_mp :]
-    near_from, spread = lax.optimization_barrier((cotangent, spread))
-    near_cot = swap(near_from, 0, 1, 1)
     lent_1 = swap(ws[1], 0, 1, 1)
     far_cot, spread = lax.optimization_barrier((far_cot, spread))
     cross_cot = swap(far_cot, 0, 1, 1)
@@ -547,6 +554,9 @@
     )
     second, pieces = made[0], made[1:]
     pieces = exchange(pieces)
+    inverse, shrink = call(
+        functools.partial(scales_kernel, width), (spread,), [INSIDE], [((rows, LANES), F32)] * 2
+    )
     pieces = call(
         functools.partial(attend_kernel, sizes),
         pieces,
@@ -604,9 +614,9 @@
         [ANYWHERE],
     )
     (grad,) = call(
-        functools.partial(leave_kernel, width),
-        (kept, got, half_seen, far, own_states, own_gain, spread),
-        [INSIDE] * 7,
+        leave_kernel,
+        (kept, got, half_seen, far, own_states, own_gain, inverse, shrink),
+        [INSIDE] * 8,
         [((rows, feats), BF16)],
         out_specs=[INSIDE],
     )

time: 132 us -> 135 us (1.023)
  waiting for transfers between devices: 62.8 us -> 65.3 us
    ppermute x25, waiting for transfers between devices: 62.8 us -> 65.3 us  [swap(): return lax.ppermute(x, AXES, pairs)]
    pallas_call x10 -> x11, Pallas kernels: 22.4 us -> 22.5 us  [call(): pl.pallas_call(body, in_specs=list(specs), out_specs=[INSIDE] * len(outs)...]
where the time goes in v1:
time: 135 us; the launch traced here: 134 us
  waiting for transfers between devices  65.3 us (48%)
  starting transfers between devices  45.8 us (34%)
  Pallas kernels  22.5 us (17%)
    ppermute x25, waiting for transfers between devices, swap(): return lax.ppermute(x, AXES, pairs)  65.3 us
    ppermute x25, starting transfers between devices, swap(): return lax.ppermute(x, AXES, pairs)  45.8 us
    pallas_call x11, Pallas kernels, call(): pl.pallas_call(body, in_specs=list(specs), out_specs=[INSIDE] * len(outs)...  22.5 us
  transfers between devices with their start and end apart: 25, of which 10 were waited for; matrix products, arithmetic and copies ran while one was open for 0% of the time, Pallas kernels for 10%

profile of v1, /device:TPU:2, one launch (start us, length us, event | category | flops | bytes accessed | tf_op | source)
XLA Modules:
  0.0 134.5 jit_solution(6462519573851948412)
XLA Ops:
  0.6 1.9 %collective-permute-start = (bf16[256,1024]{1,0:T(8,128)(2,1)}, bf16[256,1024]{1,0:T(8,128)(2,1)S(1)}, u32[]{:S(2)}, u32[]{:S(2)}) collective-permute-start(bf16[256,1024]{1,0:T(8,128)(2,1)} %c0.1), channel_id=1, source_target_pairs={{16,17},{17,16},{18,19},{19,18},{20,21},{21,20},{22,23},{23,22},{2... | collective-permute-start | bytes 1572872 | tf_op jit(solution)/shard_map/ppermute | solution.py:487
  2.6 3.4 %collective-permute-start.1 = (bf16[256,1024]{1,0:T(8,128)(2,1)}, bf16[256,1024]{1,0:T(8,128)(2,1)S(1)}, u32[]{:S(2)}, u32[]{:S(2)}) collective-permute-start(bf16[256,1024]{1,0:T(8,128)(2,1)} %c0.1), channel_id=1, source_target_pairs={{16,18},{17,19},{18,16},{19,17},{20,22},{21,23},{22,20},{23,21},{2... | collective-permute-start | bytes 1572872 | tf_op jit(solution)/shard_map/ppermute | solution.py:487
  6.0 8.9 %shard_map.68 = (bf16[4,1024,512]{2,1,0:T(8,128)(2,1)S(1)}, bf16[1024,512]{1,0:T(8,128)(2,1)S(1)}, bf16[1024,512]{1,0:T(8,128)(2,1)S(1)}, bf16[1024,512]{1,0:T(8...) custom-call(bf16[256,4096]{1,0:T(8,128)(2,1)} %bitcast.13, ...), custom_call_target="tpu_custom_call" | custom-call | flops 8589934592 | bytes 1048576 | tf_op jit(solution)/shard_map/pallas_call | solution.py:445
  14.9 4.1 %collective-permute-done.1.c2 = bf16[256,1024]{1,0:T(8,128)(2,1)S(1)} collective-permute-done((bf16[256,1024]{1,0:T(8,128)(2,1)}, bf16[256,1024]{1,0:T(8,128)(2,1)S(1)}, u32[]{:S(2)}, u32[]{:S(2)}) %collective-permute-start.1) | collective-permute-done | bytes 524320 | tf_op jit(solution)/shard_map/ppermute | solution.py:487
  19.0 1.9 %collective-permute-start.2 = (bf16[256,1024]{1,0:T(8,128)(2,1)S(1)}, bf16[256,1024]{1,0:T(8,128)(2,1)S(1)}, u32[]{:S(2)}, u32[]{:S(2)}) collective-permute-start(bf16[256,1024]{1,0:T(8,128)(2,1)S(1)} %collective-permute-done.1.c2), channel_id=1, source_target_pairs={{16,17},{17,16},{18,19},{19,18},{20,21},{21,20},{22,23},{23,22},{2... | collective-permute-start | bytes 1572872 | tf_op jit(solution)/shard_map/ppermute | solution.py:487
  22.8 1.9 %shard_map.70 = (bf16[256,512]{1,0:T(8,128)(2,1)S(1)}, bf16[272,128]{1,0:T(8,128)(2,1)S(1)}, bf16[272,128]{1,0:T(8,128)(2,1)S(1)}, bf16[272,128]{1,0:T(8,128)(2,...) custom-call(s32[1,2]{1,0:T(1,128)S(1)} %bitcast.9, ...), custom_call_target="tpu_custom_call" | custom-call | flops 1073741824 | bytes 1048576 | tf_op jit(solution)/shard_map/pallas_call | solution.py:445
  24.7 1.6 %collective-permute-start.3 = (bf16[272,128]{1,0:T(8,128)(2,1)S(1)}, bf16[272,128]{1,0:T(8,128)(2,1)S(1)}, u32[]{:S(2)}, u32[]{:S(2)}) collective-permute-start(bf16[272,128]{1,0:T(8,128)(2,1)S(1)} %get-tuple-element.50), channel_id=1, source_target_pairs={{0,4},{1,5},{2,6},{3,7},{4,0},{5,1},{6,2},{7,3},{8,12},{9,13},{10,... | collective-permute-start | bytes 208904 | tf_op jit(solution)/shard_map/ppermute | solution.py:487
  26.4 2.6 %collective-permute-start.4 = (bf16[272,128]{1,0:T(8,128)(2,1)S(1)}, bf16[272,128]{1,0:T(8,128)(2,1)S(1)}, u32[]{:S(2)}, u32[]{:S(2)}) collective-permute-start(bf16[272,128]{1,0:T(8,128)(2,1)S(1)} %get-tuple-element.51), channel_id=1, source_target_pairs={{0,8},{1,9},{2,10},{3,11},{4,12},{5,13},{6,14},{7,15},{8,0},{9,1},... | collective-permute-start | bytes 208904 | tf_op jit(solution)/shard_map/ppermute | solution.py:487
  29.2 2.1 %collective-permute-start.7 = (bf16[272,128]{1,0:T(8,128)(2,1)S(1)}, bf16[272,128]{1,0:T(8,128)(2,1)S(1)}, u32[]{:S(2)}, u32[]{:S(2)}) collective-permute-start(bf16[272,128]{1,0:T(8,128)(2,1)S(1)} %get-tuple-element.54), channel_id=1, source_target_pairs={{0,20},{1,21},{2,22},{3,23},{4,16},{5,17},{6,18},{7,19},{8,28},{9,... | collective-permute-start | bytes 208904 | tf_op jit(solution)/shard_map/ppermute | solution.py:487
  31.3 2.9 %collective-permute-start.8 = (bf16[272,128]{1,0:T(8,128)(2,1)S(1)}, bf16[272,128]{1,0:T(8,128)(2,1)S(1)}, u32[]{:S(2)}, u32[]{:S(2)}) collective-permute-start(bf16[272,128]{1,0:T(8,128)(2,1)S(1)} %get-tuple-element.55), channel_id=1, source_target_pairs={{0,24},{1,25},{2,26},{3,27},{4,28},{5,29},{6,30},{7,31},{8,16},{9,... | collective-permute-start | bytes 208904 | tf_op jit(solution)/shard_map/ppermute | solution.py:487
  34.2 1.7 %collective-permute-start.9 = (bf16[272,128]{1,0:T(8,128)(2,1)S(1)}, bf16[272,128]{1,0:T(8,128)(2,1)S(1)}, u32[]{:S(2)}, u32[]{:S(2)}) collective-permute-start(bf16[272,128]{1,0:T(8,128)(2,1)S(1)} %get-tuple-element.56), channel_id=1, source_target_pairs={{0,28},{1,29},{2,30},{3,31},{4,24},{5,25},{6,26},{7,27},{8,20},{9,... | collective-permute-start | bytes 208904 | tf_op jit(solution)/shard_map/ppermute | solution.py:487
  35.9 3.5 %collective-permute-done.8.rest_6_ = bf16[272,128]{1,0:T(8,128)(2,1)S(1)} collective-permute-done((bf16[272,128]{1,0:T(8,128)(2,1)S(1)}, bf16[272,128]{1,0:T(8,128)(2,1)S(1)}, u32[]{:S(2)}, u32[]{:S(2)}) %collective-permute-start.8) | collective-permute-done | bytes 69664 | tf_op jit(solution)/shard_map/ppermute | solution.py:487
  39.5 1.8 %collective-permute-done.9.rest_7_ = bf16[272,128]{1,0:T(8,128)(2,1)S(1)} collective-permute-done((bf16[272,128]{1,0:T(8,128)(2,1)S(1)}, bf16[272,128]{1,0:T(8,128)(2,1)S(1)}, u32[]{:S(2)}, u32[]{:S(2)}) %collective-permute-start.9) | collective-permute-done | bytes 69664 | tf_op jit(solution)/shard_map/ppermute | solution.py:487
  41.3 3.4 %shard_map.71 = (bf16[256,128]{1,0:T(8,128)(2,1)S(1)}, bf16[256,128]{1,0:T(8,128)(2,1)S(1)}, bf16[256,128]{1,0:T(8,128)(2,1)S(1)}, bf16[256,128]{1,0:T(8,128)(2,...) custom-call(bf16[272,128]{1,0:T(8,128)(2,1)S(1)} %get-tuple-element., ...), custom_call_target="tpu_custom_call" | custom-call | flops 4294967296 | bytes 1048576 | tf_op jit(solution)/shard_map/pallas_call | solution.py:445
  44.8 4.1 %collective-permute-start.11 = (bf16[256,128]{1,0:T(8,128)(2,1)S(1)}, bf16[256,128]{1,0:T(8,128)(2,1)S(1)}, u32[]{:S(2)}, u32[]{:S(2)}) collective-permute-start(bf16[256,128]{1,0:T(8,128)(2,1)S(1)} %get-tuple-element.59), channel_id=1, source_target_pairs={{0,8},{1,9},{2,10},{3,11},{4,12},{5,13},{6,14},{7,15},{8,0},{9,1},... | collective-permute-start | bytes 196616 | tf_op jit(solution)/shard_map/ppermute | solution.py:487
  49.1 2.0 %collective-permute-start.13 = (bf16[256,128]{1,0:T(8,128)(2,1)S(1)}, bf16[256,128]{1,0:T(8,128)(2,1)S(1)}, u32[]{:S(2)}, u32[]{:S(2)}) collective-permute-start(bf16[256,128]{1,0:T(8,128)(2,1)S(1)} %get-tuple-element.61), channel_id=1, source_target_pairs={{0,16},{1,17},{2,18},{3,19},{4,20},{5,21},{6,22},{7,23},{8,24},{9,... | collective-permute-start | bytes 196616 | tf_op jit(solution)/shard_map/ppermute | solution.py:487
  51.1 3.0 %collective-permute-start.15 = (bf16[256,128]{1,0:T(8,128)(2,1)S(1)}, bf16[256,128]{1,0:T(8,128)(2,1)S(1)}, u32[]{:S(2)}, u32[]{:S(2)}) collective-permute-start(bf16[256,128]{1,0:T(8,128)(2,1)S(1)} %get-tuple-element.63), channel_id=1, source_target_pairs={{0,24},{1,25},{2,26},{3,27},{4,28},{5,29},{6,30},{7,31},{8,16},{9,... | collective-permute-start | bytes 196616 | tf_op jit(solution)/shard_map/ppermute | solution.py:487
  54.2 1.7 %collective-permute-start.16 = (bf16[256,128]{1,0:T(8,128)(2,1)S(1)}, bf16[256,128]{1,0:T(8,128)(2,1)S(1)}, u32[]{:S(2)}, u32[]{:S(2)}) collective-permute-start(bf16[256,128]{1,0:T(8,128)(2,1)S(1)} %get-tuple-element.64), channel_id=1, source_target_pairs={{0,28},{1,29},{2,30},{3,31},{4,24},{5,25},{6,26},{7,27},{8,20},{9,... | collective-permute-start | bytes 196616 | tf_op jit(solution)/shard_map/ppermute | solution.py:487
  56.4 2.0 %collective-permute-done.15.rest_6_ = bf16[256,128]{1,0:T(8,128)(2,1)S(1)} collective-permute-done((bf16[256,128]{1,0:T(8,128)(2,1)S(1)}, bf16[256,128]{1,0:T(8,128)(2,1)S(1)}, u32[]{:S(2)}, u32[]{:S(2)}) %collective-permute-start.15) | collective-permute-done | bytes 65568 | tf_op jit(solution)/shard_map/ppermute | solution.py:487
  58.4 2.7 %collective-permute-done.16.rest_7_ = bf16[256,128]{1,0:T(8,128)(2,1)S(1)} collective-permute-done((bf16[256,128]{1,0:T(8,128)(2,1)S(1)}, bf16[256,128]{1,0:T(8,128)(2,1)S(1)}, u32[]{:S(2)}, u32[]{:S(2)}) %collective-permute-start.16) | collective-permute-done | bytes 65568 | tf_op jit(solution)/shard_map/ppermute | solution.py:487
  62.1 1.7 %shard_map.74.sent = bf16[2,272,1024]{2,1,0:T(8,128)(2,1)S(1)} custom-call(bf16[256,512]{1,0:T(8,128)(2,1)S(1)} %get-tuple-element.66.lp, bf16[256,512]{1,0:T(8,128)(2,1)S(1)} %get-tuple-element.70.ls.a0, bf16[256,512]{1,0:T(8,128)(2,1)S(1)} %get-tuple-element.41.prim, bf16[256,512]{1,0:T(8,128)(2,1)S(1)} %get-tuple-element.68.second, ...), custom_call_target="tpu_custom_call" | custom-call | flops 2147483648 | bytes 1048576 | tf_op jit(solution)/shard_map/pallas_call | solution.py:445
  63.9 2.4 %collective-permute-start.21 = (bf16[1024,512]{1,0:T(8,128)(2,1)S(1)}, bf16[1024,512]{1,0:T(8,128)(2,1)S(1)}, u32[]{:S(2)}, u32[]{:S(2)}) collective-permute-start(bf16[1024,512]{1,0:T(8,128)(2,1)S(1)} %get-tuple-element.46.w1), channel_id=1, source_target_pairs={{16,17},{17,16},{18,19},{19,18},{20,21},{21,20},{22,23},{23,22},{2... | collective-permute-start | bytes 3145736 | tf_op jit(solution)/shard_map/ppermute | solution.py:487
  66.3 3.4 %collective-permute-start.22 = (bf16[1024,512]{1,0:T(8,128)(2,1)S(1)}, bf16[1024,512]{1,0:T(8,128)(2,1)S(1)}, u32[]{:S(2)}, u32[]{:S(2)}) collective-permute-start(bf16[1024,512]{1,0:T(8,128)(2,1)S(1)} %get-tuple-element.72.w2), channel_id=1, source_target_pairs={{16,18},{17,19},{18,16},{19,17},{20,22},{21,23},{22,20},{23,21},{2... | collective-permute-start | bytes 3145736 | tf_op jit(solution)/shard_map/ppermute | solution.py:487
  69.7 1.9 %collective-permute-start.23 = (bf16[1024,512]{1,0:T(8,128)(2,1)S(1)}, bf16[1024,512]{1,0:T(8,128)(2,1)S(1)}, u32[]{:S(2)}, u32[]{:S(2)}) collective-permute-start(bf16[1024,512]{1,0:T(8,128)(2,1)S(1)} %get-tuple-element.73.w3), channel_id=1, source_target_pairs={{16,19},{17,18},{18,17},{19,16},{20,23},{21,22},{22,21},{23,20},{2... | collective-permute-start | bytes 3145736 | tf_op jit(solution)/shard_map/ppermute | solution.py:487
  71.6 3.3 %collective-permute-start.17 = (bf16[256,512]{1,0:T(8,128)(2,1)S(1)}, bf16[256,512]{1,0:T(8,128)(2,1)S(1)}, u32[]{:S(2)}, u32[]{:S(2)}) collective-permute-start(bf16[256,512]{1,0:T(8,128)(2,1)S(1)} %get-tuple-element.70.ls.a0), channel_id=1, source_target_pairs={{16,18},{17,19},{18,16},{19,17},{20,22},{21,23},{22,20},{23,21},{2... | collective-permute-start | bytes 786440 | tf_op jit(solution)/shard_map/ppermute | solution.py:487
  74.9 1.2 shard_map.73.kept
  77.0 45.3 %collective-permute-done.17.a2 = bf16[256,512]{1,0:T(8,128)(2,1)S(1)} collective-permute-done((bf16[256,512]{1,0:T(8,128)(2,1)S(1)}, bf16[256,512]{1,0:T(8,128)(2,1)S(1)}, u32[]{:S(2)}, u32[]{:S(2)}) %collective-permute-start.17) | collective-permute-done | bytes 262176 | tf_op jit(solution)/shard_map/ppermute | solution.py:487
  122.3 1.9 %collective-permute-start.19 = (bf16[256,512]{1,0:T(8,128)(2,1)S(1)}, bf16[256,512]{1,0:T(8,128)(2,1)S(1)}, u32[]{:S(2)}, u32[]{:S(2)}) collective-permute-start(bf16[256,512]{1,0:T(8,128)(2,1)S(1)} %get-tuple-element.70.ls.a0), channel_id=1, source_target_pairs={{16,17},{17,16},{18,19},{19,18},{20,21},{21,20},{22,23},{23,22},{2... | collective-permute-start | bytes 786440 | tf_op jit(solution)/shard_map/ppermute | solution.py:487
  124.2 2.4 %collective-permute-start.20 = (bf16[256,512]{1,0:T(8,128)(2,1)S(1)}, bf16[256,512]{1,0:T(8,128)(2,1)S(1)}, u32[]{:S(2)}, u32[]{:S(2)}) collective-permute-start(bf16[256,512]{1,0:T(8,128)(2,1)S(1)} %collective-permute-done.17.a2), channel_id=1, source_target_pairs={{16,17},{17,16},{18,19},{19,18},{20,21},{21,20},{22,23},{23,22},{2... | collective-permute-start | bytes 786440 | tf_op jit(solution)/shard_map/ppermute | solution.py:487
  127.8 2.1 %shard_map.76 = bf16[256,1024]{1,0:T(8,128)(2,1)} custom-call(bf16[256,512]{1,0:T(8,128)(2,1)S(1)} %get-tuple-element.70.ls.a0, bf16[256,512]{1,0:T(8,128)(2,1)S(1)} %collective-permute-done.19.a1, bf16[256,512]{1,0:T(8,128)(2,1)S(1)} %collective-permute-done.17.a2, bf16[256,512]{1,0:T(8,128)(2,1)S(1)} %collective-permute-done.20.a3, ...), custom_call_target="tpu_custom_call" | custom-call | flops 2147483648 | bytes 1048576 | tf_op jit(solution)/shard_map/pallas_call | solution.py:445
  129.8 3.4 %collective-permute-done.24.far = bf16[272,1024]{1,0:T(8,128)(2,1)S(1)} collective-permute-done((bf16[272,1024]{1,0:T(8,128)(2,1)S(1)}, bf16[272,1024]{1,0:T(8,128)(2,1)S(1)}, u32[]{:S(2)}, u32[]{:S(2)}) %collective-permute-start.24) | collective-permute-done | bytes 557088 | tf_op jit(solution)/shard_map/ppermute | solution.py:487
  133.3 1.2 shard_map.78
  (33 shorter events, 6.0 us)
Async XLA Ops:
  0.6 20.3 %collective-permute-start = (bf16[256,1024]{1,0:T(8,128)(2,1)}, bf16[256,1024]{1,0:T(8,128)(2,1)S(1)}, u32[]{:S(2)}, u32[]{:S(2)}) collective-permute-start(bf16[256,1024]{1,0:T(8,128)(2,1)} %c0.1), channel_id=1, source_target_pairs={{16,17},{17,16},{18,19},{19,18},{20,21},{21,20},{22,23},{23,22},{2... | collective-permute-start | bytes 1572872 | tf_op jit(solution)/shard_map/ppermute | solution.py:487
  2.6 16.4 %collective-permute-start.1 = (bf16[256,1024]{1,0:T(8,128)(2,1)}, bf16[256,1024]{1,0:T(8,128)(2,1)S(1)}, u32[]{:S(2)}, u32[]{:S(2)}) collective-permute-start(bf16[256,1024]{1,0:T(8,128)(2,1)} %c0.1), channel_id=1, source_target_pairs={{16,18},{17,19},{18,16},{19,17},{20,22},{21,23},{22,20},{23,21},{2... | collective-permute-start | bytes 1572872 | tf_op jit(solution)/shard_map/ppermute | solution.py:487
  6.0 14.9 %copy-start = (bf16[256,1024]{1,0:T(8,128)(2,1)S(1)}, bf16[256,1024]{1,0:T(8,128)(2,1)}, u32[]{:S(2)}) copy-start(bf16[256,1024]{1,0:T(8,128)(2,1)} %c0.1) | copy-start | bytes 1572868
  19.0 3.8 %collective-permute-start.2 = (bf16[256,1024]{1,0:T(8,128)(2,1)S(1)}, bf16[256,1024]{1,0:T(8,128)(2,1)S(1)}, u32[]{:S(2)}, u32[]{:S(2)}) collective-permute-start(bf16[256,1024]{1,0:T(8,128)(2,1)S(1)} %collective-permute-done.1.c2), channel_id=1, source_target_pairs={{16,17},{17,16},{18,19},{19,18},{20,21},{21,20},{22,23},{23,22},{2... | collective-permute-start | bytes 1572872 | tf_op jit(solution)/shard_map/ppermute | solution.py:487
  20.9 1.9 %copy-start.1 = (s32[2,1]{0,1:T(1,128)S(1)}, s32[2,1]{0,1:T(1,128)}, u32[]{:S(2)}) copy-start(s32[2,1]{0,1:T(1,128)} %param.8) | copy-start | bytes 28
  24.7 6.6 %collective-permute-start.3 = (bf16[272,128]{1,0:T(8,128)(2,1)S(1)}, bf16[272,128]{1,0:T(8,128)(2,1)S(1)}, u32[]{:S(2)}, u32[]{:S(2)}) collective-permute-start(bf16[272,128]{1,0:T(8,128)(2,1)S(1)} %get-tuple-element.50), channel_id=1, source_target_pairs={{0,4},{1,5},{2,6},{3,7},{4,0},{5,1},{6,2},{7,3},{8,12},{9,13},{10,... | collective-permute-start | bytes 208904 | tf_op jit(solution)/shard_map/ppermute | solution.py:487
  26.4 7.9 %collective-permute-start.4 = (bf16[272,128]{1,0:T(8,128)(2,1)S(1)}, bf16[272,128]{1,0:T(8,128)(2,1)S(1)}, u32[]{:S(2)}, u32[]{:S(2)}) collective-permute-start(bf16[272,128]{1,0:T(8,128)(2,1)S(1)} %get-tuple-element.51), channel_id=1, source_target_pairs={{0,8},{1,9},{2,10},{3,11},{4,12},{5,13},{6,14},{7,15},{8,0},{9,1},... | collective-permute-start | bytes 208904 | tf_op jit(solution)/shard_map/ppermute | solution.py:487
  28.9 7.0 %collective-permute-start.5 = (bf16[272,128]{1,0:T(8,128)(2,1)S(1)}, bf16[272,128]{1,0:T(8,128)(2,1)S(1)}, u32[]{:S(2)}, u32[]{:S(2)}) collective-permute-start(bf16[272,128]{1,0:T(8,128)(2,1)S(1)} %get-tuple-element.52), channel_id=1, source_target_pairs={{0,12},{1,13},{2,14},{3,15},{4,8},{5,9},{6,10},{7,11},{8,4},{9,5},... | collective-permute-start | bytes 208904 | tf_op jit(solution)/shard_map/ppermute | solution.py:487
  29.2 6.8 %collective-permute-start.6 = (bf16[272,128]{1,0:T(8,128)(2,1)S(1)}, bf16[272,128]{1,0:T(8,128)(2,1)S(1)}, u32[]{:S(2)}, u32[]{:S(2)}) collective-permute-start(bf16[272,128]{1,0:T(8,128)(2,1)S(1)} %get-tuple-element.53), channel_id=1, source_target_pairs={{0,16},{1,17},{2,18},{3,19},{4,20},{5,21},{6,22},{7,23},{8,24},{9,... | collective-permute-start | bytes 208904 | tf_op jit(solution)/shard_map/ppermute | solution.py:487
  29.2 6.8 %collective-permute-start.7 = (bf16[272,128]{1,0:T(8,128)(2,1)S(1)}, bf16[272,128]{1,0:T(8,128)(2,1)S(1)}, u32[]{:S(2)}, u32[]{:S(2)}) collective-permute-start(bf16[272,128]{1,0:T(8,128)(2,1)S(1)} %get-tuple-element.54), channel_id=1, source_target_pairs={{0,20},{1,21},{2,22},{3,23},{4,16},{5,17},{6,18},{7,19},{8,28},{9,... | collective-permute-start | bytes 208904 | tf_op jit(solution)/shard_map/ppermute | solution.py:487
  31.3 8.1 %collective-permute-start.8 = (bf16[272,128]{1,0:T(8,128)(2,1)S(1)}, bf16[272,128]{1,0:T(8,128)(2,1)S(1)}, u32[]{:S(2)}, u32[]{:S(2)}) collective-permute-start(bf16[272,128]{1,0:T(8,128)(2,1)S(1)} %get-tuple-element.55), channel_id=1, source_target_pairs={{0,24},{1,25},{2,26},{3,27},{4,28},{5,29},{6,30},{7,31},{8,16},{9,... | collective-permute-start | bytes 208904 | tf_op jit(solution)/shard_map/ppermute | solution.py:487
  34.2 7.0 %collective-permute-start.9 = (bf16[272,128]{1,0:T(8,128)(2,1)S(1)}, bf16[272,128]{1,0:T(8,128)(2,1)S(1)}, u32[]{:S(2)}, u32[]{:S(2)}) collective-permute-start(bf16[272,128]{1,0:T(8,128)(2,1)S(1)} %get-tuple-element.56), channel_id=1, source_target_pairs={{0,28},{1,29},{2,30},{3,31},{4,24},{5,25},{6,26},{7,27},{8,20},{9,... | collective-permute-start | bytes 208904 | tf_op jit(solution)/shard_map/ppermute | solution.py:487
  44.6 6.5 %collective-permute-start.10 = (bf16[256,128]{1,0:T(8,128)(2,1)S(1)}, bf16[256,128]{1,0:T(8,128)(2,1)S(1)}, u32[]{:S(2)}, u32[]{:S(2)}) collective-permute-start(bf16[256,128]{1,0:T(8,128)(2,1)S(1)} %get-tuple-element.58), channel_id=1, source_target_pairs={{0,4},{1,5},{2,6},{3,7},{4,0},{5,1},{6,2},{7,3},{8,12},{9,13},{10,... | collective-permute-start | bytes 196616 | tf_op jit(solution)/shard_map/ppermute | solution.py:487
  44.8 9.4 %collective-permute-start.11 = (bf16[256,128]{1,0:T(8,128)(2,1)S(1)}, bf16[256,128]{1,0:T(8,128)(2,1)S(1)}, u32[]{:S(2)}, u32[]{:S(2)}) collective-permute-start(bf16[256,128]{1,0:T(8,128)(2,1)S(1)} %get-tuple-element.59), channel_id=1, source_target_pairs={{0,8},{1,9},{2,10},{3,11},{4,12},{5,13},{6,14},{7,15},{8,0},{9,1},... | collective-permute-start | bytes 196616 | tf_op jit(solution)/shard_map/ppermute | solution.py:487
  48.9 7.0 %collective-permute-start.12 = (bf16[256,128]{1,0:T(8,128)(2,1)S(1)}, bf16[256,128]{1,0:T(8,128)(2,1)S(1)}, u32[]{:S(2)}, u32[]{:S(2)}) collective-permute-start(bf16[256,128]{1,0:T(8,128)(2,1)S(1)} %get-tuple-element.60), channel_id=1, source_target_pairs={{0,12},{1,13},{2,14},{3,15},{4,8},{5,9},{6,10},{7,11},{8,4},{9,5},... | collective-permute-start | bytes 196616 | tf_op jit(solution)/shard_map/ppermute | solution.py:487
  49.1 6.8 %collective-permute-start.13 = (bf16[256,128]{1,0:T(8,128)(2,1)S(1)}, bf16[256,128]{1,0:T(8,128)(2,1)S(1)}, u32[]{:S(2)}, u32[]{:S(2)}) collective-permute-start(bf16[256,128]{1,0:T(8,128)(2,1)S(1)} %get-tuple-element.61), channel_id=1, source_target_pairs={{0,16},{1,17},{2,18},{3,19},{4,20},{5,21},{6,22},{7,23},{8,24},{9,... | collective-permute-start | bytes 196616 | tf_op jit(solution)/shard_map/ppermute | solution.py:487
  51.1 5.3 %collective-permute-start.14 = (bf16[256,128]{1,0:T(8,128)(2,1)S(1)}, bf16[256,128]{1,0:T(8,128)(2,1)S(1)}, u32[]{:S(2)}, u32[]{:S(2)}) collective-permute-start(bf16[256,128]{1,0:T(8,128)(2,1)S(1)} %get-tuple-element.62), channel_id=1, source_target_pairs={{0,20},{1,21},{2,22},{3,23},{4,16},{5,17},{6,18},{7,19},{8,28},{9,... | collective-permute-start | bytes 196616 | tf_op jit(solution)/shard_map/ppermute | solution.py:487
  51.1 7.3 %collective-permute-start.15 = (bf16[256,128]{1,0:T(8,128)(2,1)S(1)}, bf16[256,128]{1,0:T(8,128)(2,1)S(1)}, u32[]{:S(2)}, u32[]{:S(2)}) collective-permute-start(bf16[256,128]{1,0:T(8,128)(2,1)S(1)} %get-tuple-element.63), channel_id=1, source_target_pairs={{0,24},{1,25},{2,26},{3,27},{4,28},{5,29},{6,30},{7,31},{8,16},{9,... | collective-permute-start | bytes 196616 | tf_op jit(solution)/shard_map/ppermute | solution.py:487
  54.2 7.0 %collective-permute-start.16 = (bf16[256,128]{1,0:T(8,128)(2,1)S(1)}, bf16[256,128]{1,0:T(8,128)(2,1)S(1)}, u32[]{:S(2)}, u32[]{:S(2)}) collective-permute-start(bf16[256,128]{1,0:T(8,128)(2,1)S(1)} %get-tuple-element.64), channel_id=1, source_target_pairs={{0,28},{1,29},{2,30},{3,31},{4,24},{5,25},{6,26},{7,27},{8,20},{9,... | collective-permute-start | bytes 196616 | tf_op jit(solution)/shard_map/ppermute | solution.py:487
  63.8 12.3 %collective-permute-start.18 = (bf16[2,272,1024]{2,1,0:T(8,128)(2,1)S(1)}, bf16[2,272,1024]{2,1,0:T(8,128)(2,1)S(1)}, u32[]{:S(2)}, u32[]{:S(2)}) collective-permute-start(bf16[2,272,1024]{2,1,0:T(8,128)(2,1)S(1)} %shard_map.74.sent), channel_id=1, source_target_pairs={{0,1},{1,0},{2,3},{3,2},{4,5},{5,4},{6,7},{7,6},{8,9},{9,8},{10,11... | collective-permute-start | bytes 3342344 | tf_op jit(solution)/shard_map/ppermute | solution.py:487
  63.9 60.3 %collective-permute-start.21 = (bf16[1024,512]{1,0:T(8,128)(2,1)S(1)}, bf16[1024,512]{1,0:T(8,128)(2,1)S(1)}, u32[]{:S(2)}, u32[]{:S(2)}) collective-permute-start(bf16[1024,512]{1,0:T(8,128)(2,1)S(1)} %get-tuple-element.46.w1), channel_id=1, source_target_pairs={{16,17},{17,16},{18,19},{19,18},{20,21},{21,20},{22,23},{23,22},{2... | collective-permute-start | bytes 3145736 | tf_op jit(solution)/shard_map/ppermute | solution.py:487
  66.3 60.4 %collective-permute-start.22 = (bf16[1024,512]{1,0:T(8,128)(2,1)S(1)}, bf16[1024,512]{1,0:T(8,128)(2,1)S(1)}, u32[]{:S(2)}, u32[]{:S(2)}) collective-permute-start(bf16[1024,512]{1,0:T(8,128)(2,1)S(1)} %get-tuple-element.72.w2), channel_id=1, source_target_pairs={{16,18},{17,19},{18,16},{19,17},{20,22},{21,23},{22,20},{23,21},{2... | collective-permute-start | bytes 3145736 | tf_op jit(solution)/shard_map/ppermute | solution.py:487
  69.7 57.0 %collective-permute-start.23 = (bf16[1024,512]{1,0:T(8,128)(2,1)S(1)}, bf16[1024,512]{1,0:T(8,128)(2,1)S(1)}, u32[]{:S(2)}, u32[]{:S(2)}) collective-permute-start(bf16[1024,512]{1,0:T(8,128)(2,1)S(1)} %get-tuple-element.73.w3), channel_id=1, source_target_pairs={{16,19},{17,18},{18,17},{19,16},{20,23},{21,22},{22,21},{23,20},{2... | collective-permute-start | bytes 3145736 | tf_op jit(solution)/shard_map/ppermute | solution.py:487
  71.6 50.7 %collective-permute-start.17 = (bf16[256,512]{1,0:T(8,128)(2,1)S(1)}, bf16[256,512]{1,0:T(8,128)(2,1)S(1)}, u32[]{:S(2)}, u32[]{:S(2)}) collective-permute-start(bf16[256,512]{1,0:T(8,128)(2,1)S(1)} %get-tuple-element.70.ls.a0), channel_id=1, source_target_pairs={{16,18},{17,19},{18,16},{19,17},{20,22},{21,23},{22,20},{23,21},{2... | collective-permute-start | bytes 786440 | tf_op jit(solution)/shard_map/ppermute | solution.py:487
  76.3 57.0 %collective-permute-start.24 = (bf16[272,1024]{1,0:T(8,128)(2,1)S(1)}, bf16[272,1024]{1,0:T(8,128)(2,1)S(1)}, u32[]{:S(2)}, u32[]{:S(2)}) collective-permute-start(bf16[272,1024]{1,0:T(8,128)(2,1)S(1)} %shard_map.75.half), channel_id=1, source_target_pairs={{0,2},{1,3},{2,0},{3,1},{4,6},{5,7},{6,4},{7,5},{8,10},{9,11},{10,... | collective-permute-start | bytes 1671176 | tf_op jit(solution)/shard_map/ppermute | solution.py:487
  122.3 4.4 %collective-permute-start.19 = (bf16[256,512]{1,0:T(8,128)(2,1)S(1)}, bf16[256,512]{1,0:T(8,128)(2,1)S(1)}, u32[]{:S(2)}, u32[]{:S(2)}) collective-permute-start(bf16[256,512]{1,0:T(8,128)(2,1)S(1)} %get-tuple-element.70.ls.a0), channel_id=1, source_target_pairs={{16,17},{17,16},{18,19},{19,18},{20,21},{21,20},{22,23},{23,22},{2... | collective-permute-start | bytes 786440 | tf_op jit(solution)/shard_map/ppermute | solution.py:487
  124.2 3.6 %collective-permute-start.20 = (bf16[256,512]{1,0:T(8,128)(2,1)S(1)}, bf16[256,512]{1,0:T(8,128)(2,1)S(1)}, u32[]{:S(2)}, u32[]{:S(2)}) collective-permute-start(bf16[256,512]{1,0:T(8,128)(2,1)S(1)} %collective-permute-done.17.a2), channel_id=1, source_target_pairs={{16,17},{17,16},{18,19},{19,18},{20,21},{21,20},{22,23},{23,22},{2... | collective-permute-start | bytes 786440 | tf_op jit(solution)/shard_map/ppermute | solution.py:487

commit v2 on v1

--- a/solution.py
+++ b/solution.py
@@ -453,9 +453,12 @@
     )(*ins)
 
 
-def scales_kernel(width, spread, inverse, shrink):
+def inverse_kernel(spread, inverse):
+    inverse[...] = 1.0 / spread[...]
+
+
+def shrink_kernel(width, spread, shrink):
     root = spread[...]
-    inverse[...] = 1.0 / root
     shrink[...] = 1.0 / (width * root * root * root)
 
 
@@ -478,24 +481,25 @@
     group = projections.shape[3]
     counts = live_counts.T
 
-    def swap(x, over_heads, over_mp, least=0):
+    def swap(x, over_heads, over_mp, senders=range(n_seg)):
         pairs = [
             (e * n_mp + m, (e ^ over_heads) * n_mp + (m ^ over_mp))
-            for e in range(least * n_blk, heads)
+            for e in range(heads)
             for m in range(n_mp)
+            if e // n_blk in senders
         ]
         return lax.ppermute(x, AXES, pairs)
 
-    far_first = sorted(range(1, heads), key=lambda k: -((k % n_blk) * 2 + 1 - k // n_blk))
+    document, summary = (0,), (1,)
 
     def exchange(pieces):
-        moved = {}
-        for k in far_first:
-            moved[k] = swap(pieces[k], k, 0)
-        return [pieces[0]] + [moved[k] for k in range(1, heads)]
-
-    far_cot = swap(cotangent, 0, 2, 1)
-    near_cot = swap(cotangent, 0, 1, 1)
+        moved = [pieces[0]]
+        for k in range(1, heads):
+            moved.append(swap(pieces[k], k, 0))
+        return moved
+
+    far_cot = swap(cotangent, 0, 2, summary)
+    near_cot = swap(cotangent, 0, 1, summary)
     tiles = group // LANES
     mixed = projections.reshape(width, 2, tiles, LANES).transpose(0, 2, 1, 3)
     mixed = mixed.reshape(width * 2 * tiles, LANES)
@@ -528,9 +532,9 @@
     )
     wp, ws = made[0], made[1 : 1 + n_mp]
     own, own_states, own_gain, spread, prim, sec = made[1 + n_mp :]
-    lent_1 = swap(ws[1], 0, 1, 1)
+    lent_3 = swap(ws[3], n_blk, 3, summary)
     far_cot, spread = lax.optimization_barrier((far_cot, spread))
-    cross_cot = swap(far_cot, 0, 1, 1)
+    cross_cot = swap(far_cot, 0, 1, summary)
     acc = call(
         part_kernel,
         (cotangent, near_cot, far_cot, *ws[:3]),
@@ -540,9 +544,6 @@
         16,
         1 << 30,
     )[0]
-    lent_2, lent_3, far_cot = lax.optimization_barrier((ws[2], ws[3], far_cot))
-    lent_2 = swap(lent_2, 0, 2, 1)
-    lent_3 = swap(lent_3, 0, 3, 1)
     made = call(
         functools.partial(pack_kernel, sizes),
         (counts, prim, sec, acc, cross_cot, ws[3]),
@@ -554,9 +555,8 @@
     )
     second, pieces = made[0], made[1:]
     pieces = exchange(pieces)
-    inverse, shrink = call(
-        functools.partial(scales_kernel, width), (spread,), [INSIDE], [((rows, LANES), F32)] * 2
-    )
+    lent_2 = swap(ws[2], 0, 2, summary)
+    (inverse,) = call(inverse_kernel, (spread,), [INSIDE], [((rows, LANES), F32)])
     pieces = call(
         functools.partial(attend_kernel, sizes),
         pieces,
@@ -571,6 +571,10 @@
         4 << 30,
     )
     pieces = exchange(pieces)
+    lent_3 = swap(lent_3, n_blk, 0, document)
+    (shrink,) = call(
+        functools.partial(shrink_kernel, width), (spread,), [INSIDE], [((rows, LANES), F32)]
+    )
     lp, ls = call(
         functools.partial(regroup_kernel, sizes),
         (counts, *pieces),
@@ -578,7 +582,7 @@
         [((rows, group), BF16)] * 2,
         [pltpu.VMEM((heads, rows, LANES), BF16)],
     )
-    far_att = swap(ls, 0, 2, 1)
+    far_att = swap(ls, 0, 2, summary)
     (sent,) = call(
         functools.partial(send_kernel, sizes),
         (lp, ls, prim, second, spread, wp, ws[3], ws[1]),
@@ -600,9 +604,10 @@
     )
     (half,) = call(fold_kernel, (kept, got, sent), [INSIDE] * 3, [((rows + TAIL, feats), BF16)])
     far = swap(half, 0, 2)
-    far_att, own_att, half_seen = lax.optimization_barrier((far_att, ls, half))
-    near_att = swap(own_att, 0, 1, 1)
-    cross_att = swap(far_att, 0, 1, 1)
+    far_att, own_att, lent_1, half_seen = lax.optimization_barrier((far_att, ls, ws[1], half))
+    lent_1 = swap(lent_1, 0, 1, summary)
+    near_att = swap(own_att, 0, 1, summary)
+    cross_att = swap(far_att, 0, 1, summary)
     (out,) = call(
         layer_kernel,
         (ls, near_att, far_att, cross_att, ws[0], lent_1, lent_2, lent_3, own),

time: 135 us -> 115 us (0.85)
  the two profiles are of different devices: /device:TPU:2 before, /device:TPU:3 now
where the time goes in v2:
time: 115 us
  starting transfers between devices  52.4 us (46%)
  waiting for transfers between devices  39 us (34%)
  Pallas kernels  22.5 us (20%)
    ppermute x26, starting transfers between devices, swap(): return lax.ppermute(x, AXES, pairs)  52.4 us
    ppermute x26, waiting for transfers between devices, swap(): return lax.ppermute(x, AXES, pairs)  39 us
    pallas_call x12, Pallas kernels, call(): pl.pallas_call(body, in_specs=list(specs), out_specs=[INSIDE] * len(outs)...  22.5 us
  transfers between devices with their start and end apart: 26, of which 6 were waited for; matrix products, arithmetic and copies ran while one was open for 0% of the time, Pallas kernels for 13%

profile of v2, /device:TPU:3, one launch (start us, length us, event | category | flops | bytes accessed | tf_op | source)
XLA Modules:
  0.0 115.0 jit_solution(6884961957111269666)
XLA Ops:
  0.6 2.6 %collective-permute-start = (bf16[256,1024]{1,0:T(8,128)(2,1)}, bf16[256,1024]{1,0:T(8,128)(2,1)S(1)}, u32[]{:S(2)}, u32[]{:S(2)}) collective-permute-start(bf16[256,1024]{1,0:T(8,128)(2,1)} %c0.1), channel_id=1, source_target_pairs={{16,17},{17,16},{18,19},{19,18},{20,21},{21,20},{22,23},{23,22},{2... | collective-permute-start | bytes 1572872 | tf_op jit(solution)/shard_map/ppermute | solution.py:491
  3.2 3.1 %collective-permute-start.1 = (bf16[256,1024]{1,0:T(8,128)(2,1)}, bf16[256,1024]{1,0:T(8,128)(2,1)S(1)}, u32[]{:S(2)}, u32[]{:S(2)}) collective-permute-start(bf16[256,1024]{1,0:T(8,128)(2,1)} %c0.1), channel_id=1, source_target_pairs={{16,18},{17,19},{18,16},{19,17},{20,22},{21,23},{22,20},{23,21},{2... | collective-permute-start | bytes 1572872 | tf_op jit(solution)/shard_map/ppermute | solution.py:491
  6.4 8.9 %shard_map.68 = (bf16[4,1024,512]{2,1,0:T(8,128)(2,1)S(1)}, bf16[1024,512]{1,0:T(8,128)(2,1)S(1)}, bf16[1024,512]{1,0:T(8,128)(2,1)S(1)}, bf16[1024,512]{1,0:T(8...) custom-call(bf16[256,4096]{1,0:T(8,128)(2,1)} %bitcast.13, ...), custom_call_target="tpu_custom_call" | custom-call | flops 8589934592 | bytes 1048576 | tf_op jit(solution)/shard_map/pallas_call | solution.py:445
  15.3 3.5 %collective-permute-done.1.c2 = bf16[256,1024]{1,0:T(8,128)(2,1)S(1)} collective-permute-done((bf16[256,1024]{1,0:T(8,128)(2,1)}, bf16[256,1024]{1,0:T(8,128)(2,1)S(1)}, u32[]{:S(2)}, u32[]{:S(2)}) %collective-permute-start.1) | collective-permute-done | bytes 524320 | tf_op jit(solution)/shard_map/ppermute | solution.py:491
  18.8 2.8 %collective-permute-start.2 = (bf16[256,1024]{1,0:T(8,128)(2,1)S(1)}, bf16[256,1024]{1,0:T(8,128)(2,1)S(1)}, u32[]{:S(2)}, u32[]{:S(2)}) collective-permute-start(bf16[256,1024]{1,0:T(8,128)(2,1)S(1)} %collective-permute-done.1.c2), channel_id=1, source_target_pairs={{16,17},{17,16},{18,19},{19,18},{20,21},{21,20},{22,23},{23,22},{2... | collective-permute-start | bytes 1572872 | tf_op jit(solution)/shard_map/ppermute | solution.py:491
  23.1 1.9 %shard_map.70 = (bf16[256,512]{1,0:T(8,128)(2,1)S(1)}, bf16[272,128]{1,0:T(8,128)(2,1)S(1)}, bf16[272,128]{1,0:T(8,128)(2,1)S(1)}, bf16[272,128]{1,0:T(8,128)(2,...) custom-call(s32[1,2]{1,0:T(1,128)S(1)} %bitcast.9, ...), custom_call_target="tpu_custom_call" | custom-call | flops 1073741824 | bytes 1048576 | tf_op jit(solution)/shard_map/pallas_call | solution.py:445
  25.0 1.4 %collective-permute-start.3 = (bf16[272,128]{1,0:T(8,128)(2,1)S(1)}, bf16[272,128]{1,0:T(8,128)(2,1)S(1)}, u32[]{:S(2)}, u32[]{:S(2)}) collective-permute-start(bf16[272,128]{1,0:T(8,128)(2,1)S(1)} %get-tuple-element.47), channel_id=1, source_target_pairs={{0,4},{1,5},{2,6},{3,7},{4,0},{5,1},{6,2},{7,3},{8,12},{9,13},{10,... | collective-permute-start | bytes 208904 | tf_op jit(solution)/shard_map/ppermute | solution.py:491
  26.4 2.3 %collective-permute-start.4 = (bf16[272,128]{1,0:T(8,128)(2,1)S(1)}, bf16[272,128]{1,0:T(8,128)(2,1)S(1)}, u32[]{:S(2)}, u32[]{:S(2)}) collective-permute-start(bf16[272,128]{1,0:T(8,128)(2,1)S(1)} %get-tuple-element.48), channel_id=1, source_target_pairs={{0,8},{1,9},{2,10},{3,11},{4,12},{5,13},{6,14},{7,15},{8,0},{9,1},... | collective-permute-start | bytes 208904 | tf_op jit(solution)/shard_map/ppermute | solution.py:491
  28.7 1.5 %collective-permute-start.7 = (bf16[272,128]{1,0:T(8,128)(2,1)S(1)}, bf16[272,128]{1,0:T(8,128)(2,1)S(1)}, u32[]{:S(2)}, u32[]{:S(2)}) collective-permute-start(bf16[272,128]{1,0:T(8,128)(2,1)S(1)} %get-tuple-element.51), channel_id=1, source_target_pairs={{0,20},{1,21},{2,22},{3,23},{4,16},{5,17},{6,18},{7,19},{8,28},{9,... | collective-permute-start | bytes 208904 | tf_op jit(solution)/shard_map/ppermute | solution.py:491
  30.2 2.9 %collective-permute-start.8 = (bf16[272,128]{1,0:T(8,128)(2,1)S(1)}, bf16[272,128]{1,0:T(8,128)(2,1)S(1)}, u32[]{:S(2)}, u32[]{:S(2)}) collective-permute-start(bf16[272,128]{1,0:T(8,128)(2,1)S(1)} %get-tuple-element.52), channel_id=1, source_target_pairs={{0,24},{1,25},{2,26},{3,27},{4,28},{5,29},{6,30},{7,31},{8,16},{9,... | collective-permute-start | bytes 208904 | tf_op jit(solution)/shard_map/ppermute | solution.py:491
  33.1 1.2 %collective-permute-start.9 = (bf16[272,128]{1,0:T(8,128)(2,1)S(1)}, bf16[272,128]{1,0:T(8,128)(2,1)S(1)}, u32[]{:S(2)}, u32[]{:S(2)}) collective-permute-start(bf16[272,128]{1,0:T(8,128)(2,1)S(1)} %get-tuple-element.53), channel_id=1, source_target_pairs={{0,28},{1,29},{2,30},{3,31},{4,24},{5,25},{6,26},{7,27},{8,20},{9,... | collective-permute-start | bytes 208904 | tf_op jit(solution)/shard_map/ppermute | solution.py:491
  35.5 3.6 %collective-permute-done.9.rest_7_ = bf16[272,128]{1,0:T(8,128)(2,1)S(1)} collective-permute-done((bf16[272,128]{1,0:T(8,128)(2,1)S(1)}, bf16[272,128]{1,0:T(8,128)(2,1)S(1)}, u32[]{:S(2)}, u32[]{:S(2)}) %collective-permute-start.9) | collective-permute-done | bytes 69664 | tf_op jit(solution)/shard_map/ppermute | solution.py:491
  39.0 3.4 %shard_map.71 = (bf16[256,128]{1,0:T(8,128)(2,1)S(1)}, bf16[256,128]{1,0:T(8,128)(2,1)S(1)}, bf16[256,128]{1,0:T(8,128)(2,1)S(1)}, bf16[256,128]{1,0:T(8,128)(2,...) custom-call(bf16[272,128]{1,0:T(8,128)(2,1)S(1)} %get-tuple-element., ...), custom_call_target="tpu_custom_call" | custom-call | flops 4294967296 | bytes 1048576 | tf_op jit(solution)/shard_map/pallas_call | solution.py:445
  42.4 1.2 %collective-permute-start.10 = (bf16[256,128]{1,0:T(8,128)(2,1)S(1)}, bf16[256,128]{1,0:T(8,128)(2,1)S(1)}, u32[]{:S(2)}, u32[]{:S(2)}) collective-permute-start(bf16[256,128]{1,0:T(8,128)(2,1)S(1)} %get-tuple-element.55), channel_id=1, source_target_pairs={{0,4},{1,5},{2,6},{3,7},{4,0},{5,1},{6,2},{7,3},{8,12},{9,13},{10,... | collective-permute-start | bytes 196616 | tf_op jit(solution)/shard_map/ppermute | solution.py:491
  43.9 2.2 %collective-permute-start.12 = (bf16[256,128]{1,0:T(8,128)(2,1)S(1)}, bf16[256,128]{1,0:T(8,128)(2,1)S(1)}, u32[]{:S(2)}, u32[]{:S(2)}) collective-permute-start(bf16[256,128]{1,0:T(8,128)(2,1)S(1)} %get-tuple-element.57), channel_id=1, source_target_pairs={{0,12},{1,13},{2,14},{3,15},{4,8},{5,9},{6,10},{7,11},{8,4},{9,5},... | collective-permute-start | bytes 196616 | tf_op jit(solution)/shard_map/ppermute | solution.py:491
  46.0 1.6 %collective-permute-start.13 = (bf16[256,128]{1,0:T(8,128)(2,1)S(1)}, bf16[256,128]{1,0:T(8,128)(2,1)S(1)}, u32[]{:S(2)}, u32[]{:S(2)}) collective-permute-start(bf16[256,128]{1,0:T(8,128)(2,1)S(1)} %get-tuple-element.58), channel_id=1, source_target_pairs={{0,16},{1,17},{2,18},{3,19},{4,20},{5,21},{6,22},{7,23},{8,24},{9,... | collective-permute-start | bytes 196616 | tf_op jit(solution)/shard_map/ppermute | solution.py:491
  47.9 3.1 %collective-permute-start.15 = (bf16[256,128]{1,0:T(8,128)(2,1)S(1)}, bf16[256,128]{1,0:T(8,128)(2,1)S(1)}, u32[]{:S(2)}, u32[]{:S(2)}) collective-permute-start(bf16[256,128]{1,0:T(8,128)(2,1)S(1)} %get-tuple-element.60), channel_id=1, source_target_pairs={{0,24},{1,25},{2,26},{3,27},{4,28},{5,29},{6,30},{7,31},{8,16},{9,... | collective-permute-start | bytes 196616 | tf_op jit(solution)/shard_map/ppermute | solution.py:491
  51.0 1.2 %collective-permute-start.16 = (bf16[256,128]{1,0:T(8,128)(2,1)S(1)}, bf16[256,128]{1,0:T(8,128)(2,1)S(1)}, u32[]{:S(2)}, u32[]{:S(2)}) collective-permute-start(bf16[256,128]{1,0:T(8,128)(2,1)S(1)} %get-tuple-element.61), channel_id=1, source_target_pairs={{0,28},{1,29},{2,30},{3,31},{4,24},{5,25},{6,26},{7,27},{8,20},{9,... | collective-permute-start | bytes 196616 | tf_op jit(solution)/shard_map/ppermute | solution.py:491
  52.2 8.8 %collective-permute-start.23 = (bf16[1024,512]{1,0:T(8,128)(2,1)S(1)}, bf16[1024,512]{1,0:T(8,128)(2,1)S(1)}, u32[]{:S(2)}, u32[]{:S(2)}) collective-permute-start(bf16[1024,512]{1,0:T(8,128)(2,1)S(1)} %get-tuple-element.45.w3), channel_id=1, source_target_pairs={{16,3},{17,2},{18,1},{19,0},{20,7},{21,6},{22,5},{23,4},{24,11},{2... | collective-permute-start | bytes 3145736 | tf_op jit(solution)/shard_map/ppermute | solution.py:491
  62.1 1.7 %shard_map.74.sent = bf16[2,272,1024]{2,1,0:T(8,128)(2,1)S(1)} custom-call(bf16[256,512]{1,0:T(8,128)(2,1)S(1)} %get-tuple-element.63.lp, bf16[256,512]{1,0:T(8,128)(2,1)S(1)} %get-tuple-element.67.ls.a0, bf16[256,512]{1,0:T(8,128)(2,1)S(1)} %get-tuple-element.38.prim, bf16[256,512]{1,0:T(8,128)(2,1)S(1)} %get-tuple-element.65.second, ...), custom_call_target="tpu_custom_call" | custom-call | flops 2147483648 | bytes 1048576 | tf_op jit(solution)/shard_map/pallas_call | solution.py:445
  64.5 3.1 %collective-permute-start.17 = (bf16[256,512]{1,0:T(8,128)(2,1)S(1)}, bf16[256,512]{1,0:T(8,128)(2,1)S(1)}, u32[]{:S(2)}, u32[]{:S(2)}) collective-permute-start(bf16[256,512]{1,0:T(8,128)(2,1)S(1)} %get-tuple-element.67.ls.a0), channel_id=1, source_target_pairs={{16,18},{17,19},{18,16},{19,17},{20,22},{21,23},{22,20},{23,21},{2... | collective-permute-start | bytes 786440 | tf_op jit(solution)/shard_map/ppermute | solution.py:491
  67.7 2.1 %collective-permute-start.22 = (bf16[1024,512]{1,0:T(8,128)(2,1)S(1)}, bf16[1024,512]{1,0:T(8,128)(2,1)S(1)}, u32[]{:S(2)}, u32[]{:S(2)}) collective-permute-start(bf16[1024,512]{1,0:T(8,128)(2,1)S(1)} %get-tuple-element.44.w2), channel_id=1, source_target_pairs={{16,18},{17,19},{18,16},{19,17},{20,22},{21,23},{22,20},{23,21},{2... | collective-permute-start | bytes 3145736 | tf_op jit(solution)/shard_map/ppermute | solution.py:491
  69.8 11.9 %collective-permute-done.23 = bf16[1024,512]{1,0:T(8,128)(2,1)S(1)} collective-permute-done((bf16[1024,512]{1,0:T(8,128)(2,1)S(1)}, bf16[1024,512]{1,0:T(8,128)(2,1)S(1)}, u32[]{:S(2)}, u32[]{:S(2)}) %collective-permute-start.23) | collective-permute-done | bytes 1048608 | tf_op jit(solution)/shard_map/ppermute | solution.py:491
  81.7 1.3 %collective-permute-start.24 = (bf16[1024,512]{1,0:T(8,128)(2,1)S(1)}, bf16[1024,512]{1,0:T(8,128)(2,1)S(1)}, u32[]{:S(2)}, u32[]{:S(2)}) collective-permute-start(bf16[1024,512]{1,0:T(8,128)(2,1)S(1)} %collective-permute-done.23), channel_id=1, source_target_pairs={{0,16},{1,17},{2,18},{3,19},{4,20},{5,21},{6,22},{7,23},{8,24},{9,... | collective-permute-start | bytes 3145736 | tf_op jit(solution)/shard_map/ppermute | solution.py:491
  83.0 1.2 %shard_map.73.kept = bf16[2,256,1024]{2,1,0:T(8,128)(2,1)S(1)} custom-call(bf16[256,512]{1,0:T(8,128)(2,1)S(1)} %get-tuple-element.63.lp, bf16[256,512]{1,0:T(8,128)(2,1)S(1)} %get-tuple-element.67.ls.a0, bf16[4,1024,512]{2,1,0:T(8,128)(2,1)S(1)} %get-tuple-element.64.wp, bf16[1024,512]{1,0:T(8,128)(2,1)S(1)} %get-tuple-element.44.w2, ...), custom_call_target="tpu_custom_call" | custom-call | flops 2147483648 | bytes 1048576 | tf_op jit(solution)/shard_map/pallas_call | solution.py:445
  84.3 1.9 %collective-permute-start.21 = (bf16[1024,512]{1,0:T(8,128)(2,1)S(1)}, bf16[1024,512]{1,0:T(8,128)(2,1)S(1)}, u32[]{:S(2)}, u32[]{:S(2)}) collective-permute-start(bf16[1024,512]{1,0:T(8,128)(2,1)S(1)} %get-tuple-element.69.w1), channel_id=1, source_target_pairs={{16,17},{17,16},{18,19},{19,18},{20,21},{21,20},{22,23},{23,22},{2... | collective-permute-start | bytes 3145736 | tf_op jit(solution)/shard_map/ppermute | solution.py:491
  86.3 1.3 %collective-permute-start.25 = (bf16[272,1024]{1,0:T(8,128)(2,1)S(1)}, bf16[272,1024]{1,0:T(8,128)(2,1)S(1)}, u32[]{:S(2)}, u32[]{:S(2)}) collective-permute-start(bf16[272,1024]{1,0:T(8,128)(2,1)S(1)} %shard_map.75.half), channel_id=1, source_target_pairs={{0,2},{1,3},{2,0},{3,1},{4,6},{5,7},{6,4},{7,5},{8,10},{9,11},{10,... | collective-permute-start | bytes 1671176 | tf_op jit(solution)/shard_map/ppermute | solution.py:491
  87.6 2.7 %collective-permute-start.19 = (bf16[256,512]{1,0:T(8,128)(2,1)S(1)}, bf16[256,512]{1,0:T(8,128)(2,1)S(1)}, u32[]{:S(2)}, u32[]{:S(2)}) collective-permute-start(bf16[256,512]{1,0:T(8,128)(2,1)S(1)} %get-tuple-element.67.ls.a0), channel_id=1, source_target_pairs={{16,17},{17,16},{18,19},{19,18},{20,21},{21,20},{22,23},{23,22},{2... | collective-permute-start | bytes 786440 | tf_op jit(solution)/shard_map/ppermute | solution.py:491
  90.2 18.4 %collective-permute-done.25.far = bf16[272,1024]{1,0:T(8,128)(2,1)S(1)} collective-permute-done((bf16[272,1024]{1,0:T(8,128)(2,1)S(1)}, bf16[272,1024]{1,0:T(8,128)(2,1)S(1)}, u32[]{:S(2)}, u32[]{:S(2)}) %collective-permute-start.25) | collective-permute-done | bytes 557088 | tf_op jit(solution)/shard_map/ppermute | solution.py:491
  108.7 2.8 %collective-permute-start.20 = (bf16[256,512]{1,0:T(8,128)(2,1)S(1)}, bf16[256,512]{1,0:T(8,128)(2,1)S(1)}, u32[]{:S(2)}, u32[]{:S(2)}) collective-permute-start(bf16[256,512]{1,0:T(8,128)(2,1)S(1)} %collective-permute-done.17.a2), channel_id=1, source_target_pairs={{16,17},{17,16},{18,19},{19,18},{20,21},{21,20},{22,23},{23,22},{2... | collective-permute-start | bytes 786440 | tf_op jit(solution)/shard_map/ppermute | solution.py:491
  111.5 1.2 %shard_map.79 = bf16[256,1024]{1,0:T(8,128)(2,1)} custom-call(bf16[2,256,1024]{2,1,0:T(8,128)(2,1)S(1)} %shard_map.73.kept, bf16[2,272,1024]{2,1,0:T(8,128)(2,1)S(1)} %collective-permute-done.18.got, bf16[272,1024]{1,0:T(8,128)(2,1)S(1)} %shard_map.75.half, bf16[272,1024]{1,0:T(8,128)(2,1)S(1)} %collective-permute-done.25.far, ...), custom_call_target="tpu_custom_call" | custom-call | bytes 1048576 | tf_op jit(solution)/shard_map/pallas_call | solution.py:445
  112.8 2.1 %shard_map.76 = bf16[256,1024]{1,0:T(8,128)(2,1)} custom-call(bf16[256,512]{1,0:T(8,128)(2,1)S(1)} %get-tuple-element.67.ls.a0, bf16[256,512]{1,0:T(8,128)(2,1)S(1)} %collective-permute-done.19.a1, bf16[256,512]{1,0:T(8,128)(2,1)S(1)} %collective-permute-done.17.a2, bf16[256,512]{1,0:T(8,128)(2,1)S(1)} %collective-permute-done.20.a3, ...), custom_call_target="tpu_custom_call" | custom-call | flops 2147483648 | bytes 1048576 | tf_op jit(solution)/shard_map/pallas_call | solution.py:445
  (36 shorter events, 4.9 us)
Async XLA Ops:
  0.6 20.9 %collective-permute-start = (bf16[256,1024]{1,0:T(8,128)(2,1)}, bf16[256,1024]{1,0:T(8,128)(2,1)S(1)}, u32[]{:S(2)}, u32[]{:S(2)}) collective-permute-start(bf16[256,1024]{1,0:T(8,128)(2,1)} %c0.1), channel_id=1, source_target_pairs={{16,17},{17,16},{18,19},{19,18},{20,21},{21,20},{22,23},{23,22},{2... | collective-permute-start | bytes 1572872 | tf_op jit(solution)/shard_map/ppermute | solution.py:491
  3.2 15.6 %collective-permute-start.1 = (bf16[256,1024]{1,0:T(8,128)(2,1)}, bf16[256,1024]{1,0:T(8,128)(2,1)S(1)}, u32[]{:S(2)}, u32[]{:S(2)}) collective-permute-start(bf16[256,1024]{1,0:T(8,128)(2,1)} %c0.1), channel_id=1, source_target_pairs={{16,18},{17,19},{18,16},{19,17},{20,22},{21,23},{22,20},{23,21},{2... | collective-permute-start | bytes 1572872 | tf_op jit(solution)/shard_map/ppermute | solution.py:491
  6.4 15.2 %copy-start = (bf16[256,1024]{1,0:T(8,128)(2,1)S(1)}, bf16[256,1024]{1,0:T(8,128)(2,1)}, u32[]{:S(2)}) copy-start(bf16[256,1024]{1,0:T(8,128)(2,1)} %c0.1) | copy-start | bytes 1572868
  18.8 4.3 %collective-permute-start.2 = (bf16[256,1024]{1,0:T(8,128)(2,1)S(1)}, bf16[256,1024]{1,0:T(8,128)(2,1)S(1)}, u32[]{:S(2)}, u32[]{:S(2)}) collective-permute-start(bf16[256,1024]{1,0:T(8,128)(2,1)S(1)} %collective-permute-done.1.c2), channel_id=1, source_target_pairs={{16,17},{17,16},{18,19},{19,18},{20,21},{21,20},{22,23},{23,22},{2... | collective-permute-start | bytes 1572872 | tf_op jit(solution)/shard_map/ppermute | solution.py:491
  21.6 1.5 %copy-start.1 = (s32[2,1]{0,1:T(1,128)S(1)}, s32[2,1]{0,1:T(1,128)}, u32[]{:S(2)}) copy-start(s32[2,1]{0,1:T(1,128)} %param.8) | copy-start | bytes 28
  25.0 5.2 %collective-permute-start.3 = (bf16[272,128]{1,0:T(8,128)(2,1)S(1)}, bf16[272,128]{1,0:T(8,128)(2,1)S(1)}, u32[]{:S(2)}, u32[]{:S(2)}) collective-permute-start(bf16[272,128]{1,0:T(8,128)(2,1)S(1)} %get-tuple-element.47), channel_id=1, source_target_pairs={{0,4},{1,5},{2,6},{3,7},{4,0},{5,1},{6,2},{7,3},{8,12},{9,13},{10,... | collective-permute-start | bytes 208904 | tf_op jit(solution)/shard_map/ppermute | solution.py:491
  26.4 6.8 %collective-permute-start.4 = (bf16[272,128]{1,0:T(8,128)(2,1)S(1)}, bf16[272,128]{1,0:T(8,128)(2,1)S(1)}, u32[]{:S(2)}, u32[]{:S(2)}) collective-permute-start(bf16[272,128]{1,0:T(8,128)(2,1)S(1)} %get-tuple-element.48), channel_id=1, source_target_pairs={{0,8},{1,9},{2,10},{3,11},{4,12},{5,13},{6,14},{7,15},{8,0},{9,1},... | collective-permute-start | bytes 208904 | tf_op jit(solution)/shard_map/ppermute | solution.py:491
  28.7 5.6 %collective-permute-start.5 = (bf16[272,128]{1,0:T(8,128)(2,1)S(1)}, bf16[272,128]{1,0:T(8,128)(2,1)S(1)}, u32[]{:S(2)}, u32[]{:S(2)}) collective-permute-start(bf16[272,128]{1,0:T(8,128)(2,1)S(1)} %get-tuple-element.49), channel_id=1, source_target_pairs={{0,12},{1,13},{2,14},{3,15},{4,8},{5,9},{6,10},{7,11},{8,4},{9,5},... | collective-permute-start | bytes 208904 | tf_op jit(solution)/shard_map/ppermute | solution.py:491
  28.7 5.6 %collective-permute-start.6 = (bf16[272,128]{1,0:T(8,128)(2,1)S(1)}, bf16[272,128]{1,0:T(8,128)(2,1)S(1)}, u32[]{:S(2)}, u32[]{:S(2)}) collective-permute-start(bf16[272,128]{1,0:T(8,128)(2,1)S(1)} %get-tuple-element.50), channel_id=1, source_target_pairs={{0,16},{1,17},{2,18},{3,19},{4,20},{5,21},{6,22},{7,23},{8,24},{9,... | collective-permute-start | bytes 208904 | tf_op jit(solution)/shard_map/ppermute | solution.py:491
  28.7 5.6 %collective-permute-start.7 = (bf16[272,128]{1,0:T(8,128)(2,1)S(1)}, bf16[272,128]{1,0:T(8,128)(2,1)S(1)}, u32[]{:S(2)}, u32[]{:S(2)}) collective-permute-start(bf16[272,128]{1,0:T(8,128)(2,1)S(1)} %get-tuple-element.51), channel_id=1, source_target_pairs={{0,20},{1,21},{2,22},{3,23},{4,16},{5,17},{6,18},{7,19},{8,28},{9,... | collective-permute-start | bytes 208904 | tf_op jit(solution)/shard_map/ppermute | solution.py:491
  30.2 5.3 %collective-permute-start.8 = (bf16[272,128]{1,0:T(8,128)(2,1)S(1)}, bf16[272,128]{1,0:T(8,128)(2,1)S(1)}, u32[]{:S(2)}, u32[]{:S(2)}) collective-permute-start(bf16[272,128]{1,0:T(8,128)(2,1)S(1)} %get-tuple-element.52), channel_id=1, source_target_pairs={{0,24},{1,25},{2,26},{3,27},{4,28},{5,29},{6,30},{7,31},{8,16},{9,... | collective-permute-start | bytes 208904 | tf_op jit(solution)/shard_map/ppermute | solution.py:491
  33.1 5.9 %collective-permute-start.9 = (bf16[272,128]{1,0:T(8,128)(2,1)S(1)}, bf16[272,128]{1,0:T(8,128)(2,1)S(1)}, u32[]{:S(2)}, u32[]{:S(2)}) collective-permute-start(bf16[272,128]{1,0:T(8,128)(2,1)S(1)} %get-tuple-element.53), channel_id=1, source_target_pairs={{0,28},{1,29},{2,30},{3,31},{4,24},{5,25},{6,26},{7,27},{8,20},{9,... | collective-permute-start | bytes 208904 | tf_op jit(solution)/shard_map/ppermute | solution.py:491
  42.4 5.5 %collective-permute-start.10 = (bf16[256,128]{1,0:T(8,128)(2,1)S(1)}, bf16[256,128]{1,0:T(8,128)(2,1)S(1)}, u32[]{:S(2)}, u32[]{:S(2)}) collective-permute-start(bf16[256,128]{1,0:T(8,128)(2,1)S(1)} %get-tuple-element.55), channel_id=1, source_target_pairs={{0,4},{1,5},{2,6},{3,7},{4,0},{5,1},{6,2},{7,3},{8,12},{9,13},{10,... | collective-permute-start | bytes 196616 | tf_op jit(solution)/shard_map/ppermute | solution.py:491
  43.7 7.3 %collective-permute-start.11 = (bf16[256,128]{1,0:T(8,128)(2,1)S(1)}, bf16[256,128]{1,0:T(8,128)(2,1)S(1)}, u32[]{:S(2)}, u32[]{:S(2)}) collective-permute-start(bf16[256,128]{1,0:T(8,128)(2,1)S(1)} %get-tuple-element.56), channel_id=1, source_target_pairs={{0,8},{1,9},{2,10},{3,11},{4,12},{5,13},{6,14},{7,15},{8,0},{9,1},... | collective-permute-start | bytes 196616 | tf_op jit(solution)/shard_map/ppermute | solution.py:491
  43.9 8.4 %collective-permute-start.12 = (bf16[256,128]{1,0:T(8,128)(2,1)S(1)}, bf16[256,128]{1,0:T(8,128)(2,1)S(1)}, u32[]{:S(2)}, u32[]{:S(2)}) collective-permute-start(bf16[256,128]{1,0:T(8,128)(2,1)S(1)} %get-tuple-element.57), channel_id=1, source_target_pairs={{0,12},{1,13},{2,14},{3,15},{4,8},{5,9},{6,10},{7,11},{8,4},{9,5},... | collective-permute-start | bytes 196616 | tf_op jit(solution)/shard_map/ppermute | solution.py:491
  46.0 15.0 %collective-permute-start.13 = (bf16[256,128]{1,0:T(8,128)(2,1)S(1)}, bf16[256,128]{1,0:T(8,128)(2,1)S(1)}, u32[]{:S(2)}, u32[]{:S(2)}) collective-permute-start(bf16[256,128]{1,0:T(8,128)(2,1)S(1)} %get-tuple-element.58), channel_id=1, source_target_pairs={{0,16},{1,17},{2,18},{3,19},{4,20},{5,21},{6,22},{7,23},{8,24},{9,... | collective-permute-start | bytes 196616 | tf_op jit(solution)/shard_map/ppermute | solution.py:491
  47.7 13.4 %collective-permute-start.14 = (bf16[256,128]{1,0:T(8,128)(2,1)S(1)}, bf16[256,128]{1,0:T(8,128)(2,1)S(1)}, u32[]{:S(2)}, u32[]{:S(2)}) collective-permute-start(bf16[256,128]{1,0:T(8,128)(2,1)S(1)} %get-tuple-element.59), channel_id=1, source_target_pairs={{0,20},{1,21},{2,22},{3,23},{4,16},{5,17},{6,18},{7,19},{8,28},{9,... | collective-permute-start | bytes 196616 | tf_op jit(solution)/shard_map/ppermute | solution.py:491
  47.9 13.2 %collective-permute-start.15 = (bf16[256,128]{1,0:T(8,128)(2,1)S(1)}, bf16[256,128]{1,0:T(8,128)(2,1)S(1)}, u32[]{:S(2)}, u32[]{:S(2)}) collective-permute-start(bf16[256,128]{1,0:T(8,128)(2,1)S(1)} %get-tuple-element.60), channel_id=1, source_target_pairs={{0,24},{1,25},{2,26},{3,27},{4,28},{5,29},{6,30},{7,31},{8,16},{9,... | collective-permute-start | bytes 196616 | tf_op jit(solution)/shard_map/ppermute | solution.py:491
  51.0 10.1 %collective-permute-start.16 = (bf16[256,128]{1,0:T(8,128)(2,1)S(1)}, bf16[256,128]{1,0:T(8,128)(2,1)S(1)}, u32[]{:S(2)}, u32[]{:S(2)}) collective-permute-start(bf16[256,128]{1,0:T(8,128)(2,1)S(1)} %get-tuple-element.61), channel_id=1, source_target_pairs={{0,28},{1,29},{2,30},{3,31},{4,24},{5,25},{6,26},{7,27},{8,20},{9,... | collective-permute-start | bytes 196616 | tf_op jit(solution)/shard_map/ppermute | solution.py:491
  52.2 29.4 %collective-permute-start.23 = (bf16[1024,512]{1,0:T(8,128)(2,1)S(1)}, bf16[1024,512]{1,0:T(8,128)(2,1)S(1)}, u32[]{:S(2)}, u32[]{:S(2)}) collective-permute-start(bf16[1024,512]{1,0:T(8,128)(2,1)S(1)} %get-tuple-element.45.w3), channel_id=1, source_target_pairs={{16,3},{17,2},{18,1},{19,0},{20,7},{21,6},{22,5},{23,4},{24,11},{2... | collective-permute-start | bytes 3145736 | tf_op jit(solution)/shard_map/ppermute | solution.py:491
  63.8 20.4 %collective-permute-start.18 = (bf16[2,272,1024]{2,1,0:T(8,128)(2,1)S(1)}, bf16[2,272,1024]{2,1,0:T(8,128)(2,1)S(1)}, u32[]{:S(2)}, u32[]{:S(2)}) collective-permute-start(bf16[2,272,1024]{2,1,0:T(8,128)(2,1)S(1)} %shard_map.74.sent), channel_id=1, source_target_pairs={{0,1},{1,0},{2,3},{3,2},{4,5},{5,4},{6,7},{7,6},{8,9},{9,8},{10,11... | collective-permute-start | bytes 3342344 | tf_op jit(solution)/shard_map/ppermute | solution.py:491
  64.5 19.8 %collective-permute-start.17 = (bf16[256,512]{1,0:T(8,128)(2,1)S(1)}, bf16[256,512]{1,0:T(8,128)(2,1)S(1)}, u32[]{:S(2)}, u32[]{:S(2)}) collective-permute-start(bf16[256,512]{1,0:T(8,128)(2,1)S(1)} %get-tuple-element.67.ls.a0), channel_id=1, source_target_pairs={{16,18},{17,19},{18,16},{19,17},{20,22},{21,23},{22,20},{23,21},{2... | collective-permute-start | bytes 786440 | tf_op jit(solution)/shard_map/ppermute | solution.py:491
  67.7 45.1 %collective-permute-start.22 = (bf16[1024,512]{1,0:T(8,128)(2,1)S(1)}, bf16[1024,512]{1,0:T(8,128)(2,1)S(1)}, u32[]{:S(2)}, u32[]{:S(2)}) collective-permute-start(bf16[1024,512]{1,0:T(8,128)(2,1)S(1)} %get-tuple-element.44.w2), channel_id=1, source_target_pairs={{16,18},{17,19},{18,16},{19,17},{20,22},{21,23},{22,20},{23,21},{2... | collective-permute-start | bytes 3145736 | tf_op jit(solution)/shard_map/ppermute | solution.py:491
  81.7 31.1 %collective-permute-start.24 = (bf16[1024,512]{1,0:T(8,128)(2,1)S(1)}, bf16[1024,512]{1,0:T(8,128)(2,1)S(1)}, u32[]{:S(2)}, u32[]{:S(2)}) collective-permute-start(bf16[1024,512]{1,0:T(8,128)(2,1)S(1)} %collective-permute-done.23), channel_id=1, source_target_pairs={{0,16},{1,17},{2,18},{3,19},{4,20},{5,21},{6,22},{7,23},{8,24},{9,... | collective-permute-start | bytes 3145736 | tf_op jit(solution)/shard_map/ppermute | solution.py:491
  84.3 28.4 %collective-permute-start.21 = (bf16[1024,512]{1,0:T(8,128)(2,1)S(1)}, bf16[1024,512]{1,0:T(8,128)(2,1)S(1)}, u32[]{:S(2)}, u32[]{:S(2)}) collective-permute-start(bf16[1024,512]{1,0:T(8,128)(2,1)S(1)} %get-tuple-element.69.w1), channel_id=1, source_target_pairs={{16,17},{17,16},{18,19},{19,18},{20,21},{21,20},{22,23},{23,22},{2... | collective-permute-start | bytes 3145736 | tf_op jit(solution)/shard_map/ppermute | solution.py:491
  86.3 22.4 %collective-permute-start.25 = (bf16[272,1024]{1,0:T(8,128)(2,1)S(1)}, bf16[272,1024]{1,0:T(8,128)(2,1)S(1)}, u32[]{:S(2)}, u32[]{:S(2)}) collective-permute-start(bf16[272,1024]{1,0:T(8,128)(2,1)S(1)} %shard_map.75.half), channel_id=1, source_target_pairs={{0,2},{1,3},{2,0},{3,1},{4,6},{5,7},{6,4},{7,5},{8,10},{9,11},{10,... | collective-permute-start | bytes 1671176 | tf_op jit(solution)/shard_map/ppermute | solution.py:491
  87.6 25.2 %collective-permute-start.19 = (bf16[256,512]{1,0:T(8,128)(2,1)S(1)}, bf16[256,512]{1,0:T(8,128)(2,1)S(1)}, u32[]{:S(2)}, u32[]{:S(2)}) collective-permute-start(bf16[256,512]{1,0:T(8,128)(2,1)S(1)} %get-tuple-element.67.ls.a0), channel_id=1, source_target_pairs={{16,17},{17,16},{18,19},{19,18},{20,21},{21,20},{22,23},{23,22},{2... | collective-permute-start | bytes 786440 | tf_op jit(solution)/shard_map/ppermute | solution.py:491
  108.7 4.1 %collective-permute-start.20 = (bf16[256,512]{1,0:T(8,128)(2,1)S(1)}, bf16[256,512]{1,0:T(8,128)(2,1)S(1)}, u32[]{:S(2)}, u32[]{:S(2)}) collective-permute-start(bf16[256,512]{1,0:T(8,128)(2,1)S(1)} %collective-permute-done.17.a2), channel_id=1, source_target_pairs={{16,17},{17,16},{18,19},{19,18},{20,21},{21,20},{22,23},{23,22},{2... | collective-permute-start | bytes 786440 | tf_op jit(solution)/shard_map/ppermute | solution.py:491

commit v3 on v2

--- a/solution.py
+++ b/solution.py
@@ -453,12 +453,9 @@
     )(*ins)
 
 
-def inverse_kernel(spread, inverse):
-    inverse[...] = 1.0 / spread[...]
-
-
-def shrink_kernel(width, spread, shrink):
+def scales_kernel(width, spread, inverse, shrink):
     root = spread[...]
+    inverse[...] = 1.0 / root
     shrink[...] = 1.0 / (width * root * root * root)
 
 
@@ -490,7 +487,7 @@
         ]
         return lax.ppermute(x, AXES, pairs)
 
-    document, summary = (0,), (1,)
+    summary = (1,)
 
     def exchange(pieces):
         moved = [pieces[0]]
@@ -532,7 +529,7 @@
     )
     wp, ws = made[0], made[1 : 1 + n_mp]
     own, own_states, own_gain, spread, prim, sec = made[1 + n_mp :]
-    lent_3 = swap(ws[3], n_blk, 3, summary)
+    lent_3 = swap(ws[3], 0, 3, summary)
     far_cot, spread = lax.optimization_barrier((far_cot, spread))
     cross_cot = swap(far_cot, 0, 1, summary)
     acc = call(
@@ -556,7 +553,9 @@
     second, pieces = made[0], made[1:]
     pieces = exchange(pieces)
     lent_2 = swap(ws[2], 0, 2, summary)
-    (inverse,) = call(inverse_kernel, (spread,), [INSIDE], [((rows, LANES), F32)])
+    inverse, shrink = call(
+        functools.partial(scales_kernel, width), (spread,), [INSIDE], [((rows, LANES), F32)] * 2
+    )
     pieces = call(
         functools.partial(attend_kernel, sizes),
         pieces,
@@ -571,10 +570,6 @@
         4 << 30,
     )
     pieces = exchange(pieces)
-    lent_3 = swap(lent_3, n_blk, 0, document)
-    (shrink,) = call(
-        functools.partial(shrink_kernel, width), (spread,), [INSIDE], [((rows, LANES), F32)]
-    )
     lp, ls = call(
         functools.partial(regroup_kernel, sizes),
         (counts, *pieces),
@@ -604,7 +599,7 @@
     )
     (half,) = call(fold_kernel, (kept, got, sent), [INSIDE] * 3, [((rows + TAIL, feats), BF16)])
     far = swap(half, 0, 2)
-    far_att, own_att, lent_1, half_seen = lax.optimization_barrier((far_att, ls, ws[1], half))
+    own_att, lent_1, half_seen = lax.optimization_barrier((ls, ws[1], half))
     lent_1 = swap(lent_1, 0, 1, summary)
     near_att = swap(own_att, 0, 1, summary)
     cross_att = swap(far_att, 0, 1, summary)

time: 115 us -> 140 us (1.22)
  waiting for transfers between devices: 39 us -> 68.1 us
  starting transfers between devices: 52.4 us -> 48 us
    ppermute x26 -> x25, waiting for transfers between devices: 39 us -> 68.1 us  [swap(): return lax.ppermute(x, AXES, pairs)]
    ppermute x26 -> x25, starting transfers between devices: 52.4 us -> 48 us  [swap(): return lax.ppermute(x, AXES, pairs)]
    pallas_call x12 -> x11, Pallas kernels: 22.5 us -> 22.5 us  [call(): pl.pallas_call(body, in_specs=list(specs), out_specs=[INSIDE] * len(outs)...]
  transfers between devices with their start and end apart: 26 -> 25, of which waited for: 6 -> 9; matrix products, arithmetic and copies ran while one was open for 0% -> 0% of each run, Pallas kernels for 13% -> 9%
where the time goes in v3:
time: 140 us
  waiting for transfers between devices  68.1 us (49%)
  starting transfers between devices  48 us (34%)
  Pallas kernels  22.5 us (16%)
    ppermute x25, waiting for transfers between devices, swap(): return lax.ppermute(x, AXES, pairs)  68.1 us
    ppermute x25, starting transfers between devices, swap(): return lax.ppermute(x, AXES, pairs)  48 us
    pallas_call x11, Pallas kernels, call(): pl.pallas_call(body, in_specs=list(specs), out_specs=[INSIDE] * len(outs)...  22.5 us
  transfers between devices with their start and end apart: 25, of which 9 were waited for; matrix products, arithmetic and copies ran while one was open for 0% of the time, Pallas kernels for 9%

profile of v3, /device:TPU:3, one launch (start us, length us, event | category | flops | bytes accessed | tf_op | source)
XLA Modules:
  0.0 139.6 jit_solution(11994859093368397369)
XLA Ops:
  0.6 2.6 %collective-permute-start = (bf16[256,1024]{1,0:T(8,128)(2,1)}, bf16[256,1024]{1,0:T(8,128)(2,1)S(1)}, u32[]{:S(2)}, u32[]{:S(2)}) collective-permute-start(bf16[256,1024]{1,0:T(8,128)(2,1)} %c0.1), channel_id=1, source_target_pairs={{16,17},{17,16},{18,19},{19,18},{20,21},{21,20},{22,23},{23,22},{2... | collective-permute-start | bytes 1572872 | tf_op jit(solution)/shard_map/ppermute | solution.py:488
  3.2 3.1 %collective-permute-start.1 = (bf16[256,1024]{1,0:T(8,128)(2,1)}, bf16[256,1024]{1,0:T(8,128)(2,1)S(1)}, u32[]{:S(2)}, u32[]{:S(2)}) collective-permute-start(bf16[256,1024]{1,0:T(8,128)(2,1)} %c0.1), channel_id=1, source_target_pairs={{16,18},{17,19},{18,16},{19,17},{20,22},{21,23},{22,20},{23,21},{2... | collective-permute-start | bytes 1572872 | tf_op jit(solution)/shard_map/ppermute | solution.py:488
  6.4 8.9 %shard_map.68 = (bf16[4,1024,512]{2,1,0:T(8,128)(2,1)S(1)}, bf16[1024,512]{1,0:T(8,128)(2,1)S(1)}, bf16[1024,512]{1,0:T(8,128)(2,1)S(1)}, bf16[1024,512]{1,0:T(8...) custom-call(bf16[256,4096]{1,0:T(8,128)(2,1)} %bitcast.13, ...), custom_call_target="tpu_custom_call" | custom-call | flops 8589934592 | bytes 1048576 | tf_op jit(solution)/shard_map/pallas_call | solution.py:445
  15.3 3.5 %collective-permute-done.1.c2 = bf16[256,1024]{1,0:T(8,128)(2,1)S(1)} collective-permute-done((bf16[256,1024]{1,0:T(8,128)(2,1)}, bf16[256,1024]{1,0:T(8,128)(2,1)S(1)}, u32[]{:S(2)}, u32[]{:S(2)}) %collective-permute-start.1) | collective-permute-done | bytes 524320 | tf_op jit(solution)/shard_map/ppermute | solution.py:488
  18.8 2.8 %collective-permute-start.2 = (bf16[256,1024]{1,0:T(8,128)(2,1)S(1)}, bf16[256,1024]{1,0:T(8,128)(2,1)S(1)}, u32[]{:S(2)}, u32[]{:S(2)}) collective-permute-start(bf16[256,1024]{1,0:T(8,128)(2,1)S(1)} %collective-permute-done.1.c2), channel_id=1, source_target_pairs={{16,17},{17,16},{18,19},{19,18},{20,21},{21,20},{22,23},{23,22},{2... | collective-permute-start | bytes 1572872 | tf_op jit(solution)/shard_map/ppermute | solution.py:488
  23.1 1.9 %shard_map.70 = (bf16[256,512]{1,0:T(8,128)(2,1)S(1)}, bf16[272,128]{1,0:T(8,128)(2,1)S(1)}, bf16[272,128]{1,0:T(8,128)(2,1)S(1)}, bf16[272,128]{1,0:T(8,128)(2,...) custom-call(s32[1,2]{1,0:T(1,128)S(1)} %bitcast.9, ...), custom_call_target="tpu_custom_call" | custom-call | flops 1073741824 | bytes 1048576 | tf_op jit(solution)/shard_map/pallas_call | solution.py:445
  25.0 1.4 collective-permute-start.3
  26.4 2.3 %collective-permute-start.4 = (bf16[272,128]{1,0:T(8,128)(2,1)S(1)}, bf16[272,128]{1,0:T(8,128)(2,1)S(1)}, u32[]{:S(2)}, u32[]{:S(2)}) collective-permute-start(bf16[272,128]{1,0:T(8,128)(2,1)S(1)} %get-tuple-element.49), channel_id=1, source_target_pairs={{0,8},{1,9},{2,10},{3,11},{4,12},{5,13},{6,14},{7,15},{8,0},{9,1},... | collective-permute-start | bytes 208904 | tf_op jit(solution)/shard_map/ppermute | solution.py:488
  28.7 1.5 %collective-permute-start.7 = (bf16[272,128]{1,0:T(8,128)(2,1)S(1)}, bf16[272,128]{1,0:T(8,128)(2,1)S(1)}, u32[]{:S(2)}, u32[]{:S(2)}) collective-permute-start(bf16[272,128]{1,0:T(8,128)(2,1)S(1)} %get-tuple-element.52), channel_id=1, source_target_pairs={{0,20},{1,21},{2,22},{3,23},{4,16},{5,17},{6,18},{7,19},{8,28},{9,... | collective-permute-start | bytes 208904 | tf_op jit(solution)/shard_map/ppermute | solution.py:488
  30.2 2.9 %collective-permute-start.8 = (bf16[272,128]{1,0:T(8,128)(2,1)S(1)}, bf16[272,128]{1,0:T(8,128)(2,1)S(1)}, u32[]{:S(2)}, u32[]{:S(2)}) collective-permute-start(bf16[272,128]{1,0:T(8,128)(2,1)S(1)} %get-tuple-element.53), channel_id=1, source_target_pairs={{0,24},{1,25},{2,26},{3,27},{4,28},{5,29},{6,30},{7,31},{8,16},{9,... | collective-permute-start | bytes 208904 | tf_op jit(solution)/shard_map/ppermute | solution.py:488
  35.5 3.6 %collective-permute-done.9.rest_7_ = bf16[272,128]{1,0:T(8,128)(2,1)S(1)} collective-permute-done((bf16[272,128]{1,0:T(8,128)(2,1)S(1)}, bf16[272,128]{1,0:T(8,128)(2,1)S(1)}, u32[]{:S(2)}, u32[]{:S(2)}) %collective-permute-start.9) | collective-permute-done | bytes 69664 | tf_op jit(solution)/shard_map/ppermute | solution.py:488
  39.0 3.4 %shard_map.71 = (bf16[256,128]{1,0:T(8,128)(2,1)S(1)}, bf16[256,128]{1,0:T(8,128)(2,1)S(1)}, bf16[256,128]{1,0:T(8,128)(2,1)S(1)}, bf16[256,128]{1,0:T(8,128)(2,...) custom-call(bf16[272,128]{1,0:T(8,128)(2,1)S(1)} %get-tuple-element., ...), custom_call_target="tpu_custom_call" | custom-call | flops 4294967296 | bytes 1048576 | tf_op jit(solution)/shard_map/pallas_call | solution.py:445
  42.4 1.2 collective-permute-start.10
  43.9 2.2 %collective-permute-start.12 = (bf16[256,128]{1,0:T(8,128)(2,1)S(1)}, bf16[256,128]{1,0:T(8,128)(2,1)S(1)}, u32[]{:S(2)}, u32[]{:S(2)}) collective-permute-start(bf16[256,128]{1,0:T(8,128)(2,1)S(1)} %get-tuple-element.58), channel_id=1, source_target_pairs={{0,12},{1,13},{2,14},{3,15},{4,8},{5,9},{6,10},{7,11},{8,4},{9,5},... | collective-permute-start | bytes 196616 | tf_op jit(solution)/shard_map/ppermute | solution.py:488
  46.0 1.6 %collective-permute-start.13 = (bf16[256,128]{1,0:T(8,128)(2,1)S(1)}, bf16[256,128]{1,0:T(8,128)(2,1)S(1)}, u32[]{:S(2)}, u32[]{:S(2)}) collective-permute-start(bf16[256,128]{1,0:T(8,128)(2,1)S(1)} %get-tuple-element.59), channel_id=1, source_target_pairs={{0,16},{1,17},{2,18},{3,19},{4,20},{5,21},{6,22},{7,23},{8,24},{9,... | collective-permute-start | bytes 196616 | tf_op jit(solution)/shard_map/ppermute | solution.py:488
  47.9 3.1 %collective-permute-start.15 = (bf16[256,128]{1,0:T(8,128)(2,1)S(1)}, bf16[256,128]{1,0:T(8,128)(2,1)S(1)}, u32[]{:S(2)}, u32[]{:S(2)}) collective-permute-start(bf16[256,128]{1,0:T(8,128)(2,1)S(1)} %get-tuple-element.61), channel_id=1, source_target_pairs={{0,24},{1,25},{2,26},{3,27},{4,28},{5,29},{6,30},{7,31},{8,16},{9,... | collective-permute-start | bytes 196616 | tf_op jit(solution)/shard_map/ppermute | solution.py:488
  51.0 1.2 collective-permute-start.16
  53.1 2.2 %collective-permute-done.15.rest_6_ = bf16[256,128]{1,0:T(8,128)(2,1)S(1)} collective-permute-done((bf16[256,128]{1,0:T(8,128)(2,1)S(1)}, bf16[256,128]{1,0:T(8,128)(2,1)S(1)}, u32[]{:S(2)}, u32[]{:S(2)}) %collective-permute-start.15) | collective-permute-done | bytes 65568 | tf_op jit(solution)/shard_map/ppermute | solution.py:488
  55.4 1.8 %collective-permute-done.16.rest_7_ = bf16[256,128]{1,0:T(8,128)(2,1)S(1)} collective-permute-done((bf16[256,128]{1,0:T(8,128)(2,1)S(1)}, bf16[256,128]{1,0:T(8,128)(2,1)S(1)}, u32[]{:S(2)}, u32[]{:S(2)}) %collective-permute-start.16) | collective-permute-done | bytes 65568 | tf_op jit(solution)/shard_map/ppermute | solution.py:488
  58.1 1.8 %shard_map.74.sent = bf16[2,272,1024]{2,1,0:T(8,128)(2,1)S(1)} custom-call(bf16[256,512]{1,0:T(8,128)(2,1)S(1)} %get-tuple-element.64.lp, bf16[256,512]{1,0:T(8,128)(2,1)S(1)} %get-tuple-element.68.ls.a0, bf16[256,512]{1,0:T(8,128)(2,1)S(1)} %get-tuple-element.39.prim, bf16[256,512]{1,0:T(8,128)(2,1)S(1)} %get-tuple-element.66.second, ...), custom_call_target="tpu_custom_call" | custom-call | flops 2147483648 | bytes 1048576 | tf_op jit(solution)/shard_map/pallas_call | solution.py:445
  59.9 4.7 %collective-permute-start.17 = (bf16[2,272,1024]{2,1,0:T(8,128)(2,1)S(1)}, bf16[2,272,1024]{2,1,0:T(8,128)(2,1)S(1)}, u32[]{:S(2)}, u32[]{:S(2)}) collective-permute-start(bf16[2,272,1024]{2,1,0:T(8,128)(2,1)S(1)} %shard_map.74.sent), channel_id=1, source_target_pairs={{0,1},{1,0},{2,3},{3,2},{4,5},{5,4},{6,7},{7,6},{8,9},{9,8},{10,11... | collective-permute-start | bytes 3342344 | tf_op jit(solution)/shard_map/ppermute | solution.py:488
  64.5 3.1 %collective-permute-start.22 = (bf16[1024,512]{1,0:T(8,128)(2,1)S(1)}, bf16[1024,512]{1,0:T(8,128)(2,1)S(1)}, u32[]{:S(2)}, u32[]{:S(2)}) collective-permute-start(bf16[1024,512]{1,0:T(8,128)(2,1)S(1)} %get-tuple-element.45.w2), channel_id=1, source_target_pairs={{16,18},{17,19},{18,16},{19,17},{20,22},{21,23},{22,20},{23,21},{2... | collective-permute-start | bytes 3145736 | tf_op jit(solution)/shard_map/ppermute | solution.py:488
  67.7 2.3 %collective-permute-start.23 = (bf16[1024,512]{1,0:T(8,128)(2,1)S(1)}, bf16[1024,512]{1,0:T(8,128)(2,1)S(1)}, u32[]{:S(2)}, u32[]{:S(2)}) collective-permute-start(bf16[1024,512]{1,0:T(8,128)(2,1)S(1)} %get-tuple-element.46.w3), channel_id=1, source_target_pairs={{16,19},{17,18},{18,17},{19,16},{20,23},{21,22},{22,21},{23,20},{2... | collective-permute-start | bytes 3145736 | tf_op jit(solution)/shard_map/ppermute | solution.py:488
  70.0 1.2 shard_map.73.kept
  71.4 2.1 %collective-permute-start.21 = (bf16[1024,512]{1,0:T(8,128)(2,1)S(1)}, bf16[1024,512]{1,0:T(8,128)(2,1)S(1)}, u32[]{:S(2)}, u32[]{:S(2)}) collective-permute-start(bf16[1024,512]{1,0:T(8,128)(2,1)S(1)} %get-tuple-element.69.w1), channel_id=1, source_target_pairs={{16,17},{17,16},{18,19},{19,18},{20,21},{21,20},{22,23},{23,22},{2... | collective-permute-start | bytes 3145736 | tf_op jit(solution)/shard_map/ppermute | solution.py:488
  73.5 1.3 collective-permute-start.24
  74.8 2.1 %collective-permute-start.19 = (bf16[256,512]{1,0:T(8,128)(2,1)S(1)}, bf16[256,512]{1,0:T(8,128)(2,1)S(1)}, u32[]{:S(2)}, u32[]{:S(2)}) collective-permute-start(bf16[256,512]{1,0:T(8,128)(2,1)S(1)} %get-tuple-element.68.ls.a0), channel_id=1, source_target_pairs={{16,18},{17,19},{18,16},{19,17},{20,22},{21,23},{22,20},{23,21},{2... | collective-permute-start | bytes 786440 | tf_op jit(solution)/shard_map/ppermute | solution.py:488
  76.9 54.2 %collective-permute-done.19.a2 = bf16[256,512]{1,0:T(8,128)(2,1)S(1)} collective-permute-done((bf16[256,512]{1,0:T(8,128)(2,1)S(1)}, bf16[256,512]{1,0:T(8,128)(2,1)S(1)}, u32[]{:S(2)}, u32[]{:S(2)}) %collective-permute-start.19) | collective-permute-done | bytes 262176 | tf_op jit(solution)/shard_map/ppermute | solution.py:488
  131.1 2.8 %collective-permute-start.20 = (bf16[256,512]{1,0:T(8,128)(2,1)S(1)}, bf16[256,512]{1,0:T(8,128)(2,1)S(1)}, u32[]{:S(2)}, u32[]{:S(2)}) collective-permute-start(bf16[256,512]{1,0:T(8,128)(2,1)S(1)} %collective-permute-done.19.a2), channel_id=1, source_target_pairs={{16,17},{17,16},{18,19},{19,18},{20,21},{21,20},{22,23},{23,22},{2... | collective-permute-start | bytes 786440 | tf_op jit(solution)/shard_map/ppermute | solution.py:488
  133.9 1.9 %collective-permute-start.18 = (bf16[256,512]{1,0:T(8,128)(2,1)S(1)}, bf16[256,512]{1,0:T(8,128)(2,1)S(1)}, u32[]{:S(2)}, u32[]{:S(2)}) collective-permute-start(bf16[256,512]{1,0:T(8,128)(2,1)S(1)} %get-tuple-element.68.ls.a0), channel_id=1, source_target_pairs={{16,17},{17,16},{18,19},{19,18},{20,21},{21,20},{22,23},{23,22},{2... | collective-permute-start | bytes 786440 | tf_op jit(solution)/shard_map/ppermute | solution.py:488
  135.9 1.2 shard_map.78
  137.4 2.1 %shard_map.76 = bf16[256,1024]{1,0:T(8,128)(2,1)} custom-call(bf16[256,512]{1,0:T(8,128)(2,1)S(1)} %get-tuple-element.68.ls.a0, bf16[256,512]{1,0:T(8,128)(2,1)S(1)} %collective-permute-done.18.a1, bf16[256,512]{1,0:T(8,128)(2,1)S(1)} %collective-permute-done.19.a2, bf16[256,512]{1,0:T(8,128)(2,1)S(1)} %collective-permute-done.20.a3, ...), custom_call_target="tpu_custom_call" | custom-call | flops 2147483648 | bytes 1048576 | tf_op jit(solution)/shard_map/pallas_call | solution.py:445
  (33 shorter events, 6.5 us)
Async XLA Ops:
  0.6 20.9 %collective-permute-start = (bf16[256,1024]{1,0:T(8,128)(2,1)}, bf16[256,1024]{1,0:T(8,128)(2,1)S(1)}, u32[]{:S(2)}, u32[]{:S(2)}) collective-permute-start(bf16[256,1024]{1,0:T(8,128)(2,1)} %c0.1), channel_id=1, source_target_pairs={{16,17},{17,16},{18,19},{19,18},{20,21},{21,20},{22,23},{23,22},{2... | collective-permute-start | bytes 1572872 | tf_op jit(solution)/shard_map/ppermute | solution.py:488
  3.2 15.6 %collective-permute-start.1 = (bf16[256,1024]{1,0:T(8,128)(2,1)}, bf16[256,1024]{1,0:T(8,128)(2,1)S(1)}, u32[]{:S(2)}, u32[]{:S(2)}) collective-permute-start(bf16[256,1024]{1,0:T(8,128)(2,1)} %c0.1), channel_id=1, source_target_pairs={{16,18},{17,19},{18,16},{19,17},{20,22},{21,23},{22,20},{23,21},{2... | collective-permute-start | bytes 1572872 | tf_op jit(solution)/shard_map/ppermute | solution.py:488
  6.4 15.2 %copy-start = (bf16[256,1024]{1,0:T(8,128)(2,1)S(1)}, bf16[256,1024]{1,0:T(8,128)(2,1)}, u32[]{:S(2)}) copy-start(bf16[256,1024]{1,0:T(8,128)(2,1)} %c0.1) | copy-start | bytes 1572868
  18.8 4.3 %collective-permute-start.2 = (bf16[256,1024]{1,0:T(8,128)(2,1)S(1)}, bf16[256,1024]{1,0:T(8,128)(2,1)S(1)}, u32[]{:S(2)}, u32[]{:S(2)}) collective-permute-start(bf16[256,1024]{1,0:T(8,128)(2,1)S(1)} %collective-permute-done.1.c2), channel_id=1, source_target_pairs={{16,17},{17,16},{18,19},{19,18},{20,21},{21,20},{22,23},{23,22},{2... | collective-permute-start | bytes 1572872 | tf_op jit(solution)/shard_map/ppermute | solution.py:488
  21.6 1.5 %copy-start.1 = (s32[2,1]{0,1:T(1,128)S(1)}, s32[2,1]{0,1:T(1,128)}, u32[]{:S(2)}) copy-start(s32[2,1]{0,1:T(1,128)} %param.8) | copy-start | bytes 28
  25.0 5.2 %collective-permute-start.3 = (bf16[272,128]{1,0:T(8,128)(2,1)S(1)}, bf16[272,128]{1,0:T(8,128)(2,1)S(1)}, u32[]{:S(2)}, u32[]{:S(2)}) collective-permute-start(bf16[272,128]{1,0:T(8,128)(2,1)S(1)} %get-tuple-element.48), channel_id=1, source_target_pairs={{0,4},{1,5},{2,6},{3,7},{4,0},{5,1},{6,2},{7,3},{8,12},{9,13},{10,... | collective-permute-start | bytes 208904 | tf_op jit(solution)/shard_map/ppermute | solution.py:488
  26.4 6.8 %collective-permute-start.4 = (bf16[272,128]{1,0:T(8,128)(2,1)S(1)}, bf16[272,128]{1,0:T(8,128)(2,1)S(1)}, u32[]{:S(2)}, u32[]{:S(2)}) collective-permute-start(bf16[272,128]{1,0:T(8,128)(2,1)S(1)} %get-tuple-element.49), channel_id=1, source_target_pairs={{0,8},{1,9},{2,10},{3,11},{4,12},{5,13},{6,14},{7,15},{8,0},{9,1},... | collective-permute-start | bytes 208904 | tf_op jit(solution)/shard_map/ppermute | solution.py:488
  28.7 5.6 %collective-permute-start.5 = (bf16[272,128]{1,0:T(8,128)(2,1)S(1)}, bf16[272,128]{1,0:T(8,128)(2,1)S(1)}, u32[]{:S(2)}, u32[]{:S(2)}) collective-permute-start(bf16[272,128]{1,0:T(8,128)(2,1)S(1)} %get-tuple-element.50), channel_id=1, source_target_pairs={{0,12},{1,13},{2,14},{3,15},{4,8},{5,9},{6,10},{7,11},{8,4},{9,5},... | collective-permute-start | bytes 208904 | tf_op jit(solution)/shard_map/ppermute | solution.py:488
  28.7 5.6 %collective-permute-start.6 = (bf16[272,128]{1,0:T(8,128)(2,1)S(1)}, bf16[272,128]{1,0:T(8,128)(2,1)S(1)}, u32[]{:S(2)}, u32[]{:S(2)}) collective-permute-start(bf16[272,128]{1,0:T(8,128)(2,1)S(1)} %get-tuple-element.51), channel_id=1, source_target_pairs={{0,16},{1,17},{2,18},{3,19},{4,20},{5,21},{6,22},{7,23},{8,24},{9,... | collective-permute-start | bytes 208904 | tf_op jit(solution)/shard_map/ppermute | solution.py:488
  28.7 5.6 %collective-permute-start.7 = (bf16[272,128]{1,0:T(8,128)(2,1)S(1)}, bf16[272,128]{1,0:T(8,128)(2,1)S(1)}, u32[]{:S(2)}, u32[]{:S(2)}) collective-permute-start(bf16[272,128]{1,0:T(8,128)(2,1)S(1)} %get-tuple-element.52), channel_id=1, source_target_pairs={{0,20},{1,21},{2,22},{3,23},{4,16},{5,17},{6,18},{7,19},{8,28},{9,... | collective-permute-start | bytes 208904 | tf_op jit(solution)/shard_map/ppermute | solution.py:488
  30.2 5.3 %collective-permute-start.8 = (bf16[272,128]{1,0:T(8,128)(2,1)S(1)}, bf16[272,128]{1,0:T(8,128)(2,1)S(1)}, u32[]{:S(2)}, u32[]{:S(2)}) collective-permute-start(bf16[272,128]{1,0:T(8,128)(2,1)S(1)} %get-tuple-element.53), channel_id=1, source_target_pairs={{0,24},{1,25},{2,26},{3,27},{4,28},{5,29},{6,30},{7,31},{8,16},{9,... | collective-permute-start | bytes 208904 | tf_op jit(solution)/shard_map/ppermute | solution.py:488
  33.1 5.9 %collective-permute-start.9 = (bf16[272,128]{1,0:T(8,128)(2,1)S(1)}, bf16[272,128]{1,0:T(8,128)(2,1)S(1)}, u32[]{:S(2)}, u32[]{:S(2)}) collective-permute-start(bf16[272,128]{1,0:T(8,128)(2,1)S(1)} %get-tuple-element.54), channel_id=1, source_target_pairs={{0,28},{1,29},{2,30},{3,31},{4,24},{5,25},{6,26},{7,27},{8,20},{9,... | collective-permute-start | bytes 208904 | tf_op jit(solution)/shard_map/ppermute | solution.py:488
  42.4 5.5 %collective-permute-start.10 = (bf16[256,128]{1,0:T(8,128)(2,1)S(1)}, bf16[256,128]{1,0:T(8,128)(2,1)S(1)}, u32[]{:S(2)}, u32[]{:S(2)}) collective-permute-start(bf16[256,128]{1,0:T(8,128)(2,1)S(1)} %get-tuple-element.56), channel_id=1, source_target_pairs={{0,4},{1,5},{2,6},{3,7},{4,0},{5,1},{6,2},{7,3},{8,12},{9,13},{10,... | collective-permute-start | bytes 196616 | tf_op jit(solution)/shard_map/ppermute | solution.py:488
  43.7 7.3 %collective-permute-start.11 = (bf16[256,128]{1,0:T(8,128)(2,1)S(1)}, bf16[256,128]{1,0:T(8,128)(2,1)S(1)}, u32[]{:S(2)}, u32[]{:S(2)}) collective-permute-start(bf16[256,128]{1,0:T(8,128)(2,1)S(1)} %get-tuple-element.57), channel_id=1, source_target_pairs={{0,8},{1,9},{2,10},{3,11},{4,12},{5,13},{6,14},{7,15},{8,0},{9,1},... | collective-permute-start | bytes 196616 | tf_op jit(solution)/shard_map/ppermute | solution.py:488
  43.9 8.4 %collective-permute-start.12 = (bf16[256,128]{1,0:T(8,128)(2,1)S(1)}, bf16[256,128]{1,0:T(8,128)(2,1)S(1)}, u32[]{:S(2)}, u32[]{:S(2)}) collective-permute-start(bf16[256,128]{1,0:T(8,128)(2,1)S(1)} %get-tuple-element.58), channel_id=1, source_target_pairs={{0,12},{1,13},{2,14},{3,15},{4,8},{5,9},{6,10},{7,11},{8,4},{9,5},... | collective-permute-start | bytes 196616 | tf_op jit(solution)/shard_map/ppermute | solution.py:488
  46.0 6.2 %collective-permute-start.13 = (bf16[256,128]{1,0:T(8,128)(2,1)S(1)}, bf16[256,128]{1,0:T(8,128)(2,1)S(1)}, u32[]{:S(2)}, u32[]{:S(2)}) collective-permute-start(bf16[256,128]{1,0:T(8,128)(2,1)S(1)} %get-tuple-element.59), channel_id=1, source_target_pairs={{0,16},{1,17},{2,18},{3,19},{4,20},{5,21},{6,22},{7,23},{8,24},{9,... | collective-permute-start | bytes 196616 | tf_op jit(solution)/shard_map/ppermute | solution.py:488
  47.7 5.4 %collective-permute-start.14 = (bf16[256,128]{1,0:T(8,128)(2,1)S(1)}, bf16[256,128]{1,0:T(8,128)(2,1)S(1)}, u32[]{:S(2)}, u32[]{:S(2)}) collective-permute-start(bf16[256,128]{1,0:T(8,128)(2,1)S(1)} %get-tuple-element.60), channel_id=1, source_target_pairs={{0,20},{1,21},{2,22},{3,23},{4,16},{5,17},{6,18},{7,19},{8,28},{9,... | collective-permute-start | bytes 196616 | tf_op jit(solution)/shard_map/ppermute | solution.py:488
  47.9 7.5 %collective-permute-start.15 = (bf16[256,128]{1,0:T(8,128)(2,1)S(1)}, bf16[256,128]{1,0:T(8,128)(2,1)S(1)}, u32[]{:S(2)}, u32[]{:S(2)}) collective-permute-start(bf16[256,128]{1,0:T(8,128)(2,1)S(1)} %get-tuple-element.61), channel_id=1, source_target_pairs={{0,24},{1,25},{2,26},{3,27},{4,28},{5,29},{6,30},{7,31},{8,16},{9,... | collective-permute-start | bytes 196616 | tf_op jit(solution)/shard_map/ppermute | solution.py:488
  51.0 6.2 %collective-permute-start.16 = (bf16[256,128]{1,0:T(8,128)(2,1)S(1)}, bf16[256,128]{1,0:T(8,128)(2,1)S(1)}, u32[]{:S(2)}, u32[]{:S(2)}) collective-permute-start(bf16[256,128]{1,0:T(8,128)(2,1)S(1)} %get-tuple-element.62), channel_id=1, source_target_pairs={{0,28},{1,29},{2,30},{3,31},{4,24},{5,25},{6,26},{7,27},{8,20},{9,... | collective-permute-start | bytes 196616 | tf_op jit(solution)/shard_map/ppermute | solution.py:488
  59.9 11.4 %collective-permute-start.17 = (bf16[2,272,1024]{2,1,0:T(8,128)(2,1)S(1)}, bf16[2,272,1024]{2,1,0:T(8,128)(2,1)S(1)}, u32[]{:S(2)}, u32[]{:S(2)}) collective-permute-start(bf16[2,272,1024]{2,1,0:T(8,128)(2,1)S(1)} %shard_map.74.sent), channel_id=1, source_target_pairs={{0,1},{1,0},{2,3},{3,2},{4,5},{5,4},{6,7},{7,6},{8,9},{9,8},{10,11... | collective-permute-start | bytes 3342344 | tf_op jit(solution)/shard_map/ppermute | solution.py:488
  64.5 72.6 %collective-permute-start.22 = (bf16[1024,512]{1,0:T(8,128)(2,1)S(1)}, bf16[1024,512]{1,0:T(8,128)(2,1)S(1)}, u32[]{:S(2)}, u32[]{:S(2)}) collective-permute-start(bf16[1024,512]{1,0:T(8,128)(2,1)S(1)} %get-tuple-element.45.w2), channel_id=1, source_target_pairs={{16,18},{17,19},{18,16},{19,17},{20,22},{21,23},{22,20},{23,21},{2... | collective-permute-start | bytes 3145736 | tf_op jit(solution)/shard_map/ppermute | solution.py:488
  67.7 69.5 %collective-permute-start.23 = (bf16[1024,512]{1,0:T(8,128)(2,1)S(1)}, bf16[1024,512]{1,0:T(8,128)(2,1)S(1)}, u32[]{:S(2)}, u32[]{:S(2)}) collective-permute-start(bf16[1024,512]{1,0:T(8,128)(2,1)S(1)} %get-tuple-element.46.w3), channel_id=1, source_target_pairs={{16,19},{17,18},{18,17},{19,16},{20,23},{21,22},{22,21},{23,20},{2... | collective-permute-start | bytes 3145736 | tf_op jit(solution)/shard_map/ppermute | solution.py:488
  71.4 66.0 %collective-permute-start.21 = (bf16[1024,512]{1,0:T(8,128)(2,1)S(1)}, bf16[1024,512]{1,0:T(8,128)(2,1)S(1)}, u32[]{:S(2)}, u32[]{:S(2)}) collective-permute-start(bf16[1024,512]{1,0:T(8,128)(2,1)S(1)} %get-tuple-element.69.w1), channel_id=1, source_target_pairs={{16,17},{17,16},{18,19},{19,18},{20,21},{21,20},{22,23},{23,22},{2... | collective-permute-start | bytes 3145736 | tf_op jit(solution)/shard_map/ppermute | solution.py:488
  73.5 60.4 %collective-permute-start.24 = (bf16[272,1024]{1,0:T(8,128)(2,1)S(1)}, bf16[272,1024]{1,0:T(8,128)(2,1)S(1)}, u32[]{:S(2)}, u32[]{:S(2)}) collective-permute-start(bf16[272,1024]{1,0:T(8,128)(2,1)S(1)} %shard_map.75.half), channel_id=1, source_target_pairs={{0,2},{1,3},{2,0},{3,1},{4,6},{5,7},{6,4},{7,5},{8,10},{9,11},{10,... | collective-permute-start | bytes 1671176 | tf_op jit(solution)/shard_map/ppermute | solution.py:488
  74.8 56.3 %collective-permute-start.19 = (bf16[256,512]{1,0:T(8,128)(2,1)S(1)}, bf16[256,512]{1,0:T(8,128)(2,1)S(1)}, u32[]{:S(2)}, u32[]{:S(2)}) collective-permute-start(bf16[256,512]{1,0:T(8,128)(2,1)S(1)} %get-tuple-element.68.ls.a0), channel_id=1, source_target_pairs={{16,18},{17,19},{18,16},{19,17},{20,22},{21,23},{22,20},{23,21},{2... | collective-permute-start | bytes 786440 | tf_op jit(solution)/shard_map/ppermute | solution.py:488
  131.1 6.0 %collective-permute-start.20 = (bf16[256,512]{1,0:T(8,128)(2,1)S(1)}, bf16[256,512]{1,0:T(8,128)(2,1)S(1)}, u32[]{:S(2)}, u32[]{:S(2)}) collective-permute-start(bf16[256,512]{1,0:T(8,128)(2,1)S(1)} %collective-permute-done.19.a2), channel_id=1, source_target_pairs={{16,17},{17,16},{18,19},{19,18},{20,21},{21,20},{22,23},{23,22},{2... | collective-permute-start | bytes 786440 | tf_op jit(solution)/shard_map/ppermute | solution.py:488
  133.9 3.4 %collective-permute-start.18 = (bf16[256,512]{1,0:T(8,128)(2,1)S(1)}, bf16[256,512]{1,0:T(8,128)(2,1)S(1)}, u32[]{:S(2)}, u32[]{:S(2)}) collective-permute-start(bf16[256,512]{1,0:T(8,128)(2,1)S(1)} %get-tuple-element.68.ls.a0), channel_id=1, source_target_pairs={{16,17},{17,16},{18,19},{19,18},{20,21},{21,20},{22,23},{23,22},{2... | collective-permute-start | bytes 786440 | tf_op jit(solution)/shard_map/ppermute | solution.py:488

commit v4 on v3

--- a/solution.py
+++ b/solution.py
@@ -171,7 +171,7 @@
     n_mp = sizes[2]
     wp, ws = rest[0], rest[1 : 1 + n_mp]
     own, own_states, own_gain, spread, prim, sec = rest[1 + n_mp : 7 + n_mp]
-    xbuf, gbuf, wbuf, normed, pacc, sacc, sems, ready = rest[7 + n_mp :]
+    xbuf, gbuf, wbuf, normed, sems, ready = rest[7 + n_mp :]
     seg, _, model = place(sizes)
     rows, width = xbuf.shape
     depth = width // n_mp
@@ -197,23 +197,25 @@
     there = lax.broadcasted_iota(jnp.int32, (2 * LANES, 2 * LANES), 1)
     source = pack * lax.rem(here, group) + lax.div(here, group)
     mix = jnp.where(there == source, 1.0, 0.0).astype(BF16)
-    for copy in first_copies:
-        copy.wait()
-    part_rows = 32
-
-    def norm_rows(at, _):
-        line = pl.ds(pl.multiple_of(at * part_rows, part_rows), part_rows)
+    part_rows = 16
+
+    def norm_rows(first):
+        line = slice(first, first + part_rows)
         wide = xbuf[line, :].astype(F32)
         mean = jnp.sum(wide * wide, axis=1, keepdims=True) * (1.0 / width)
         root = jnp.sqrt(mean + EPSILON)
         normed[line, :] = (wide * (1.0 / root) * gbuf[...]).astype(BF16)
         spread[line, :] = jnp.broadcast_to(root, (part_rows, LANES))
-        return 0
-
-    lax.fori_loop(0, rows // part_rows, norm_rows, 0)
+
+    for copy in first_copies:
+        copy.wait()
+    pairs = depth // (2 * group)
+    every = n_mp * pairs * part_rows // rows
     for c in range(n_mp):
         copies[c].wait()
-        for pair in range(depth // (2 * group)):
+        for pair in range(pairs):
+            if (c * pairs + pair) % every == 0:
+                norm_rows((c * pairs + pair) // every * part_rows)
             base = c * lines + pair * 4 * LANES
             left = wbuf[base : base + 2 * LANES, :]
             right = wbuf[base + 2 * LANES : base + 4 * LANES, :]
@@ -226,26 +228,20 @@
                 part = ordered[slot * group : (slot + 1) * group, :]
                 target[first : first + group, tile] = part[:, :LANES]
                 target[first + group : first + 2 * group, tile] = part[:, LANES:]
-        span = pl.ds(pl.multiple_of(jnp.bitwise_xor(model, c) * depth, depth), depth)
-        term = jnp.dot(normed[:, span], wp[c], preferred_element_type=F32)
-        if c == 0:
-            pacc[...] = term
-        else:
-            pacc[...] += term
-
-        @pl.when(seg == 0)
-        def _():
-            other = jnp.dot(normed[:, span], ws[c][...], preferred_element_type=F32)
-            if c == 0:
-                sacc[...] = other
-            else:
-                sacc[...] += other
-
-    prim[...] = pacc[...].astype(BF16)
+
+    def product(weights):
+        total = None
+        for c in range(n_mp):
+            span = pl.ds(pl.multiple_of(jnp.bitwise_xor(model, c) * depth, depth), depth)
+            term = jnp.dot(normed[:, span], weights(c), preferred_element_type=F32)
+            total = term if total is None else total + term
+        return total.astype(BF16)
+
+    prim[...] = product(lambda c: wp[c])
 
     @pl.when(seg == 0)
     def _():
-        sec[...] = sacc[...].astype(BF16)
+        sec[...] = product(lambda c: ws[c][...])
 
     mine = pl.ds(pl.multiple_of(model * depth, depth), depth)
     own[...] = normed[:, mine]
@@ -359,12 +355,14 @@
     rows = lp.shape[0]
     for k, piece in enumerate(ins):
         parts[jnp.bitwise_xor(entry, k)] = piece[...]
-    line = lax.broadcasted_iota(jnp.int32, (rows, DH), 0)
-    alive = line < jnp.where(seg == 0, rows, counts[0, 1])
-    for head in range(heads):
-        cols = slice(head * DH, (head + 1) * DH)
-        lp[:, cols] = parts[head, :, :DH]
-        ls[:, cols] = jnp.where(alive, parts[head, :, DH:].astype(F32), 0.0).astype(BF16)
+    low = lax.broadcasted_iota(jnp.int32, (rows, LANES), 0)
+    alive = low < jnp.where(seg == 0, rows, counts[0, 1])
+    for head in range(0, heads, 2):
+        cols = slice(head * DH, (head + 2) * DH)
+        one, two = parts[head], parts[head + 1]
+        lp[:, cols] = jnp.concatenate([one[:, :DH], two[:, :DH]], axis=1)
+        both = jnp.concatenate([one[:, DH:], two[:, DH:]], axis=1)
+        ls[:, cols] = jnp.where(alive, both.astype(F32), 0.0).astype(BF16)
 
 
 def project_block(seg, wp, ws, lp, ls, out, slot):
@@ -419,16 +417,13 @@
     leaving.wait()
 
 
-def fold_kernel(kept, got, sent, out):
+def fold_kernel(kept, got, sent, out, ends):
     rows = kept.shape[1]
-    out[:rows, :] = (kept[0].astype(F32) + got[0, :rows, :].astype(F32)).astype(BF16)
-    mine = sent[0, rows:, :].astype(F32)
-    theirs = got[0, rows:, :].astype(F32)
+    out[...] = (kept[0].astype(F32) + got[0, :rows, :].astype(F32)).astype(BF16)
+    mine = sent[0, rows:, :rows].astype(F32)
+    theirs = got[0, rows:, :rows].astype(F32)
     total = mine[0:1] + mine[1:2] + theirs[0:1] + theirs[1:2]
-    total = jnp.broadcast_to(total, mine.shape)
-    high = total.astype(BF16).astype(F32)
-    line = lax.broadcasted_iota(jnp.int32, mine.shape, 0)
-    out[rows:, :] = jnp.where(line == 0, high, total - high).astype(BF16)
+    ends[...] = jnp.broadcast_to(total, ends.shape)
 
 
 ANYWHERE = pl.BlockSpec(memory_space=pltpu.HBM)
@@ -459,13 +454,12 @@
     shrink[...] = 1.0 / (width * root * root * root)
 
 
-def leave_kernel(kept, got, half, far, states, gain, inverse, shrink, grad):
+def leave_kernel(kept, got, ends, far_ends, far, states, gain, inverse, shrink, grad):
     rows = states.shape[0]
-    ends = half[rows:, :].astype(F32) + far[rows:, :].astype(F32)
-    row = jnp.broadcast_to(ends[0:1, :rows] + ends[1:2, :rows], (LANES, rows))
-    term = row.T[:, :1]
+    row = ends[...] + far_ends[...]
+    term = jnp.broadcast_to(row[:1], (LANES, rows)).T[:, :1]
     scaled = term * shrink[:, :1]
-    total = kept[1].astype(F32) + got[1, :rows, :].astype(F32) + far[:rows, :].astype(F32)
+    total = kept[1].astype(F32) + got[1, :rows, :].astype(F32) + far[...].astype(F32)
     grad[...] = (gain[...] * total * inverse[:, :1] - states[...].astype(F32) * scaled).astype(BF16)
 
 
@@ -519,8 +513,6 @@
             pltpu.VMEM((1, width), F32),
             pltpu.VMEM((width * 2 * tiles, LANES), BF16),
             pltpu.VMEM((rows, width), BF16),
-            pltpu.VMEM((rows, group), F32),
-            pltpu.VMEM((rows, group), F32),
             pltpu.SemaphoreType.DMA((n_mp,)),
             pltpu.SemaphoreType.DMA((2,)),
         ],
@@ -597,9 +589,12 @@
         16,
         2 << 30,
     )
-    (half,) = call(fold_kernel, (kept, got, sent), [INSIDE] * 3, [((rows + TAIL, feats), BF16)])
+    half, ends = call(
+        fold_kernel, (kept, got, sent), [INSIDE] * 3, [((rows, feats), BF16), ((8, rows), F32)]
+    )
     far = swap(half, 0, 2)
-    own_att, lent_1, half_seen = lax.optimization_barrier((ls, ws[1], half))
+    far_ends = swap(ends, 0, 2)
+    own_att, lent_1, ends = lax.optimization_barrier((ls, ws[1], ends))
     lent_1 = swap(lent_1, 0, 1, summary)
     near_att = swap(own_att, 0, 1, summary)
     cross_att = swap(far_att, 0, 1, summary)
@@ -615,8 +610,8 @@
     )
     (grad,) = call(
         leave_kernel,
-        (kept, got, half_seen, far, own_states, own_gain, inverse, shrink),
-        [INSIDE] * 8,
+        (kept, got, ends, far_ends, far, own_states, own_gain, inverse, shrink),
+        [INSIDE] * 9,
         [((rows, feats), BF16)],
         out_specs=[INSIDE],
     )

time: 140 us -> 143 us (1.021)
  starting transfers between devices: 48 us -> 50.4 us
  waiting for transfers between devices: 68.1 us -> 69.7 us
    ppermute x25 -> x26, starting transfers between devices: 48 us -> 50.4 us  [swap(): return lax.ppermute(x, AXES, pairs)]
    ppermute x25 -> x26, waiting for transfers between devices: 68.1 us -> 69.7 us  [swap(): return lax.ppermute(x, AXES, pairs)]
  transfers between devices with their start and end apart: 25 -> 26, of which waited for: 9 -> 10; matrix products, arithmetic and copies ran while one was open for 0% -> 0% of each run, Pallas kernels for 9% -> 8%
where the time goes in v4:
time: 143 us; the launch traced here: 142 us
  waiting for transfers between devices  69.7 us (49%)
  starting transfers between devices  50.4 us (35%)
  Pallas kernels  21.3 us (15%)
    ppermute x26, waiting for transfers between devices, swap(): return lax.ppermute(x, AXES, pairs)  69.7 us
    ppermute x26, starting transfers between devices, swap(): return lax.ppermute(x, AXES, pairs)  50.4 us
    pallas_call x11, Pallas kernels, call(): pl.pallas_call(body, in_specs=list(specs), out_specs=[INSIDE] * len(outs)...  21.3 us
  transfers between devices with their start and end apart: 26, of which 10 were waited for; matrix products, arithmetic and copies ran while one was open for 0% of the time, Pallas kernels for 8%

profile of v4, /device:TPU:3, one launch (start us, length us, event | category | flops | bytes accessed | tf_op | source)
XLA Modules:
  0.0 142.4 jit_solution(1170666923220502148)
XLA Ops:
  0.6 2.6 %collective-permute-start = (bf16[256,1024]{1,0:T(8,128)(2,1)}, bf16[256,1024]{1,0:T(8,128)(2,1)S(1)}, u32[]{:S(2)}, u32[]{:S(2)}) collective-permute-start(bf16[256,1024]{1,0:T(8,128)(2,1)} %c0.1), channel_id=1, source_target_pairs={{16,17},{17,16},{18,19},{19,18},{20,21},{21,20},{22,23},{23,22},{2... | collective-permute-start | bytes 1572872 | tf_op jit(solution)/shard_map/ppermute | solution.py:482
  3.2 3.1 %collective-permute-start.1 = (bf16[256,1024]{1,0:T(8,128)(2,1)}, bf16[256,1024]{1,0:T(8,128)(2,1)S(1)}, u32[]{:S(2)}, u32[]{:S(2)}) collective-permute-start(bf16[256,1024]{1,0:T(8,128)(2,1)} %c0.1), channel_id=1, source_target_pairs={{16,18},{17,19},{18,16},{19,17},{20,22},{21,23},{22,20},{23,21},{2... | collective-permute-start | bytes 1572872 | tf_op jit(solution)/shard_map/ppermute | solution.py:482
  6.4 7.8 %shard_map.68 = (bf16[4,1024,512]{2,1,0:T(8,128)(2,1)S(1)}, bf16[1024,512]{1,0:T(8,128)(2,1)S(1)}, bf16[1024,512]{1,0:T(8,128)(2,1)S(1)}, bf16[1024,512]{1,0:T(8...) custom-call(bf16[256,4096]{1,0:T(8,128)(2,1)} %bitcast.13, ...), custom_call_target="tpu_custom_call" | custom-call | flops 8589934592 | bytes 1048576 | tf_op jit(solution)/shard_map/pallas_call | solution.py:440
  14.2 4.6 %collective-permute-done.1.c2 = bf16[256,1024]{1,0:T(8,128)(2,1)S(1)} collective-permute-done((bf16[256,1024]{1,0:T(8,128)(2,1)}, bf16[256,1024]{1,0:T(8,128)(2,1)S(1)}, u32[]{:S(2)}, u32[]{:S(2)}) %collective-permute-start.1) | collective-permute-done | bytes 524320 | tf_op jit(solution)/shard_map/ppermute | solution.py:482
  18.8 2.8 %collective-permute-start.2 = (bf16[256,1024]{1,0:T(8,128)(2,1)S(1)}, bf16[256,1024]{1,0:T(8,128)(2,1)S(1)}, u32[]{:S(2)}, u32[]{:S(2)}) collective-permute-start(bf16[256,1024]{1,0:T(8,128)(2,1)S(1)} %collective-permute-done.1.c2), channel_id=1, source_target_pairs={{16,17},{17,16},{18,19},{19,18},{20,21},{21,20},{22,23},{23,22},{2... | collective-permute-start | bytes 1572872 | tf_op jit(solution)/shard_map/ppermute | solution.py:482
  23.1 1.9 %shard_map.70 = (bf16[256,512]{1,0:T(8,128)(2,1)S(1)}, bf16[272,128]{1,0:T(8,128)(2,1)S(1)}, bf16[272,128]{1,0:T(8,128)(2,1)S(1)}, bf16[272,128]{1,0:T(8,128)(2,...) custom-call(s32[1,2]{1,0:T(1,128)S(1)} %bitcast.9, ...), custom_call_target="tpu_custom_call" | custom-call | flops 1073741824 | bytes 1048576 | tf_op jit(solution)/shard_map/pallas_call | solution.py:440
  25.0 1.4 collective-permute-start.3
  26.4 2.3 %collective-permute-start.4 = (bf16[272,128]{1,0:T(8,128)(2,1)S(1)}, bf16[272,128]{1,0:T(8,128)(2,1)S(1)}, u32[]{:S(2)}, u32[]{:S(2)}) collective-permute-start(bf16[272,128]{1,0:T(8,128)(2,1)S(1)} %get-tuple-element.51), channel_id=1, source_target_pairs={{0,8},{1,9},{2,10},{3,11},{4,12},{5,13},{6,14},{7,15},{8,0},{9,1},... | collective-permute-start | bytes 208904 | tf_op jit(solution)/shard_map/ppermute | solution.py:482
  28.7 1.5 %collective-permute-start.7 = (bf16[272,128]{1,0:T(8,128)(2,1)S(1)}, bf16[272,128]{1,0:T(8,128)(2,1)S(1)}, u32[]{:S(2)}, u32[]{:S(2)}) collective-permute-start(bf16[272,128]{1,0:T(8,128)(2,1)S(1)} %get-tuple-element.54), channel_id=1, source_target_pairs={{0,20},{1,21},{2,22},{3,23},{4,16},{5,17},{6,18},{7,19},{8,28},{9,... | collective-permute-start | bytes 208904 | tf_op jit(solution)/shard_map/ppermute | solution.py:482
  30.2 2.9 %collective-permute-start.8 = (bf16[272,128]{1,0:T(8,128)(2,1)S(1)}, bf16[272,128]{1,0:T(8,128)(2,1)S(1)}, u32[]{:S(2)}, u32[]{:S(2)}) collective-permute-start(bf16[272,128]{1,0:T(8,128)(2,1)S(1)} %get-tuple-element.55), channel_id=1, source_target_pairs={{0,24},{1,25},{2,26},{3,27},{4,28},{5,29},{6,30},{7,31},{8,16},{9,... | collective-permute-start | bytes 208904 | tf_op jit(solution)/shard_map/ppermute | solution.py:482
  35.5 3.6 %collective-permute-done.9.rest_7_ = bf16[272,128]{1,0:T(8,128)(2,1)S(1)} collective-permute-done((bf16[272,128]{1,0:T(8,128)(2,1)S(1)}, bf16[272,128]{1,0:T(8,128)(2,1)S(1)}, u32[]{:S(2)}, u32[]{:S(2)}) %collective-permute-start.9) | collective-permute-done | bytes 69664 | tf_op jit(solution)/shard_map/ppermute | solution.py:482
  39.0 3.4 %shard_map.71 = (bf16[256,128]{1,0:T(8,128)(2,1)S(1)}, bf16[256,128]{1,0:T(8,128)(2,1)S(1)}, bf16[256,128]{1,0:T(8,128)(2,1)S(1)}, bf16[256,128]{1,0:T(8,128)(2,...) custom-call(bf16[272,128]{1,0:T(8,128)(2,1)S(1)} %get-tuple-element., ...), custom_call_target="tpu_custom_call" | custom-call | flops 4294967296 | bytes 1048576 | tf_op jit(solution)/shard_map/pallas_call | solution.py:440
  42.4 1.2 collective-permute-start.10
  43.9 2.2 %collective-permute-start.12 = (bf16[256,128]{1,0:T(8,128)(2,1)S(1)}, bf16[256,128]{1,0:T(8,128)(2,1)S(1)}, u32[]{:S(2)}, u32[]{:S(2)}) collective-permute-start(bf16[256,128]{1,0:T(8,128)(2,1)S(1)} %get-tuple-element.60), channel_id=1, source_target_pairs={{0,12},{1,13},{2,14},{3,15},{4,8},{5,9},{6,10},{7,11},{8,4},{9,5},... | collective-permute-start | bytes 196616 | tf_op jit(solution)/shard_map/ppermute | solution.py:482
  46.0 1.6 %collective-permute-start.13 = (bf16[256,128]{1,0:T(8,128)(2,1)S(1)}, bf16[256,128]{1,0:T(8,128)(2,1)S(1)}, u32[]{:S(2)}, u32[]{:S(2)}) collective-permute-start(bf16[256,128]{1,0:T(8,128)(2,1)S(1)} %get-tuple-element.61), channel_id=1, source_target_pairs={{0,16},{1,17},{2,18},{3,19},{4,20},{5,21},{6,22},{7,23},{8,24},{9,... | collective-permute-start | bytes 196616 | tf_op jit(solution)/shard_map/ppermute | solution.py:482
  47.9 3.1 %collective-permute-start.15 = (bf16[256,128]{1,0:T(8,128)(2,1)S(1)}, bf16[256,128]{1,0:T(8,128)(2,1)S(1)}, u32[]{:S(2)}, u32[]{:S(2)}) collective-permute-start(bf16[256,128]{1,0:T(8,128)(2,1)S(1)} %get-tuple-element.63), channel_id=1, source_target_pairs={{0,24},{1,25},{2,26},{3,27},{4,28},{5,29},{6,30},{7,31},{8,16},{9,... | collective-permute-start | bytes 196616 | tf_op jit(solution)/shard_map/ppermute | solution.py:482
  51.0 1.2 collective-permute-start.16
  53.1 2.2 %collective-permute-done.15.rest_6_ = bf16[256,128]{1,0:T(8,128)(2,1)S(1)} collective-permute-done((bf16[256,128]{1,0:T(8,128)(2,1)S(1)}, bf16[256,128]{1,0:T(8,128)(2,1)S(1)}, u32[]{:S(2)}, u32[]{:S(2)}) %collective-permute-start.15) | collective-permute-done | bytes 65568 | tf_op jit(solution)/shard_map/ppermute | solution.py:482
  55.4 1.8 %collective-permute-done.16.rest_7_ = bf16[256,128]{1,0:T(8,128)(2,1)S(1)} collective-permute-done((bf16[256,128]{1,0:T(8,128)(2,1)S(1)}, bf16[256,128]{1,0:T(8,128)(2,1)S(1)}, u32[]{:S(2)}, u32[]{:S(2)}) %collective-permute-start.16) | collective-permute-done | bytes 65568 | tf_op jit(solution)/shard_map/ppermute | solution.py:482
  58.0 1.7 %shard_map.74.sent = bf16[2,272,1024]{2,1,0:T(8,128)(2,1)S(1)} custom-call(bf16[256,512]{1,0:T(8,128)(2,1)S(1)} %get-tuple-element.66.lp, bf16[256,512]{1,0:T(8,128)(2,1)S(1)} %get-tuple-element.71.ls.a0, bf16[256,512]{1,0:T(8,128)(2,1)S(1)} %get-tuple-element.41.prim, bf16[256,512]{1,0:T(8,128)(2,1)S(1)} %get-tuple-element.68.second, ...), custom_call_target="tpu_custom_call" | custom-call | flops 2147483648 | bytes 1048576 | tf_op jit(solution)/shard_map/pallas_call | solution.py:440
  59.7 4.7 %collective-permute-start.17 = (bf16[2,272,1024]{2,1,0:T(8,128)(2,1)S(1)}, bf16[2,272,1024]{2,1,0:T(8,128)(2,1)S(1)}, u32[]{:S(2)}, u32[]{:S(2)}) collective-permute-start(bf16[2,272,1024]{2,1,0:T(8,128)(2,1)S(1)} %shard_map.74.sent), channel_id=1, source_target_pairs={{0,1},{1,0},{2,3},{3,2},{4,5},{5,4},{6,7},{7,6},{8,9},{9,8},{10,11... | collective-permute-start | bytes 3342344 | tf_op jit(solution)/shard_map/ppermute | solution.py:482
  64.4 3.1 %collective-permute-start.22 = (bf16[1024,512]{1,0:T(8,128)(2,1)S(1)}, bf16[1024,512]{1,0:T(8,128)(2,1)S(1)}, u32[]{:S(2)}, u32[]{:S(2)}) collective-permute-start(bf16[1024,512]{1,0:T(8,128)(2,1)S(1)} %get-tuple-element.47.w2), channel_id=1, source_target_pairs={{16,18},{17,19},{18,16},{19,17},{20,22},{21,23},{22,20},{23,21},{2... | collective-permute-start | bytes 3145736 | tf_op jit(solution)/shard_map/ppermute | solution.py:482
  67.5 2.3 %collective-permute-start.23 = (bf16[1024,512]{1,0:T(8,128)(2,1)S(1)}, bf16[1024,512]{1,0:T(8,128)(2,1)S(1)}, u32[]{:S(2)}, u32[]{:S(2)}) collective-permute-start(bf16[1024,512]{1,0:T(8,128)(2,1)S(1)} %get-tuple-element.48.w3), channel_id=1, source_target_pairs={{16,19},{17,18},{18,17},{19,16},{20,23},{21,22},{22,21},{23,20},{2... | collective-permute-start | bytes 3145736 | tf_op jit(solution)/shard_map/ppermute | solution.py:482
  71.2 2.1 %collective-permute-start.21 = (bf16[1024,512]{1,0:T(8,128)(2,1)S(1)}, bf16[1024,512]{1,0:T(8,128)(2,1)S(1)}, u32[]{:S(2)}, u32[]{:S(2)}) collective-permute-start(bf16[1024,512]{1,0:T(8,128)(2,1)S(1)} %get-tuple-element.72.w1), channel_id=1, source_target_pairs={{16,17},{17,16},{18,19},{19,18},{20,21},{21,20},{22,23},{23,22},{2... | collective-permute-start | bytes 3145736 | tf_op jit(solution)/shard_map/ppermute | solution.py:482
  73.3 1.3 collective-permute-start.25
  74.7 2.1 %collective-permute-start.19 = (bf16[256,512]{1,0:T(8,128)(2,1)S(1)}, bf16[256,512]{1,0:T(8,128)(2,1)S(1)}, u32[]{:S(2)}, u32[]{:S(2)}) collective-permute-start(bf16[256,512]{1,0:T(8,128)(2,1)S(1)} %get-tuple-element.71.ls.a0), channel_id=1, source_target_pairs={{16,18},{17,19},{18,16},{19,17},{20,22},{21,23},{22,20},{23,21},{2... | collective-permute-start | bytes 786440 | tf_op jit(solution)/shard_map/ppermute | solution.py:482
  76.8 53.5 %collective-permute-done.19.a2 = bf16[256,512]{1,0:T(8,128)(2,1)S(1)} collective-permute-done((bf16[256,512]{1,0:T(8,128)(2,1)S(1)}, bf16[256,512]{1,0:T(8,128)(2,1)S(1)}, u32[]{:S(2)}, u32[]{:S(2)}) %collective-permute-start.19) | collective-permute-done | bytes 262176 | tf_op jit(solution)/shard_map/ppermute | solution.py:482
  130.3 1.2 collective-permute-start.24
  131.5 1.3 collective-permute-done.24.far_ends
  132.8 3.9 %collective-permute-start.20 = (bf16[256,512]{1,0:T(8,128)(2,1)S(1)}, bf16[256,512]{1,0:T(8,128)(2,1)S(1)}, u32[]{:S(2)}, u32[]{:S(2)}) collective-permute-start(bf16[256,512]{1,0:T(8,128)(2,1)S(1)} %collective-permute-done.19.a2), channel_id=1, source_target_pairs={{16,17},{17,16},{18,19},{19,18},{20,21},{21,20},{22,23},{23,22},{2... | collective-permute-start | bytes 786440 | tf_op jit(solution)/shard_map/ppermute | solution.py:482
  136.7 1.9 %collective-permute-start.18 = (bf16[256,512]{1,0:T(8,128)(2,1)S(1)}, bf16[256,512]{1,0:T(8,128)(2,1)S(1)}, u32[]{:S(2)}, u32[]{:S(2)}) collective-permute-start(bf16[256,512]{1,0:T(8,128)(2,1)S(1)} %get-tuple-element.71.ls.a0), channel_id=1, source_target_pairs={{16,17},{17,16},{18,19},{19,18},{20,21},{21,20},{22,23},{23,22},{2... | collective-permute-start | bytes 786440 | tf_op jit(solution)/shard_map/ppermute | solution.py:482
  140.2 2.1 %shard_map.76 = bf16[256,1024]{1,0:T(8,128)(2,1)} custom-call(bf16[256,512]{1,0:T(8,128)(2,1)S(1)} %get-tuple-element.71.ls.a0, bf16[256,512]{1,0:T(8,128)(2,1)S(1)} %collective-permute-done.18.a1, bf16[256,512]{1,0:T(8,128)(2,1)S(1)} %collective-permute-done.19.a2, bf16[256,512]{1,0:T(8,128)(2,1)S(1)} %collective-permute-done.20.a3, ...), custom_call_target="tpu_custom_call" | custom-call | flops 2147483648 | bytes 1048576 | tf_op jit(solution)/shard_map/pallas_call | solution.py:440
  (35 shorter events, 8.7 us)
Async XLA Ops:
  0.6 20.9 %collective-permute-start = (bf16[256,1024]{1,0:T(8,128)(2,1)}, bf16[256,1024]{1,0:T(8,128)(2,1)S(1)}, u32[]{:S(2)}, u32[]{:S(2)}) collective-permute-start(bf16[256,1024]{1,0:T(8,128)(2,1)} %c0.1), channel_id=1, source_target_pairs={{16,17},{17,16},{18,19},{19,18},{20,21},{21,20},{22,23},{23,22},{2... | collective-permute-start | bytes 1572872 | tf_op jit(solution)/shard_map/ppermute | solution.py:482
  3.2 15.6 %collective-permute-start.1 = (bf16[256,1024]{1,0:T(8,128)(2,1)}, bf16[256,1024]{1,0:T(8,128)(2,1)S(1)}, u32[]{:S(2)}, u32[]{:S(2)}) collective-permute-start(bf16[256,1024]{1,0:T(8,128)(2,1)} %c0.1), channel_id=1, source_target_pairs={{16,18},{17,19},{18,16},{19,17},{20,22},{21,23},{22,20},{23,21},{2... | collective-permute-start | bytes 1572872 | tf_op jit(solution)/shard_map/ppermute | solution.py:482
  6.4 15.2 %copy-start = (bf16[256,1024]{1,0:T(8,128)(2,1)S(1)}, bf16[256,1024]{1,0:T(8,128)(2,1)}, u32[]{:S(2)}) copy-start(bf16[256,1024]{1,0:T(8,128)(2,1)} %c0.1) | copy-start | bytes 1572868
  18.8 4.3 %collective-permute-start.2 = (bf16[256,1024]{1,0:T(8,128)(2,1)S(1)}, bf16[256,1024]{1,0:T(8,128)(2,1)S(1)}, u32[]{:S(2)}, u32[]{:S(2)}) collective-permute-start(bf16[256,1024]{1,0:T(8,128)(2,1)S(1)} %collective-permute-done.1.c2), channel_id=1, source_target_pairs={{16,17},{17,16},{18,19},{19,18},{20,21},{21,20},{22,23},{23,22},{2... | collective-permute-start | bytes 1572872 | tf_op jit(solution)/shard_map/ppermute | solution.py:482
  21.6 1.5 %copy-start.1 = (s32[2,1]{0,1:T(1,128)S(1)}, s32[2,1]{0,1:T(1,128)}, u32[]{:S(2)}) copy-start(s32[2,1]{0,1:T(1,128)} %param.8) | copy-start | bytes 28
  25.0 5.2 %collective-permute-start.3 = (bf16[272,128]{1,0:T(8,128)(2,1)S(1)}, bf16[272,128]{1,0:T(8,128)(2,1)S(1)}, u32[]{:S(2)}, u32[]{:S(2)}) collective-permute-start(bf16[272,128]{1,0:T(8,128)(2,1)S(1)} %get-tuple-element.50), channel_id=1, source_target_pairs={{0,4},{1,5},{2,6},{3,7},{4,0},{5,1},{6,2},{7,3},{8,12},{9,13},{10,... | collective-permute-start | bytes 208904 | tf_op jit(solution)/shard_map/ppermute | solution.py:482
  26.4 6.8 %collective-permute-start.4 = (bf16[272,128]{1,0:T(8,128)(2,1)S(1)}, bf16[272,128]{1,0:T(8,128)(2,1)S(1)}, u32[]{:S(2)}, u32[]{:S(2)}) collective-permute-start(bf16[272,128]{1,0:T(8,128)(2,1)S(1)} %get-tuple-element.51), channel_id=1, source_target_pairs={{0,8},{1,9},{2,10},{3,11},{4,12},{5,13},{6,14},{7,15},{8,0},{9,1},... | collective-permute-start | bytes 208904 | tf_op jit(solution)/shard_map/ppermute | solution.py:482
  28.7 5.6 %collective-permute-start.5 = (bf16[272,128]{1,0:T(8,128)(2,1)S(1)}, bf16[272,128]{1,0:T(8,128)(2,1)S(1)}, u32[]{:S(2)}, u32[]{:S(2)}) collective-permute-start(bf16[272,128]{1,0:T(8,128)(2,1)S(1)} %get-tuple-element.52), channel_id=1, source_target_pairs={{0,12},{1,13},{2,14},{3,15},{4,8},{5,9},{6,10},{7,11},{8,4},{9,5},... | collective-permute-start | bytes 208904 | tf_op jit(solution)/shard_map/ppermute | solution.py:482
  28.7 5.6 %collective-permute-start.6 = (bf16[272,128]{1,0:T(8,128)(2,1)S(1)}, bf16[272,128]{1,0:T(8,128)(2,1)S(1)}, u32[]{:S(2)}, u32[]{:S(2)}) collective-permute-start(bf16[272,128]{1,0:T(8,128)(2,1)S(1)} %get-tuple-element.53), channel_id=1, source_target_pairs={{0,16},{1,17},{2,18},{3,19},{4,20},{5,21},{6,22},{7,23},{8,24},{9,... | collective-permute-start | bytes 208904 | tf_op jit(solution)/shard_map/ppermute | solution.py:482
  28.7 5.6 %collective-permute-start.7 = (bf16[272,128]{1,0:T(8,128)(2,1)S(1)}, bf16[272,128]{1,0:T(8,128)(2,1)S(1)}, u32[]{:S(2)}, u32[]{:S(2)}) collective-permute-start(bf16[272,128]{1,0:T(8,128)(2,1)S(1)} %get-tuple-element.54), channel_id=1, source_target_pairs={{0,20},{1,21},{2,22},{3,23},{4,16},{5,17},{6,18},{7,19},{8,28},{9,... | collective-permute-start | bytes 208904 | tf_op jit(solution)/shard_map/ppermute | solution.py:482
  30.2 5.3 %collective-permute-start.8 = (bf16[272,128]{1,0:T(8,128)(2,1)S(1)}, bf16[272,128]{1,0:T(8,128)(2,1)S(1)}, u32[]{:S(2)}, u32[]{:S(2)}) collective-permute-start(bf16[272,128]{1,0:T(8,128)(2,1)S(1)} %get-tuple-element.55), channel_id=1, source_target_pairs={{0,24},{1,25},{2,26},{3,27},{4,28},{5,29},{6,30},{7,31},{8,16},{9,... | collective-permute-start | bytes 208904 | tf_op jit(solution)/shard_map/ppermute | solution.py:482
  33.1 5.9 %collective-permute-start.9 = (bf16[272,128]{1,0:T(8,128)(2,1)S(1)}, bf16[272,128]{1,0:T(8,128)(2,1)S(1)}, u32[]{:S(2)}, u32[]{:S(2)}) collective-permute-start(bf16[272,128]{1,0:T(8,128)(2,1)S(1)} %get-tuple-element.56), channel_id=1, source_target_pairs={{0,28},{1,29},{2,30},{3,31},{4,24},{5,25},{6,26},{7,27},{8,20},{9,... | collective-permute-start | bytes 208904 | tf_op jit(solution)/shard_map/ppermute | solution.py:482
  42.4 5.5 %collective-permute-start.10 = (bf16[256,128]{1,0:T(8,128)(2,1)S(1)}, bf16[256,128]{1,0:T(8,128)(2,1)S(1)}, u32[]{:S(2)}, u32[]{:S(2)}) collective-permute-start(bf16[256,128]{1,0:T(8,128)(2,1)S(1)} %get-tuple-element.58), channel_id=1, source_target_pairs={{0,4},{1,5},{2,6},{3,7},{4,0},{5,1},{6,2},{7,3},{8,12},{9,13},{10,... | collective-permute-start | bytes 196616 | tf_op jit(solution)/shard_map/ppermute | solution.py:482
  43.7 7.3 %collective-permute-start.11 = (bf16[256,128]{1,0:T(8,128)(2,1)S(1)}, bf16[256,128]{1,0:T(8,128)(2,1)S(1)}, u32[]{:S(2)}, u32[]{:S(2)}) collective-permute-start(bf16[256,128]{1,0:T(8,128)(2,1)S(1)} %get-tuple-element.59), channel_id=1, source_target_pairs={{0,8},{1,9},{2,10},{3,11},{4,12},{5,13},{6,14},{7,15},{8,0},{9,1},... | collective-permute-start | bytes 196616 | tf_op jit(solution)/shard_map/ppermute | solution.py:482
  43.9 8.4 %collective-permute-start.12 = (bf16[256,128]{1,0:T(8,128)(2,1)S(1)}, bf16[256,128]{1,0:T(8,128)(2,1)S(1)}, u32[]{:S(2)}, u32[]{:S(2)}) collective-permute-start(bf16[256,128]{1,0:T(8,128)(2,1)S(1)} %get-tuple-element.60), channel_id=1, source_target_pairs={{0,12},{1,13},{2,14},{3,15},{4,8},{5,9},{6,10},{7,11},{8,4},{9,5},... | collective-permute-start | bytes 196616 | tf_op jit(solution)/shard_map/ppermute | solution.py:482
  46.0 6.2 %collective-permute-start.13 = (bf16[256,128]{1,0:T(8,128)(2,1)S(1)}, bf16[256,128]{1,0:T(8,128)(2,1)S(1)}, u32[]{:S(2)}, u32[]{:S(2)}) collective-permute-start(bf16[256,128]{1,0:T(8,128)(2,1)S(1)} %get-tuple-element.61), channel_id=1, source_target_pairs={{0,16},{1,17},{2,18},{3,19},{4,20},{5,21},{6,22},{7,23},{8,24},{9,... | collective-permute-start | bytes 196616 | tf_op jit(solution)/shard_map/ppermute | solution.py:482
  47.7 5.4 %collective-permute-start.14 = (bf16[256,128]{1,0:T(8,128)(2,1)S(1)}, bf16[256,128]{1,0:T(8,128)(2,1)S(1)}, u32[]{:S(2)}, u32[]{:S(2)}) collective-permute-start(bf16[256,128]{1,0:T(8,128)(2,1)S(1)} %get-tuple-element.62), channel_id=1, source_target_pairs={{0,20},{1,21},{2,22},{3,23},{4,16},{5,17},{6,18},{7,19},{8,28},{9,... | collective-permute-start | bytes 196616 | tf_op jit(solution)/shard_map/ppermute | solution.py:482
  47.9 7.5 %collective-permute-start.15 = (bf16[256,128]{1,0:T(8,128)(2,1)S(1)}, bf16[256,128]{1,0:T(8,128)(2,1)S(1)}, u32[]{:S(2)}, u32[]{:S(2)}) collective-permute-start(bf16[256,128]{1,0:T(8,128)(2,1)S(1)} %get-tuple-element.63), channel_id=1, source_target_pairs={{0,24},{1,25},{2,26},{3,27},{4,28},{5,29},{6,30},{7,31},{8,16},{9,... | collective-permute-start | bytes 196616 | tf_op jit(solution)/shard_map/ppermute | solution.py:482
  51.0 6.2 %collective-permute-start.16 = (bf16[256,128]{1,0:T(8,128)(2,1)S(1)}, bf16[256,128]{1,0:T(8,128)(2,1)S(1)}, u32[]{:S(2)}, u32[]{:S(2)}) collective-permute-start(bf16[256,128]{1,0:T(8,128)(2,1)S(1)} %get-tuple-element.64), channel_id=1, source_target_pairs={{0,28},{1,29},{2,30},{3,31},{4,24},{5,25},{6,26},{7,27},{8,20},{9,... | collective-permute-start | bytes 196616 | tf_op jit(solution)/shard_map/ppermute | solution.py:482
  59.7 11.4 %collective-permute-start.17 = (bf16[2,272,1024]{2,1,0:T(8,128)(2,1)S(1)}, bf16[2,272,1024]{2,1,0:T(8,128)(2,1)S(1)}, u32[]{:S(2)}, u32[]{:S(2)}) collective-permute-start(bf16[2,272,1024]{2,1,0:T(8,128)(2,1)S(1)} %shard_map.74.sent), channel_id=1, source_target_pairs={{0,1},{1,0},{2,3},{3,2},{4,5},{5,4},{6,7},{7,6},{8,9},{9,8},{10,11... | collective-permute-start | bytes 3342344 | tf_op jit(solution)/shard_map/ppermute | solution.py:482
  64.4 75.5 %collective-permute-start.22 = (bf16[1024,512]{1,0:T(8,128)(2,1)S(1)}, bf16[1024,512]{1,0:T(8,128)(2,1)S(1)}, u32[]{:S(2)}, u32[]{:S(2)}) collective-permute-start(bf16[1024,512]{1,0:T(8,128)(2,1)S(1)} %get-tuple-element.47.w2), channel_id=1, source_target_pairs={{16,18},{17,19},{18,16},{19,17},{20,22},{21,23},{22,20},{23,21},{2... | collective-permute-start | bytes 3145736 | tf_op jit(solution)/shard_map/ppermute | solution.py:482
  67.5 72.4 %collective-permute-start.23 = (bf16[1024,512]{1,0:T(8,128)(2,1)S(1)}, bf16[1024,512]{1,0:T(8,128)(2,1)S(1)}, u32[]{:S(2)}, u32[]{:S(2)}) collective-permute-start(bf16[1024,512]{1,0:T(8,128)(2,1)S(1)} %get-tuple-element.48.w3), channel_id=1, source_target_pairs={{16,19},{17,18},{18,17},{19,16},{20,23},{21,22},{22,21},{23,20},{2... | collective-permute-start | bytes 3145736 | tf_op jit(solution)/shard_map/ppermute | solution.py:482
  71.2 69.0 %collective-permute-start.21 = (bf16[1024,512]{1,0:T(8,128)(2,1)S(1)}, bf16[1024,512]{1,0:T(8,128)(2,1)S(1)}, u32[]{:S(2)}, u32[]{:S(2)}) collective-permute-start(bf16[1024,512]{1,0:T(8,128)(2,1)S(1)} %get-tuple-element.72.w1), channel_id=1, source_target_pairs={{16,17},{17,16},{18,19},{19,18},{20,21},{21,20},{22,23},{23,22},{2... | collective-permute-start | bytes 3145736 | tf_op jit(solution)/shard_map/ppermute | solution.py:482
  73.3 63.4 %collective-permute-start.25 = (bf16[256,1024]{1,0:T(8,128)(2,1)S(1)}, bf16[256,1024]{1,0:T(8,128)(2,1)S(1)}, u32[]{:S(2)}, u32[]{:S(2)}) collective-permute-start(bf16[256,1024]{1,0:T(8,128)(2,1)S(1)} %get-tuple-element.75), channel_id=1, source_target_pairs={{0,2},{1,3},{2,0},{3,1},{4,6},{5,7},{6,4},{7,5},{8,10},{9,11},{10,... | collective-permute-start | bytes 1572872 | tf_op jit(solution)/shard_map/ppermute | solution.py:482
  74.7 55.6 %collective-permute-start.19 = (bf16[256,512]{1,0:T(8,128)(2,1)S(1)}, bf16[256,512]{1,0:T(8,128)(2,1)S(1)}, u32[]{:S(2)}, u32[]{:S(2)}) collective-permute-start(bf16[256,512]{1,0:T(8,128)(2,1)S(1)} %get-tuple-element.71.ls.a0), channel_id=1, source_target_pairs={{16,18},{17,19},{18,16},{19,17},{20,22},{21,23},{22,20},{23,21},{2... | collective-permute-start | bytes 786440 | tf_op jit(solution)/shard_map/ppermute | solution.py:482
  130.3 2.5 %collective-permute-start.24 = (f32[8,256]{1,0:T(8,128)S(1)}, f32[8,256]{1,0:T(8,128)S(1)}, u32[]{:S(2)}, u32[]{:S(2)}) collective-permute-start(f32[8,256]{1,0:T(8,128)S(1)} %get-tuple-element.74.ends), channel_id=1, source_target_pairs={{0,2},{1,3},{2,0},{3,1},{4,6},{5,7},{6,4},{7,5},{8,10},{9,11},{10,... | collective-permute-start | bytes 24584 | tf_op jit(solution)/shard_map/ppermute | solution.py:482
  132.8 7.1 %collective-permute-start.20 = (bf16[256,512]{1,0:T(8,128)(2,1)S(1)}, bf16[256,512]{1,0:T(8,128)(2,1)S(1)}, u32[]{:S(2)}, u32[]{:S(2)}) collective-permute-start(bf16[256,512]{1,0:T(8,128)(2,1)S(1)} %collective-permute-done.19.a2), channel_id=1, source_target_pairs={{16,17},{17,16},{18,19},{19,18},{20,21},{21,20},{22,23},{23,22},{2... | collective-permute-start | bytes 786440 | tf_op jit(solution)/shard_map/ppermute | solution.py:482
  136.7 3.4 %collective-permute-start.18 = (bf16[256,512]{1,0:T(8,128)(2,1)S(1)}, bf16[256,512]{1,0:T(8,128)(2,1)S(1)}, u32[]{:S(2)}, u32[]{:S(2)}) collective-permute-start(bf16[256,512]{1,0:T(8,128)(2,1)S(1)} %get-tuple-element.71.ls.a0), channel_id=1, source_target_pairs={{16,17},{17,16},{18,19},{19,18},{20,21},{21,20},{22,23},{23,22},{2... | collective-permute-start | bytes 786440 | tf_op jit(solution)/shard_map/ppermute | solution.py:482

commit v5 on v4

--- a/solution.py
+++ b/solution.py
@@ -472,16 +472,13 @@
     group = projections.shape[3]
     counts = live_counts.T
 
-    def swap(x, over_heads, over_mp, senders=range(n_seg)):
+    def swap(x, over_heads, over_mp):
         pairs = [
             (e * n_mp + m, (e ^ over_heads) * n_mp + (m ^ over_mp))
             for e in range(heads)
             for m in range(n_mp)
-            if e // n_blk in senders
         ]
         return lax.ppermute(x, AXES, pairs)
-
-    summary = (1,)
 
     def exchange(pieces):
         moved = [pieces[0]]
@@ -489,8 +486,8 @@
             moved.append(swap(pieces[k], k, 0))
         return moved
 
-    far_cot = swap(cotangent, 0, 2, summary)
-    near_cot = swap(cotangent, 0, 1, summary)
+    far_cot = swap(cotangent, 0, 2)
+    near_cot = swap(cotangent, 0, 1)
     tiles = group // LANES
     mixed = projections.reshape(width, 2, tiles, LANES).transpose(0, 2, 1, 3)
     mixed = mixed.reshape(width * 2 * tiles, LANES)
@@ -521,9 +518,9 @@
     )
     wp, ws = made[0], made[1 : 1 + n_mp]
     own, own_states, own_gain, spread, prim, sec = made[1 + n_mp :]
-    lent_3 = swap(ws[3], 0, 3, summary)
+    lent_3 = swap(ws[3], 0, 3)
     far_cot, spread = lax.optimization_barrier((far_cot, spread))
-    cross_cot = swap(far_cot, 0, 1, summary)
+    cross_cot = swap(far_cot, 0, 1)
     acc = call(
         part_kernel,
         (cotangent, near_cot, far_cot, *ws[:3]),
@@ -544,7 +541,7 @@
     )
     second, pieces = made[0], made[1:]
     pieces = exchange(pieces)
-    lent_2 = swap(ws[2], 0, 2, summary)
+    lent_2 = swap(ws[2], 0, 2)
     inverse, shrink = call(
         functools.partial(scales_kernel, width), (spread,), [INSIDE], [((rows, LANES), F32)] * 2
     )
@@ -569,7 +566,7 @@
         [((rows, group), BF16)] * 2,
         [pltpu.VMEM((heads, rows, LANES), BF16)],
     )
-    far_att = swap(ls, 0, 2, summary)
+    far_att = swap(ls, 0, 2)
     (sent,) = call(
         functools.partial(send_kernel, sizes),
         (lp, ls, prim, second, spread, wp, ws[3], ws[1]),
@@ -595,9 +592,9 @@
     far = swap(half, 0, 2)
     far_ends = swap(ends, 0, 2)
     own_att, lent_1, ends = lax.optimization_barrier((ls, ws[1], ends))
-    lent_1 = swap(lent_1, 0, 1, summary)
-    near_att = swap(own_att, 0, 1, summary)
-    cross_att = swap(far_att, 0, 1, summary)
+    lent_1 = swap(lent_1, 0, 1)
+    near_att = swap(own_att, 0, 1)
+    cross_att = swap(far_att, 0, 1)
     (out,) = call(
         layer_kernel,
         (ls, near_att, far_att, cross_att, ws[0], lent_1, lent_2, lent_3, own),

time: 143 us -> 133 us (0.930)
  the two profiles are of different devices: /device:TPU:3 before, /device:TPU:0 now
where the time goes in v5:
time: 133 us
  waiting for transfers between devices  76.8 us (58%)
  starting transfers between devices  34.3 us (26%)
  Pallas kernels  21 us (16%)
    ppermute x26, waiting for transfers between devices, swap(): return lax.ppermute(x, AXES, pairs)  76.8 us
    ppermute x26, starting transfers between devices, swap(): return lax.ppermute(x, AXES, pairs)  34.3 us
    pallas_call x11, Pallas kernels, call(): pl.pallas_call(body, in_specs=list(specs), out_specs=[INSIDE] * len(outs)...  21 us
  transfers between devices with their start and end apart: 26, of which 10 were waited for; matrix products, arithmetic and copies ran while one was open for 0% of the time, Pallas kernels for 9%

profile of v5, /device:TPU:0, one launch (start us, length us, event | category | flops | bytes accessed | tf_op | source)
XLA Modules:
  0.0 133.1 jit_solution(13336244988302825180)
XLA Ops:
  0.6 0.6 collective-permute-start
  1.2 2.6 %collective-permute-start.1 = (bf16[256,1024]{1,0:T(8,128)(2,1)}, bf16[256,1024]{1,0:T(8,128)(2,1)S(1)}, u32[]{:S(2)}, u32[]{:S(2)}) collective-permute-start(bf16[256,1024]{1,0:T(8,128)(2,1)} %c0.1), channel_id=1, source_target_pairs={{0,2},{1,3},{2,0},{3,1},{4,6},{5,7},{6,4},{7,5},{8,10},{9,11},{10,... | collective-permute-start | bytes 1572872 | tf_op jit(solution)/shard_map/ppermute | solution.py:481
  3.8 9.1 %shard_map.68 = (bf16[4,1024,512]{2,1,0:T(8,128)(2,1)S(1)}, bf16[1024,512]{1,0:T(8,128)(2,1)S(1)}, bf16[1024,512]{1,0:T(8,128)(2,1)S(1)}, bf16[1024,512]{1,0:T(8...) custom-call(bf16[256,4096]{1,0:T(8,128)(2,1)} %bitcast.13, ...), custom_call_target="tpu_custom_call" | custom-call | flops 8589934592 | bytes 1048576 | tf_op jit(solution)/shard_map/pallas_call | solution.py:440
  12.8 3.7 %collective-permute-done.1.c2 = bf16[256,1024]{1,0:T(8,128)(2,1)S(1)} collective-permute-done((bf16[256,1024]{1,0:T(8,128)(2,1)}, bf16[256,1024]{1,0:T(8,128)(2,1)S(1)}, u32[]{:S(2)}, u32[]{:S(2)}) %collective-permute-start.1) | collective-permute-done | bytes 524320 | tf_op jit(solution)/shard_map/ppermute | solution.py:481
  16.5 1.9 %collective-permute-done.2.c3 = bf16[256,1024]{1,0:T(8,128)(2,1)S(1)} collective-permute-done((bf16[256,1024]{1,0:T(8,128)(2,1)S(1)}, bf16[256,1024]{1,0:T(8,128)(2,1)S(1)}, u32[]{:S(2)}, u32[]{:S(2)}) %collective-permute-start.2) | collective-permute-done | bytes 524320 | tf_op jit(solution)/shard_map/ppermute | solution.py:481
  18.4 1.5 %shard_map.70 = (bf16[256,512]{1,0:T(8,128)(2,1)S(1)}, bf16[272,128]{1,0:T(8,128)(2,1)S(1)}, bf16[272,128]{1,0:T(8,128)(2,1)S(1)}, bf16[272,128]{1,0:T(8,128)(2,...) custom-call(s32[1,2]{1,0:T(1,128)S(1)} %bitcast.9, ...), custom_call_target="tpu_custom_call" | custom-call | flops 1073741824 | bytes 1048576 | tf_op jit(solution)/shard_map/pallas_call | solution.py:440
  19.9 1.9 %collective-permute-start.3 = (bf16[272,128]{1,0:T(8,128)(2,1)S(1)}, bf16[272,128]{1,0:T(8,128)(2,1)S(1)}, u32[]{:S(2)}, u32[]{:S(2)}) collective-permute-start(bf16[272,128]{1,0:T(8,128)(2,1)S(1)} %get-tuple-element.50), channel_id=1, source_target_pairs={{0,4},{1,5},{2,6},{3,7},{4,0},{5,1},{6,2},{7,3},{8,12},{9,13},{10,... | collective-permute-start | bytes 208904 | tf_op jit(solution)/shard_map/ppermute | solution.py:481
  21.8 2.6 %collective-permute-start.4 = (bf16[272,128]{1,0:T(8,128)(2,1)S(1)}, bf16[272,128]{1,0:T(8,128)(2,1)S(1)}, u32[]{:S(2)}, u32[]{:S(2)}) collective-permute-start(bf16[272,128]{1,0:T(8,128)(2,1)S(1)} %get-tuple-element.51), channel_id=1, source_target_pairs={{0,8},{1,9},{2,10},{3,11},{4,12},{5,13},{6,14},{7,15},{8,0},{9,1},... | collective-permute-start | bytes 208904 | tf_op jit(solution)/shard_map/ppermute | solution.py:481
  24.4 2.1 %collective-permute-start.6 = (bf16[272,128]{1,0:T(8,128)(2,1)S(1)}, bf16[272,128]{1,0:T(8,128)(2,1)S(1)}, u32[]{:S(2)}, u32[]{:S(2)}) collective-permute-start(bf16[272,128]{1,0:T(8,128)(2,1)S(1)} %get-tuple-element.53), channel_id=1, source_target_pairs={{0,16},{1,17},{2,18},{3,19},{4,20},{5,21},{6,22},{7,23},{8,24},{9,... | collective-permute-start | bytes 208904 | tf_op jit(solution)/shard_map/ppermute | solution.py:481
  26.7 4.8 %collective-permute-start.8 = (bf16[272,128]{1,0:T(8,128)(2,1)S(1)}, bf16[272,128]{1,0:T(8,128)(2,1)S(1)}, u32[]{:S(2)}, u32[]{:S(2)}) collective-permute-start(bf16[272,128]{1,0:T(8,128)(2,1)S(1)} %get-tuple-element.55), channel_id=1, source_target_pairs={{0,24},{1,25},{2,26},{3,27},{4,28},{5,29},{6,30},{7,31},{8,16},{9,... | collective-permute-start | bytes 208904 | tf_op jit(solution)/shard_map/ppermute | solution.py:481
  31.6 3.0 %collective-permute-start.9 = (bf16[272,128]{1,0:T(8,128)(2,1)S(1)}, bf16[272,128]{1,0:T(8,128)(2,1)S(1)}, u32[]{:S(2)}, u32[]{:S(2)}) collective-permute-start(bf16[272,128]{1,0:T(8,128)(2,1)S(1)} %get-tuple-element.56), channel_id=1, source_target_pairs={{0,28},{1,29},{2,30},{3,31},{4,24},{5,25},{6,26},{7,27},{8,20},{9,... | collective-permute-start | bytes 208904 | tf_op jit(solution)/shard_map/ppermute | solution.py:481
  34.6 2.3 %collective-permute-done.8.rest_6_ = bf16[272,128]{1,0:T(8,128)(2,1)S(1)} collective-permute-done((bf16[272,128]{1,0:T(8,128)(2,1)S(1)}, bf16[272,128]{1,0:T(8,128)(2,1)S(1)}, u32[]{:S(2)}, u32[]{:S(2)}) %collective-permute-start.8) | collective-permute-done | bytes 69664 | tf_op jit(solution)/shard_map/ppermute | solution.py:481
  36.9 1.7 %collective-permute-done.9.rest_7_ = bf16[272,128]{1,0:T(8,128)(2,1)S(1)} collective-permute-done((bf16[272,128]{1,0:T(8,128)(2,1)S(1)}, bf16[272,128]{1,0:T(8,128)(2,1)S(1)}, u32[]{:S(2)}, u32[]{:S(2)}) %collective-permute-start.9) | collective-permute-done | bytes 69664 | tf_op jit(solution)/shard_map/ppermute | solution.py:481
  38.6 3.4 %shard_map.71 = (bf16[256,128]{1,0:T(8,128)(2,1)S(1)}, bf16[256,128]{1,0:T(8,128)(2,1)S(1)}, bf16[256,128]{1,0:T(8,128)(2,1)S(1)}, bf16[256,128]{1,0:T(8,128)(2,...) custom-call(bf16[272,128]{1,0:T(8,128)(2,1)S(1)} %get-tuple-element., ...), custom_call_target="tpu_custom_call" | custom-call | flops 4294967296 | bytes 1048576 | tf_op jit(solution)/shard_map/pallas_call | solution.py:440
  42.1 2.1 %collective-permute-start.11 = (bf16[256,128]{1,0:T(8,128)(2,1)S(1)}, bf16[256,128]{1,0:T(8,128)(2,1)S(1)}, u32[]{:S(2)}, u32[]{:S(2)}) collective-permute-start(bf16[256,128]{1,0:T(8,128)(2,1)S(1)} %get-tuple-element.59), channel_id=1, source_target_pairs={{0,8},{1,9},{2,10},{3,11},{4,12},{5,13},{6,14},{7,15},{8,0},{9,1},... | collective-permute-start | bytes 196616 | tf_op jit(solution)/shard_map/ppermute | solution.py:481
  44.2 2.3 %collective-permute-start.12 = (bf16[256,128]{1,0:T(8,128)(2,1)S(1)}, bf16[256,128]{1,0:T(8,128)(2,1)S(1)}, u32[]{:S(2)}, u32[]{:S(2)}) collective-permute-start(bf16[256,128]{1,0:T(8,128)(2,1)S(1)} %get-tuple-element.60), channel_id=1, source_target_pairs={{0,12},{1,13},{2,14},{3,15},{4,8},{5,9},{6,10},{7,11},{8,4},{9,5},... | collective-permute-start | bytes 196616 | tf_op jit(solution)/shard_map/ppermute | solution.py:481
  46.5 0.5 collective-permute-start.14
  47.1 1.1 collective-permute-done.10.rest_1_
  48.2 3.3 %collective-permute-start.15 = (bf16[256,128]{1,0:T(8,128)(2,1)S(1)}, bf16[256,128]{1,0:T(8,128)(2,1)S(1)}, u32[]{:S(2)}, u32[]{:S(2)}) collective-permute-start(bf16[256,128]{1,0:T(8,128)(2,1)S(1)} %get-tuple-element.63), channel_id=1, source_target_pairs={{0,24},{1,25},{2,26},{3,27},{4,28},{5,29},{6,30},{7,31},{8,16},{9,... | collective-permute-start | bytes 196616 | tf_op jit(solution)/shard_map/ppermute | solution.py:481
  51.5 1.7 %collective-permute-start.16 = (bf16[256,128]{1,0:T(8,128)(2,1)S(1)}, bf16[256,128]{1,0:T(8,128)(2,1)S(1)}, u32[]{:S(2)}, u32[]{:S(2)}) collective-permute-start(bf16[256,128]{1,0:T(8,128)(2,1)S(1)} %get-tuple-element.64), channel_id=1, source_target_pairs={{0,28},{1,29},{2,30},{3,31},{4,24},{5,25},{6,26},{7,27},{8,20},{9,... | collective-permute-start | bytes 196616 | tf_op jit(solution)/shard_map/ppermute | solution.py:481
  53.2 1.0 collective-permute-done.15.rest_6_
  54.2 4.2 %collective-permute-done.16.rest_7_ = bf16[256,128]{1,0:T(8,128)(2,1)S(1)} collective-permute-done((bf16[256,128]{1,0:T(8,128)(2,1)S(1)}, bf16[256,128]{1,0:T(8,128)(2,1)S(1)}, u32[]{:S(2)}, u32[]{:S(2)}) %collective-permute-start.16) | collective-permute-done | bytes 65568 | tf_op jit(solution)/shard_map/ppermute | solution.py:481
  58.5 0.8 shard_map.72
  59.3 2.3 %shard_map.74.sent = bf16[2,272,1024]{2,1,0:T(8,128)(2,1)S(1)} custom-call(bf16[256,512]{1,0:T(8,128)(2,1)S(1)} %get-tuple-element.66.lp, bf16[256,512]{1,0:T(8,128)(2,1)S(1)} %get-tuple-element.71.ls.a0, bf16[256,512]{1,0:T(8,128)(2,1)S(1)} %get-tuple-element.41.prim, bf16[256,512]{1,0:T(8,128)(2,1)S(1)} %get-tuple-element.68.second, ...), custom_call_target="tpu_custom_call" | custom-call | flops 2147483648 | bytes 1048576 | tf_op jit(solution)/shard_map/pallas_call | solution.py:440
  61.6 1.6 %collective-permute-start.22 = (bf16[1024,512]{1,0:T(8,128)(2,1)S(1)}, bf16[1024,512]{1,0:T(8,128)(2,1)S(1)}, u32[]{:S(2)}, u32[]{:S(2)}) collective-permute-start(bf16[1024,512]{1,0:T(8,128)(2,1)S(1)} %get-tuple-element.47.w2), channel_id=1, source_target_pairs={{0,2},{1,3},{2,0},{3,1},{4,6},{5,7},{6,4},{7,5},{8,10},{9,11},{10,... | collective-permute-start | bytes 3145736 | tf_op jit(solution)/shard_map/ppermute | solution.py:481
  63.5 1.7 %shard_map.73.kept = bf16[2,256,1024]{2,1,0:T(8,128)(2,1)S(1)} custom-call(bf16[256,512]{1,0:T(8,128)(2,1)S(1)} %get-tuple-element.66.lp, bf16[256,512]{1,0:T(8,128)(2,1)S(1)} %get-tuple-element.71.ls.a0, bf16[4,1024,512]{2,1,0:T(8,128)(2,1)S(1)} %get-tuple-element.67.wp, bf16[1024,512]{1,0:T(8,128)(2,1)S(1)} %get-tuple-element.47.w2, ...), custom_call_target="tpu_custom_call" | custom-call | flops 2147483648 | bytes 1048576 | tf_op jit(solution)/shard_map/pallas_call | solution.py:440
  65.8 1.5 %collective-permute-start.25 = (bf16[256,1024]{1,0:T(8,128)(2,1)S(1)}, bf16[256,1024]{1,0:T(8,128)(2,1)S(1)}, u32[]{:S(2)}, u32[]{:S(2)}) collective-permute-start(bf16[256,1024]{1,0:T(8,128)(2,1)S(1)} %get-tuple-element.75), channel_id=1, source_target_pairs={{0,2},{1,3},{2,0},{3,1},{4,6},{5,7},{6,4},{7,5},{8,10},{9,11},{10,... | collective-permute-start | bytes 1572872 | tf_op jit(solution)/shard_map/ppermute | solution.py:481
  67.8 58.7 %collective-permute-done.19.a2 = bf16[256,512]{1,0:T(8,128)(2,1)S(1)} collective-permute-done((bf16[256,512]{1,0:T(8,128)(2,1)S(1)}, bf16[256,512]{1,0:T(8,128)(2,1)S(1)}, u32[]{:S(2)}, u32[]{:S(2)}) %collective-permute-start.19) | collective-permute-done | bytes 262176 | tf_op jit(solution)/shard_map/ppermute | solution.py:481
  126.5 1.5 %collective-permute-start.24 = (f32[8,256]{1,0:T(8,128)S(1)}, f32[8,256]{1,0:T(8,128)S(1)}, u32[]{:S(2)}, u32[]{:S(2)}) collective-permute-start(f32[8,256]{1,0:T(8,128)S(1)} %get-tuple-element.74.ends), channel_id=1, source_target_pairs={{0,2},{1,3},{2,0},{3,1},{4,6},{5,7},{6,4},{7,5},{8,10},{9,11},{10,... | collective-permute-start | bytes 24584 | tf_op jit(solution)/shard_map/ppermute | solution.py:481
  128.0 2.1 %collective-permute-done.24.far_ends = f32[8,256]{1,0:T(8,128)S(1)} collective-permute-done((f32[8,256]{1,0:T(8,128)S(1)}, f32[8,256]{1,0:T(8,128)S(1)}, u32[]{:S(2)}, u32[]{:S(2)}) %collective-permute-start.24) | collective-permute-done | bytes 8224 | tf_op jit(solution)/shard_map/ppermute | solution.py:481
  130.7 1.2 shard_map.78
  132.1 0.8 shard_map.76
  (35 shorter events, 2.5 us)
Async XLA Ops:
  0.6 15.9 %collective-permute-start = (bf16[256,1024]{1,0:T(8,128)(2,1)}, bf16[256,1024]{1,0:T(8,128)(2,1)S(1)}, u32[]{:S(2)}, u32[]{:S(2)}) collective-permute-start(bf16[256,1024]{1,0:T(8,128)(2,1)} %c0.1), channel_id=1, source_target_pairs={{0,1},{1,0},{2,3},{3,2},{4,5},{5,4},{6,7},{7,6},{8,9},{9,8},{10,11... | collective-permute-start | bytes 1572872 | tf_op jit(solution)/shard_map/ppermute | solution.py:481
  1.2 15.3 %collective-permute-start.1 = (bf16[256,1024]{1,0:T(8,128)(2,1)}, bf16[256,1024]{1,0:T(8,128)(2,1)S(1)}, u32[]{:S(2)}, u32[]{:S(2)}) collective-permute-start(bf16[256,1024]{1,0:T(8,128)(2,1)} %c0.1), channel_id=1, source_target_pairs={{0,2},{1,3},{2,0},{3,1},{4,6},{5,7},{6,4},{7,5},{8,10},{9,11},{10,... | collective-permute-start | bytes 1572872 | tf_op jit(solution)/shard_map/ppermute | solution.py:481
  3.8 12.7 %copy-start = (bf16[256,1024]{1,0:T(8,128)(2,1)S(1)}, bf16[256,1024]{1,0:T(8,128)(2,1)}, u32[]{:S(2)}) copy-start(bf16[256,1024]{1,0:T(8,128)(2,1)} %c0.1) | copy-start | bytes 1572868
  16.5 1.9 %collective-permute-start.2 = (bf16[256,1024]{1,0:T(8,128)(2,1)S(1)}, bf16[256,1024]{1,0:T(8,128)(2,1)S(1)}, u32[]{:S(2)}, u32[]{:S(2)}) collective-permute-start(bf16[256,1024]{1,0:T(8,128)(2,1)S(1)} %collective-permute-done.1.c2), channel_id=1, source_target_pairs={{0,1},{1,0},{2,3},{3,2},{4,5},{5,4},{6,7},{7,6},{8,9},{9,8},{10,11... | collective-permute-start | bytes 1572872 | tf_op jit(solution)/shard_map/ppermute | solution.py:481
  16.5 1.9 %copy-start.1 = (s32[2,1]{0,1:T(1,128)S(1)}, s32[2,1]{0,1:T(1,128)}, u32[]{:S(2)}) copy-start(s32[2,1]{0,1:T(1,128)} %param.8) | copy-start | bytes 28
  19.9 6.8 %collective-permute-start.3 = (bf16[272,128]{1,0:T(8,128)(2,1)S(1)}, bf16[272,128]{1,0:T(8,128)(2,1)S(1)}, u32[]{:S(2)}, u32[]{:S(2)}) collective-permute-start(bf16[272,128]{1,0:T(8,128)(2,1)S(1)} %get-tuple-element.50), channel_id=1, source_target_pairs={{0,4},{1,5},{2,6},{3,7},{4,0},{5,1},{6,2},{7,3},{8,12},{9,13},{10,... | collective-permute-start | bytes 208904 | tf_op jit(solution)/shard_map/ppermute | solution.py:481
  21.8 9.8 %collective-permute-start.4 = (bf16[272,128]{1,0:T(8,128)(2,1)S(1)}, bf16[272,128]{1,0:T(8,128)(2,1)S(1)}, u32[]{:S(2)}, u32[]{:S(2)}) collective-permute-start(bf16[272,128]{1,0:T(8,128)(2,1)S(1)} %get-tuple-element.51), channel_id=1, source_target_pairs={{0,8},{1,9},{2,10},{3,11},{4,12},{5,13},{6,14},{7,15},{8,0},{9,1},... | collective-permute-start | bytes 208904 | tf_op jit(solution)/shard_map/ppermute | solution.py:481
  24.4 10.2 %collective-permute-start.5 = (bf16[272,128]{1,0:T(8,128)(2,1)S(1)}, bf16[272,128]{1,0:T(8,128)(2,1)S(1)}, u32[]{:S(2)}, u32[]{:S(2)}) collective-permute-start(bf16[272,128]{1,0:T(8,128)(2,1)S(1)} %get-tuple-element.52), channel_id=1, source_target_pairs={{0,12},{1,13},{2,14},{3,15},{4,8},{5,9},{6,10},{7,11},{8,4},{9,5},... | collective-permute-start | bytes 208904 | tf_op jit(solution)/shard_map/ppermute | solution.py:481
  24.4 10.2 %collective-permute-start.6 = (bf16[272,128]{1,0:T(8,128)(2,1)S(1)}, bf16[272,128]{1,0:T(8,128)(2,1)S(1)}, u32[]{:S(2)}, u32[]{:S(2)}) collective-permute-start(bf16[272,128]{1,0:T(8,128)(2,1)S(1)} %get-tuple-element.53), channel_id=1, source_target_pairs={{0,16},{1,17},{2,18},{3,19},{4,20},{5,21},{6,22},{7,23},{8,24},{9,... | collective-permute-start | bytes 208904 | tf_op jit(solution)/shard_map/ppermute | solution.py:481
  26.5 8.1 %collective-permute-start.7 = (bf16[272,128]{1,0:T(8,128)(2,1)S(1)}, bf16[272,128]{1,0:T(8,128)(2,1)S(1)}, u32[]{:S(2)}, u32[]{:S(2)}) collective-permute-start(bf16[272,128]{1,0:T(8,128)(2,1)S(1)} %get-tuple-element.54), channel_id=1, source_target_pairs={{0,20},{1,21},{2,22},{3,23},{4,16},{5,17},{6,18},{7,19},{8,28},{9,... | collective-permute-start | bytes 208904 | tf_op jit(solution)/shard_map/ppermute | solution.py:481
  26.7 10.1 %collective-permute-start.8 = (bf16[272,128]{1,0:T(8,128)(2,1)S(1)}, bf16[272,128]{1,0:T(8,128)(2,1)S(1)}, u32[]{:S(2)}, u32[]{:S(2)}) collective-permute-start(bf16[272,128]{1,0:T(8,128)(2,1)S(1)} %get-tuple-element.55), channel_id=1, source_target_pairs={{0,24},{1,25},{2,26},{3,27},{4,28},{5,29},{6,30},{7,31},{8,16},{9,... | collective-permute-start | bytes 208904 | tf_op jit(solution)/shard_map/ppermute | solution.py:481
  31.6 7.0 %collective-permute-start.9 = (bf16[272,128]{1,0:T(8,128)(2,1)S(1)}, bf16[272,128]{1,0:T(8,128)(2,1)S(1)}, u32[]{:S(2)}, u32[]{:S(2)}) collective-permute-start(bf16[272,128]{1,0:T(8,128)(2,1)S(1)} %get-tuple-element.56), channel_id=1, source_target_pairs={{0,28},{1,29},{2,30},{3,31},{4,24},{5,25},{6,26},{7,27},{8,20},{9,... | collective-permute-start | bytes 208904 | tf_op jit(solution)/shard_map/ppermute | solution.py:481
  42.0 6.2 %collective-permute-start.10 = (bf16[256,128]{1,0:T(8,128)(2,1)S(1)}, bf16[256,128]{1,0:T(8,128)(2,1)S(1)}, u32[]{:S(2)}, u32[]{:S(2)}) collective-permute-start(bf16[256,128]{1,0:T(8,128)(2,1)S(1)} %get-tuple-element.58), channel_id=1, source_target_pairs={{0,4},{1,5},{2,6},{3,7},{4,0},{5,1},{6,2},{7,3},{8,12},{9,13},{10,... | collective-permute-start | bytes 196616 | tf_op jit(solution)/shard_map/ppermute | solution.py:481
  42.1 9.4 %collective-permute-start.11 = (bf16[256,128]{1,0:T(8,128)(2,1)S(1)}, bf16[256,128]{1,0:T(8,128)(2,1)S(1)}, u32[]{:S(2)}, u32[]{:S(2)}) collective-permute-start(bf16[256,128]{1,0:T(8,128)(2,1)S(1)} %get-tuple-element.59), channel_id=1, source_target_pairs={{0,8},{1,9},{2,10},{3,11},{4,12},{5,13},{6,14},{7,15},{8,0},{9,1},... | collective-permute-start | bytes 196616 | tf_op jit(solution)/shard_map/ppermute | solution.py:481
  44.2 9.0 %collective-permute-start.12 = (bf16[256,128]{1,0:T(8,128)(2,1)S(1)}, bf16[256,128]{1,0:T(8,128)(2,1)S(1)}, u32[]{:S(2)}, u32[]{:S(2)}) collective-permute-start(bf16[256,128]{1,0:T(8,128)(2,1)S(1)} %get-tuple-element.60), channel_id=1, source_target_pairs={{0,12},{1,13},{2,14},{3,15},{4,8},{5,9},{6,10},{7,11},{8,4},{9,5},... | collective-permute-start | bytes 196616 | tf_op jit(solution)/shard_map/ppermute | solution.py:481
  46.4 6.8 %collective-permute-start.13 = (bf16[256,128]{1,0:T(8,128)(2,1)S(1)}, bf16[256,128]{1,0:T(8,128)(2,1)S(1)}, u32[]{:S(2)}, u32[]{:S(2)}) collective-permute-start(bf16[256,128]{1,0:T(8,128)(2,1)S(1)} %get-tuple-element.61), channel_id=1, source_target_pairs={{0,16},{1,17},{2,18},{3,19},{4,20},{5,21},{6,22},{7,23},{8,24},{9,... | collective-permute-start | bytes 196616 | tf_op jit(solution)/shard_map/ppermute | solution.py:481
  46.5 6.7 %collective-permute-start.14 = (bf16[256,128]{1,0:T(8,128)(2,1)S(1)}, bf16[256,128]{1,0:T(8,128)(2,1)S(1)}, u32[]{:S(2)}, u32[]{:S(2)}) collective-permute-start(bf16[256,128]{1,0:T(8,128)(2,1)S(1)} %get-tuple-element.62), channel_id=1, source_target_pairs={{0,20},{1,21},{2,22},{3,23},{4,16},{5,17},{6,18},{7,19},{8,28},{9,... | collective-permute-start | bytes 196616 | tf_op jit(solution)/shard_map/ppermute | solution.py:481
  48.2 6.1 %collective-permute-start.15 = (bf16[256,128]{1,0:T(8,128)(2,1)S(1)}, bf16[256,128]{1,0:T(8,128)(2,1)S(1)}, u32[]{:S(2)}, u32[]{:S(2)}) collective-permute-start(bf16[256,128]{1,0:T(8,128)(2,1)S(1)} %get-tuple-element.63), channel_id=1, source_target_pairs={{0,24},{1,25},{2,26},{3,27},{4,28},{5,29},{6,30},{7,31},{8,16},{9,... | collective-permute-start | bytes 196616 | tf_op jit(solution)/shard_map/ppermute | solution.py:481
  51.5 7.0 %collective-permute-start.16 = (bf16[256,128]{1,0:T(8,128)(2,1)S(1)}, bf16[256,128]{1,0:T(8,128)(2,1)S(1)}, u32[]{:S(2)}, u32[]{:S(2)}) collective-permute-start(bf16[256,128]{1,0:T(8,128)(2,1)S(1)} %get-tuple-element.64), channel_id=1, source_target_pairs={{0,28},{1,29},{2,30},{3,31},{4,24},{5,25},{6,26},{7,27},{8,20},{9,... | collective-permute-start | bytes 196616 | tf_op jit(solution)/shard_map/ppermute | solution.py:481
  61.5 3.7 %collective-permute-start.17 = (bf16[2,272,1024]{2,1,0:T(8,128)(2,1)S(1)}, bf16[2,272,1024]{2,1,0:T(8,128)(2,1)S(1)}, u32[]{:S(2)}, u32[]{:S(2)}) collective-permute-start(bf16[2,272,1024]{2,1,0:T(8,128)(2,1)S(1)} %shard_map.74.sent), channel_id=1, source_target_pairs={{0,1},{1,0},{2,3},{3,2},{4,5},{5,4},{6,7},{7,6},{8,9},{9,8},{10,11... | collective-permute-start | bytes 3342344 | tf_op jit(solution)/shard_map/ppermute | solution.py:481
  61.6 70.3 %collective-permute-start.22 = (bf16[1024,512]{1,0:T(8,128)(2,1)S(1)}, bf16[1024,512]{1,0:T(8,128)(2,1)S(1)}, u32[]{:S(2)}, u32[]{:S(2)}) collective-permute-start(bf16[1024,512]{1,0:T(8,128)(2,1)S(1)} %get-tuple-element.47.w2), channel_id=1, source_target_pairs={{0,2},{1,3},{2,0},{3,1},{4,6},{5,7},{6,4},{7,5},{8,10},{9,11},{10,... | collective-permute-start | bytes 3145736 | tf_op jit(solution)/shard_map/ppermute | solution.py:481
  63.2 68.7 %collective-permute-start.23 = (bf16[1024,512]{1,0:T(8,128)(2,1)S(1)}, bf16[1024,512]{1,0:T(8,128)(2,1)S(1)}, u32[]{:S(2)}, u32[]{:S(2)}) collective-permute-start(bf16[1024,512]{1,0:T(8,128)(2,1)S(1)} %get-tuple-element.48.w3), channel_id=1, source_target_pairs={{0,3},{1,2},{2,1},{3,0},{4,7},{5,6},{6,5},{7,4},{8,11},{9,10},{10,... | collective-permute-start | bytes 3145736 | tf_op jit(solution)/shard_map/ppermute | solution.py:481
  65.3 66.7 %collective-permute-start.21 = (bf16[1024,512]{1,0:T(8,128)(2,1)S(1)}, bf16[1024,512]{1,0:T(8,128)(2,1)S(1)}, u32[]{:S(2)}, u32[]{:S(2)}) collective-permute-start(bf16[1024,512]{1,0:T(8,128)(2,1)S(1)} %get-tuple-element.72.w1), channel_id=1, source_target_pairs={{0,1},{1,0},{2,3},{3,2},{4,5},{5,4},{6,7},{7,6},{8,9},{9,8},{10,11... | collective-permute-start | bytes 3145736 | tf_op jit(solution)/shard_map/ppermute | solution.py:481
  65.8 64.4 %collective-permute-start.25 = (bf16[256,1024]{1,0:T(8,128)(2,1)S(1)}, bf16[256,1024]{1,0:T(8,128)(2,1)S(1)}, u32[]{:S(2)}, u32[]{:S(2)}) collective-permute-start(bf16[256,1024]{1,0:T(8,128)(2,1)S(1)} %get-tuple-element.75), channel_id=1, source_target_pairs={{0,2},{1,3},{2,0},{3,1},{4,6},{5,7},{6,4},{7,5},{8,10},{9,11},{10,... | collective-permute-start | bytes 1572872 | tf_op jit(solution)/shard_map/ppermute | solution.py:481
  67.3 59.2 %collective-permute-start.19 = (bf16[256,512]{1,0:T(8,128)(2,1)S(1)}, bf16[256,512]{1,0:T(8,128)(2,1)S(1)}, u32[]{:S(2)}, u32[]{:S(2)}) collective-permute-start(bf16[256,512]{1,0:T(8,128)(2,1)S(1)} %get-tuple-element.71.ls.a0), channel_id=1, source_target_pairs={{0,2},{1,3},{2,0},{3,1},{4,6},{5,7},{6,4},{7,5},{8,10},{9,11},{10,... | collective-permute-start | bytes 786440 | tf_op jit(solution)/shard_map/ppermute | solution.py:481
  126.5 3.7 %collective-permute-start.24 = (f32[8,256]{1,0:T(8,128)S(1)}, f32[8,256]{1,0:T(8,128)S(1)}, u32[]{:S(2)}, u32[]{:S(2)}) collective-permute-start(f32[8,256]{1,0:T(8,128)S(1)} %get-tuple-element.74.ends), channel_id=1, source_target_pairs={{0,2},{1,3},{2,0},{3,1},{4,6},{5,7},{6,4},{7,5},{8,10},{9,11},{10,... | collective-permute-start | bytes 24584 | tf_op jit(solution)/shard_map/ppermute | solution.py:481
  130.1 1.8 %collective-permute-start.20 = (bf16[256,512]{1,0:T(8,128)(2,1)S(1)}, bf16[256,512]{1,0:T(8,128)(2,1)S(1)}, u32[]{:S(2)}, u32[]{:S(2)}) collective-permute-start(bf16[256,512]{1,0:T(8,128)(2,1)S(1)} %collective-permute-done.19.a2), channel_id=1, source_target_pairs={{0,1},{1,0},{2,3},{3,2},{4,5},{5,4},{6,7},{7,6},{8,9},{9,8},{10,11... | collective-permute-start | bytes 786440 | tf_op jit(solution)/shard_map/ppermute | solution.py:481
  130.2 1.9 %collective-permute-start.18 = (bf16[256,512]{1,0:T(8,128)(2,1)S(1)}, bf16[256,512]{1,0:T(8,128)(2,1)S(1)}, u32[]{:S(2)}, u32[]{:S(2)}) collective-permute-start(bf16[256,512]{1,0:T(8,128)(2,1)S(1)} %get-tuple-element.71.ls.a0), channel_id=1, source_target_pairs={{0,1},{1,0},{2,3},{3,2},{4,5},{5,4},{6,7},{7,6},{8,9},{9,8},{10,11... | collective-permute-start | bytes 786440 | tf_op jit(solution)/shard_map/ppermute | solution.py:481

commit v6 on v5

--- a/solution.py
+++ b/solution.py
@@ -249,6 +249,14 @@
     own_gain[...] = gbuf[:, mine]
 
 
+def lend_kernel(w2, middle, edge):
+    parity = lax.rem(lax.axis_index("blk"), 2)
+    depth, quarter = w2.shape[0], edge.shape[0]
+    middle[...] = w2[quarter : depth - quarter, :]
+    start = pl.multiple_of(parity * (depth - quarter), quarter)
+    edge[...] = w2[pl.ds(start, quarter), :]
+
+
 def part_kernel(c0, c1, c2, w0, w1, w2, acc):
     @pl.when(lax.axis_index("segment") == 1)
     def _():
@@ -259,7 +267,7 @@
 
 def pack_kernel(sizes, counts, prim, sec, acc, c3, w3, *rest):
     heads = sizes[0] * sizes[1]
-    second, outs = rest[0], rest[1:]
+    second, outs, (parts,) = rest[0], rest[1 : 1 + heads], rest[1 + heads :]
     seg, entry, _ = place(sizes)
     rows = prim.shape[0]
 
@@ -276,13 +284,10 @@
     tail = jnp.full((TAIL, LANES), 1.0, F32) * counts[0, 0].astype(F32)
     for head in range(heads):
         cols = slice(head * DH, (head + 1) * DH)
-        pair = jnp.concatenate([prim[:, cols], second[:, cols]], axis=1)
-        for k, out in enumerate(outs):
-
-            @pl.when(jnp.bitwise_xor(entry, k) == head)
-            def _():
-                out[:rows, :] = pair
-                out[rows:, :] = tail.astype(BF16)
+        parts[head] = jnp.concatenate([prim[:, cols], second[:, cols]], axis=1)
+    for k, out in enumerate(outs):
+        out[:rows, :] = parts[jnp.bitwise_xor(entry, k)]
+        out[rows:, :] = tail.astype(BF16)
 
 
 def live_keys(piece, rows):
@@ -348,19 +353,22 @@
     return jnp.where(line == 0, high, row - high).astype(BF16)
 
 
-def regroup_kernel(sizes, counts, *rest):
+def regroup(sizes, ins, parts):
     heads = sizes[0] * sizes[1]
-    ins, (lp, ls, parts) = rest[:heads], rest[heads:]
-    seg, entry, _ = place(sizes)
-    rows = lp.shape[0]
+    _, entry, _ = place(sizes)
     for k, piece in enumerate(ins):
         parts[jnp.bitwise_xor(entry, k)] = piece[...]
-    low = lax.broadcasted_iota(jnp.int32, (rows, LANES), 0)
-    alive = low < jnp.where(seg == 0, rows, counts[0, 1])
     for head in range(0, heads, 2):
-        cols = slice(head * DH, (head + 2) * DH)
-        one, two = parts[head], parts[head + 1]
-        lp[:, cols] = jnp.concatenate([one[:, :DH], two[:, :DH]], axis=1)
+        yield slice(head * DH, (head + 2) * DH), parts[head], parts[head + 1]
+
+
+def attended_kernel(sizes, counts, *rest):
+    heads = sizes[0] * sizes[1]
+    ins, (ls, parts) = rest[:heads], rest[heads:]
+    rows = ls.shape[0]
+    line = lax.broadcasted_iota(jnp.int32, (rows, LANES), 0)
+    alive = line < jnp.where(lax.axis_index("segment") == 0, rows, counts[0, 1])
+    for cols, one, two in regroup(sizes, ins, parts):
         both = jnp.concatenate([one[:, DH:], two[:, DH:]], axis=1)
         ls[:, cols] = jnp.where(alive, both.astype(F32), 0.0).astype(BF16)
 
@@ -378,7 +386,11 @@
         out[slot, :rows, :] = right_product(lp[...], wp).astype(BF16)
 
 
-def send_kernel(sizes, lp, ls, prim, second, spread, wp, w3, w1, sent):
+def send_kernel(sizes, ls, prim, second, spread, wp, w3, w1, *rest):
+    heads = sizes[0] * sizes[1]
+    ins, (sent, lp, parts) = rest[:heads], rest[heads:]
+    for cols, one, two in regroup(sizes, ins, parts):
+        lp[:, cols] = jnp.concatenate([one[:, :DH], two[:, :DH]], axis=1)
     seg, _, _ = place(sizes)
     rows, feats = prim.shape[0], sent.shape[2]
     project_block(seg, wp[3], w3[...], lp, ls, sent, 0)
@@ -398,7 +410,7 @@
     project_block(seg, wp[0], w0[...], lp, ls, kept, 1)
 
 
-def layer_kernel(a0, a1, a2, a3, w0, w1, w2, w3, own, out, obuf, sem):
+def layer_kernel(a0, a1, a2, a3, w0, w1, middle, edge, mirrored, w3, own, out, obuf, w2, sem):
     seg = lax.axis_index("segment")
 
     @pl.when(seg == 0)
@@ -407,6 +419,12 @@
 
     @pl.when(seg == 1)
     def _():
+        parity = lax.rem(lax.axis_index("blk"), 2)
+        depth, quarter = w2.shape[0], edge.shape[0]
+        for lent, side in ((edge, parity), (mirrored, 1 - parity)):
+            start = pl.multiple_of(side * (depth - quarter), quarter)
+            w2[pl.ds(start, quarter), :] = lent[...]
+        w2[quarter : depth - quarter, :] = middle[...]
         total = right_product(a0[...], w0[...])
         for a, w in ((a1, w1), (a2, w2), (a3, w3)):
             total += right_product(a[...], w[...])
@@ -518,6 +536,13 @@
     )
     wp, ws = made[0], made[1 : 1 + n_mp]
     own, own_states, own_gain, spread, prim, sec = made[1 + n_mp :]
+    quarter = feats // 4
+    middle, edge = call(
+        lend_kernel,
+        (ws[2],),
+        [INSIDE],
+        [((feats - 2 * quarter, group), BF16), ((quarter, group), BF16)],
+    )
     lent_3 = swap(ws[3], 0, 3)
     far_cot, spread = lax.optimization_barrier((far_cot, spread))
     cross_cot = swap(far_cot, 0, 1)
@@ -535,13 +560,14 @@
         (counts, prim, sec, acc, cross_cot, ws[3]),
         [SCALARS] + [INSIDE] * 5,
         [((rows, group), BF16)] + [((rows + TAIL, LANES), BF16)] * heads,
-        (),
+        [pltpu.VMEM((heads, rows, LANES), BF16)],
         16,
         1 << 30,
     )
     second, pieces = made[0], made[1:]
     pieces = exchange(pieces)
-    lent_2 = swap(ws[2], 0, 2)
+    lent_2 = swap(middle, 0, 2)
+    lent_edge = swap(edge, 0, 2)
     inverse, shrink = call(
         functools.partial(scales_kernel, width), (spread,), [INSIDE], [((rows, LANES), F32)] * 2
     )
@@ -559,24 +585,25 @@
         4 << 30,
     )
     pieces = exchange(pieces)
-    lp, ls = call(
-        functools.partial(regroup_kernel, sizes),
+    (ls,) = call(
+        functools.partial(attended_kernel, sizes),
         (counts, *pieces),
         [SCALARS] + [INSIDE] * heads,
-        [((rows, group), BF16)] * 2,
+        [((rows, group), BF16)],
         [pltpu.VMEM((heads, rows, LANES), BF16)],
     )
     far_att = swap(ls, 0, 2)
-    (sent,) = call(
+    sent, lp = call(
         functools.partial(send_kernel, sizes),
-        (lp, ls, prim, second, spread, wp, ws[3], ws[1]),
-        [INSIDE] * 8,
-        [((2, rows + TAIL, feats), BF16)],
-        (),
+        (ls, prim, second, spread, wp, ws[3], ws[1], *pieces),
+        [INSIDE] * (7 + heads),
+        [((2, rows + TAIL, feats), BF16), ((rows, group), BF16)],
+        [pltpu.VMEM((heads, rows, LANES), BF16)],
         16,
         2 << 30,
     )
     got = swap(sent, 0, 1)
+    mirrored = swap(lent_edge, 1, 0)
     (kept,) = call(
         functools.partial(keep_kernel, sizes),
         (lp, ls, wp, ws[2], ws[0]),
@@ -597,10 +624,17 @@
     cross_att = swap(far_att, 0, 1)
     (out,) = call(
         layer_kernel,
-        (ls, near_att, far_att, cross_att, ws[0], lent_1, lent_2, lent_3, own),
-        [INSIDE] * 9,
+        (
+            *(ls, near_att, far_att, cross_att),
+            *(ws[0], lent_1, lent_2, lent_edge, mirrored, lent_3, own),
+        ),
+        [INSIDE] * 11,
         [((rows, feats), BF16)],
-        [pltpu.VMEM((rows, feats), BF16), pltpu.SemaphoreType.DMA],
+        [
+            pltpu.VMEM((rows, feats), BF16),
+            pltpu.VMEM((feats, group), BF16),
+            pltpu.SemaphoreType.DMA,
+        ],
         16,
         2 << 30,
         [ANYWHERE],
@@ -618,7 +652,7 @@
 def solution(mesh):
     sizes = tuple(mesh.shape[axis] for axis in AXES)
     n_seg, n_blk, n_mp = sizes
-    by_heads = n_seg == 2 and n_blk <= WIN and n_blk & (n_blk - 1) == 0 and n_mp == 4
+    by_heads = n_seg == 2 and n_blk <= WIN and n_blk & (n_blk - 1) == 0 and n_blk > 1 and n_mp == 4
 
     def body(segment_in, norm_gains, projections, live_counts, cotangent):
         rows, group = segment_in.shape[1], projections.shape[3]

time: 133 us -> 129 us (0.970)
  waiting for transfers between devices: 76.8 us -> 72.3 us
    ppermute x26 -> x28, waiting for transfers between devices: 76.8 us -> 72.3 us  [swap(): return lax.ppermute(x, AXES, pairs)]
    ppermute x26 -> x28, starting transfers between devices: 34.3 us -> 35.3 us  [swap(): return lax.ppermute(x, AXES, pairs)]
    pallas_call x11 -> x12, Pallas kernels: 21 us -> 20.4 us  [call(): pl.pallas_call(body, in_specs=list(specs), out_specs=[INSIDE] * len(outs)...]
  transfers between devices with their start and end apart: 26 -> 28, of which waited for: 10 -> 11; matrix products, arithmetic and copies ran while one was open for 0% -> 0% of each run, Pallas kernels for 9% -> 10%
where the time goes in v6:
time: 129 us
  waiting for transfers between devices  72.3 us (56%)
  starting transfers between devices  35.3 us (27%)
  Pallas kernels  20.4 us (16%)
    ppermute x28, waiting for transfers between devices, swap(): return lax.ppermute(x, AXES, pairs)  72.3 us
    ppermute x28, starting transfers between devices, swap(): return lax.ppermute(x, AXES, pairs)  35.3 us
    pallas_call x12, Pallas kernels, call(): pl.pallas_call(body, in_specs=list(specs), out_specs=[INSIDE] * len(outs)...  20.4 us
  transfers between devices with their start and end apart: 28, of which 11 were waited for; matrix products, arithmetic and copies ran while one was open for 0% of the time, Pallas kernels for 10%

profile of v6, /device:TPU:0, one launch (start us, length us, event | category | flops | bytes accessed | tf_op | source)
XLA Modules:
  0.0 129.0 jit_solution(13770948646283106673)
XLA Ops:
  1.2 2.6 %collective-permute-start.1 = (bf16[256,1024]{1,0:T(8,128)(2,1)}, bf16[256,1024]{1,0:T(8,128)(2,1)S(1)}, u32[]{:S(2)}, u32[]{:S(2)}) collective-permute-start(bf16[256,1024]{1,0:T(8,128)(2,1)} %c0.1), channel_id=1, source_target_pairs={{0,2},{1,3},{2,0},{3,1},{4,6},{5,7},{6,4},{7,5},{8,10},{9,11},{10,... | collective-permute-start | bytes 1572872 | tf_op jit(solution)/shard_map/ppermute | solution.py:499
  3.8 9.1 %shard_map.68 = (bf16[4,1024,512]{2,1,0:T(8,128)(2,1)S(1)}, bf16[1024,512]{1,0:T(8,128)(2,1)S(1)}, bf16[1024,512]{1,0:T(8,128)(2,1)S(1)}, bf16[1024,512]{1,0:T(8...) custom-call(bf16[256,4096]{1,0:T(8,128)(2,1)} %bitcast.13, ...), custom_call_target="tpu_custom_call" | custom-call | flops 8589934592 | bytes 1048576 | tf_op jit(solution)/shard_map/pallas_call | solution.py:458
  12.9 3.6 %collective-permute-done.1.c2 = bf16[256,1024]{1,0:T(8,128)(2,1)S(1)} collective-permute-done((bf16[256,1024]{1,0:T(8,128)(2,1)}, bf16[256,1024]{1,0:T(8,128)(2,1)S(1)}, u32[]{:S(2)}, u32[]{:S(2)}) %collective-permute-start.1) | collective-permute-done | bytes 524320 | tf_op jit(solution)/shard_map/ppermute | solution.py:499
  16.5 1.9 %collective-permute-done.2.c3 = bf16[256,1024]{1,0:T(8,128)(2,1)S(1)} collective-permute-done((bf16[256,1024]{1,0:T(8,128)(2,1)S(1)}, bf16[256,1024]{1,0:T(8,128)(2,1)S(1)}, u32[]{:S(2)}, u32[]{:S(2)}) %collective-permute-start.2) | collective-permute-done | bytes 524320 | tf_op jit(solution)/shard_map/ppermute | solution.py:499
  18.4 0.8 shard_map.70
  19.2 1.9 %collective-permute-start.3 = (bf16[272,128]{1,0:T(8,128)(2,1)S(1)}, bf16[272,128]{1,0:T(8,128)(2,1)S(1)}, u32[]{:S(2)}, u32[]{:S(2)}) collective-permute-start(bf16[272,128]{1,0:T(8,128)(2,1)S(1)} %get-tuple-element.52), channel_id=1, source_target_pairs={{0,4},{1,5},{2,6},{3,7},{4,0},{5,1},{6,2},{7,3},{8,12},{9,13},{10,... | collective-permute-start | bytes 208904 | tf_op jit(solution)/shard_map/ppermute | solution.py:499
  21.1 2.6 %collective-permute-start.4 = (bf16[272,128]{1,0:T(8,128)(2,1)S(1)}, bf16[272,128]{1,0:T(8,128)(2,1)S(1)}, u32[]{:S(2)}, u32[]{:S(2)}) collective-permute-start(bf16[272,128]{1,0:T(8,128)(2,1)S(1)} %get-tuple-element.53), channel_id=1, source_target_pairs={{0,8},{1,9},{2,10},{3,11},{4,12},{5,13},{6,14},{7,15},{8,0},{9,1},... | collective-permute-start | bytes 208904 | tf_op jit(solution)/shard_map/ppermute | solution.py:499
  23.7 2.1 %collective-permute-start.6 = (bf16[272,128]{1,0:T(8,128)(2,1)S(1)}, bf16[272,128]{1,0:T(8,128)(2,1)S(1)}, u32[]{:S(2)}, u32[]{:S(2)}) collective-permute-start(bf16[272,128]{1,0:T(8,128)(2,1)S(1)} %get-tuple-element.55), channel_id=1, source_target_pairs={{0,16},{1,17},{2,18},{3,19},{4,20},{5,21},{6,22},{7,23},{8,24},{9,... | collective-permute-start | bytes 208904 | tf_op jit(solution)/shard_map/ppermute | solution.py:499
  26.0 4.8 %collective-permute-start.8 = (bf16[272,128]{1,0:T(8,128)(2,1)S(1)}, bf16[272,128]{1,0:T(8,128)(2,1)S(1)}, u32[]{:S(2)}, u32[]{:S(2)}) collective-permute-start(bf16[272,128]{1,0:T(8,128)(2,1)S(1)} %get-tuple-element.57), channel_id=1, source_target_pairs={{0,24},{1,25},{2,26},{3,27},{4,28},{5,29},{6,30},{7,31},{8,16},{9,... | collective-permute-start | bytes 208904 | tf_op jit(solution)/shard_map/ppermute | solution.py:499
  30.9 3.0 %collective-permute-start.9 = (bf16[272,128]{1,0:T(8,128)(2,1)S(1)}, bf16[272,128]{1,0:T(8,128)(2,1)S(1)}, u32[]{:S(2)}, u32[]{:S(2)}) collective-permute-start(bf16[272,128]{1,0:T(8,128)(2,1)S(1)} %get-tuple-element.58), channel_id=1, source_target_pairs={{0,28},{1,29},{2,30},{3,31},{4,24},{5,25},{6,26},{7,27},{8,20},{9,... | collective-permute-start | bytes 208904 | tf_op jit(solution)/shard_map/ppermute | solution.py:499
  33.9 2.3 %collective-permute-done.8.rest_6_ = bf16[272,128]{1,0:T(8,128)(2,1)S(1)} collective-permute-done((bf16[272,128]{1,0:T(8,128)(2,1)S(1)}, bf16[272,128]{1,0:T(8,128)(2,1)S(1)}, u32[]{:S(2)}, u32[]{:S(2)}) %collective-permute-start.8) | collective-permute-done | bytes 69664 | tf_op jit(solution)/shard_map/ppermute | solution.py:499
  36.2 1.7 %collective-permute-done.9.rest_7_ = bf16[272,128]{1,0:T(8,128)(2,1)S(1)} collective-permute-done((bf16[272,128]{1,0:T(8,128)(2,1)S(1)}, bf16[272,128]{1,0:T(8,128)(2,1)S(1)}, u32[]{:S(2)}, u32[]{:S(2)}) %collective-permute-start.9) | collective-permute-done | bytes 69664 | tf_op jit(solution)/shard_map/ppermute | solution.py:499
  37.9 3.4 %shard_map.71 = (bf16[256,128]{1,0:T(8,128)(2,1)S(1)}, bf16[256,128]{1,0:T(8,128)(2,1)S(1)}, bf16[256,128]{1,0:T(8,128)(2,1)S(1)}, bf16[256,128]{1,0:T(8,128)(2,...) custom-call(bf16[272,128]{1,0:T(8,128)(2,1)S(1)} %get-tuple-element., ...), custom_call_target="tpu_custom_call" | custom-call | flops 4294967296 | bytes 1048576 | tf_op jit(solution)/shard_map/pallas_call | solution.py:458
  41.4 2.1 %collective-permute-start.11 = (bf16[256,128]{1,0:T(8,128)(2,1)S(1)}, bf16[256,128]{1,0:T(8,128)(2,1)S(1)}, u32[]{:S(2)}, u32[]{:S(2)}) collective-permute-start(bf16[256,128]{1,0:T(8,128)(2,1)S(1)} %get-tuple-element.61), channel_id=1, source_target_pairs={{0,8},{1,9},{2,10},{3,11},{4,12},{5,13},{6,14},{7,15},{8,0},{9,1},... | collective-permute-start | bytes 196616 | tf_op jit(solution)/shard_map/ppermute | solution.py:499
  43.5 2.3 %collective-permute-start.12 = (bf16[256,128]{1,0:T(8,128)(2,1)S(1)}, bf16[256,128]{1,0:T(8,128)(2,1)S(1)}, u32[]{:S(2)}, u32[]{:S(2)}) collective-permute-start(bf16[256,128]{1,0:T(8,128)(2,1)S(1)} %get-tuple-element.62), channel_id=1, source_target_pairs={{0,12},{1,13},{2,14},{3,15},{4,8},{5,9},{6,10},{7,11},{8,4},{9,5},... | collective-permute-start | bytes 196616 | tf_op jit(solution)/shard_map/ppermute | solution.py:499
  46.4 1.1 collective-permute-done.10.rest_1_
  47.5 3.3 %collective-permute-start.15 = (bf16[256,128]{1,0:T(8,128)(2,1)S(1)}, bf16[256,128]{1,0:T(8,128)(2,1)S(1)}, u32[]{:S(2)}, u32[]{:S(2)}) collective-permute-start(bf16[256,128]{1,0:T(8,128)(2,1)S(1)} %get-tuple-element.65), channel_id=1, source_target_pairs={{0,24},{1,25},{2,26},{3,27},{4,28},{5,29},{6,30},{7,31},{8,16},{9,... | collective-permute-start | bytes 196616 | tf_op jit(solution)/shard_map/ppermute | solution.py:499
  50.8 1.7 %collective-permute-start.16 = (bf16[256,128]{1,0:T(8,128)(2,1)S(1)}, bf16[256,128]{1,0:T(8,128)(2,1)S(1)}, u32[]{:S(2)}, u32[]{:S(2)}) collective-permute-start(bf16[256,128]{1,0:T(8,128)(2,1)S(1)} %get-tuple-element.66), channel_id=1, source_target_pairs={{0,28},{1,29},{2,30},{3,31},{4,24},{5,25},{6,26},{7,27},{8,20},{9,... | collective-permute-start | bytes 196616 | tf_op jit(solution)/shard_map/ppermute | solution.py:499
  52.5 1.0 collective-permute-done.15.rest_6_
  53.5 4.2 %collective-permute-done.16.rest_7_ = bf16[256,128]{1,0:T(8,128)(2,1)S(1)} collective-permute-done((bf16[256,128]{1,0:T(8,128)(2,1)S(1)}, bf16[256,128]{1,0:T(8,128)(2,1)S(1)}, u32[]{:S(2)}, u32[]{:S(2)}) %collective-permute-start.16) | collective-permute-done | bytes 65568 | tf_op jit(solution)/shard_map/ppermute | solution.py:499
  58.5 2.4 %shard_map.73 = (bf16[2,272,1024]{2,1,0:T(8,128)(2,1)S(1)}, bf16[256,512]{1,0:T(8,128)(2,1)S(1)}) custom-call(bf16[256,512]{1,0:T(8,128)(2,1)S(1)} %shard_map.72.ls.a0, bf16[256,512]{1,0:T(8,128)(2,1)S(1)} %get-tuple-element.43.prim, bf16[256,512]{1,0:T(8,128)(2,1)S(1)} %get-tuple-element.67.second, f32[256,128]{1,0:T(8,128)S(1)} %get-tuple-element.68.spread, ...), custom_call_target="tpu_custom_call" | custom-call | flops 2147483648 | bytes 1048576 | tf_op jit(solution)/shard_map/pallas_call | solution.py:458
  61.0 1.6 %collective-permute-start.25 = (bf16[1024,512]{1,0:T(8,128)(2,1)S(1)}, bf16[1024,512]{1,0:T(8,128)(2,1)S(1)}, u32[]{:S(2)}, u32[]{:S(2)}) collective-permute-start(bf16[1024,512]{1,0:T(8,128)(2,1)S(1)} %get-tuple-element.50.w3), channel_id=1, source_target_pairs={{0,3},{1,2},{2,1},{3,0},{4,7},{5,6},{6,5},{7,4},{8,11},{9,10},{10,... | collective-permute-start | bytes 3145736 | tf_op jit(solution)/shard_map/ppermute | solution.py:499
  62.6 1.7 %shard_map.74.kept = bf16[2,256,1024]{2,1,0:T(8,128)(2,1)S(1)} custom-call(bf16[256,512]{1,0:T(8,128)(2,1)S(1)} %get-tuple-element.70.lp, bf16[256,512]{1,0:T(8,128)(2,1)S(1)} %shard_map.72.ls.a0, bf16[4,1024,512]{2,1,0:T(8,128)(2,1)S(1)} %get-tuple-element.69.wp, bf16[1024,512]{1,0:T(8,128)(2,1)S(1)} %get-tuple-element.49.w2, ...), custom_call_target="tpu_custom_call" | custom-call | flops 2147483648 | bytes 1048576 | tf_op jit(solution)/shard_map/pallas_call | solution.py:458
  64.7 1.0 collective-permute-start.22
  65.7 1.1 collective-permute-start.23
  66.8 0.9 collective-permute-start.27
  67.7 36.3 %collective-permute-done.23.edge = bf16[256,512]{1,0:T(8,128)(2,1)S(1)} collective-permute-done((bf16[256,512]{1,0:T(8,128)(2,1)S(1)}, bf16[256,512]{1,0:T(8,128)(2,1)S(1)}, u32[]{:S(2)}, u32[]{:S(2)}) %collective-permute-start.23) | collective-permute-done | bytes 262176 | tf_op jit(solution)/shard_map/ppermute | solution.py:499
  104.0 1.5 %collective-permute-start.19 = (bf16[256,512]{1,0:T(8,128)(2,1)S(1)}, bf16[256,512]{1,0:T(8,128)(2,1)S(1)}, u32[]{:S(2)}, u32[]{:S(2)}) collective-permute-start(bf16[256,512]{1,0:T(8,128)(2,1)S(1)} %shard_map.72.ls.a0), channel_id=1, source_target_pairs={{0,2},{1,3},{2,0},{3,1},{4,6},{5,7},{6,4},{7,5},{8,10},{9,11},{10,... | collective-permute-start | bytes 786440 | tf_op jit(solution)/shard_map/ppermute | solution.py:499
  106.0 14.3 %collective-permute-done.19.a2 = bf16[256,512]{1,0:T(8,128)(2,1)S(1)} collective-permute-done((bf16[256,512]{1,0:T(8,128)(2,1)S(1)}, bf16[256,512]{1,0:T(8,128)(2,1)S(1)}, u32[]{:S(2)}, u32[]{:S(2)}) %collective-permute-start.19) | collective-permute-done | bytes 262176 | tf_op jit(solution)/shard_map/ppermute | solution.py:499
  120.9 1.2 shard_map.79
  122.2 5.8 %collective-permute-done.24.mirrored = bf16[256,512]{1,0:T(8,128)(2,1)S(1)} collective-permute-done((bf16[256,512]{1,0:T(8,128)(2,1)S(1)}, bf16[256,512]{1,0:T(8,128)(2,1)S(1)}, u32[]{:S(2)}, u32[]{:S(2)}) %collective-permute-start.24) | collective-permute-done | bytes 262176 | tf_op jit(solution)/shard_map/ppermute | solution.py:499
  127.9 0.9 shard_map.77
  (40 shorter events, 3.8 us)
Async XLA Ops:
  0.6 15.9 %collective-permute-start = (bf16[256,1024]{1,0:T(8,128)(2,1)}, bf16[256,1024]{1,0:T(8,128)(2,1)S(1)}, u32[]{:S(2)}, u32[]{:S(2)}) collective-permute-start(bf16[256,1024]{1,0:T(8,128)(2,1)} %c0.1), channel_id=1, source_target_pairs={{0,1},{1,0},{2,3},{3,2},{4,5},{5,4},{6,7},{7,6},{8,9},{9,8},{10,11... | collective-permute-start | bytes 1572872 | tf_op jit(solution)/shard_map/ppermute | solution.py:499
  1.2 15.3 %collective-permute-start.1 = (bf16[256,1024]{1,0:T(8,128)(2,1)}, bf16[256,1024]{1,0:T(8,128)(2,1)S(1)}, u32[]{:S(2)}, u32[]{:S(2)}) collective-permute-start(bf16[256,1024]{1,0:T(8,128)(2,1)} %c0.1), channel_id=1, source_target_pairs={{0,2},{1,3},{2,0},{3,1},{4,6},{5,7},{6,4},{7,5},{8,10},{9,11},{10,... | collective-permute-start | bytes 1572872 | tf_op jit(solution)/shard_map/ppermute | solution.py:499
  3.8 12.7 %copy-start = (bf16[256,1024]{1,0:T(8,128)(2,1)S(1)}, bf16[256,1024]{1,0:T(8,128)(2,1)}, u32[]{:S(2)}) copy-start(bf16[256,1024]{1,0:T(8,128)(2,1)} %c0.1) | copy-start | bytes 1572868
  16.5 1.9 %collective-permute-start.2 = (bf16[256,1024]{1,0:T(8,128)(2,1)S(1)}, bf16[256,1024]{1,0:T(8,128)(2,1)S(1)}, u32[]{:S(2)}, u32[]{:S(2)}) collective-permute-start(bf16[256,1024]{1,0:T(8,128)(2,1)S(1)} %collective-permute-done.1.c2), channel_id=1, source_target_pairs={{0,1},{1,0},{2,3},{3,2},{4,5},{5,4},{6,7},{7,6},{8,9},{9,8},{10,11... | collective-permute-start | bytes 1572872 | tf_op jit(solution)/shard_map/ppermute | solution.py:499
  16.5 1.9 %copy-start.1 = (s32[2,1]{0,1:T(1,128)S(1)}, s32[2,1]{0,1:T(1,128)}, u32[]{:S(2)}) copy-start(s32[2,1]{0,1:T(1,128)} %param.8) | copy-start | bytes 28
  19.2 6.8 %collective-permute-start.3 = (bf16[272,128]{1,0:T(8,128)(2,1)S(1)}, bf16[272,128]{1,0:T(8,128)(2,1)S(1)}, u32[]{:S(2)}, u32[]{:S(2)}) collective-permute-start(bf16[272,128]{1,0:T(8,128)(2,1)S(1)} %get-tuple-element.52), channel_id=1, source_target_pairs={{0,4},{1,5},{2,6},{3,7},{4,0},{5,1},{6,2},{7,3},{8,12},{9,13},{10,... | collective-permute-start | bytes 208904 | tf_op jit(solution)/shard_map/ppermute | solution.py:499
  21.1 9.8 %collective-permute-start.4 = (bf16[272,128]{1,0:T(8,128)(2,1)S(1)}, bf16[272,128]{1,0:T(8,128)(2,1)S(1)}, u32[]{:S(2)}, u32[]{:S(2)}) collective-permute-start(bf16[272,128]{1,0:T(8,128)(2,1)S(1)} %get-tuple-element.53), channel_id=1, source_target_pairs={{0,8},{1,9},{2,10},{3,11},{4,12},{5,13},{6,14},{7,15},{8,0},{9,1},... | collective-permute-start | bytes 208904 | tf_op jit(solution)/shard_map/ppermute | solution.py:499
  23.7 10.2 %collective-permute-start.5 = (bf16[272,128]{1,0:T(8,128)(2,1)S(1)}, bf16[272,128]{1,0:T(8,128)(2,1)S(1)}, u32[]{:S(2)}, u32[]{:S(2)}) collective-permute-start(bf16[272,128]{1,0:T(8,128)(2,1)S(1)} %get-tuple-element.54), channel_id=1, source_target_pairs={{0,12},{1,13},{2,14},{3,15},{4,8},{5,9},{6,10},{7,11},{8,4},{9,5},... | collective-permute-start | bytes 208904 | tf_op jit(solution)/shard_map/ppermute | solution.py:499
  23.7 10.2 %collective-permute-start.6 = (bf16[272,128]{1,0:T(8,128)(2,1)S(1)}, bf16[272,128]{1,0:T(8,128)(2,1)S(1)}, u32[]{:S(2)}, u32[]{:S(2)}) collective-permute-start(bf16[272,128]{1,0:T(8,128)(2,1)S(1)} %get-tuple-element.55), channel_id=1, source_target_pairs={{0,16},{1,17},{2,18},{3,19},{4,20},{5,21},{6,22},{7,23},{8,24},{9,... | collective-permute-start | bytes 208904 | tf_op jit(solution)/shard_map/ppermute | solution.py:499
  25.8 8.1 %collective-permute-start.7 = (bf16[272,128]{1,0:T(8,128)(2,1)S(1)}, bf16[272,128]{1,0:T(8,128)(2,1)S(1)}, u32[]{:S(2)}, u32[]{:S(2)}) collective-permute-start(bf16[272,128]{1,0:T(8,128)(2,1)S(1)} %get-tuple-element.56), channel_id=1, source_target_pairs={{0,20},{1,21},{2,22},{3,23},{4,16},{5,17},{6,18},{7,19},{8,28},{9,... | collective-permute-start | bytes 208904 | tf_op jit(solution)/shard_map/ppermute | solution.py:499
  26.0 10.1 %collective-permute-start.8 = (bf16[272,128]{1,0:T(8,128)(2,1)S(1)}, bf16[272,128]{1,0:T(8,128)(2,1)S(1)}, u32[]{:S(2)}, u32[]{:S(2)}) collective-permute-start(bf16[272,128]{1,0:T(8,128)(2,1)S(1)} %get-tuple-element.57), channel_id=1, source_target_pairs={{0,24},{1,25},{2,26},{3,27},{4,28},{5,29},{6,30},{7,31},{8,16},{9,... | collective-permute-start | bytes 208904 | tf_op jit(solution)/shard_map/ppermute | solution.py:499
  30.9 7.0 %collective-permute-start.9 = (bf16[272,128]{1,0:T(8,128)(2,1)S(1)}, bf16[272,128]{1,0:T(8,128)(2,1)S(1)}, u32[]{:S(2)}, u32[]{:S(2)}) collective-permute-start(bf16[272,128]{1,0:T(8,128)(2,1)S(1)} %get-tuple-element.58), channel_id=1, source_target_pairs={{0,28},{1,29},{2,30},{3,31},{4,24},{5,25},{6,26},{7,27},{8,20},{9,... | collective-permute-start | bytes 208904 | tf_op jit(solution)/shard_map/ppermute | solution.py:499
  41.3 6.2 %collective-permute-start.10 = (bf16[256,128]{1,0:T(8,128)(2,1)S(1)}, bf16[256,128]{1,0:T(8,128)(2,1)S(1)}, u32[]{:S(2)}, u32[]{:S(2)}) collective-permute-start(bf16[256,128]{1,0:T(8,128)(2,1)S(1)} %get-tuple-element.60), channel_id=1, source_target_pairs={{0,4},{1,5},{2,6},{3,7},{4,0},{5,1},{6,2},{7,3},{8,12},{9,13},{10,... | collective-permute-start | bytes 196616 | tf_op jit(solution)/shard_map/ppermute | solution.py:499
  41.4 9.4 %collective-permute-start.11 = (bf16[256,128]{1,0:T(8,128)(2,1)S(1)}, bf16[256,128]{1,0:T(8,128)(2,1)S(1)}, u32[]{:S(2)}, u32[]{:S(2)}) collective-permute-start(bf16[256,128]{1,0:T(8,128)(2,1)S(1)} %get-tuple-element.61), channel_id=1, source_target_pairs={{0,8},{1,9},{2,10},{3,11},{4,12},{5,13},{6,14},{7,15},{8,0},{9,1},... | collective-permute-start | bytes 196616 | tf_op jit(solution)/shard_map/ppermute | solution.py:499
  43.5 9.0 %collective-permute-start.12 = (bf16[256,128]{1,0:T(8,128)(2,1)S(1)}, bf16[256,128]{1,0:T(8,128)(2,1)S(1)}, u32[]{:S(2)}, u32[]{:S(2)}) collective-permute-start(bf16[256,128]{1,0:T(8,128)(2,1)S(1)} %get-tuple-element.62), channel_id=1, source_target_pairs={{0,12},{1,13},{2,14},{3,15},{4,8},{5,9},{6,10},{7,11},{8,4},{9,5},... | collective-permute-start | bytes 196616 | tf_op jit(solution)/shard_map/ppermute | solution.py:499
  45.7 6.8 %collective-permute-start.13 = (bf16[256,128]{1,0:T(8,128)(2,1)S(1)}, bf16[256,128]{1,0:T(8,128)(2,1)S(1)}, u32[]{:S(2)}, u32[]{:S(2)}) collective-permute-start(bf16[256,128]{1,0:T(8,128)(2,1)S(1)} %get-tuple-element.63), channel_id=1, source_target_pairs={{0,16},{1,17},{2,18},{3,19},{4,20},{5,21},{6,22},{7,23},{8,24},{9,... | collective-permute-start | bytes 196616 | tf_op jit(solution)/shard_map/ppermute | solution.py:499
  45.9 6.7 %collective-permute-start.14 = (bf16[256,128]{1,0:T(8,128)(2,1)S(1)}, bf16[256,128]{1,0:T(8,128)(2,1)S(1)}, u32[]{:S(2)}, u32[]{:S(2)}) collective-permute-start(bf16[256,128]{1,0:T(8,128)(2,1)S(1)} %get-tuple-element.64), channel_id=1, source_target_pairs={{0,20},{1,21},{2,22},{3,23},{4,16},{5,17},{6,18},{7,19},{8,28},{9,... | collective-permute-start | bytes 196616 | tf_op jit(solution)/shard_map/ppermute | solution.py:499
  47.5 6.1 %collective-permute-start.15 = (bf16[256,128]{1,0:T(8,128)(2,1)S(1)}, bf16[256,128]{1,0:T(8,128)(2,1)S(1)}, u32[]{:S(2)}, u32[]{:S(2)}) collective-permute-start(bf16[256,128]{1,0:T(8,128)(2,1)S(1)} %get-tuple-element.65), channel_id=1, source_target_pairs={{0,24},{1,25},{2,26},{3,27},{4,28},{5,29},{6,30},{7,31},{8,16},{9,... | collective-permute-start | bytes 196616 | tf_op jit(solution)/shard_map/ppermute | solution.py:499
  50.8 7.0 %collective-permute-start.16 = (bf16[256,128]{1,0:T(8,128)(2,1)S(1)}, bf16[256,128]{1,0:T(8,128)(2,1)S(1)}, u32[]{:S(2)}, u32[]{:S(2)}) collective-permute-start(bf16[256,128]{1,0:T(8,128)(2,1)S(1)} %get-tuple-element.66), channel_id=1, source_target_pairs={{0,28},{1,29},{2,30},{3,31},{4,24},{5,25},{6,26},{7,27},{8,20},{9,... | collective-permute-start | bytes 196616 | tf_op jit(solution)/shard_map/ppermute | solution.py:499
  60.9 3.4 %collective-permute-start.17 = (bf16[2,272,1024]{2,1,0:T(8,128)(2,1)S(1)}, bf16[2,272,1024]{2,1,0:T(8,128)(2,1)S(1)}, u32[]{:S(2)}, u32[]{:S(2)}) collective-permute-start(bf16[2,272,1024]{2,1,0:T(8,128)(2,1)S(1)} %get-tuple-element.71.sent), channel_id=1, source_target_pairs={{0,1},{1,0},{2,3},{3,2},{4,5},{5,4},{6,7},{7,6},{8,9},{9,8},{10,11... | collective-permute-start | bytes 3342344 | tf_op jit(solution)/shard_map/ppermute | solution.py:499
  61.0 66.9 %collective-permute-start.25 = (bf16[1024,512]{1,0:T(8,128)(2,1)S(1)}, bf16[1024,512]{1,0:T(8,128)(2,1)S(1)}, u32[]{:S(2)}, u32[]{:S(2)}) collective-permute-start(bf16[1024,512]{1,0:T(8,128)(2,1)S(1)} %get-tuple-element.50.w3), channel_id=1, source_target_pairs={{0,3},{1,2},{2,1},{3,0},{4,7},{5,6},{6,5},{7,4},{8,11},{9,10},{10,... | collective-permute-start | bytes 3145736 | tf_op jit(solution)/shard_map/ppermute | solution.py:499
  64.5 63.5 %collective-permute-start.21 = (bf16[1024,512]{1,0:T(8,128)(2,1)S(1)}, bf16[1024,512]{1,0:T(8,128)(2,1)S(1)}, u32[]{:S(2)}, u32[]{:S(2)}) collective-permute-start(bf16[1024,512]{1,0:T(8,128)(2,1)S(1)} %get-tuple-element.74.w1), channel_id=1, source_target_pairs={{0,1},{1,0},{2,3},{3,2},{4,5},{5,4},{6,7},{7,6},{8,9},{9,8},{10,11... | collective-permute-start | bytes 3145736 | tf_op jit(solution)/shard_map/ppermute | solution.py:499
  64.7 40.8 %collective-permute-start.22 = (bf16[512,512]{1,0:T(8,128)(2,1)S(1)}, bf16[512,512]{1,0:T(8,128)(2,1)S(1)}, u32[]{:S(2)}, u32[]{:S(2)}) collective-permute-start(bf16[512,512]{1,0:T(8,128)(2,1)S(1)} %get-tuple-element.75), channel_id=1, source_target_pairs={{0,2},{1,3},{2,0},{3,1},{4,6},{5,7},{6,4},{7,5},{8,10},{9,11},{10,... | collective-permute-start | bytes 1572872 | tf_op jit(solution)/shard_map/ppermute | solution.py:499
  65.7 38.3 %collective-permute-start.23 = (bf16[256,512]{1,0:T(8,128)(2,1)S(1)}, bf16[256,512]{1,0:T(8,128)(2,1)S(1)}, u32[]{:S(2)}, u32[]{:S(2)}) collective-permute-start(bf16[256,512]{1,0:T(8,128)(2,1)S(1)} %get-tuple-element.76), channel_id=1, source_target_pairs={{0,2},{1,3},{2,0},{3,1},{4,6},{5,7},{6,4},{7,5},{8,10},{9,11},{10,... | collective-permute-start | bytes 786440 | tf_op jit(solution)/shard_map/ppermute | solution.py:499
  66.8 53.6 %collective-permute-start.27 = (bf16[256,1024]{1,0:T(8,128)(2,1)S(1)}, bf16[256,1024]{1,0:T(8,128)(2,1)S(1)}, u32[]{:S(2)}, u32[]{:S(2)}) collective-permute-start(bf16[256,1024]{1,0:T(8,128)(2,1)S(1)} %get-tuple-element.79), channel_id=1, source_target_pairs={{0,2},{1,3},{2,0},{3,1},{4,6},{5,7},{6,4},{7,5},{8,10},{9,11},{10,... | collective-permute-start | bytes 1572872 | tf_op jit(solution)/shard_map/ppermute | solution.py:499
  104.0 16.3 %collective-permute-start.19 = (bf16[256,512]{1,0:T(8,128)(2,1)S(1)}, bf16[256,512]{1,0:T(8,128)(2,1)S(1)}, u32[]{:S(2)}, u32[]{:S(2)}) collective-permute-start(bf16[256,512]{1,0:T(8,128)(2,1)S(1)} %shard_map.72.ls.a0), channel_id=1, source_target_pairs={{0,2},{1,3},{2,0},{3,1},{4,6},{5,7},{6,4},{7,5},{8,10},{9,11},{10,... | collective-permute-start | bytes 786440 | tf_op jit(solution)/shard_map/ppermute | solution.py:499
  105.5 14.9 %collective-permute-start.26 = (f32[8,256]{1,0:T(8,128)S(1)}, f32[8,256]{1,0:T(8,128)S(1)}, u32[]{:S(2)}, u32[]{:S(2)}) collective-permute-start(f32[8,256]{1,0:T(8,128)S(1)} %get-tuple-element.78.ends), channel_id=1, source_target_pairs={{0,2},{1,3},{2,0},{3,1},{4,6},{5,7},{6,4},{7,5},{8,10},{9,11},{10,... | collective-permute-start | bytes 24584 | tf_op jit(solution)/shard_map/ppermute | solution.py:499
  120.3 7.6 %collective-permute-start.24 = (bf16[256,512]{1,0:T(8,128)(2,1)S(1)}, bf16[256,512]{1,0:T(8,128)(2,1)S(1)}, u32[]{:S(2)}, u32[]{:S(2)}) collective-permute-start(bf16[256,512]{1,0:T(8,128)(2,1)S(1)} %collective-permute-done.23.edge), channel_id=1, source_target_pairs={{0,4},{1,5},{2,6},{3,7},{4,0},{5,1},{6,2},{7,3},{8,12},{9,13},{10,... | collective-permute-start | bytes 786440 | tf_op jit(solution)/shard_map/ppermute | solution.py:499
  120.4 7.5 %collective-permute-start.20 = (bf16[256,512]{1,0:T(8,128)(2,1)S(1)}, bf16[256,512]{1,0:T(8,128)(2,1)S(1)}, u32[]{:S(2)}, u32[]{:S(2)}) collective-permute-start(bf16[256,512]{1,0:T(8,128)(2,1)S(1)} %collective-permute-done.19.a2), channel_id=1, source_target_pairs={{0,1},{1,0},{2,3},{3,2},{4,5},{5,4},{6,7},{7,6},{8,9},{9,8},{10,11... | collective-permute-start | bytes 786440 | tf_op jit(solution)/shard_map/ppermute | solution.py:499
  120.4 7.5 %collective-permute-start.18 = (bf16[256,512]{1,0:T(8,128)(2,1)S(1)}, bf16[256,512]{1,0:T(8,128)(2,1)S(1)}, u32[]{:S(2)}, u32[]{:S(2)}) collective-permute-start(bf16[256,512]{1,0:T(8,128)(2,1)S(1)} %shard_map.72.ls.a0), channel_id=1, source_target_pairs={{0,1},{1,0},{2,3},{3,2},{4,5},{5,4},{6,7},{7,6},{8,9},{9,8},{10,11... | collective-permute-start | bytes 786440 | tf_op jit(solution)/shard_map/ppermute | solution.py:499

commit v7 on v6

--- a/solution.py
+++ b/solution.py
@@ -167,11 +167,11 @@
     return seg, seg * sizes[1] + lax.axis_index("blk"), lax.axis_index("mp")
 
 
-def enter_kernel(sizes, states, gain, w, *rest):
+def enter_kernel(sizes, states, gain, w, counts, *rest):
     n_mp = sizes[2]
     wp, ws = rest[0], rest[1 : 1 + n_mp]
-    own, own_states, own_gain, spread, prim, sec = rest[1 + n_mp : 7 + n_mp]
-    xbuf, gbuf, wbuf, normed, sems, ready = rest[7 + n_mp :]
+    own, own_states, own_gain, spread, prim, sec, alive, tail = rest[1 + n_mp : 9 + n_mp]
+    xbuf, gbuf, wbuf, normed, sems, ready = rest[9 + n_mp :]
     seg, _, model = place(sizes)
     rows, width = xbuf.shape
     depth = width // n_mp
@@ -243,6 +243,15 @@
     def _():
         sec[...] = product(lambda c: ws[c][...])
 
+    @pl.when(seg == 1)
+    def _():
+        sec[...] = jnp.zeros_like(sec)
+
+    line = lax.broadcasted_iota(jnp.int32, alive.shape, 0)
+    last = jnp.where(seg == 0, rows, counts[0, 1])
+    alive[...] = jnp.where(line < last, 1.0, 0.0)
+    tail[...] = (jnp.full(tail.shape, 1.0, F32) * counts[0, 0].astype(F32)).astype(BF16)
+
     mine = pl.ds(pl.multiple_of(model * depth, depth), depth)
     own[...] = normed[:, mine]
     own_states[...] = xbuf[:, mine]
@@ -265,29 +274,51 @@
         acc[...] += jnp.dot(c2[...], w2[...], preferred_element_type=F32)
 
 
-def pack_kernel(sizes, counts, prim, sec, acc, c3, w3, *rest):
+def prepare_kernel(sizes, prim, sec, tail, *rest):
     heads = sizes[0] * sizes[1]
-    second, outs, (parts,) = rest[0], rest[1 : 1 + heads], rest[1 + heads :]
-    seg, entry, _ = place(sizes)
+    outs, (parts,) = rest[:heads], rest[heads:]
+    _, entry, _ = place(sizes)
     rows = prim.shape[0]
-
-    @pl.when(seg == 0)
-    def _():
-        second[...] = sec[...]
-
-    @pl.when(seg == 1)
-    def _():
-        total = acc[...] + jnp.dot(c3[...], w3[...], preferred_element_type=F32)
-        line = lax.broadcasted_iota(jnp.int32, acc.shape, 0)
-        second[...] = jnp.where(line < counts[0, 1], total, 0.0).astype(BF16)
-
-    tail = jnp.full((TAIL, LANES), 1.0, F32) * counts[0, 0].astype(F32)
     for head in range(heads):
         cols = slice(head * DH, (head + 1) * DH)
-        parts[head] = jnp.concatenate([prim[:, cols], second[:, cols]], axis=1)
+        parts[head] = jnp.concatenate([prim[:, cols], sec[:, cols]], axis=1)
     for k, out in enumerate(outs):
         out[:rows, :] = parts[jnp.bitwise_xor(entry, k)]
-        out[rows:, :] = tail.astype(BF16)
+        out[rows:, :] = tail[...]
+
+
+def pack_kernel(acc, alive, c3, w3, *halves):
+    @pl.when(lax.axis_index("segment") == 1)
+    def _():
+        total = acc[...] + jnp.dot(c3[...], w3[...], preferred_element_type=F32)
+        for tile in range(total.shape[1] // LANES):
+            part = total[:, tile * LANES : (tile + 1) * LANES]
+            part = jnp.where(alive[...] > 0.0, part, 0.0).astype(BF16)
+            width = halves[0].shape[1]
+            at = tile * LANES % width
+            halves[tile * LANES // width][:, at : at + LANES] = part
+
+
+def deal_kernel(sizes, here, turned, *rest):
+    blocks = sizes[1]
+    outs, (parts,) = rest[:blocks], rest[blocks:]
+    half_rows = here.shape[0] // 2
+
+    def split(source):
+        for head in range(blocks):
+            cols = slice(head * DH, (head + 1) * DH)
+            parts[head] = jnp.concatenate([source[:half_rows, cols], source[half_rows:, cols]], axis=1)
+
+    @pl.when(lax.axis_index("segment") == 0)
+    def _():
+        split(turned)
+
+    @pl.when(lax.axis_index("segment") == 1)
+    def _():
+        split(here)
+
+    for k, out in enumerate(outs):
+        out[...] = parts[jnp.bitwise_xor(lax.axis_index("blk"), k)]
 
 
 def live_keys(piece, rows):
@@ -299,19 +330,23 @@
 def attend_kernel(sizes, *rest):
     heads = sizes[0] * sizes[1]
     blocks = sizes[1]
-    ins, outs = rest[:heads], rest[heads : 2 * heads]
-    parts, back, totals = rest[2 * heads :]
+    ins, grads = rest[:heads], rest[heads : heads + blocks]
+    outs, (parts, slots, back, totals) = rest[heads + blocks : -4], rest[-4:]
     _, entry, _ = place(sizes)
     rows = outs[0].shape[0]
     for k, piece in enumerate(ins):
         parts[jnp.bitwise_xor(entry, k)] = piece[...]
+    for k, piece in enumerate(grads):
+        slots[jnp.bitwise_xor(lax.axis_index("blk"), k)] = piece[...]
     low = lax.broadcasted_iota(jnp.int32, (rows, LANES), 1) < DH
     zero = jnp.zeros((rows, LANES), BF16)
     live = [live_keys(parts[j], rows) for j in range(blocks)]
     for i in range(blocks):
         both = parts[blocks + i, :rows, :]
         query = jnp.where(low, both * BF16(SCALE), zero)
-        grad = jnp.where(low, zero, both)
+        half = slots[i]
+        turned = jnp.concatenate([half[:, DH:], half[:, :DH]], axis=1)
+        grad = jnp.where(low, zero, jnp.concatenate([turned, half], axis=0))
         flip_query = query.astype(F32).T.astype(BF16)
         flip_grad = grad.astype(F32).T.astype(BF16)
         scores = []
@@ -362,15 +397,12 @@
         yield slice(head * DH, (head + 2) * DH), parts[head], parts[head + 1]
 
 
-def attended_kernel(sizes, counts, *rest):
+def attended_kernel(sizes, alive, *rest):
     heads = sizes[0] * sizes[1]
     ins, (ls, parts) = rest[:heads], rest[heads:]
-    rows = ls.shape[0]
-    line = lax.broadcasted_iota(jnp.int32, (rows, LANES), 0)
-    alive = line < jnp.where(lax.axis_index("segment") == 0, rows, counts[0, 1])
     for cols, one, two in regroup(sizes, ins, parts):
         both = jnp.concatenate([one[:, DH:], two[:, DH:]], axis=1)
-        ls[:, cols] = jnp.where(alive, both.astype(F32), 0.0).astype(BF16)
+        ls[:, cols] = jnp.where(alive[...] > 0.0, both.astype(F32), 0.0).astype(BF16)
 
 
 def project_block(seg, wp, ws, lp, ls, out, slot):
@@ -498,9 +530,9 @@
         ]
         return lax.ppermute(x, AXES, pairs)
 
-    def exchange(pieces):
+    def exchange(pieces, among=heads):
         moved = [pieces[0]]
-        for k in range(1, heads):
+        for k in range(1, among):
             moved.append(swap(pieces[k], k, 0))
         return moved
 
@@ -511,8 +543,8 @@
     mixed = mixed.reshape(width * 2 * tiles, LANES)
     made = call(
         functools.partial(enter_kernel, sizes),
-        (states, norm_gains, mixed),
-        [ANYWHERE] * 3,
+        (states, norm_gains, mixed, counts),
+        [ANYWHERE] * 3 + [SCALARS],
         [((n_mp, feats, group), BF16)]
         + [((feats, group), BF16)] * n_mp
         + [
@@ -522,6 +554,8 @@
             ((rows, LANES), F32),
             ((rows, group), BF16),
             ((rows, group), BF16),
+            ((rows, LANES), F32),
+            ((TAIL, LANES), BF16),
         ],
         [
             pltpu.VMEM((rows, width), BF16),
@@ -535,7 +569,15 @@
         8 << 30,
     )
     wp, ws = made[0], made[1 : 1 + n_mp]
-    own, own_states, own_gain, spread, prim, sec = made[1 + n_mp :]
+    own, own_states, own_gain, spread, prim, sec, alive, tail = made[1 + n_mp :]
+    pieces = call(
+        functools.partial(prepare_kernel, sizes),
+        (prim, sec, tail),
+        [INSIDE] * 3,
+        [((rows + TAIL, LANES), BF16)] * heads,
+        [pltpu.VMEM((heads, rows, LANES), BF16)],
+    )
+    pieces = exchange(pieces)
     quarter = feats // 4
     middle, edge = call(
         lend_kernel,
@@ -555,17 +597,24 @@
         16,
         1 << 30,
     )[0]
-    made = call(
-        functools.partial(pack_kernel, sizes),
-        (counts, prim, sec, acc, cross_cot, ws[3]),
-        [SCALARS] + [INSIDE] * 5,
-        [((rows, group), BF16)] + [((rows + TAIL, LANES), BF16)] * heads,
-        [pltpu.VMEM((heads, rows, LANES), BF16)],
+    here, turning = call(
+        pack_kernel,
+        (acc, alive, cross_cot, ws[3]),
+        [INSIDE] * 4,
+        [((rows, group // n_seg), BF16)] * n_seg,
+        (),
         16,
         1 << 30,
-    )
-    second, pieces = made[0], made[1:]
-    pieces = exchange(pieces)
+    )[::-1]
+    turned = swap(turning, n_blk, 0)
+    grads = call(
+        functools.partial(deal_kernel, sizes),
+        (here, turned),
+        [INSIDE] * 2,
+        [((rows // 2, LANES), BF16)] * n_blk,
+        [pltpu.VMEM((n_blk, rows // 2, LANES), BF16)],
+    )
+    grads = exchange(grads, n_blk)
     lent_2 = swap(middle, 0, 2)
     lent_edge = swap(edge, 0, 2)
     inverse, shrink = call(
@@ -573,11 +622,12 @@
     )
     pieces = call(
         functools.partial(attend_kernel, sizes),
-        pieces,
-        [INSIDE] * heads,
+        (*pieces, *grads),
+        [INSIDE] * (heads + n_blk),
         [((rows, LANES), BF16)] * heads,
         [
             pltpu.VMEM((heads, rows + TAIL, LANES), BF16),
+            pltpu.VMEM((n_blk, rows // 2, LANES), BF16),
             pltpu.VMEM((heads, rows, LANES), BF16),
             pltpu.VMEM((n_blk, LANES, rows), F32),
         ],
@@ -587,15 +637,15 @@
     pieces = exchange(pieces)
     (ls,) = call(
         functools.partial(attended_kernel, sizes),
-        (counts, *pieces),
-        [SCALARS] + [INSIDE] * heads,
+        (alive, *pieces),
+        [INSIDE] * (1 + heads),
         [((rows, group), BF16)],
         [pltpu.VMEM((heads, rows, LANES), BF16)],
     )
     far_att = swap(ls, 0, 2)
     sent, lp = call(
         functools.partial(send_kernel, sizes),
-        (ls, prim, second, spread, wp, ws[3], ws[1], *pieces),
+        (ls, prim, sec, spread, wp, ws[3], ws[1], *pieces),
         [INSIDE] * (7 + heads),
         [((2, rows + TAIL, feats), BF16), ((rows, group), BF16)],
         [pltpu.VMEM((heads, rows, LANES), BF16)],

time: 129 us -> 133 us (1.031)
  starting transfers between devices: 35.3 us -> 38.3 us
    ppermute x28 -> x32, starting transfers between devices: 35.3 us -> 38.3 us  [swap(): return lax.ppermute(x, AXES, pairs)]
    pallas_call x12 -> x14, Pallas kernels: 20.4 us -> 20.3 us  [call(): pl.pallas_call(body, in_specs=list(specs), out_specs=[INSIDE] * len(outs)...]
    ppermute x28 -> x32, waiting for transfers between devices: 72.3 us -> 72.4 us  [swap(): return lax.ppermute(x, AXES, pairs)]
  transfers between devices with their start and end apart: 28 -> 32, of which waited for: 11 -> 14; matrix products, arithmetic and copies ran while one was open for 0% -> 0% of each run, Pallas kernels for 10% -> 10%
where the time goes in v7:
time: 133 us
  waiting for transfers between devices  72.4 us (54%)
  starting transfers between devices  38.3 us (29%)
  Pallas kernels  20.3 us (15%)
    ppermute x32, waiting for transfers between devices, swap(): return lax.ppermute(x, AXES, pairs)  72.4 us
    ppermute x32, starting transfers between devices, swap(): return lax.ppermute(x, AXES, pairs)  38.3 us
    pallas_call x14, Pallas kernels, call(): pl.pallas_call(body, in_specs=list(specs), out_specs=[INSIDE] * len(outs)...  20.3 us
  transfers between devices with their start and end apart: 32, of which 14 were waited for; matrix products, arithmetic and copies ran while one was open for 0% of the time, Pallas kernels for 10%

profile of v7, /device:TPU:0, one launch (start us, length us, event | category | flops | bytes accessed | tf_op | source)
XLA Modules:
  0.0 132.5 jit_solution(9645671439836888550)
XLA Ops:
  1.2 2.6 %collective-permute-start.8 = (bf16[256,1024]{1,0:T(8,128)(2,1)}, bf16[256,1024]{1,0:T(8,128)(2,1)S(1)}, u32[]{:S(2)}, u32[]{:S(2)}) collective-permute-start(bf16[256,1024]{1,0:T(8,128)(2,1)} %c0.1), channel_id=1, source_target_pairs={{0,2},{1,3},{2,0},{3,1},{4,6},{5,7},{6,4},{7,5},{8,10},{9,11},{10,... | collective-permute-start | bytes 1572872 | tf_op jit(solution)/shard_map/ppermute | solution.py:531
  4.4 9.9 %shard_map.68 = (bf16[4,1024,512]{2,1,0:T(8,128)(2,1)S(1)}, bf16[1024,512]{1,0:T(8,128)(2,1)S(1)}, bf16[1024,512]{1,0:T(8,128)(2,1)S(1)}, bf16[1024,512]{1,0:T(8...) custom-call(bf16[256,4096]{1,0:T(8,128)(2,1)} %bitcast.12, ...), custom_call_target="tpu_custom_call" | custom-call | flops 8589934592 | bytes 1048576 | tf_op jit(solution)/shard_map/pallas_call | solution.py:490
  14.3 2.2 %collective-permute-done.8.c2 = bf16[256,1024]{1,0:T(8,128)(2,1)S(1)} collective-permute-done((bf16[256,1024]{1,0:T(8,128)(2,1)}, bf16[256,1024]{1,0:T(8,128)(2,1)S(1)}, u32[]{:S(2)}, u32[]{:S(2)}) %collective-permute-start.8) | collective-permute-done | bytes 524320 | tf_op jit(solution)/shard_map/ppermute | solution.py:531
  16.5 1.9 %collective-permute-done.9.c3 = bf16[256,1024]{1,0:T(8,128)(2,1)S(1)} collective-permute-done((bf16[256,1024]{1,0:T(8,128)(2,1)S(1)}, bf16[256,1024]{1,0:T(8,128)(2,1)S(1)}, u32[]{:S(2)}, u32[]{:S(2)}) %collective-permute-start.9) | collective-permute-done | bytes 524320 | tf_op jit(solution)/shard_map/ppermute | solution.py:531
  18.4 2.2 %collective-permute-start.10 = (bf16[256,256]{1,0:T(8,128)(2,1)S(1)}, bf16[256,256]{1,0:T(8,128)(2,1)S(1)}, u32[]{:S(2)}, u32[]{:S(2)}) collective-permute-start(bf16[256,256]{1,0:T(8,128)(2,1)S(1)} %get-tuple-element.69), channel_id=1, source_target_pairs={{0,16},{1,17},{2,18},{3,19},{4,20},{5,21},{6,22},{7,23},{8,24},{9,... | collective-permute-start | bytes 393224 | tf_op jit(solution)/shard_map/ppermute | solution.py:531
  20.9 1.6 %collective-permute-start = (bf16[272,128]{1,0:T(8,128)(2,1)S(1)}, bf16[272,128]{1,0:T(8,128)(2,1)S(1)}, u32[]{:S(2)}, u32[]{:S(2)}) collective-permute-start(bf16[272,128]{1,0:T(8,128)(2,1)S(1)} %get-tuple-element.55), channel_id=1, source_target_pairs={{0,4},{1,5},{2,6},{3,7},{4,0},{5,1},{6,2},{7,3},{8,12},{9,13},{10,... | collective-permute-start | bytes 208904 | tf_op jit(solution)/shard_map/ppermute | solution.py:531
  22.5 2.6 %collective-permute-start.1 = (bf16[272,128]{1,0:T(8,128)(2,1)S(1)}, bf16[272,128]{1,0:T(8,128)(2,1)S(1)}, u32[]{:S(2)}, u32[]{:S(2)}) collective-permute-start(bf16[272,128]{1,0:T(8,128)(2,1)S(1)} %get-tuple-element.56), channel_id=1, source_target_pairs={{0,8},{1,9},{2,10},{3,11},{4,12},{5,13},{6,14},{7,15},{8,0},{9,1},... | collective-permute-start | bytes 208904 | tf_op jit(solution)/shard_map/ppermute | solution.py:531
  25.4 2.1 %collective-permute-start.4 = (bf16[272,128]{1,0:T(8,128)(2,1)S(1)}, bf16[272,128]{1,0:T(8,128)(2,1)S(1)}, u32[]{:S(2)}, u32[]{:S(2)}) collective-permute-start(bf16[272,128]{1,0:T(8,128)(2,1)S(1)} %get-tuple-element.59), channel_id=1, source_target_pairs={{0,20},{1,21},{2,22},{3,23},{4,16},{5,17},{6,18},{7,19},{8,28},{9,... | collective-permute-start | bytes 208904 | tf_op jit(solution)/shard_map/ppermute | solution.py:531
  27.5 2.6 %collective-permute-done.1.rest_2_ = bf16[272,128]{1,0:T(8,128)(2,1)S(1)} collective-permute-done((bf16[272,128]{1,0:T(8,128)(2,1)S(1)}, bf16[272,128]{1,0:T(8,128)(2,1)S(1)}, u32[]{:S(2)}, u32[]{:S(2)}) %collective-permute-start.1) | collective-permute-done | bytes 69664 | tf_op jit(solution)/shard_map/ppermute | solution.py:531
  30.1 1.0 collective-permute-start.5
  31.0 3.2 %collective-permute-start.6 = (bf16[272,128]{1,0:T(8,128)(2,1)S(1)}, bf16[272,128]{1,0:T(8,128)(2,1)S(1)}, u32[]{:S(2)}, u32[]{:S(2)}) collective-permute-start(bf16[272,128]{1,0:T(8,128)(2,1)S(1)} %get-tuple-element.61), channel_id=1, source_target_pairs={{0,28},{1,29},{2,30},{3,31},{4,24},{5,25},{6,26},{7,27},{8,20},{9,... | collective-permute-start | bytes 208904 | tf_op jit(solution)/shard_map/ppermute | solution.py:531
  34.7 2.3 %collective-permute-start.12 = (bf16[128,128]{1,0:T(8,128)(2,1)S(1)}, bf16[128,128]{1,0:T(8,128)(2,1)S(1)}, u32[]{:S(2)}, u32[]{:S(2)}) collective-permute-start(bf16[128,128]{1,0:T(8,128)(2,1)S(1)} %get-tuple-element.72), channel_id=1, source_target_pairs={{0,8},{1,9},{2,10},{3,11},{4,12},{5,13},{6,14},{7,15},{8,0},{9,1},... | collective-permute-start | bytes 98312 | tf_op jit(solution)/shard_map/ppermute | solution.py:531
  36.9 1.9 %collective-permute-start.13 = (bf16[128,128]{1,0:T(8,128)(2,1)S(1)}, bf16[128,128]{1,0:T(8,128)(2,1)S(1)}, u32[]{:S(2)}, u32[]{:S(2)}) collective-permute-start(bf16[128,128]{1,0:T(8,128)(2,1)S(1)} %get-tuple-element.73), channel_id=1, source_target_pairs={{0,12},{1,13},{2,14},{3,15},{4,8},{5,9},{6,10},{7,11},{8,4},{9,5},... | collective-permute-start | bytes 98312 | tf_op jit(solution)/shard_map/ppermute | solution.py:531
  39.7 2.9 %collective-permute-done.13.rest_11_ = bf16[128,128]{1,0:T(8,128)(2,1)S(1)} collective-permute-done((bf16[128,128]{1,0:T(8,128)(2,1)S(1)}, bf16[128,128]{1,0:T(8,128)(2,1)S(1)}, u32[]{:S(2)}, u32[]{:S(2)}) %collective-permute-start.13) | collective-permute-done | bytes 32800 | tf_op jit(solution)/shard_map/ppermute | solution.py:531
  42.6 3.4 %shard_map.73 = (bf16[256,128]{1,0:T(8,128)(2,1)S(1)}, bf16[256,128]{1,0:T(8,128)(2,1)S(1)}, bf16[256,128]{1,0:T(8,128)(2,1)S(1)}, bf16[256,128]{1,0:T(8,128)(2,...) custom-call(bf16[272,128]{1,0:T(8,128)(2,1)S(1)} %get-tuple-element., ...), custom_call_target="tpu_custom_call" | custom-call | flops 4294967296 | bytes 1048576 | tf_op jit(solution)/shard_map/pallas_call | solution.py:490
  46.2 2.3 %collective-permute-start.15 = (bf16[256,128]{1,0:T(8,128)(2,1)S(1)}, bf16[256,128]{1,0:T(8,128)(2,1)S(1)}, u32[]{:S(2)}, u32[]{:S(2)}) collective-permute-start(bf16[256,128]{1,0:T(8,128)(2,1)S(1)} %get-tuple-element.76), channel_id=1, source_target_pairs={{0,8},{1,9},{2,10},{3,11},{4,12},{5,13},{6,14},{7,15},{8,0},{9,1},... | collective-permute-start | bytes 196616 | tf_op jit(solution)/shard_map/ppermute | solution.py:531
  48.6 1.9 %collective-permute-start.16 = (bf16[256,128]{1,0:T(8,128)(2,1)S(1)}, bf16[256,128]{1,0:T(8,128)(2,1)S(1)}, u32[]{:S(2)}, u32[]{:S(2)}) collective-permute-start(bf16[256,128]{1,0:T(8,128)(2,1)S(1)} %get-tuple-element.77), channel_id=1, source_target_pairs={{0,12},{1,13},{2,14},{3,15},{4,8},{5,9},{6,10},{7,11},{8,4},{9,5},... | collective-permute-start | bytes 196616 | tf_op jit(solution)/shard_map/ppermute | solution.py:531
  52.0 2.8 %collective-permute-start.19 = (bf16[256,128]{1,0:T(8,128)(2,1)S(1)}, bf16[256,128]{1,0:T(8,128)(2,1)S(1)}, u32[]{:S(2)}, u32[]{:S(2)}) collective-permute-start(bf16[256,128]{1,0:T(8,128)(2,1)S(1)} %get-tuple-element.80), channel_id=1, source_target_pairs={{0,24},{1,25},{2,26},{3,27},{4,28},{5,29},{6,30},{7,31},{8,16},{9,... | collective-permute-start | bytes 196616 | tf_op jit(solution)/shard_map/ppermute | solution.py:531
  54.9 2.3 %collective-permute-start.20 = (bf16[256,128]{1,0:T(8,128)(2,1)S(1)}, bf16[256,128]{1,0:T(8,128)(2,1)S(1)}, u32[]{:S(2)}, u32[]{:S(2)}) collective-permute-start(bf16[256,128]{1,0:T(8,128)(2,1)S(1)} %get-tuple-element.81), channel_id=1, source_target_pairs={{0,28},{1,29},{2,30},{3,31},{4,24},{5,25},{6,26},{7,27},{8,20},{9,... | collective-permute-start | bytes 196616 | tf_op jit(solution)/shard_map/ppermute | solution.py:531
  58.0 3.8 %collective-permute-done.20.rest_7_ = bf16[256,128]{1,0:T(8,128)(2,1)S(1)} collective-permute-done((bf16[256,128]{1,0:T(8,128)(2,1)S(1)}, bf16[256,128]{1,0:T(8,128)(2,1)S(1)}, u32[]{:S(2)}, u32[]{:S(2)}) %collective-permute-start.20) | collective-permute-done | bytes 65568 | tf_op jit(solution)/shard_map/ppermute | solution.py:531
  62.1 2.4 %shard_map.75 = (bf16[2,272,1024]{2,1,0:T(8,128)(2,1)S(1)}, bf16[256,512]{1,0:T(8,128)(2,1)S(1)}) custom-call(bf16[256,512]{1,0:T(8,128)(2,1)S(1)} %shard_map.74.ls.a0, bf16[256,512]{1,0:T(8,128)(2,1)S(1)} %get-tuple-element.51.prim, bf16[256,512]{1,0:T(8,128)(2,1)S(1)} %get-tuple-element.52.sec.second, f32[256,128]{1,0:T(8,128)S(1)} %get-tuple-element.82.spread, ...), custom_call_target="tpu_custom_call" | custom-call | flops 2147483648 | bytes 1048576 | tf_op jit(solution)/shard_map/pallas_call | solution.py:490
  64.6 1.6 %collective-permute-start.29 = (bf16[1024,512]{1,0:T(8,128)(2,1)S(1)}, bf16[1024,512]{1,0:T(8,128)(2,1)S(1)}, u32[]{:S(2)}, u32[]{:S(2)}) collective-permute-start(bf16[1024,512]{1,0:T(8,128)(2,1)S(1)} %get-tuple-element.67.w3), channel_id=1, source_target_pairs={{0,3},{1,2},{2,1},{3,0},{4,7},{5,6},{6,5},{7,4},{8,11},{9,10},{10,... | collective-permute-start | bytes 3145736 | tf_op jit(solution)/shard_map/ppermute | solution.py:531
  66.2 1.7 %shard_map.76.kept = bf16[2,256,1024]{2,1,0:T(8,128)(2,1)S(1)} custom-call(bf16[256,512]{1,0:T(8,128)(2,1)S(1)} %get-tuple-element.84.lp, bf16[256,512]{1,0:T(8,128)(2,1)S(1)} %shard_map.74.ls.a0, bf16[4,1024,512]{2,1,0:T(8,128)(2,1)S(1)} %get-tuple-element.83.wp, bf16[1024,512]{1,0:T(8,128)(2,1)S(1)} %get-tuple-element.66.w2, ...), custom_call_target="tpu_custom_call" | custom-call | flops 2147483648 | bytes 1048576 | tf_op jit(solution)/shard_map/pallas_call | solution.py:490
  68.3 1.0 collective-permute-start.26
  69.3 1.1 collective-permute-start.27
  70.4 0.9 collective-permute-start.31
  71.3 36.3 %collective-permute-done.27.edge = bf16[256,512]{1,0:T(8,128)(2,1)S(1)} collective-permute-done((bf16[256,512]{1,0:T(8,128)(2,1)S(1)}, bf16[256,512]{1,0:T(8,128)(2,1)S(1)}, u32[]{:S(2)}, u32[]{:S(2)}) %collective-permute-start.27) | collective-permute-done | bytes 262176 | tf_op jit(solution)/shard_map/ppermute | solution.py:531
  107.5 1.5 %collective-permute-start.23 = (bf16[256,512]{1,0:T(8,128)(2,1)S(1)}, bf16[256,512]{1,0:T(8,128)(2,1)S(1)}, u32[]{:S(2)}, u32[]{:S(2)}) collective-permute-start(bf16[256,512]{1,0:T(8,128)(2,1)S(1)} %shard_map.74.ls.a0), channel_id=1, source_target_pairs={{0,2},{1,3},{2,0},{3,1},{4,6},{5,7},{6,4},{7,5},{8,10},{9,11},{10,... | collective-permute-start | bytes 786440 | tf_op jit(solution)/shard_map/ppermute | solution.py:531
  109.6 14.3 %collective-permute-done.23.a2 = bf16[256,512]{1,0:T(8,128)(2,1)S(1)} collective-permute-done((bf16[256,512]{1,0:T(8,128)(2,1)S(1)}, bf16[256,512]{1,0:T(8,128)(2,1)S(1)}, u32[]{:S(2)}, u32[]{:S(2)}) %collective-permute-start.23) | collective-permute-done | bytes 262176 | tf_op jit(solution)/shard_map/ppermute | solution.py:531
  124.5 1.2 shard_map.81
  125.8 5.7 %collective-permute-done.28.mirrored = bf16[256,512]{1,0:T(8,128)(2,1)S(1)} collective-permute-done((bf16[256,512]{1,0:T(8,128)(2,1)S(1)}, bf16[256,512]{1,0:T(8,128)(2,1)S(1)}, u32[]{:S(2)}, u32[]{:S(2)}) %collective-permute-start.28) | collective-permute-done | bytes 262176 | tf_op jit(solution)/shard_map/ppermute | solution.py:531
  131.5 0.9 shard_map.79
  (50 shorter events, 7.3 us)
Async XLA Ops:
  0.6 15.9 %collective-permute-start.7 = (bf16[256,1024]{1,0:T(8,128)(2,1)}, bf16[256,1024]{1,0:T(8,128)(2,1)S(1)}, u32[]{:S(2)}, u32[]{:S(2)}) collective-permute-start(bf16[256,1024]{1,0:T(8,128)(2,1)} %c0.1), channel_id=1, source_target_pairs={{0,1},{1,0},{2,3},{3,2},{4,5},{5,4},{6,7},{7,6},{8,9},{9,8},{10,11... | collective-permute-start | bytes 1572872 | tf_op jit(solution)/shard_map/ppermute | solution.py:531
  1.2 15.3 %collective-permute-start.8 = (bf16[256,1024]{1,0:T(8,128)(2,1)}, bf16[256,1024]{1,0:T(8,128)(2,1)S(1)}, u32[]{:S(2)}, u32[]{:S(2)}) collective-permute-start(bf16[256,1024]{1,0:T(8,128)(2,1)} %c0.1), channel_id=1, source_target_pairs={{0,2},{1,3},{2,0},{3,1},{4,6},{5,7},{6,4},{7,5},{8,10},{9,11},{10,... | collective-permute-start | bytes 1572872 | tf_op jit(solution)/shard_map/ppermute | solution.py:531
  16.5 1.9 %collective-permute-start.9 = (bf16[256,1024]{1,0:T(8,128)(2,1)S(1)}, bf16[256,1024]{1,0:T(8,128)(2,1)S(1)}, u32[]{:S(2)}, u32[]{:S(2)}) collective-permute-start(bf16[256,1024]{1,0:T(8,128)(2,1)S(1)} %collective-permute-done.8.c2), channel_id=1, source_target_pairs={{0,1},{1,0},{2,3},{3,2},{4,5},{5,4},{6,7},{7,6},{8,9},{9,8},{10,11... | collective-permute-start | bytes 1572872 | tf_op jit(solution)/shard_map/ppermute | solution.py:531
  18.4 12.6 %collective-permute-start.10 = (bf16[256,256]{1,0:T(8,128)(2,1)S(1)}, bf16[256,256]{1,0:T(8,128)(2,1)S(1)}, u32[]{:S(2)}, u32[]{:S(2)}) collective-permute-start(bf16[256,256]{1,0:T(8,128)(2,1)S(1)} %get-tuple-element.69), channel_id=1, source_target_pairs={{0,16},{1,17},{2,18},{3,19},{4,20},{5,21},{6,22},{7,23},{8,24},{9,... | collective-permute-start | bytes 393224 | tf_op jit(solution)/shard_map/ppermute | solution.py:531
  20.9 4.5 %collective-permute-start = (bf16[272,128]{1,0:T(8,128)(2,1)S(1)}, bf16[272,128]{1,0:T(8,128)(2,1)S(1)}, u32[]{:S(2)}, u32[]{:S(2)}) collective-permute-start(bf16[272,128]{1,0:T(8,128)(2,1)S(1)} %get-tuple-element.55), channel_id=1, source_target_pairs={{0,4},{1,5},{2,6},{3,7},{4,0},{5,1},{6,2},{7,3},{8,12},{9,13},{10,... | collective-permute-start | bytes 208904 | tf_op jit(solution)/shard_map/ppermute | solution.py:531
  22.5 7.5 %collective-permute-start.1 = (bf16[272,128]{1,0:T(8,128)(2,1)S(1)}, bf16[272,128]{1,0:T(8,128)(2,1)S(1)}, u32[]{:S(2)}, u32[]{:S(2)}) collective-permute-start(bf16[272,128]{1,0:T(8,128)(2,1)S(1)} %get-tuple-element.56), channel_id=1, source_target_pairs={{0,8},{1,9},{2,10},{3,11},{4,12},{5,13},{6,14},{7,15},{8,0},{9,1},... | collective-permute-start | bytes 208904 | tf_op jit(solution)/shard_map/ppermute | solution.py:531
  25.1 9.2 %collective-permute-start.2 = (bf16[272,128]{1,0:T(8,128)(2,1)S(1)}, bf16[272,128]{1,0:T(8,128)(2,1)S(1)}, u32[]{:S(2)}, u32[]{:S(2)}) collective-permute-start(bf16[272,128]{1,0:T(8,128)(2,1)S(1)} %get-tuple-element.57), channel_id=1, source_target_pairs={{0,12},{1,13},{2,14},{3,15},{4,8},{5,9},{6,10},{7,11},{8,4},{9,5},... | collective-permute-start | bytes 208904 | tf_op jit(solution)/shard_map/ppermute | solution.py:531
  25.3 9.3 %collective-permute-start.3 = (bf16[272,128]{1,0:T(8,128)(2,1)S(1)}, bf16[272,128]{1,0:T(8,128)(2,1)S(1)}, u32[]{:S(2)}, u32[]{:S(2)}) collective-permute-start(bf16[272,128]{1,0:T(8,128)(2,1)S(1)} %get-tuple-element.58), channel_id=1, source_target_pairs={{0,16},{1,17},{2,18},{3,19},{4,20},{5,21},{6,22},{7,23},{8,24},{9,... | collective-permute-start | bytes 208904 | tf_op jit(solution)/shard_map/ppermute | solution.py:531
  25.4 11.6 %collective-permute-start.4 = (bf16[272,128]{1,0:T(8,128)(2,1)S(1)}, bf16[272,128]{1,0:T(8,128)(2,1)S(1)}, u32[]{:S(2)}, u32[]{:S(2)}) collective-permute-start(bf16[272,128]{1,0:T(8,128)(2,1)S(1)} %get-tuple-element.59), channel_id=1, source_target_pairs={{0,20},{1,21},{2,22},{3,23},{4,16},{5,17},{6,18},{7,19},{8,28},{9,... | collective-permute-start | bytes 208904 | tf_op jit(solution)/shard_map/ppermute | solution.py:531
  30.1 8.7 %collective-permute-start.5 = (bf16[272,128]{1,0:T(8,128)(2,1)S(1)}, bf16[272,128]{1,0:T(8,128)(2,1)S(1)}, u32[]{:S(2)}, u32[]{:S(2)}) collective-permute-start(bf16[272,128]{1,0:T(8,128)(2,1)S(1)} %get-tuple-element.60), channel_id=1, source_target_pairs={{0,24},{1,25},{2,26},{3,27},{4,28},{5,29},{6,30},{7,31},{8,16},{9,... | collective-permute-start | bytes 208904 | tf_op jit(solution)/shard_map/ppermute | solution.py:531
  31.0 7.8 %collective-permute-start.6 = (bf16[272,128]{1,0:T(8,128)(2,1)S(1)}, bf16[272,128]{1,0:T(8,128)(2,1)S(1)}, u32[]{:S(2)}, u32[]{:S(2)}) collective-permute-start(bf16[272,128]{1,0:T(8,128)(2,1)S(1)} %get-tuple-element.61), channel_id=1, source_target_pairs={{0,28},{1,29},{2,30},{3,31},{4,24},{5,25},{6,26},{7,27},{8,20},{9,... | collective-permute-start | bytes 208904 | tf_op jit(solution)/shard_map/ppermute | solution.py:531
  34.4 4.5 %collective-permute-start.11 = (bf16[128,128]{1,0:T(8,128)(2,1)S(1)}, bf16[128,128]{1,0:T(8,128)(2,1)S(1)}, u32[]{:S(2)}, u32[]{:S(2)}) collective-permute-start(bf16[128,128]{1,0:T(8,128)(2,1)S(1)} %get-tuple-element.71), channel_id=1, source_target_pairs={{0,4},{1,5},{2,6},{3,7},{4,0},{5,1},{6,2},{7,3},{8,12},{9,13},{10,... | collective-permute-start | bytes 98312 | tf_op jit(solution)/shard_map/ppermute | solution.py:531
  34.7 5.0 %collective-permute-start.12 = (bf16[128,128]{1,0:T(8,128)(2,1)S(1)}, bf16[128,128]{1,0:T(8,128)(2,1)S(1)}, u32[]{:S(2)}, u32[]{:S(2)}) collective-permute-start(bf16[128,128]{1,0:T(8,128)(2,1)S(1)} %get-tuple-element.72), channel_id=1, source_target_pairs={{0,8},{1,9},{2,10},{3,11},{4,12},{5,13},{6,14},{7,15},{8,0},{9,1},... | collective-permute-start | bytes 98312 | tf_op jit(solution)/shard_map/ppermute | solution.py:531
  36.9 5.7 %collective-permute-start.13 = (bf16[128,128]{1,0:T(8,128)(2,1)S(1)}, bf16[128,128]{1,0:T(8,128)(2,1)S(1)}, u32[]{:S(2)}, u32[]{:S(2)}) collective-permute-start(bf16[128,128]{1,0:T(8,128)(2,1)S(1)} %get-tuple-element.73), channel_id=1, source_target_pairs={{0,12},{1,13},{2,14},{3,15},{4,8},{5,9},{6,10},{7,11},{8,4},{9,5},... | collective-permute-start | bytes 98312 | tf_op jit(solution)/shard_map/ppermute | solution.py:531
  46.0 5.9 %collective-permute-start.14 = (bf16[256,128]{1,0:T(8,128)(2,1)S(1)}, bf16[256,128]{1,0:T(8,128)(2,1)S(1)}, u32[]{:S(2)}, u32[]{:S(2)}) collective-permute-start(bf16[256,128]{1,0:T(8,128)(2,1)S(1)} %get-tuple-element.75), channel_id=1, source_target_pairs={{0,4},{1,5},{2,6},{3,7},{4,0},{5,1},{6,2},{7,3},{8,12},{9,13},{10,... | collective-permute-start | bytes 196616 | tf_op jit(solution)/shard_map/ppermute | solution.py:531
  46.2 8.7 %collective-permute-start.15 = (bf16[256,128]{1,0:T(8,128)(2,1)S(1)}, bf16[256,128]{1,0:T(8,128)(2,1)S(1)}, u32[]{:S(2)}, u32[]{:S(2)}) collective-permute-start(bf16[256,128]{1,0:T(8,128)(2,1)S(1)} %get-tuple-element.76), channel_id=1, source_target_pairs={{0,8},{1,9},{2,10},{3,11},{4,12},{5,13},{6,14},{7,15},{8,0},{9,1},... | collective-permute-start | bytes 196616 | tf_op jit(solution)/shard_map/ppermute | solution.py:531
  48.6 8.7 %collective-permute-start.16 = (bf16[256,128]{1,0:T(8,128)(2,1)S(1)}, bf16[256,128]{1,0:T(8,128)(2,1)S(1)}, u32[]{:S(2)}, u32[]{:S(2)}) collective-permute-start(bf16[256,128]{1,0:T(8,128)(2,1)S(1)} %get-tuple-element.77), channel_id=1, source_target_pairs={{0,12},{1,13},{2,14},{3,15},{4,8},{5,9},{6,10},{7,11},{8,4},{9,5},... | collective-permute-start | bytes 196616 | tf_op jit(solution)/shard_map/ppermute | solution.py:531
  50.5 6.8 %collective-permute-start.17 = (bf16[256,128]{1,0:T(8,128)(2,1)S(1)}, bf16[256,128]{1,0:T(8,128)(2,1)S(1)}, u32[]{:S(2)}, u32[]{:S(2)}) collective-permute-start(bf16[256,128]{1,0:T(8,128)(2,1)S(1)} %get-tuple-element.78), channel_id=1, source_target_pairs={{0,16},{1,17},{2,18},{3,19},{4,20},{5,21},{6,22},{7,23},{8,24},{9,... | collective-permute-start | bytes 196616 | tf_op jit(solution)/shard_map/ppermute | solution.py:531
  50.6 6.6 %collective-permute-start.18 = (bf16[256,128]{1,0:T(8,128)(2,1)S(1)}, bf16[256,128]{1,0:T(8,128)(2,1)S(1)}, u32[]{:S(2)}, u32[]{:S(2)}) collective-permute-start(bf16[256,128]{1,0:T(8,128)(2,1)S(1)} %get-tuple-element.79), channel_id=1, source_target_pairs={{0,20},{1,21},{2,22},{3,23},{4,16},{5,17},{6,18},{7,19},{8,28},{9,... | collective-permute-start | bytes 196616 | tf_op jit(solution)/shard_map/ppermute | solution.py:531
  52.0 6.1 %collective-permute-start.19 = (bf16[256,128]{1,0:T(8,128)(2,1)S(1)}, bf16[256,128]{1,0:T(8,128)(2,1)S(1)}, u32[]{:S(2)}, u32[]{:S(2)}) collective-permute-start(bf16[256,128]{1,0:T(8,128)(2,1)S(1)} %get-tuple-element.80), channel_id=1, source_target_pairs={{0,24},{1,25},{2,26},{3,27},{4,28},{5,29},{6,30},{7,31},{8,16},{9,... | collective-permute-start | bytes 196616 | tf_op jit(solution)/shard_map/ppermute | solution.py:531
  54.9 7.0 %collective-permute-start.20 = (bf16[256,128]{1,0:T(8,128)(2,1)S(1)}, bf16[256,128]{1,0:T(8,128)(2,1)S(1)}, u32[]{:S(2)}, u32[]{:S(2)}) collective-permute-start(bf16[256,128]{1,0:T(8,128)(2,1)S(1)} %get-tuple-element.81), channel_id=1, source_target_pairs={{0,28},{1,29},{2,30},{3,31},{4,24},{5,25},{6,26},{7,27},{8,20},{9,... | collective-permute-start | bytes 196616 | tf_op jit(solution)/shard_map/ppermute | solution.py:531
  64.5 3.5 %collective-permute-start.21 = (bf16[2,272,1024]{2,1,0:T(8,128)(2,1)S(1)}, bf16[2,272,1024]{2,1,0:T(8,128)(2,1)S(1)}, u32[]{:S(2)}, u32[]{:S(2)}) collective-permute-start(bf16[2,272,1024]{2,1,0:T(8,128)(2,1)S(1)} %get-tuple-element.85.sent), channel_id=1, source_target_pairs={{0,1},{1,0},{2,3},{3,2},{4,5},{5,4},{6,7},{7,6},{8,9},{9,8},{10,11... | collective-permute-start | bytes 3342344 | tf_op jit(solution)/shard_map/ppermute | solution.py:531
  64.6 66.9 %collective-permute-start.29 = (bf16[1024,512]{1,0:T(8,128)(2,1)S(1)}, bf16[1024,512]{1,0:T(8,128)(2,1)S(1)}, u32[]{:S(2)}, u32[]{:S(2)}) collective-permute-start(bf16[1024,512]{1,0:T(8,128)(2,1)S(1)} %get-tuple-element.67.w3), channel_id=1, source_target_pairs={{0,3},{1,2},{2,1},{3,0},{4,7},{5,6},{6,5},{7,4},{8,11},{9,10},{10,... | collective-permute-start | bytes 3145736 | tf_op jit(solution)/shard_map/ppermute | solution.py:531
  68.1 63.4 %collective-permute-start.25 = (bf16[1024,512]{1,0:T(8,128)(2,1)S(1)}, bf16[1024,512]{1,0:T(8,128)(2,1)S(1)}, u32[]{:S(2)}, u32[]{:S(2)}) collective-permute-start(bf16[1024,512]{1,0:T(8,128)(2,1)S(1)} %get-tuple-element.88.w1), channel_id=1, source_target_pairs={{0,1},{1,0},{2,3},{3,2},{4,5},{5,4},{6,7},{7,6},{8,9},{9,8},{10,11... | collective-permute-start | bytes 3145736 | tf_op jit(solution)/shard_map/ppermute | solution.py:531
  68.3 40.8 %collective-permute-start.26 = (bf16[512,512]{1,0:T(8,128)(2,1)S(1)}, bf16[512,512]{1,0:T(8,128)(2,1)S(1)}, u32[]{:S(2)}, u32[]{:S(2)}) collective-permute-start(bf16[512,512]{1,0:T(8,128)(2,1)S(1)} %get-tuple-element.89), channel_id=1, source_target_pairs={{0,2},{1,3},{2,0},{3,1},{4,6},{5,7},{6,4},{7,5},{8,10},{9,11},{10,... | collective-permute-start | bytes 1572872 | tf_op jit(solution)/shard_map/ppermute | solution.py:531
  69.3 38.3 %collective-permute-start.27 = (bf16[256,512]{1,0:T(8,128)(2,1)S(1)}, bf16[256,512]{1,0:T(8,128)(2,1)S(1)}, u32[]{:S(2)}, u32[]{:S(2)}) collective-permute-start(bf16[256,512]{1,0:T(8,128)(2,1)S(1)} %get-tuple-element.90), channel_id=1, source_target_pairs={{0,2},{1,3},{2,0},{3,1},{4,6},{5,7},{6,4},{7,5},{8,10},{9,11},{10,... | collective-permute-start | bytes 786440 | tf_op jit(solution)/shard_map/ppermute | solution.py:531
  70.4 53.6 %collective-permute-start.31 = (bf16[256,1024]{1,0:T(8,128)(2,1)S(1)}, bf16[256,1024]{1,0:T(8,128)(2,1)S(1)}, u32[]{:S(2)}, u32[]{:S(2)}) collective-permute-start(bf16[256,1024]{1,0:T(8,128)(2,1)S(1)} %get-tuple-element.93), channel_id=1, source_target_pairs={{0,2},{1,3},{2,0},{3,1},{4,6},{5,7},{6,4},{7,5},{8,10},{9,11},{10,... | collective-permute-start | bytes 1572872 | tf_op jit(solution)/shard_map/ppermute | solution.py:531
  107.5 16.3 %collective-permute-start.23 = (bf16[256,512]{1,0:T(8,128)(2,1)S(1)}, bf16[256,512]{1,0:T(8,128)(2,1)S(1)}, u32[]{:S(2)}, u32[]{:S(2)}) collective-permute-start(bf16[256,512]{1,0:T(8,128)(2,1)S(1)} %shard_map.74.ls.a0), channel_id=1, source_target_pairs={{0,2},{1,3},{2,0},{3,1},{4,6},{5,7},{6,4},{7,5},{8,10},{9,11},{10,... | collective-permute-start | bytes 786440 | tf_op jit(solution)/shard_map/ppermute | solution.py:531
  109.1 14.9 %collective-permute-start.30 = (f32[8,256]{1,0:T(8,128)S(1)}, f32[8,256]{1,0:T(8,128)S(1)}, u32[]{:S(2)}, u32[]{:S(2)}) collective-permute-start(f32[8,256]{1,0:T(8,128)S(1)} %get-tuple-element.92.ends), channel_id=1, source_target_pairs={{0,2},{1,3},{2,0},{3,1},{4,6},{5,7},{6,4},{7,5},{8,10},{9,11},{10,... | collective-permute-start | bytes 24584 | tf_op jit(solution)/shard_map/ppermute | solution.py:531
  123.9 7.6 %collective-permute-start.28 = (bf16[256,512]{1,0:T(8,128)(2,1)S(1)}, bf16[256,512]{1,0:T(8,128)(2,1)S(1)}, u32[]{:S(2)}, u32[]{:S(2)}) collective-permute-start(bf16[256,512]{1,0:T(8,128)(2,1)S(1)} %collective-permute-done.27.edge), channel_id=1, source_target_pairs={{0,4},{1,5},{2,6},{3,7},{4,0},{5,1},{6,2},{7,3},{8,12},{9,13},{10,... | collective-permute-start | bytes 786440 | tf_op jit(solution)/shard_map/ppermute | solution.py:531
  124.0 7.5 %collective-permute-start.24 = (bf16[256,512]{1,0:T(8,128)(2,1)S(1)}, bf16[256,512]{1,0:T(8,128)(2,1)S(1)}, u32[]{:S(2)}, u32[]{:S(2)}) collective-permute-start(bf16[256,512]{1,0:T(8,128)(2,1)S(1)} %collective-permute-done.23.a2), channel_id=1, source_target_pairs={{0,1},{1,0},{2,3},{3,2},{4,5},{5,4},{6,7},{7,6},{8,9},{9,8},{10,11... | collective-permute-start | bytes 786440 | tf_op jit(solution)/shard_map/ppermute | solution.py:531
  124.0 7.5 %collective-permute-start.22 = (bf16[256,512]{1,0:T(8,128)(2,1)S(1)}, bf16[256,512]{1,0:T(8,128)(2,1)S(1)}, u32[]{:S(2)}, u32[]{:S(2)}) collective-permute-start(bf16[256,512]{1,0:T(8,128)(2,1)S(1)} %shard_map.74.ls.a0), channel_id=1, source_target_pairs={{0,1},{1,0},{2,3},{3,2},{4,5},{5,4},{6,7},{7,6},{8,9},{9,8},{10,11... | collective-permute-start | bytes 786440 | tf_op jit(solution)/shard_map/ppermute | solution.py:531
  (2 other events, 12.7 us)

commit v8 on v6

--- a/solution.py
+++ b/solution.py
@@ -249,6 +249,13 @@
     own_gain[...] = gbuf[:, mine]
 
 
+def marks_kernel(counts, alive, tail):
+    line = lax.broadcasted_iota(jnp.int32, alive.shape, 0)
+    last = jnp.where(lax.axis_index("segment") == 0, alive.shape[0], counts[0, 1])
+    alive[...] = jnp.where(line < last, 1.0, 0.0)
+    tail[...] = (jnp.full(tail.shape, 1.0, F32) * counts[0, 0].astype(F32)).astype(BF16)
+
+
 def lend_kernel(w2, middle, edge):
     parity = lax.rem(lax.axis_index("blk"), 2)
     depth, quarter = w2.shape[0], edge.shape[0]
@@ -265,7 +272,7 @@
         acc[...] += jnp.dot(c2[...], w2[...], preferred_element_type=F32)
 
 
-def pack_kernel(sizes, counts, prim, sec, acc, c3, w3, *rest):
+def pack_kernel(sizes, prim, sec, acc, alive, tail, c3, w3, *rest):
     heads = sizes[0] * sizes[1]
     second, outs, (parts,) = rest[0], rest[1 : 1 + heads], rest[1 + heads :]
     seg, entry, _ = place(sizes)
@@ -278,16 +285,16 @@
     @pl.when(seg == 1)
     def _():
         total = acc[...] + jnp.dot(c3[...], w3[...], preferred_element_type=F32)
-        line = lax.broadcasted_iota(jnp.int32, acc.shape, 0)
-        second[...] = jnp.where(line < counts[0, 1], total, 0.0).astype(BF16)
-
-    tail = jnp.full((TAIL, LANES), 1.0, F32) * counts[0, 0].astype(F32)
+        for tile in range(total.shape[1] // LANES):
+            cols = slice(tile * LANES, (tile + 1) * LANES)
+            second[:, cols] = jnp.where(alive[...] > 0.0, total[:, cols], 0.0).astype(BF16)
+
     for head in range(heads):
         cols = slice(head * DH, (head + 1) * DH)
         parts[head] = jnp.concatenate([prim[:, cols], second[:, cols]], axis=1)
     for k, out in enumerate(outs):
         out[:rows, :] = parts[jnp.bitwise_xor(entry, k)]
-        out[rows:, :] = tail.astype(BF16)
+        out[rows:, :] = tail[...]
 
 
 def live_keys(piece, rows):
@@ -362,15 +369,12 @@
         yield slice(head * DH, (head + 2) * DH), parts[head], parts[head + 1]
 
 
-def attended_kernel(sizes, counts, *rest):
+def attended_kernel(sizes, alive, *rest):
     heads = sizes[0] * sizes[1]
     ins, (ls, parts) = rest[:heads], rest[heads:]
-    rows = ls.shape[0]
-    line = lax.broadcasted_iota(jnp.int32, (rows, LANES), 0)
-    alive = line < jnp.where(lax.axis_index("segment") == 0, rows, counts[0, 1])
     for cols, one, two in regroup(sizes, ins, parts):
         both = jnp.concatenate([one[:, DH:], two[:, DH:]], axis=1)
-        ls[:, cols] = jnp.where(alive, both.astype(F32), 0.0).astype(BF16)
+        ls[:, cols] = jnp.where(alive[...] > 0.0, both.astype(F32), 0.0).astype(BF16)
 
 
 def project_block(seg, wp, ws, lp, ls, out, slot):
@@ -536,6 +540,9 @@
     )
     wp, ws = made[0], made[1 : 1 + n_mp]
     own, own_states, own_gain, spread, prim, sec = made[1 + n_mp :]
+    alive, tail = call(
+        marks_kernel, (counts,), [SCALARS], [((rows, LANES), F32), ((TAIL, LANES), BF16)]
+    )
     quarter = feats // 4
     middle, edge = call(
         lend_kernel,
@@ -557,8 +564,8 @@
     )[0]
     made = call(
         functools.partial(pack_kernel, sizes),
-        (counts, prim, sec, acc, cross_cot, ws[3]),
-        [SCALARS] + [INSIDE] * 5,
+        (prim, sec, acc, alive, tail, cross_cot, ws[3]),
+        [INSIDE] * 7,
         [((rows, group), BF16)] + [((rows + TAIL, LANES), BF16)] * heads,
         [pltpu.VMEM((heads, rows, LANES), BF16)],
         16,
@@ -587,8 +594,8 @@
     pieces = exchange(pieces)
     (ls,) = call(
         functools.partial(attended_kernel, sizes),
-        (counts, *pieces),
-        [SCALARS] + [INSIDE] * heads,
+        (alive, *pieces),
+        [INSIDE] * (1 + heads),
         [((rows, group), BF16)],
         [pltpu.VMEM((heads, rows, LANES), BF16)],
     )

time: 129 us -> 128 us (level)
  waiting for transfers between devices: 72.3 us -> 70.6 us
    ppermute x28, waiting for transfers between devices: 72.3 us -> 70.6 us  [swap(): return lax.ppermute(x, AXES, pairs)]
    pallas_call x12 -> x13, Pallas kernels: 20.4 us -> 19.9 us  [call(): pl.pallas_call(body, in_specs=list(specs), out_specs=[INSIDE] * len(outs)...]
  transfers between devices with their start and end apart: 28 -> 28, of which waited for: 11 -> 10; matrix products, arithmetic and copies ran while one was open for 0% -> 0% of each run, Pallas kernels for 10% -> 10%
where the time goes in v8:
time: 128 us
  waiting for transfers between devices  70.6 us (55%)
  starting transfers between devices  36.4 us (28%)
  Pallas kernels  19.9 us (16%)
    ppermute x28, waiting for transfers between devices, swap(): return lax.ppermute(x, AXES, pairs)  70.6 us
    ppermute x28, starting transfers between devices, swap(): return lax.ppermute(x, AXES, pairs)  36.4 us
    pallas_call x13, Pallas kernels, call(): pl.pallas_call(body, in_specs=list(specs), out_specs=[INSIDE] * len(outs)...  19.9 us
  transfers between devices with their start and end apart: 28, of which 10 were waited for; matrix products, arithmetic and copies ran while one was open for 0% of the time, Pallas kernels for 10%

profile of v8, /device:TPU:0, one launch (start us, length us, event | category | flops | bytes accessed | tf_op | source)
XLA Modules:
  0.0 127.8 jit_solution(5236670452782503742)
XLA Ops:
  0.6 0.6 collective-permute-start
  1.2 2.6 %collective-permute-start.1 = (bf16[256,1024]{1,0:T(8,128)(2,1)}, bf16[256,1024]{1,0:T(8,128)(2,1)S(1)}, u32[]{:S(2)}, u32[]{:S(2)}) collective-permute-start(bf16[256,1024]{1,0:T(8,128)(2,1)} %c0.1), channel_id=1, source_target_pairs={{0,2},{1,3},{2,0},{3,1},{4,6},{5,7},{6,4},{7,5},{8,10},{9,11},{10,... | collective-permute-start | bytes 1572872 | tf_op jit(solution)/shard_map/ppermute | solution.py:503
  3.8 9.1 %shard_map.69 = (bf16[4,1024,512]{2,1,0:T(8,128)(2,1)S(1)}, bf16[1024,512]{1,0:T(8,128)(2,1)S(1)}, bf16[1024,512]{1,0:T(8,128)(2,1)S(1)}, bf16[1024,512]{1,0:T(8...) custom-call(bf16[256,4096]{1,0:T(8,128)(2,1)} %bitcast.12, ...), custom_call_target="tpu_custom_call" | custom-call | flops 8589934592 | bytes 1048576 | tf_op jit(solution)/shard_map/pallas_call | solution.py:462
  12.9 3.6 %collective-permute-done.1.c2 = bf16[256,1024]{1,0:T(8,128)(2,1)S(1)} collective-permute-done((bf16[256,1024]{1,0:T(8,128)(2,1)}, bf16[256,1024]{1,0:T(8,128)(2,1)S(1)}, u32[]{:S(2)}, u32[]{:S(2)}) %collective-permute-start.1) | collective-permute-done | bytes 524320 | tf_op jit(solution)/shard_map/ppermute | solution.py:503
  16.5 0.6 shard_map.68
  17.1 1.3 %collective-permute-done.2.c3 = bf16[256,1024]{1,0:T(8,128)(2,1)S(1)} collective-permute-done((bf16[256,1024]{1,0:T(8,128)(2,1)S(1)}, bf16[256,1024]{1,0:T(8,128)(2,1)S(1)}, u32[]{:S(2)}, u32[]{:S(2)}) %collective-permute-start.2) | collective-permute-done | bytes 524320 | tf_op jit(solution)/shard_map/ppermute | solution.py:503
  18.7 1.9 %collective-permute-start.3 = (bf16[272,128]{1,0:T(8,128)(2,1)S(1)}, bf16[272,128]{1,0:T(8,128)(2,1)S(1)}, u32[]{:S(2)}, u32[]{:S(2)}) collective-permute-start(bf16[272,128]{1,0:T(8,128)(2,1)S(1)} %get-tuple-element.56), channel_id=1, source_target_pairs={{0,4},{1,5},{2,6},{3,7},{4,0},{5,1},{6,2},{7,3},{8,12},{9,13},{10,... | collective-permute-start | bytes 208904 | tf_op jit(solution)/shard_map/ppermute | solution.py:503
  20.5 2.6 %collective-permute-start.4 = (bf16[272,128]{1,0:T(8,128)(2,1)S(1)}, bf16[272,128]{1,0:T(8,128)(2,1)S(1)}, u32[]{:S(2)}, u32[]{:S(2)}) collective-permute-start(bf16[272,128]{1,0:T(8,128)(2,1)S(1)} %get-tuple-element.57), channel_id=1, source_target_pairs={{0,8},{1,9},{2,10},{3,11},{4,12},{5,13},{6,14},{7,15},{8,0},{9,1},... | collective-permute-start | bytes 208904 | tf_op jit(solution)/shard_map/ppermute | solution.py:503
  23.1 2.1 %collective-permute-start.6 = (bf16[272,128]{1,0:T(8,128)(2,1)S(1)}, bf16[272,128]{1,0:T(8,128)(2,1)S(1)}, u32[]{:S(2)}, u32[]{:S(2)}) collective-permute-start(bf16[272,128]{1,0:T(8,128)(2,1)S(1)} %get-tuple-element.59), channel_id=1, source_target_pairs={{0,16},{1,17},{2,18},{3,19},{4,20},{5,21},{6,22},{7,23},{8,24},{9,... | collective-permute-start | bytes 208904 | tf_op jit(solution)/shard_map/ppermute | solution.py:503
  25.5 4.8 %collective-permute-start.8 = (bf16[272,128]{1,0:T(8,128)(2,1)S(1)}, bf16[272,128]{1,0:T(8,128)(2,1)S(1)}, u32[]{:S(2)}, u32[]{:S(2)}) collective-permute-start(bf16[272,128]{1,0:T(8,128)(2,1)S(1)} %get-tuple-element.61), channel_id=1, source_target_pairs={{0,24},{1,25},{2,26},{3,27},{4,28},{5,29},{6,30},{7,31},{8,16},{9,... | collective-permute-start | bytes 208904 | tf_op jit(solution)/shard_map/ppermute | solution.py:503
  30.3 3.0 %collective-permute-start.9 = (bf16[272,128]{1,0:T(8,128)(2,1)S(1)}, bf16[272,128]{1,0:T(8,128)(2,1)S(1)}, u32[]{:S(2)}, u32[]{:S(2)}) collective-permute-start(bf16[272,128]{1,0:T(8,128)(2,1)S(1)} %get-tuple-element.62), channel_id=1, source_target_pairs={{0,28},{1,29},{2,30},{3,31},{4,24},{5,25},{6,26},{7,27},{8,20},{9,... | collective-permute-start | bytes 208904 | tf_op jit(solution)/shard_map/ppermute | solution.py:503
  33.3 2.4 %collective-permute-done.8.rest_6_ = bf16[272,128]{1,0:T(8,128)(2,1)S(1)} collective-permute-done((bf16[272,128]{1,0:T(8,128)(2,1)S(1)}, bf16[272,128]{1,0:T(8,128)(2,1)S(1)}, u32[]{:S(2)}, u32[]{:S(2)}) %collective-permute-start.8) | collective-permute-done | bytes 69664 | tf_op jit(solution)/shard_map/ppermute | solution.py:503
  35.7 1.7 %collective-permute-done.9.rest_7_ = bf16[272,128]{1,0:T(8,128)(2,1)S(1)} collective-permute-done((bf16[272,128]{1,0:T(8,128)(2,1)S(1)}, bf16[272,128]{1,0:T(8,128)(2,1)S(1)}, u32[]{:S(2)}, u32[]{:S(2)}) %collective-permute-start.9) | collective-permute-done | bytes 69664 | tf_op jit(solution)/shard_map/ppermute | solution.py:503
  37.3 3.4 %shard_map.72 = (bf16[256,128]{1,0:T(8,128)(2,1)S(1)}, bf16[256,128]{1,0:T(8,128)(2,1)S(1)}, bf16[256,128]{1,0:T(8,128)(2,1)S(1)}, bf16[256,128]{1,0:T(8,128)(2,...) custom-call(bf16[272,128]{1,0:T(8,128)(2,1)S(1)} %get-tuple-element., ...), custom_call_target="tpu_custom_call" | custom-call | flops 4294967296 | bytes 1048576 | tf_op jit(solution)/shard_map/pallas_call | solution.py:462
  40.8 2.2 %collective-permute-start.11 = (bf16[256,128]{1,0:T(8,128)(2,1)S(1)}, bf16[256,128]{1,0:T(8,128)(2,1)S(1)}, u32[]{:S(2)}, u32[]{:S(2)}) collective-permute-start(bf16[256,128]{1,0:T(8,128)(2,1)S(1)} %get-tuple-element.65), channel_id=1, source_target_pairs={{0,8},{1,9},{2,10},{3,11},{4,12},{5,13},{6,14},{7,15},{8,0},{9,1},... | collective-permute-start | bytes 196616 | tf_op jit(solution)/shard_map/ppermute | solution.py:503
  43.0 2.2 %collective-permute-start.12 = (bf16[256,128]{1,0:T(8,128)(2,1)S(1)}, bf16[256,128]{1,0:T(8,128)(2,1)S(1)}, u32[]{:S(2)}, u32[]{:S(2)}) collective-permute-start(bf16[256,128]{1,0:T(8,128)(2,1)S(1)} %get-tuple-element.66), channel_id=1, source_target_pairs={{0,12},{1,13},{2,14},{3,15},{4,8},{5,9},{6,10},{7,11},{8,4},{9,5},... | collective-permute-start | bytes 196616 | tf_op jit(solution)/shard_map/ppermute | solution.py:503
  45.8 4.4 %collective-permute-start.15 = (bf16[256,128]{1,0:T(8,128)(2,1)S(1)}, bf16[256,128]{1,0:T(8,128)(2,1)S(1)}, u32[]{:S(2)}, u32[]{:S(2)}) collective-permute-start(bf16[256,128]{1,0:T(8,128)(2,1)S(1)} %get-tuple-element.69), channel_id=1, source_target_pairs={{0,24},{1,25},{2,26},{3,27},{4,28},{5,29},{6,30},{7,31},{8,16},{9,... | collective-permute-start | bytes 196616 | tf_op jit(solution)/shard_map/ppermute | solution.py:503
  50.2 1.7 %collective-permute-start.16 = (bf16[256,128]{1,0:T(8,128)(2,1)S(1)}, bf16[256,128]{1,0:T(8,128)(2,1)S(1)}, u32[]{:S(2)}, u32[]{:S(2)}) collective-permute-start(bf16[256,128]{1,0:T(8,128)(2,1)S(1)} %get-tuple-element.70), channel_id=1, source_target_pairs={{0,28},{1,29},{2,30},{3,31},{4,24},{5,25},{6,26},{7,27},{8,20},{9,... | collective-permute-start | bytes 196616 | tf_op jit(solution)/shard_map/ppermute | solution.py:503
  52.0 0.6 collective-permute-done.15.rest_6_
  52.5 4.6 %collective-permute-done.16.rest_7_ = bf16[256,128]{1,0:T(8,128)(2,1)S(1)} collective-permute-done((bf16[256,128]{1,0:T(8,128)(2,1)S(1)}, bf16[256,128]{1,0:T(8,128)(2,1)S(1)}, u32[]{:S(2)}, u32[]{:S(2)}) %collective-permute-start.16) | collective-permute-done | bytes 65568 | tf_op jit(solution)/shard_map/ppermute | solution.py:503
  57.4 2.4 %shard_map.74 = (bf16[2,272,1024]{2,1,0:T(8,128)(2,1)S(1)}, bf16[256,512]{1,0:T(8,128)(2,1)S(1)}) custom-call(bf16[256,512]{1,0:T(8,128)(2,1)S(1)} %shard_map.73.ls.a0, bf16[256,512]{1,0:T(8,128)(2,1)S(1)} %get-tuple-element.46.prim, bf16[256,512]{1,0:T(8,128)(2,1)S(1)} %get-tuple-element.71.second, f32[256,128]{1,0:T(8,128)S(1)} %get-tuple-element.72.spread, ...), custom_call_target="tpu_custom_call" | custom-call | flops 2147483648 | bytes 1048576 | tf_op jit(solution)/shard_map/pallas_call | solution.py:462
  59.8 1.6 %collective-permute-start.25 = (bf16[1024,512]{1,0:T(8,128)(2,1)S(1)}, bf16[1024,512]{1,0:T(8,128)(2,1)S(1)}, u32[]{:S(2)}, u32[]{:S(2)}) collective-permute-start(bf16[1024,512]{1,0:T(8,128)(2,1)S(1)} %get-tuple-element.54.w3), channel_id=1, source_target_pairs={{0,3},{1,2},{2,1},{3,0},{4,7},{5,6},{6,5},{7,4},{8,11},{9,10},{10,... | collective-permute-start | bytes 3145736 | tf_op jit(solution)/shard_map/ppermute | solution.py:503
  61.4 1.7 %shard_map.75.kept = bf16[2,256,1024]{2,1,0:T(8,128)(2,1)S(1)} custom-call(bf16[256,512]{1,0:T(8,128)(2,1)S(1)} %get-tuple-element.74.lp, bf16[256,512]{1,0:T(8,128)(2,1)S(1)} %shard_map.73.ls.a0, bf16[4,1024,512]{2,1,0:T(8,128)(2,1)S(1)} %get-tuple-element.73.wp, bf16[1024,512]{1,0:T(8,128)(2,1)S(1)} %get-tuple-element.52.w2, ...), custom_call_target="tpu_custom_call" | custom-call | flops 2147483648 | bytes 1048576 | tf_op jit(solution)/shard_map/pallas_call | solution.py:462
  63.5 1.0 collective-permute-start.22
  64.5 1.1 collective-permute-start.23
  65.6 0.9 collective-permute-start.27
  66.6 36.3 %collective-permute-done.23.edge = bf16[256,512]{1,0:T(8,128)(2,1)S(1)} collective-permute-done((bf16[256,512]{1,0:T(8,128)(2,1)S(1)}, bf16[256,512]{1,0:T(8,128)(2,1)S(1)}, u32[]{:S(2)}, u32[]{:S(2)}) %collective-permute-start.23) | collective-permute-done | bytes 262176 | tf_op jit(solution)/shard_map/ppermute | solution.py:503
  102.8 1.5 %collective-permute-start.19 = (bf16[256,512]{1,0:T(8,128)(2,1)S(1)}, bf16[256,512]{1,0:T(8,128)(2,1)S(1)}, u32[]{:S(2)}, u32[]{:S(2)}) collective-permute-start(bf16[256,512]{1,0:T(8,128)(2,1)S(1)} %shard_map.73.ls.a0), channel_id=1, source_target_pairs={{0,2},{1,3},{2,0},{3,1},{4,6},{5,7},{6,4},{7,5},{8,10},{9,11},{10,... | collective-permute-start | bytes 786440 | tf_op jit(solution)/shard_map/ppermute | solution.py:503
  104.8 14.3 %collective-permute-done.19.a2 = bf16[256,512]{1,0:T(8,128)(2,1)S(1)} collective-permute-done((bf16[256,512]{1,0:T(8,128)(2,1)S(1)}, bf16[256,512]{1,0:T(8,128)(2,1)S(1)}, u32[]{:S(2)}, u32[]{:S(2)}) %collective-permute-start.19) | collective-permute-done | bytes 262176 | tf_op jit(solution)/shard_map/ppermute | solution.py:503
  119.8 1.2 shard_map.80
  121.0 5.8 %collective-permute-done.24.mirrored = bf16[256,512]{1,0:T(8,128)(2,1)S(1)} collective-permute-done((bf16[256,512]{1,0:T(8,128)(2,1)S(1)}, bf16[256,512]{1,0:T(8,128)(2,1)S(1)}, u32[]{:S(2)}, u32[]{:S(2)}) %collective-permute-start.24) | collective-permute-done | bytes 262176 | tf_op jit(solution)/shard_map/ppermute | solution.py:503
  126.8 0.9 shard_map.78
  (41 shorter events, 3.0 us)
Async XLA Ops:
  0.6 16.4 %collective-permute-start = (bf16[256,1024]{1,0:T(8,128)(2,1)}, bf16[256,1024]{1,0:T(8,128)(2,1)S(1)}, u32[]{:S(2)}, u32[]{:S(2)}) collective-permute-start(bf16[256,1024]{1,0:T(8,128)(2,1)} %c0.1), channel_id=1, source_target_pairs={{0,1},{1,0},{2,3},{3,2},{4,5},{5,4},{6,7},{7,6},{8,9},{9,8},{10,11... | collective-permute-start | bytes 1572872 | tf_op jit(solution)/shard_map/ppermute | solution.py:503
  1.2 15.3 %collective-permute-start.1 = (bf16[256,1024]{1,0:T(8,128)(2,1)}, bf16[256,1024]{1,0:T(8,128)(2,1)S(1)}, u32[]{:S(2)}, u32[]{:S(2)}) collective-permute-start(bf16[256,1024]{1,0:T(8,128)(2,1)} %c0.1), channel_id=1, source_target_pairs={{0,2},{1,3},{2,0},{3,1},{4,6},{5,7},{6,4},{7,5},{8,10},{9,11},{10,... | collective-permute-start | bytes 1572872 | tf_op jit(solution)/shard_map/ppermute | solution.py:503
  3.8 12.7 %copy-start.1 = (s32[2,1]{0,1:T(1,128)S(1)}, s32[2,1]{0,1:T(1,128)}, u32[]{:S(2)}) copy-start(s32[2,1]{0,1:T(1,128)} %param.8) | copy-start | bytes 28
  3.8 13.3 %copy-start = (bf16[256,1024]{1,0:T(8,128)(2,1)S(1)}, bf16[256,1024]{1,0:T(8,128)(2,1)}, u32[]{:S(2)}) copy-start(bf16[256,1024]{1,0:T(8,128)(2,1)} %c0.1) | copy-start | bytes 1572868
  16.5 1.9 %collective-permute-start.2 = (bf16[256,1024]{1,0:T(8,128)(2,1)S(1)}, bf16[256,1024]{1,0:T(8,128)(2,1)S(1)}, u32[]{:S(2)}, u32[]{:S(2)}) collective-permute-start(bf16[256,1024]{1,0:T(8,128)(2,1)S(1)} %collective-permute-done.1.c2), channel_id=1, source_target_pairs={{0,1},{1,0},{2,3},{3,2},{4,5},{5,4},{6,7},{7,6},{8,9},{9,8},{10,11... | collective-permute-start | bytes 1572872 | tf_op jit(solution)/shard_map/ppermute | solution.py:503
  18.7 6.8 %collective-permute-start.3 = (bf16[272,128]{1,0:T(8,128)(2,1)S(1)}, bf16[272,128]{1,0:T(8,128)(2,1)S(1)}, u32[]{:S(2)}, u32[]{:S(2)}) collective-permute-start(bf16[272,128]{1,0:T(8,128)(2,1)S(1)} %get-tuple-element.56), channel_id=1, source_target_pairs={{0,4},{1,5},{2,6},{3,7},{4,0},{5,1},{6,2},{7,3},{8,12},{9,13},{10,... | collective-permute-start | bytes 208904 | tf_op jit(solution)/shard_map/ppermute | solution.py:503
  20.5 9.8 %collective-permute-start.4 = (bf16[272,128]{1,0:T(8,128)(2,1)S(1)}, bf16[272,128]{1,0:T(8,128)(2,1)S(1)}, u32[]{:S(2)}, u32[]{:S(2)}) collective-permute-start(bf16[272,128]{1,0:T(8,128)(2,1)S(1)} %get-tuple-element.57), channel_id=1, source_target_pairs={{0,8},{1,9},{2,10},{3,11},{4,12},{5,13},{6,14},{7,15},{8,0},{9,1},... | collective-permute-start | bytes 208904 | tf_op jit(solution)/shard_map/ppermute | solution.py:503
  23.1 10.2 %collective-permute-start.5 = (bf16[272,128]{1,0:T(8,128)(2,1)S(1)}, bf16[272,128]{1,0:T(8,128)(2,1)S(1)}, u32[]{:S(2)}, u32[]{:S(2)}) collective-permute-start(bf16[272,128]{1,0:T(8,128)(2,1)S(1)} %get-tuple-element.58), channel_id=1, source_target_pairs={{0,12},{1,13},{2,14},{3,15},{4,8},{5,9},{6,10},{7,11},{8,4},{9,5},... | collective-permute-start | bytes 208904 | tf_op jit(solution)/shard_map/ppermute | solution.py:503
  23.1 10.2 %collective-permute-start.6 = (bf16[272,128]{1,0:T(8,128)(2,1)S(1)}, bf16[272,128]{1,0:T(8,128)(2,1)S(1)}, u32[]{:S(2)}, u32[]{:S(2)}) collective-permute-start(bf16[272,128]{1,0:T(8,128)(2,1)S(1)} %get-tuple-element.59), channel_id=1, source_target_pairs={{0,16},{1,17},{2,18},{3,19},{4,20},{5,21},{6,22},{7,23},{8,24},{9,... | collective-permute-start | bytes 208904 | tf_op jit(solution)/shard_map/ppermute | solution.py:503
  25.3 8.1 %collective-permute-start.7 = (bf16[272,128]{1,0:T(8,128)(2,1)S(1)}, bf16[272,128]{1,0:T(8,128)(2,1)S(1)}, u32[]{:S(2)}, u32[]{:S(2)}) collective-permute-start(bf16[272,128]{1,0:T(8,128)(2,1)S(1)} %get-tuple-element.60), channel_id=1, source_target_pairs={{0,20},{1,21},{2,22},{3,23},{4,16},{5,17},{6,18},{7,19},{8,28},{9,... | collective-permute-start | bytes 208904 | tf_op jit(solution)/shard_map/ppermute | solution.py:503
  25.5 10.2 %collective-permute-start.8 = (bf16[272,128]{1,0:T(8,128)(2,1)S(1)}, bf16[272,128]{1,0:T(8,128)(2,1)S(1)}, u32[]{:S(2)}, u32[]{:S(2)}) collective-permute-start(bf16[272,128]{1,0:T(8,128)(2,1)S(1)} %get-tuple-element.61), channel_id=1, source_target_pairs={{0,24},{1,25},{2,26},{3,27},{4,28},{5,29},{6,30},{7,31},{8,16},{9,... | collective-permute-start | bytes 208904 | tf_op jit(solution)/shard_map/ppermute | solution.py:503
  30.3 7.0 %collective-permute-start.9 = (bf16[272,128]{1,0:T(8,128)(2,1)S(1)}, bf16[272,128]{1,0:T(8,128)(2,1)S(1)}, u32[]{:S(2)}, u32[]{:S(2)}) collective-permute-start(bf16[272,128]{1,0:T(8,128)(2,1)S(1)} %get-tuple-element.62), channel_id=1, source_target_pairs={{0,28},{1,29},{2,30},{3,31},{4,24},{5,25},{6,26},{7,27},{8,20},{9,... | collective-permute-start | bytes 208904 | tf_op jit(solution)/shard_map/ppermute | solution.py:503
  40.7 5.1 %collective-permute-start.10 = (bf16[256,128]{1,0:T(8,128)(2,1)S(1)}, bf16[256,128]{1,0:T(8,128)(2,1)S(1)}, u32[]{:S(2)}, u32[]{:S(2)}) collective-permute-start(bf16[256,128]{1,0:T(8,128)(2,1)S(1)} %get-tuple-element.64), channel_id=1, source_target_pairs={{0,4},{1,5},{2,6},{3,7},{4,0},{5,1},{6,2},{7,3},{8,12},{9,13},{10,... | collective-permute-start | bytes 196616 | tf_op jit(solution)/shard_map/ppermute | solution.py:503
  40.8 9.4 %collective-permute-start.11 = (bf16[256,128]{1,0:T(8,128)(2,1)S(1)}, bf16[256,128]{1,0:T(8,128)(2,1)S(1)}, u32[]{:S(2)}, u32[]{:S(2)}) collective-permute-start(bf16[256,128]{1,0:T(8,128)(2,1)S(1)} %get-tuple-element.65), channel_id=1, source_target_pairs={{0,8},{1,9},{2,10},{3,11},{4,12},{5,13},{6,14},{7,15},{8,0},{9,1},... | collective-permute-start | bytes 196616 | tf_op jit(solution)/shard_map/ppermute | solution.py:503
  43.0 8.9 %collective-permute-start.12 = (bf16[256,128]{1,0:T(8,128)(2,1)S(1)}, bf16[256,128]{1,0:T(8,128)(2,1)S(1)}, u32[]{:S(2)}, u32[]{:S(2)}) collective-permute-start(bf16[256,128]{1,0:T(8,128)(2,1)S(1)} %get-tuple-element.66), channel_id=1, source_target_pairs={{0,12},{1,13},{2,14},{3,15},{4,8},{5,9},{6,10},{7,11},{8,4},{9,5},... | collective-permute-start | bytes 196616 | tf_op jit(solution)/shard_map/ppermute | solution.py:503
  45.2 6.8 %collective-permute-start.13 = (bf16[256,128]{1,0:T(8,128)(2,1)S(1)}, bf16[256,128]{1,0:T(8,128)(2,1)S(1)}, u32[]{:S(2)}, u32[]{:S(2)}) collective-permute-start(bf16[256,128]{1,0:T(8,128)(2,1)S(1)} %get-tuple-element.67), channel_id=1, source_target_pairs={{0,16},{1,17},{2,18},{3,19},{4,20},{5,21},{6,22},{7,23},{8,24},{9,... | collective-permute-start | bytes 196616 | tf_op jit(solution)/shard_map/ppermute | solution.py:503
  45.3 6.7 %collective-permute-start.14 = (bf16[256,128]{1,0:T(8,128)(2,1)S(1)}, bf16[256,128]{1,0:T(8,128)(2,1)S(1)}, u32[]{:S(2)}, u32[]{:S(2)}) collective-permute-start(bf16[256,128]{1,0:T(8,128)(2,1)S(1)} %get-tuple-element.68), channel_id=1, source_target_pairs={{0,20},{1,21},{2,22},{3,23},{4,16},{5,17},{6,18},{7,19},{8,28},{9,... | collective-permute-start | bytes 196616 | tf_op jit(solution)/shard_map/ppermute | solution.py:503
  45.8 6.7 %collective-permute-start.15 = (bf16[256,128]{1,0:T(8,128)(2,1)S(1)}, bf16[256,128]{1,0:T(8,128)(2,1)S(1)}, u32[]{:S(2)}, u32[]{:S(2)}) collective-permute-start(bf16[256,128]{1,0:T(8,128)(2,1)S(1)} %get-tuple-element.69), channel_id=1, source_target_pairs={{0,24},{1,25},{2,26},{3,27},{4,28},{5,29},{6,30},{7,31},{8,16},{9,... | collective-permute-start | bytes 196616 | tf_op jit(solution)/shard_map/ppermute | solution.py:503
  50.2 7.0 %collective-permute-start.16 = (bf16[256,128]{1,0:T(8,128)(2,1)S(1)}, bf16[256,128]{1,0:T(8,128)(2,1)S(1)}, u32[]{:S(2)}, u32[]{:S(2)}) collective-permute-start(bf16[256,128]{1,0:T(8,128)(2,1)S(1)} %get-tuple-element.70), channel_id=1, source_target_pairs={{0,28},{1,29},{2,30},{3,31},{4,24},{5,25},{6,26},{7,27},{8,20},{9,... | collective-permute-start | bytes 196616 | tf_op jit(solution)/shard_map/ppermute | solution.py:503
  59.8 3.4 %collective-permute-start.17 = (bf16[2,272,1024]{2,1,0:T(8,128)(2,1)S(1)}, bf16[2,272,1024]{2,1,0:T(8,128)(2,1)S(1)}, u32[]{:S(2)}, u32[]{:S(2)}) collective-permute-start(bf16[2,272,1024]{2,1,0:T(8,128)(2,1)S(1)} %get-tuple-element.75.sent), channel_id=1, source_target_pairs={{0,1},{1,0},{2,3},{3,2},{4,5},{5,4},{6,7},{7,6},{8,9},{9,8},{10,11... | collective-permute-start | bytes 3342344 | tf_op jit(solution)/shard_map/ppermute | solution.py:503
  59.8 66.9 %collective-permute-start.25 = (bf16[1024,512]{1,0:T(8,128)(2,1)S(1)}, bf16[1024,512]{1,0:T(8,128)(2,1)S(1)}, u32[]{:S(2)}, u32[]{:S(2)}) collective-permute-start(bf16[1024,512]{1,0:T(8,128)(2,1)S(1)} %get-tuple-element.54.w3), channel_id=1, source_target_pairs={{0,3},{1,2},{2,1},{3,0},{4,7},{5,6},{6,5},{7,4},{8,11},{9,10},{10,... | collective-permute-start | bytes 3145736 | tf_op jit(solution)/shard_map/ppermute | solution.py:503
  63.3 63.5 %collective-permute-start.21 = (bf16[1024,512]{1,0:T(8,128)(2,1)S(1)}, bf16[1024,512]{1,0:T(8,128)(2,1)S(1)}, u32[]{:S(2)}, u32[]{:S(2)}) collective-permute-start(bf16[1024,512]{1,0:T(8,128)(2,1)S(1)} %get-tuple-element.78.w1), channel_id=1, source_target_pairs={{0,1},{1,0},{2,3},{3,2},{4,5},{5,4},{6,7},{7,6},{8,9},{9,8},{10,11... | collective-permute-start | bytes 3145736 | tf_op jit(solution)/shard_map/ppermute | solution.py:503
  63.5 40.8 %collective-permute-start.22 = (bf16[512,512]{1,0:T(8,128)(2,1)S(1)}, bf16[512,512]{1,0:T(8,128)(2,1)S(1)}, u32[]{:S(2)}, u32[]{:S(2)}) collective-permute-start(bf16[512,512]{1,0:T(8,128)(2,1)S(1)} %get-tuple-element.79), channel_id=1, source_target_pairs={{0,2},{1,3},{2,0},{3,1},{4,6},{5,7},{6,4},{7,5},{8,10},{9,11},{10,... | collective-permute-start | bytes 1572872 | tf_op jit(solution)/shard_map/ppermute | solution.py:503
  64.5 38.3 %collective-permute-start.23 = (bf16[256,512]{1,0:T(8,128)(2,1)S(1)}, bf16[256,512]{1,0:T(8,128)(2,1)S(1)}, u32[]{:S(2)}, u32[]{:S(2)}) collective-permute-start(bf16[256,512]{1,0:T(8,128)(2,1)S(1)} %get-tuple-element.80), channel_id=1, source_target_pairs={{0,2},{1,3},{2,0},{3,1},{4,6},{5,7},{6,4},{7,5},{8,10},{9,11},{10,... | collective-permute-start | bytes 786440 | tf_op jit(solution)/shard_map/ppermute | solution.py:503
  65.6 53.6 %collective-permute-start.27 = (bf16[256,1024]{1,0:T(8,128)(2,1)S(1)}, bf16[256,1024]{1,0:T(8,128)(2,1)S(1)}, u32[]{:S(2)}, u32[]{:S(2)}) collective-permute-start(bf16[256,1024]{1,0:T(8,128)(2,1)S(1)} %get-tuple-element.83), channel_id=1, source_target_pairs={{0,2},{1,3},{2,0},{3,1},{4,6},{5,7},{6,4},{7,5},{8,10},{9,11},{10,... | collective-permute-start | bytes 1572872 | tf_op jit(solution)/shard_map/ppermute | solution.py:503
  102.8 16.3 %collective-permute-start.19 = (bf16[256,512]{1,0:T(8,128)(2,1)S(1)}, bf16[256,512]{1,0:T(8,128)(2,1)S(1)}, u32[]{:S(2)}, u32[]{:S(2)}) collective-permute-start(bf16[256,512]{1,0:T(8,128)(2,1)S(1)} %shard_map.73.ls.a0), channel_id=1, source_target_pairs={{0,2},{1,3},{2,0},{3,1},{4,6},{5,7},{6,4},{7,5},{8,10},{9,11},{10,... | collective-permute-start | bytes 786440 | tf_op jit(solution)/shard_map/ppermute | solution.py:503
  104.3 14.9 %collective-permute-start.26 = (f32[8,256]{1,0:T(8,128)S(1)}, f32[8,256]{1,0:T(8,128)S(1)}, u32[]{:S(2)}, u32[]{:S(2)}) collective-permute-start(f32[8,256]{1,0:T(8,128)S(1)} %get-tuple-element.82.ends), channel_id=1, source_target_pairs={{0,2},{1,3},{2,0},{3,1},{4,6},{5,7},{6,4},{7,5},{8,10},{9,11},{10,... | collective-permute-start | bytes 24584 | tf_op jit(solution)/shard_map/ppermute | solution.py:503
  119.1 7.6 %collective-permute-start.24 = (bf16[256,512]{1,0:T(8,128)(2,1)S(1)}, bf16[256,512]{1,0:T(8,128)(2,1)S(1)}, u32[]{:S(2)}, u32[]{:S(2)}) collective-permute-start(bf16[256,512]{1,0:T(8,128)(2,1)S(1)} %collective-permute-done.23.edge), channel_id=1, source_target_pairs={{0,4},{1,5},{2,6},{3,7},{4,0},{5,1},{6,2},{7,3},{8,12},{9,13},{10,... | collective-permute-start | bytes 786440 | tf_op jit(solution)/shard_map/ppermute | solution.py:503
  119.2 7.5 %collective-permute-start.20 = (bf16[256,512]{1,0:T(8,128)(2,1)S(1)}, bf16[256,512]{1,0:T(8,128)(2,1)S(1)}, u32[]{:S(2)}, u32[]{:S(2)}) collective-permute-start(bf16[256,512]{1,0:T(8,128)(2,1)S(1)} %collective-permute-done.19.a2), channel_id=1, source_target_pairs={{0,1},{1,0},{2,3},{3,2},{4,5},{5,4},{6,7},{7,6},{8,9},{9,8},{10,11... | collective-permute-start | bytes 786440 | tf_op jit(solution)/shard_map/ppermute | solution.py:503
  119.2 7.5 %collective-permute-start.18 = (bf16[256,512]{1,0:T(8,128)(2,1)S(1)}, bf16[256,512]{1,0:T(8,128)(2,1)S(1)}, u32[]{:S(2)}, u32[]{:S(2)}) collective-permute-start(bf16[256,512]{1,0:T(8,128)(2,1)S(1)} %shard_map.73.ls.a0), channel_id=1, source_target_pairs={{0,1},{1,0},{2,3},{3,2},{4,5},{5,4},{6,7},{7,6},{8,9},{9,8},{10,11... | collective-permute-start | bytes 786440 | tf_op jit(solution)/shard_map/ppermute | solution.py:503

commit v9 on v8

--- a/solution.py
+++ b/solution.py
@@ -439,9 +439,10 @@
     leaving.wait()
 
 
-def fold_kernel(kept, got, sent, out, ends):
+def fold_kernel(kept, got, sent, top, bottom, ends):
     rows = kept.shape[1]
-    out[...] = (kept[0].astype(F32) + got[0, :rows, :].astype(F32)).astype(BF16)
+    for out, line in ((top, slice(0, rows // 2)), (bottom, slice(rows // 2, rows))):
+        out[...] = (kept[0, line, :].astype(F32) + got[0, line, :].astype(F32)).astype(BF16)
     mine = sent[0, rows:, :rows].astype(F32)
     theirs = got[0, rows:, :rows].astype(F32)
     total = mine[0:1] + mine[1:2] + theirs[0:1] + theirs[1:2]
@@ -476,13 +477,31 @@
     shrink[...] = 1.0 / (width * root * root * root)
 
 
-def leave_kernel(kept, got, ends, far_ends, far, states, gain, inverse, shrink, grad):
-    rows = states.shape[0]
+def leave_rows(first, kept, got, ends, far_ends, far, states, gain, inverse, shrink):
+    rows, size = states.shape[0], far.shape[0]
+    line = slice(first, first + size)
     row = ends[...] + far_ends[...]
-    term = jnp.broadcast_to(row[:1], (LANES, rows)).T[:, :1]
-    scaled = term * shrink[:, :1]
-    total = kept[1].astype(F32) + got[1, :rows, :].astype(F32) + far[...].astype(F32)
-    grad[...] = (gain[...] * total * inverse[:, :1] - states[...].astype(F32) * scaled).astype(BF16)
+    term = jnp.broadcast_to(row[:1], (LANES, rows)).T[line, :1]
+    scaled = term * shrink[line, :1]
+    total = kept[1, line, :].astype(F32) + got[1, line, :].astype(F32) + far[...].astype(F32)
+    direct = gain[...] * total * inverse[line, :1]
+    return (direct - states[line, :].astype(F32) * scaled).astype(BF16)
+
+
+def leave_top_kernel(*refs):
+    refs[-1][...] = leave_rows(0, *refs[:-1])
+
+
+def leave_kernel(top, *refs):
+    ins, (grad, obuf, sems) = refs[:-3], refs[-3:]
+    size = top.shape[0]
+    early = pltpu.make_async_copy(top, grad.at[:size, :], sems.at[0])
+    early.start()
+    obuf[...] = leave_rows(size, *ins)
+    late = pltpu.make_async_copy(obuf, grad.at[size:, :], sems.at[1])
+    late.start()
+    early.wait()
+    late.wait()
 
 
 def per_device_heads(sizes, segment_in, norm_gains, projections, live_counts, cotangent):
@@ -620,10 +639,14 @@
         16,
         2 << 30,
     )
-    half, ends = call(
-        fold_kernel, (kept, got, sent), [INSIDE] * 3, [((rows, feats), BF16), ((8, rows), F32)]
-    )
-    far = swap(half, 0, 2)
+    top, bottom, ends = call(
+        fold_kernel,
+        (kept, got, sent),
+        [INSIDE] * 3,
+        [((rows // 2, feats), BF16)] * 2 + [((8, rows), F32)],
+    )
+    far_top = swap(top, 0, 2)
+    far_bottom = swap(bottom, 0, 2)
     far_ends = swap(ends, 0, 2)
     own_att, lent_1, ends = lax.optimization_barrier((ls, ws[1], ends))
     lent_1 = swap(lent_1, 0, 1)
@@ -646,12 +669,22 @@
         2 << 30,
         [ANYWHERE],
     )
+    (leave_top,) = call(
+        leave_top_kernel,
+        (kept, got, ends, far_ends, far_top, own_states, own_gain, inverse, shrink),
+        [INSIDE] * 9,
+        [((rows // 2, feats), BF16)],
+    )
     (grad,) = call(
         leave_kernel,
-        (kept, got, ends, far_ends, far, own_states, own_gain, inverse, shrink),
-        [INSIDE] * 9,
+        (
+            *(leave_top, kept, got, ends, far_ends, far_bottom),
+            *(own_states, own_gain, inverse, shrink),
+        ),
+        [INSIDE] * 10,
         [((rows, feats), BF16)],
-        out_specs=[INSIDE],
+        [pltpu.VMEM((rows // 2, feats), BF16), pltpu.SemaphoreType.DMA((2,))],
+        out_specs=[ANYWHERE],
     )
     return (out[None], grad[None])
 

time: 128 us -> 128 us (level)
    ppermute x28 -> x29, starting transfers between devices: 36.4 us -> 37.4 us  [swap(): return lax.ppermute(x, AXES, pairs)]
    ppermute x28 -> x29, waiting for transfers between devices: 70.6 us -> 69.8 us  [swap(): return lax.ppermute(x, AXES, pairs)]
    pallas_call x13 -> x14, Pallas kernels: 19.9 us -> 19.8 us  [call(): pl.pallas_call(body, in_specs=list(specs), out_specs=[INSIDE] * len(outs)...]
  transfers between devices with their start and end apart: 28 -> 29, of which waited for: 10 -> 10; matrix products, arithmetic and copies ran while one was open for 0% -> 0% of each run, Pallas kernels for 10% -> 10%
where the time goes in v9:
time: 128 us
  waiting for transfers between devices  69.8 us (55%)
  starting transfers between devices  37.4 us (29%)
  Pallas kernels  19.8 us (15%)
    ppermute x29, waiting for transfers between devices, swap(): return lax.ppermute(x, AXES, pairs)  69.8 us
    ppermute x29, starting transfers between devices, swap(): return lax.ppermute(x, AXES, pairs)  37.4 us
    pallas_call x14, Pallas kernels, call(): pl.pallas_call(body, in_specs=list(specs), out_specs=[INSIDE] * len(outs)...  19.8 us
  transfers between devices with their start and end apart: 29, of which 10 were waited for; matrix products, arithmetic and copies ran while one was open for 0% of the time, Pallas kernels for 10%

profile of v9, /device:TPU:0, one launch (start us, length us, event | category | flops | bytes accessed | tf_op | source)
XLA Modules:
  0.0 128.0 jit_solution(8668095268867966487)
XLA Ops:
  1.2 2.6 %collective-permute-start.1 = (bf16[256,1024]{1,0:T(8,128)(2,1)}, bf16[256,1024]{1,0:T(8,128)(2,1)S(1)}, u32[]{:S(2)}, u32[]{:S(2)}) collective-permute-start(bf16[256,1024]{1,0:T(8,128)(2,1)} %c0.1), channel_id=1, source_target_pairs={{0,2},{1,3},{2,0},{3,1},{4,6},{5,7},{6,4},{7,5},{8,10},{9,11},{10,... | collective-permute-start | bytes 1572872 | tf_op jit(solution)/shard_map/ppermute | solution.py:522
  3.8 9.1 %shard_map.69 = (bf16[4,1024,512]{2,1,0:T(8,128)(2,1)S(1)}, bf16[1024,512]{1,0:T(8,128)(2,1)S(1)}, bf16[1024,512]{1,0:T(8,128)(2,1)S(1)}, bf16[1024,512]{1,0:T(8...) custom-call(bf16[256,4096]{1,0:T(8,128)(2,1)} %bitcast.12, ...), custom_call_target="tpu_custom_call" | custom-call | flops 8589934592 | bytes 1048576 | tf_op jit(solution)/shard_map/pallas_call | solution.py:463
  12.9 3.6 %collective-permute-done.1.c2 = bf16[256,1024]{1,0:T(8,128)(2,1)S(1)} collective-permute-done((bf16[256,1024]{1,0:T(8,128)(2,1)}, bf16[256,1024]{1,0:T(8,128)(2,1)S(1)}, u32[]{:S(2)}, u32[]{:S(2)}) %collective-permute-start.1) | collective-permute-done | bytes 524320 | tf_op jit(solution)/shard_map/ppermute | solution.py:522
  16.5 0.6 shard_map.68
  17.1 1.3 %collective-permute-done.2.c3 = bf16[256,1024]{1,0:T(8,128)(2,1)S(1)} collective-permute-done((bf16[256,1024]{1,0:T(8,128)(2,1)S(1)}, bf16[256,1024]{1,0:T(8,128)(2,1)S(1)}, u32[]{:S(2)}, u32[]{:S(2)}) %collective-permute-start.2) | collective-permute-done | bytes 524320 | tf_op jit(solution)/shard_map/ppermute | solution.py:522
  18.7 1.9 %collective-permute-start.3 = (bf16[272,128]{1,0:T(8,128)(2,1)S(1)}, bf16[272,128]{1,0:T(8,128)(2,1)S(1)}, u32[]{:S(2)}, u32[]{:S(2)}) collective-permute-start(bf16[272,128]{1,0:T(8,128)(2,1)S(1)} %get-tuple-element.57), channel_id=1, source_target_pairs={{0,4},{1,5},{2,6},{3,7},{4,0},{5,1},{6,2},{7,3},{8,12},{9,13},{10,... | collective-permute-start | bytes 208904 | tf_op jit(solution)/shard_map/ppermute | solution.py:522
  20.5 2.6 %collective-permute-start.4 = (bf16[272,128]{1,0:T(8,128)(2,1)S(1)}, bf16[272,128]{1,0:T(8,128)(2,1)S(1)}, u32[]{:S(2)}, u32[]{:S(2)}) collective-permute-start(bf16[272,128]{1,0:T(8,128)(2,1)S(1)} %get-tuple-element.58), channel_id=1, source_target_pairs={{0,8},{1,9},{2,10},{3,11},{4,12},{5,13},{6,14},{7,15},{8,0},{9,1},... | collective-permute-start | bytes 208904 | tf_op jit(solution)/shard_map/ppermute | solution.py:522
  23.1 2.1 %collective-permute-start.6 = (bf16[272,128]{1,0:T(8,128)(2,1)S(1)}, bf16[272,128]{1,0:T(8,128)(2,1)S(1)}, u32[]{:S(2)}, u32[]{:S(2)}) collective-permute-start(bf16[272,128]{1,0:T(8,128)(2,1)S(1)} %get-tuple-element.60), channel_id=1, source_target_pairs={{0,16},{1,17},{2,18},{3,19},{4,20},{5,21},{6,22},{7,23},{8,24},{9,... | collective-permute-start | bytes 208904 | tf_op jit(solution)/shard_map/ppermute | solution.py:522
  25.5 4.8 %collective-permute-start.8 = (bf16[272,128]{1,0:T(8,128)(2,1)S(1)}, bf16[272,128]{1,0:T(8,128)(2,1)S(1)}, u32[]{:S(2)}, u32[]{:S(2)}) collective-permute-start(bf16[272,128]{1,0:T(8,128)(2,1)S(1)} %get-tuple-element.62), channel_id=1, source_target_pairs={{0,24},{1,25},{2,26},{3,27},{4,28},{5,29},{6,30},{7,31},{8,16},{9,... | collective-permute-start | bytes 208904 | tf_op jit(solution)/shard_map/ppermute | solution.py:522
  30.3 3.0 %collective-permute-start.9 = (bf16[272,128]{1,0:T(8,128)(2,1)S(1)}, bf16[272,128]{1,0:T(8,128)(2,1)S(1)}, u32[]{:S(2)}, u32[]{:S(2)}) collective-permute-start(bf16[272,128]{1,0:T(8,128)(2,1)S(1)} %get-tuple-element.63), channel_id=1, source_target_pairs={{0,28},{1,29},{2,30},{3,31},{4,24},{5,25},{6,26},{7,27},{8,20},{9,... | collective-permute-start | bytes 208904 | tf_op jit(solution)/shard_map/ppermute | solution.py:522
  33.3 2.4 %collective-permute-done.8.rest_6_ = bf16[272,128]{1,0:T(8,128)(2,1)S(1)} collective-permute-done((bf16[272,128]{1,0:T(8,128)(2,1)S(1)}, bf16[272,128]{1,0:T(8,128)(2,1)S(1)}, u32[]{:S(2)}, u32[]{:S(2)}) %collective-permute-start.8) | collective-permute-done | bytes 69664 | tf_op jit(solution)/shard_map/ppermute | solution.py:522
  35.7 1.7 %collective-permute-done.9.rest_7_ = bf16[272,128]{1,0:T(8,128)(2,1)S(1)} collective-permute-done((bf16[272,128]{1,0:T(8,128)(2,1)S(1)}, bf16[272,128]{1,0:T(8,128)(2,1)S(1)}, u32[]{:S(2)}, u32[]{:S(2)}) %collective-permute-start.9) | collective-permute-done | bytes 69664 | tf_op jit(solution)/shard_map/ppermute | solution.py:522
  37.3 3.4 %shard_map.72 = (bf16[256,128]{1,0:T(8,128)(2,1)S(1)}, bf16[256,128]{1,0:T(8,128)(2,1)S(1)}, bf16[256,128]{1,0:T(8,128)(2,1)S(1)}, bf16[256,128]{1,0:T(8,128)(2,...) custom-call(bf16[272,128]{1,0:T(8,128)(2,1)S(1)} %get-tuple-element., ...), custom_call_target="tpu_custom_call" | custom-call | flops 4294967296 | bytes 1048576 | tf_op jit(solution)/shard_map/pallas_call | solution.py:463
  40.8 2.2 %collective-permute-start.11 = (bf16[256,128]{1,0:T(8,128)(2,1)S(1)}, bf16[256,128]{1,0:T(8,128)(2,1)S(1)}, u32[]{:S(2)}, u32[]{:S(2)}) collective-permute-start(bf16[256,128]{1,0:T(8,128)(2,1)S(1)} %get-tuple-element.66), channel_id=1, source_target_pairs={{0,8},{1,9},{2,10},{3,11},{4,12},{5,13},{6,14},{7,15},{8,0},{9,1},... | collective-permute-start | bytes 196616 | tf_op jit(solution)/shard_map/ppermute | solution.py:522
  43.0 2.2 %collective-permute-start.12 = (bf16[256,128]{1,0:T(8,128)(2,1)S(1)}, bf16[256,128]{1,0:T(8,128)(2,1)S(1)}, u32[]{:S(2)}, u32[]{:S(2)}) collective-permute-start(bf16[256,128]{1,0:T(8,128)(2,1)S(1)} %get-tuple-element.67), channel_id=1, source_target_pairs={{0,12},{1,13},{2,14},{3,15},{4,8},{5,9},{6,10},{7,11},{8,4},{9,5},... | collective-permute-start | bytes 196616 | tf_op jit(solution)/shard_map/ppermute | solution.py:522
  45.8 4.4 %collective-permute-start.15 = (bf16[256,128]{1,0:T(8,128)(2,1)S(1)}, bf16[256,128]{1,0:T(8,128)(2,1)S(1)}, u32[]{:S(2)}, u32[]{:S(2)}) collective-permute-start(bf16[256,128]{1,0:T(8,128)(2,1)S(1)} %get-tuple-element.70), channel_id=1, source_target_pairs={{0,24},{1,25},{2,26},{3,27},{4,28},{5,29},{6,30},{7,31},{8,16},{9,... | collective-permute-start | bytes 196616 | tf_op jit(solution)/shard_map/ppermute | solution.py:522
  50.2 1.7 %collective-permute-start.16 = (bf16[256,128]{1,0:T(8,128)(2,1)S(1)}, bf16[256,128]{1,0:T(8,128)(2,1)S(1)}, u32[]{:S(2)}, u32[]{:S(2)}) collective-permute-start(bf16[256,128]{1,0:T(8,128)(2,1)S(1)} %get-tuple-element.71), channel_id=1, source_target_pairs={{0,28},{1,29},{2,30},{3,31},{4,24},{5,25},{6,26},{7,27},{8,20},{9,... | collective-permute-start | bytes 196616 | tf_op jit(solution)/shard_map/ppermute | solution.py:522
  52.0 0.6 collective-permute-done.15.rest_6_
  52.5 4.6 %collective-permute-done.16.rest_7_ = bf16[256,128]{1,0:T(8,128)(2,1)S(1)} collective-permute-done((bf16[256,128]{1,0:T(8,128)(2,1)S(1)}, bf16[256,128]{1,0:T(8,128)(2,1)S(1)}, u32[]{:S(2)}, u32[]{:S(2)}) %collective-permute-start.16) | collective-permute-done | bytes 65568 | tf_op jit(solution)/shard_map/ppermute | solution.py:522
  57.4 2.4 %shard_map.74 = (bf16[2,272,1024]{2,1,0:T(8,128)(2,1)S(1)}, bf16[256,512]{1,0:T(8,128)(2,1)S(1)}) custom-call(bf16[256,512]{1,0:T(8,128)(2,1)S(1)} %shard_map.73.ls.a0, bf16[256,512]{1,0:T(8,128)(2,1)S(1)} %get-tuple-element.47.prim, bf16[256,512]{1,0:T(8,128)(2,1)S(1)} %get-tuple-element.72.second, f32[256,128]{1,0:T(8,128)S(1)} %get-tuple-element.73.spread, ...), custom_call_target="tpu_custom_call" | custom-call | flops 2147483648 | bytes 1048576 | tf_op jit(solution)/shard_map/pallas_call | solution.py:463
  59.8 1.6 %collective-permute-start.25 = (bf16[1024,512]{1,0:T(8,128)(2,1)S(1)}, bf16[1024,512]{1,0:T(8,128)(2,1)S(1)}, u32[]{:S(2)}, u32[]{:S(2)}) collective-permute-start(bf16[1024,512]{1,0:T(8,128)(2,1)S(1)} %get-tuple-element.55.w3), channel_id=1, source_target_pairs={{0,3},{1,2},{2,1},{3,0},{4,7},{5,6},{6,5},{7,4},{8,11},{9,10},{10,... | collective-permute-start | bytes 3145736 | tf_op jit(solution)/shard_map/ppermute | solution.py:522
  61.5 0.6 collective-permute-start.22
  62.1 1.7 %shard_map.75.kept.refs_0_ = bf16[2,256,1024]{2,1,0:T(8,128)(2,1)S(1)} custom-call(bf16[256,512]{1,0:T(8,128)(2,1)S(1)} %get-tuple-element.75.lp, bf16[256,512]{1,0:T(8,128)(2,1)S(1)} %shard_map.73.ls.a0, bf16[4,1024,512]{2,1,0:T(8,128)(2,1)S(1)} %get-tuple-element.74.wp, bf16[1024,512]{1,0:T(8,128)(2,1)S(1)} %get-tuple-element.53.w2, ...), custom_call_target="tpu_custom_call" | custom-call | flops 2147483648 | bytes 1048576 | tf_op jit(solution)/shard_map/pallas_call | solution.py:463
  64.1 1.6 %collective-permute-start.23 = (bf16[256,512]{1,0:T(8,128)(2,1)S(1)}, bf16[256,512]{1,0:T(8,128)(2,1)S(1)}, u32[]{:S(2)}, u32[]{:S(2)}) collective-permute-start(bf16[256,512]{1,0:T(8,128)(2,1)S(1)} %get-tuple-element.81), channel_id=1, source_target_pairs={{0,2},{1,3},{2,0},{3,1},{4,6},{5,7},{6,4},{7,5},{8,10},{9,11},{10,... | collective-permute-start | bytes 786440 | tf_op jit(solution)/shard_map/ppermute | solution.py:522
  66.2 36.7 %collective-permute-done.23.edge = bf16[256,512]{1,0:T(8,128)(2,1)S(1)} collective-permute-done((bf16[256,512]{1,0:T(8,128)(2,1)S(1)}, bf16[256,512]{1,0:T(8,128)(2,1)S(1)}, u32[]{:S(2)}, u32[]{:S(2)}) %collective-permute-start.23) | collective-permute-done | bytes 262176 | tf_op jit(solution)/shard_map/ppermute | solution.py:522
  102.8 1.5 %collective-permute-start.27 = (bf16[128,1024]{1,0:T(8,128)(2,1)S(1)}, bf16[128,1024]{1,0:T(8,128)(2,1)S(1)}, u32[]{:S(2)}, u32[]{:S(2)}) collective-permute-start(bf16[128,1024]{1,0:T(8,128)(2,1)S(1)} %get-tuple-element.84), channel_id=1, source_target_pairs={{0,2},{1,3},{2,0},{3,1},{4,6},{5,7},{6,4},{7,5},{8,10},{9,11},{10,... | collective-permute-start | bytes 786440 | tf_op jit(solution)/shard_map/ppermute | solution.py:522
  104.9 3.6 %collective-permute-done.19.a2 = bf16[256,512]{1,0:T(8,128)(2,1)S(1)} collective-permute-done((bf16[256,512]{1,0:T(8,128)(2,1)S(1)}, bf16[256,512]{1,0:T(8,128)(2,1)S(1)}, u32[]{:S(2)}, u32[]{:S(2)}) %collective-permute-start.19) | collective-permute-done | bytes 262176 | tf_op jit(solution)/shard_map/ppermute | solution.py:522
  108.4 1.5 %collective-permute-start.26 = (f32[8,256]{1,0:T(8,128)S(1)}, f32[8,256]{1,0:T(8,128)S(1)}, u32[]{:S(2)}, u32[]{:S(2)}) collective-permute-start(f32[8,256]{1,0:T(8,128)S(1)} %get-tuple-element.83.refs_2_), channel_id=1, source_target_pairs={{0,2},{1,3},{2,0},{3,1},{4,6},{5,7},{6,4},{7,5},{8,10},{9,11},{10,... | collective-permute-start | bytes 24584 | tf_op jit(solution)/shard_map/ppermute | solution.py:522
  110.0 9.3 %collective-permute-done.26.refs_3_ = f32[8,256]{1,0:T(8,128)S(1)} collective-permute-done((f32[8,256]{1,0:T(8,128)S(1)}, f32[8,256]{1,0:T(8,128)S(1)}, u32[]{:S(2)}, u32[]{:S(2)}) %collective-permute-start.26) | collective-permute-done | bytes 8224 | tf_op jit(solution)/shard_map/ppermute | solution.py:522
  120.0 0.9 shard_map.81
  121.0 6.0 %collective-permute-done.24.mirrored = bf16[256,512]{1,0:T(8,128)(2,1)S(1)} collective-permute-done((bf16[256,512]{1,0:T(8,128)(2,1)S(1)}, bf16[256,512]{1,0:T(8,128)(2,1)S(1)}, u32[]{:S(2)}, u32[]{:S(2)}) %collective-permute-start.24) | collective-permute-done | bytes 262176 | tf_op jit(solution)/shard_map/ppermute | solution.py:522
  127.0 0.9 shard_map.78
  (44 shorter events, 4.1 us)
Async XLA Ops:
  0.6 16.4 %collective-permute-start = (bf16[256,1024]{1,0:T(8,128)(2,1)}, bf16[256,1024]{1,0:T(8,128)(2,1)S(1)}, u32[]{:S(2)}, u32[]{:S(2)}) collective-permute-start(bf16[256,1024]{1,0:T(8,128)(2,1)} %c0.1), channel_id=1, source_target_pairs={{0,1},{1,0},{2,3},{3,2},{4,5},{5,4},{6,7},{7,6},{8,9},{9,8},{10,11... | collective-permute-start | bytes 1572872 | tf_op jit(solution)/shard_map/ppermute | solution.py:522
  1.2 15.3 %collective-permute-start.1 = (bf16[256,1024]{1,0:T(8,128)(2,1)}, bf16[256,1024]{1,0:T(8,128)(2,1)S(1)}, u32[]{:S(2)}, u32[]{:S(2)}) collective-permute-start(bf16[256,1024]{1,0:T(8,128)(2,1)} %c0.1), channel_id=1, source_target_pairs={{0,2},{1,3},{2,0},{3,1},{4,6},{5,7},{6,4},{7,5},{8,10},{9,11},{10,... | collective-permute-start | bytes 1572872 | tf_op jit(solution)/shard_map/ppermute | solution.py:522
  3.8 12.7 %copy-start.1 = (s32[2,1]{0,1:T(1,128)S(1)}, s32[2,1]{0,1:T(1,128)}, u32[]{:S(2)}) copy-start(s32[2,1]{0,1:T(1,128)} %param.8) | copy-start | bytes 28
  3.8 13.3 %copy-start = (bf16[256,1024]{1,0:T(8,128)(2,1)S(1)}, bf16[256,1024]{1,0:T(8,128)(2,1)}, u32[]{:S(2)}) copy-start(bf16[256,1024]{1,0:T(8,128)(2,1)} %c0.1) | copy-start | bytes 1572868
  16.5 1.9 %collective-permute-start.2 = (bf16[256,1024]{1,0:T(8,128)(2,1)S(1)}, bf16[256,1024]{1,0:T(8,128)(2,1)S(1)}, u32[]{:S(2)}, u32[]{:S(2)}) collective-permute-start(bf16[256,1024]{1,0:T(8,128)(2,1)S(1)} %collective-permute-done.1.c2), channel_id=1, source_target_pairs={{0,1},{1,0},{2,3},{3,2},{4,5},{5,4},{6,7},{7,6},{8,9},{9,8},{10,11... | collective-permute-start | bytes 1572872 | tf_op jit(solution)/shard_map/ppermute | solution.py:522
  18.7 6.8 %collective-permute-start.3 = (bf16[272,128]{1,0:T(8,128)(2,1)S(1)}, bf16[272,128]{1,0:T(8,128)(2,1)S(1)}, u32[]{:S(2)}, u32[]{:S(2)}) collective-permute-start(bf16[272,128]{1,0:T(8,128)(2,1)S(1)} %get-tuple-element.57), channel_id=1, source_target_pairs={{0,4},{1,5},{2,6},{3,7},{4,0},{5,1},{6,2},{7,3},{8,12},{9,13},{10,... | collective-permute-start | bytes 208904 | tf_op jit(solution)/shard_map/ppermute | solution.py:522
  20.5 9.8 %collective-permute-start.4 = (bf16[272,128]{1,0:T(8,128)(2,1)S(1)}, bf16[272,128]{1,0:T(8,128)(2,1)S(1)}, u32[]{:S(2)}, u32[]{:S(2)}) collective-permute-start(bf16[272,128]{1,0:T(8,128)(2,1)S(1)} %get-tuple-element.58), channel_id=1, source_target_pairs={{0,8},{1,9},{2,10},{3,11},{4,12},{5,13},{6,14},{7,15},{8,0},{9,1},... | collective-permute-start | bytes 208904 | tf_op jit(solution)/shard_map/ppermute | solution.py:522
  23.1 10.2 %collective-permute-start.5 = (bf16[272,128]{1,0:T(8,128)(2,1)S(1)}, bf16[272,128]{1,0:T(8,128)(2,1)S(1)}, u32[]{:S(2)}, u32[]{:S(2)}) collective-permute-start(bf16[272,128]{1,0:T(8,128)(2,1)S(1)} %get-tuple-element.59), channel_id=1, source_target_pairs={{0,12},{1,13},{2,14},{3,15},{4,8},{5,9},{6,10},{7,11},{8,4},{9,5},... | collective-permute-start | bytes 208904 | tf_op jit(solution)/shard_map/ppermute | solution.py:522
  23.1 10.2 %collective-permute-start.6 = (bf16[272,128]{1,0:T(8,128)(2,1)S(1)}, bf16[272,128]{1,0:T(8,128)(2,1)S(1)}, u32[]{:S(2)}, u32[]{:S(2)}) collective-permute-start(bf16[272,128]{1,0:T(8,128)(2,1)S(1)} %get-tuple-element.60), channel_id=1, source_target_pairs={{0,16},{1,17},{2,18},{3,19},{4,20},{5,21},{6,22},{7,23},{8,24},{9,... | collective-permute-start | bytes 208904 | tf_op jit(solution)/shard_map/ppermute | solution.py:522
  25.3 8.1 %collective-permute-start.7 = (bf16[272,128]{1,0:T(8,128)(2,1)S(1)}, bf16[272,128]{1,0:T(8,128)(2,1)S(1)}, u32[]{:S(2)}, u32[]{:S(2)}) collective-permute-start(bf16[272,128]{1,0:T(8,128)(2,1)S(1)} %get-tuple-element.61), channel_id=1, source_target_pairs={{0,20},{1,21},{2,22},{3,23},{4,16},{5,17},{6,18},{7,19},{8,28},{9,... | collective-permute-start | bytes 208904 | tf_op jit(solution)/shard_map/ppermute | solution.py:522
  25.5 10.2 %collective-permute-start.8 = (bf16[272,128]{1,0:T(8,128)(2,1)S(1)}, bf16[272,128]{1,0:T(8,128)(2,1)S(1)}, u32[]{:S(2)}, u32[]{:S(2)}) collective-permute-start(bf16[272,128]{1,0:T(8,128)(2,1)S(1)} %get-tuple-element.62), channel_id=1, source_target_pairs={{0,24},{1,25},{2,26},{3,27},{4,28},{5,29},{6,30},{7,31},{8,16},{9,... | collective-permute-start | bytes 208904 | tf_op jit(solution)/shard_map/ppermute | solution.py:522
  30.3 7.0 %collective-permute-start.9 = (bf16[272,128]{1,0:T(8,128)(2,1)S(1)}, bf16[272,128]{1,0:T(8,128)(2,1)S(1)}, u32[]{:S(2)}, u32[]{:S(2)}) collective-permute-start(bf16[272,128]{1,0:T(8,128)(2,1)S(1)} %get-tuple-element.63), channel_id=1, source_target_pairs={{0,28},{1,29},{2,30},{3,31},{4,24},{5,25},{6,26},{7,27},{8,20},{9,... | collective-permute-start | bytes 208904 | tf_op jit(solution)/shard_map/ppermute | solution.py:522
  40.7 5.1 %collective-permute-start.10 = (bf16[256,128]{1,0:T(8,128)(2,1)S(1)}, bf16[256,128]{1,0:T(8,128)(2,1)S(1)}, u32[]{:S(2)}, u32[]{:S(2)}) collective-permute-start(bf16[256,128]{1,0:T(8,128)(2,1)S(1)} %get-tuple-element.65), channel_id=1, source_target_pairs={{0,4},{1,5},{2,6},{3,7},{4,0},{5,1},{6,2},{7,3},{8,12},{9,13},{10,... | collective-permute-start | bytes 196616 | tf_op jit(solution)/shard_map/ppermute | solution.py:522
  40.8 9.4 %collective-permute-start.11 = (bf16[256,128]{1,0:T(8,128)(2,1)S(1)}, bf16[256,128]{1,0:T(8,128)(2,1)S(1)}, u32[]{:S(2)}, u32[]{:S(2)}) collective-permute-start(bf16[256,128]{1,0:T(8,128)(2,1)S(1)} %get-tuple-element.66), channel_id=1, source_target_pairs={{0,8},{1,9},{2,10},{3,11},{4,12},{5,13},{6,14},{7,15},{8,0},{9,1},... | collective-permute-start | bytes 196616 | tf_op jit(solution)/shard_map/ppermute | solution.py:522
  43.0 8.9 %collective-permute-start.12 = (bf16[256,128]{1,0:T(8,128)(2,1)S(1)}, bf16[256,128]{1,0:T(8,128)(2,1)S(1)}, u32[]{:S(2)}, u32[]{:S(2)}) collective-permute-start(bf16[256,128]{1,0:T(8,128)(2,1)S(1)} %get-tuple-element.67), channel_id=1, source_target_pairs={{0,12},{1,13},{2,14},{3,15},{4,8},{5,9},{6,10},{7,11},{8,4},{9,5},... | collective-permute-start | bytes 196616 | tf_op jit(solution)/shard_map/ppermute | solution.py:522
  45.2 6.8 %collective-permute-start.13 = (bf16[256,128]{1,0:T(8,128)(2,1)S(1)}, bf16[256,128]{1,0:T(8,128)(2,1)S(1)}, u32[]{:S(2)}, u32[]{:S(2)}) collective-permute-start(bf16[256,128]{1,0:T(8,128)(2,1)S(1)} %get-tuple-element.68), channel_id=1, source_target_pairs={{0,16},{1,17},{2,18},{3,19},{4,20},{5,21},{6,22},{7,23},{8,24},{9,... | collective-permute-start | bytes 196616 | tf_op jit(solution)/shard_map/ppermute | solution.py:522
  45.3 6.7 %collective-permute-start.14 = (bf16[256,128]{1,0:T(8,128)(2,1)S(1)}, bf16[256,128]{1,0:T(8,128)(2,1)S(1)}, u32[]{:S(2)}, u32[]{:S(2)}) collective-permute-start(bf16[256,128]{1,0:T(8,128)(2,1)S(1)} %get-tuple-element.69), channel_id=1, source_target_pairs={{0,20},{1,21},{2,22},{3,23},{4,16},{5,17},{6,18},{7,19},{8,28},{9,... | collective-permute-start | bytes 196616 | tf_op jit(solution)/shard_map/ppermute | solution.py:522
  45.8 6.7 %collective-permute-start.15 = (bf16[256,128]{1,0:T(8,128)(2,1)S(1)}, bf16[256,128]{1,0:T(8,128)(2,1)S(1)}, u32[]{:S(2)}, u32[]{:S(2)}) collective-permute-start(bf16[256,128]{1,0:T(8,128)(2,1)S(1)} %get-tuple-element.70), channel_id=1, source_target_pairs={{0,24},{1,25},{2,26},{3,27},{4,28},{5,29},{6,30},{7,31},{8,16},{9,... | collective-permute-start | bytes 196616 | tf_op jit(solution)/shard_map/ppermute | solution.py:522
  50.2 7.0 %collective-permute-start.16 = (bf16[256,128]{1,0:T(8,128)(2,1)S(1)}, bf16[256,128]{1,0:T(8,128)(2,1)S(1)}, u32[]{:S(2)}, u32[]{:S(2)}) collective-permute-start(bf16[256,128]{1,0:T(8,128)(2,1)S(1)} %get-tuple-element.71), channel_id=1, source_target_pairs={{0,28},{1,29},{2,30},{3,31},{4,24},{5,25},{6,26},{7,27},{8,20},{9,... | collective-permute-start | bytes 196616 | tf_op jit(solution)/shard_map/ppermute | solution.py:522
  59.8 4.1 %collective-permute-start.17 = (bf16[2,272,1024]{2,1,0:T(8,128)(2,1)S(1)}, bf16[2,272,1024]{2,1,0:T(8,128)(2,1)S(1)}, u32[]{:S(2)}, u32[]{:S(2)}) collective-permute-start(bf16[2,272,1024]{2,1,0:T(8,128)(2,1)S(1)} %get-tuple-element.76.sent), channel_id=1, source_target_pairs={{0,1},{1,0},{2,3},{3,2},{4,5},{5,4},{6,7},{7,6},{8,9},{9,8},{10,11... | collective-permute-start | bytes 3342344 | tf_op jit(solution)/shard_map/ppermute | solution.py:522
  59.8 67.1 %collective-permute-start.25 = (bf16[1024,512]{1,0:T(8,128)(2,1)S(1)}, bf16[1024,512]{1,0:T(8,128)(2,1)S(1)}, u32[]{:S(2)}, u32[]{:S(2)}) collective-permute-start(bf16[1024,512]{1,0:T(8,128)(2,1)S(1)} %get-tuple-element.55.w3), channel_id=1, source_target_pairs={{0,3},{1,2},{2,1},{3,0},{4,7},{5,6},{6,5},{7,4},{8,11},{9,10},{10,... | collective-permute-start | bytes 3145736 | tf_op jit(solution)/shard_map/ppermute | solution.py:522
  61.5 42.8 %collective-permute-start.22 = (bf16[512,512]{1,0:T(8,128)(2,1)S(1)}, bf16[512,512]{1,0:T(8,128)(2,1)S(1)}, u32[]{:S(2)}, u32[]{:S(2)}) collective-permute-start(bf16[512,512]{1,0:T(8,128)(2,1)S(1)} %get-tuple-element.80), channel_id=1, source_target_pairs={{0,2},{1,3},{2,0},{3,1},{4,6},{5,7},{6,4},{7,5},{8,10},{9,11},{10,... | collective-permute-start | bytes 1572872 | tf_op jit(solution)/shard_map/ppermute | solution.py:522
  64.0 63.0 %collective-permute-start.21 = (bf16[1024,512]{1,0:T(8,128)(2,1)S(1)}, bf16[1024,512]{1,0:T(8,128)(2,1)S(1)}, u32[]{:S(2)}, u32[]{:S(2)}) collective-permute-start(bf16[1024,512]{1,0:T(8,128)(2,1)S(1)} %get-tuple-element.79.w1), channel_id=1, source_target_pairs={{0,1},{1,0},{2,3},{3,2},{4,5},{5,4},{6,7},{7,6},{8,9},{9,8},{10,11... | collective-permute-start | bytes 3145736 | tf_op jit(solution)/shard_map/ppermute | solution.py:522
  64.1 38.8 %collective-permute-start.23 = (bf16[256,512]{1,0:T(8,128)(2,1)S(1)}, bf16[256,512]{1,0:T(8,128)(2,1)S(1)}, u32[]{:S(2)}, u32[]{:S(2)}) collective-permute-start(bf16[256,512]{1,0:T(8,128)(2,1)S(1)} %get-tuple-element.81), channel_id=1, source_target_pairs={{0,2},{1,3},{2,0},{3,1},{4,6},{5,7},{6,4},{7,5},{8,10},{9,11},{10,... | collective-permute-start | bytes 786440 | tf_op jit(solution)/shard_map/ppermute | solution.py:522
  65.6 42.8 %collective-permute-start.19 = (bf16[256,512]{1,0:T(8,128)(2,1)S(1)}, bf16[256,512]{1,0:T(8,128)(2,1)S(1)}, u32[]{:S(2)}, u32[]{:S(2)}) collective-permute-start(bf16[256,512]{1,0:T(8,128)(2,1)S(1)} %shard_map.73.ls.a0), channel_id=1, source_target_pairs={{0,2},{1,3},{2,0},{3,1},{4,6},{5,7},{6,4},{7,5},{8,10},{9,11},{10,... | collective-permute-start | bytes 786440 | tf_op jit(solution)/shard_map/ppermute | solution.py:522
  102.8 16.4 %collective-permute-start.27 = (bf16[128,1024]{1,0:T(8,128)(2,1)S(1)}, bf16[128,1024]{1,0:T(8,128)(2,1)S(1)}, u32[]{:S(2)}, u32[]{:S(2)}) collective-permute-start(bf16[128,1024]{1,0:T(8,128)(2,1)S(1)} %get-tuple-element.84), channel_id=1, source_target_pairs={{0,2},{1,3},{2,0},{3,1},{4,6},{5,7},{6,4},{7,5},{8,10},{9,11},{10,... | collective-permute-start | bytes 786440 | tf_op jit(solution)/shard_map/ppermute | solution.py:522
  104.3 14.9 %collective-permute-start.28 = (bf16[128,1024]{1,0:T(8,128)(2,1)S(1)}, bf16[128,1024]{1,0:T(8,128)(2,1)S(1)}, u32[]{:S(2)}, u32[]{:S(2)}) collective-permute-start(bf16[128,1024]{1,0:T(8,128)(2,1)S(1)} %get-tuple-element.89), channel_id=1, source_target_pairs={{0,2},{1,3},{2,0},{3,1},{4,6},{5,7},{6,4},{7,5},{8,10},{9,11},{10,... | collective-permute-start | bytes 786440 | tf_op jit(solution)/shard_map/ppermute | solution.py:522
  108.4 10.8 %collective-permute-start.26 = (f32[8,256]{1,0:T(8,128)S(1)}, f32[8,256]{1,0:T(8,128)S(1)}, u32[]{:S(2)}, u32[]{:S(2)}) collective-permute-start(f32[8,256]{1,0:T(8,128)S(1)} %get-tuple-element.83.refs_2_), channel_id=1, source_target_pairs={{0,2},{1,3},{2,0},{3,1},{4,6},{5,7},{6,4},{7,5},{8,10},{9,11},{10,... | collective-permute-start | bytes 24584 | tf_op jit(solution)/shard_map/ppermute | solution.py:522
  119.3 7.7 %collective-permute-start.24 = (bf16[256,512]{1,0:T(8,128)(2,1)S(1)}, bf16[256,512]{1,0:T(8,128)(2,1)S(1)}, u32[]{:S(2)}, u32[]{:S(2)}) collective-permute-start(bf16[256,512]{1,0:T(8,128)(2,1)S(1)} %collective-permute-done.23.edge), channel_id=1, source_target_pairs={{0,4},{1,5},{2,6},{3,7},{4,0},{5,1},{6,2},{7,3},{8,12},{9,13},{10,... | collective-permute-start | bytes 786440 | tf_op jit(solution)/shard_map/ppermute | solution.py:522
  119.3 7.7 %collective-permute-start.20 = (bf16[256,512]{1,0:T(8,128)(2,1)S(1)}, bf16[256,512]{1,0:T(8,128)(2,1)S(1)}, u32[]{:S(2)}, u32[]{:S(2)}) collective-permute-start(bf16[256,512]{1,0:T(8,128)(2,1)S(1)} %collective-permute-done.19.a2), channel_id=1, source_target_pairs={{0,1},{1,0},{2,3},{3,2},{4,5},{5,4},{6,7},{7,6},{8,9},{9,8},{10,11... | collective-permute-start | bytes 786440 | tf_op jit(solution)/shard_map/ppermute | solution.py:522
  119.3 7.7 %collective-permute-start.18 = (bf16[256,512]{1,0:T(8,128)(2,1)S(1)}, bf16[256,512]{1,0:T(8,128)(2,1)S(1)}, u32[]{:S(2)}, u32[]{:S(2)}) collective-permute-start(bf16[256,512]{1,0:T(8,128)(2,1)S(1)} %shard_map.73.ls.a0), channel_id=1, source_target_pairs={{0,1},{1,0},{2,3},{3,2},{4,5},{5,4},{6,7},{7,6},{8,9},{9,8},{10,11... | collective-permute-start | bytes 786440 | tf_op jit(solution)/shard_map/ppermute | solution.py:522
